TPU v7x, 32 devices: a whole 2x2x4 slice. The times are simulated.
32 devices in a mesh: groups: 2 (over x), row: 16 (over z, y, core).
Axes of the slice: x: 2, y: 2, z: 4, core: 2. Of those that a mesh axis runs over, the one named last changes fastest.
Arguments:
- gated_hidden_rows: bfloat16 [2, 384, 28672], P(None, 'groups', 'row'), parts along dimension 1, may hold values from -6 to 6
- down_base_weight: bfloat16 [8192, 28672], P('row'), may hold values from -0.03125 to 0.03125
- adapter_input_factor: bfloat16 [8, 64, 28672], P(None, None, 'row'), may hold values from -0.03125 to 0.03125
- adapter_output_weight: bfloat16 [8, 64, 8192], P(None, None, 'row'), may hold values from -0.75 to 0.75
- request_adapter_index: int32 [2, 384], P(None, 'groups'), parts along dimension 1, may hold values from 0 to 7, as said below
Outputs:
- ffn_out: bfloat16 [2, 384, 8192], P(None, 'groups', 'row'), parts along dimension 1
There are 2 independent parts, one for each index of `groups`. A program takes and returns all parts, laid end to end along the dimension named above; an argument that names none is the same for every part. Nothing has to cross between parts.
Inputs may be any that keep to these rules, and one draw needn't show every extreme that they name: `request_adapter_index`: each entry names one of the 8 adapters; adapter 0 is the resident adapter that is merged into the weights.
All inputs are finite; a program needn't handle non-finite values.
Results may differ from a plain program's by a relative error of at most 0.0038.
Values may be sent and summed in bfloat16 or wider, within the bound.
No kernel may reach another device: no remote copies, remote signals or barrier semaphores. Data moves between devices by JAX's collectives and lax.ppermute only.
A program may use at most 128 MiB of HBM per device.

v0:
```python
import jax
import jax.numpy as jnp
from jax import lax
from jax.sharding import PartitionSpec as P


def select_both(project_rows, adapter_labels, request_count, rank_index):
    choose = (
        adapter_labels[:, None] == jnp.arange(request_count, dtype=jnp.int32)[None, :]
    ).astype(jnp.float32)
    total = project_rows.shape[0]
    own = jnp.sum(
        project_rows.reshape(total, request_count, rank_index) * choose[:, :, None], axis=1
    )
    return jnp.concatenate([own, project_rows[:, :rank_index]], axis=1)


def expand_factor(shrunk_rows, adapter_labels, adapter_output_weight):
    request_count = adapter_output_weight.shape[0]
    rank_index = adapter_output_weight.shape[1]
    total = shrunk_rows.shape[0]
    choose = (
        adapter_labels[:, None] == jnp.arange(request_count, dtype=jnp.int32)[None, :]
    ).astype(jnp.float32)
    spread = (choose[:, :, None] * shrunk_rows[:, None, :rank_index].astype(jnp.float32)).reshape(
        total, request_count * rank_index
    )
    operand = jnp.concatenate([spread.astype(jnp.bfloat16), shrunk_rows[:, rank_index:]], axis=1)
    stacked_weights = jnp.concatenate(
        [
            adapter_output_weight.reshape(
                request_count * rank_index, adapter_output_weight.shape[2]
            ),
            -adapter_output_weight[0],
        ],
        axis=0,
    )
    return jnp.dot(operand, stacked_weights, preferred_element_type=jnp.float32)


def local(
    gated_hidden_rows,
    down_base_weight,
    adapter_input_factor,
    adapter_output_weight,
    request_adapter_index,
):
    steps, requests, device_units = gated_hidden_rows.shape
    request_count = adapter_input_factor.shape[0]
    rank_index = adapter_input_factor.shape[1]
    flattened_rows = gated_hidden_rows.reshape(steps * requests, device_units)
    adapter_labels = request_adapter_index.reshape(steps * requests)
    project_rows = jnp.dot(
        flattened_rows,
        adapter_input_factor.reshape(request_count * rank_index, device_units).T,
        preferred_element_type=jnp.float32,
    )
    summand = select_both(project_rows, adapter_labels, request_count, rank_index)
    summed = lax.psum(summand, "row")
    keep = (adapter_labels != 0).astype(jnp.float32)[:, None]
    shrunk_rows = (summed * keep).astype(jnp.bfloat16)
    resident_sum = summed[:, rank_index:]
    contract = (((1,), (1,)), ((), ()))
    highest = lax.Precision.HIGHEST
    base = lax.dot_general(
        lax.all_gather(flattened_rows, "row", axis=1, tiled=True),
        down_base_weight,
        contract,
        preferred_element_type=jnp.float32,
    )
    base = base + jnp.dot(
        resident_sum, adapter_output_weight[0].astype(jnp.float32), precision=highest
    )
    adapter_update = expand_factor(shrunk_rows, adapter_labels, adapter_output_weight)
    return (base + adapter_update).astype(jnp.bfloat16).reshape(steps, requests, base.shape[1])


def solution(mesh):
    placed = (
        P(None, "groups", "row"),
        P("row", None),
        P(None, None, "row"),
        P(None, None, "row"),
        P(None, "groups"),
    )
    return jax.shard_map(
        local, mesh=mesh, in_specs=placed, out_specs=P(None, "groups", "row"), check_vma=False
    )
```

profile of v0, /device:TPU:0, one launch (start us, length us, event | category | flops | bytes accessed | tf_op | source)
XLA Modules:
  0.0 250.0 jit_solution(5993442033640294135)
XLA Ops:
  6.5 0.0 copy-start
  6.5 0.0 all-reduce.2.cloned.1.call-start
  6.5 0.9 eq.12
  7.4 0.6 copy-done
  8.1 2.5 fusion.13
  10.5 0.1 multiply_reduce_fusion
  10.6 0.7 pad_maximum_fusion
  11.3 0.0 all-reduce.2.cloned.1.call-update
  11.3 0.0 all-gather.2.cloned.1.call-start
  11.4 0.7 all-gather.2.cloned.1.call-update
  12.1 0.8 bitcast_negate_fusion
  12.9 92.2 %all-reduce.2.cloned.1.call-done = f32[384,128]{0,1:T(8,128)} async-done(((f32[384,128]{0,1:T(8,128)}), f32[384,128]{0,1:T(8,128)}) %all-reduce.2.cloned.1.call-update) | async-done | bytes 196624 | tf_op jit(solution)/shard_map/psum | solution.py:59
  105.1 0.9 multiply_convert_fusion.1
  106.1 0.1 multiply_convert_fusion
  106.1 0.0 copy-start.1
  106.1 113.3 %all-gather.2.cloned.1.call-done = bf16[384,28672]{1,0:T(8,128)(2,1)} async-done(((bf16[384,1792]{1,0:T(8,128)(2,1)}), bf16[384,28672]{1,0:T(8,128)(2,1)}) %all-gather.2.cloned.1.call-update) | async-done | bytes 22020112 | tf_op jit(solution)/shard_map/all_gather | solution.py:66
  219.4 20.0 %fusion.12 = f32[384,512]{1,0:T(8,128)S(1)} fusion(bf16[384,28672]{1,0:T(8,128)(2,1)} %all-gather.2.cloned.1.call-done, bf16[512,28672]{1,0:T(8,128)(2,1)} %param.6), kind=kOutput, calls=%fused_computation.22 | convolution fusion | flops 11274289152 | bytes 52166656 | tf_op jit(solution)/shard_map/dot_general | solution.py:65
  239.5 0.0 copy-done.1
  239.5 1.4 convolution_add_fusion.1
  240.8 2.3 fusion
  (4 shorter events, 0.0 us)
Async XLA Ops:
  6.5 1.5 copy-start
  6.5 98.5 %all-reduce.2.cloned.1.call-start = ((), (), s32[]{:S(2)}) async-start(), calls=%async_computation.1 | async-start | bytes 393216 | tf_op jit(solution)/shard_map/psum | solution.py:59
  11.3 208.1 %all-gather.2.cloned.1.call-start = ((), (), s32[]{:S(2)}) async-start(), calls=%async_computation | async-start | bytes 23396352 | tf_op jit(solution)/shard_map/all_gather | solution.py:66
  106.1 133.4 %copy-start.1 = (f32[384,128]{0,1:T(8,128)S(1)}, f32[384,128]{0,1:T(8,128)}, u32[]{:S(2)}) copy-start(f32[384,128]{0,1:T(8,128)} %all-reduce.2.cloned.1.call-done) | copy-start | bytes 589828
Sparse Core Ops, SparseCore 0:
  11.4 93.6 all-reduce.1
  106.6 112.7 all-gather.1
where the time goes:
time: 250 us
  waiting for transfers between devices  206 us (82%)
  matrix products  26.2 us (10%)
  between operations  13.5 us (5%)
  other arithmetic  2.62 us (1%)
    all_gather x1, waiting for transfers between devices, local(): lax.all_gather(flattened_rows, 'row', axis=1, tiled=True)  113 us
    psum x1, waiting for transfers between devices, local(): summed = lax.psum(summand, 'row')  92.2 us
    dot_general x1, matrix products, local(): lax.dot_general(lax.all_gather(flattened_rows, 'row', axis=1, tiled=True)...  20 us
  transfers between devices with their start and end apart: 2, of which 2 were waited for; matrix products, arithmetic and copies ran while one was open for 1% of the time, Pallas kernels for 0%

commit v1 on v0

v1 whole, which is shorter than its diff:
```python
import jax
import jax.numpy as jnp
import numpy as np
from jax import lax
from jax.experimental import pallas as pl
from jax.experimental.pallas import tpu as pltpu
from jax.sharding import PartitionSpec as P


LANES = 128


def chip_ring(mesh):
    line = mesh.devices.reshape(mesh.devices.shape[0], -1)[0]
    chips = {}
    for at, device in enumerate(line):
        place = tuple(getattr(device, "coords", (at, 0, 0)))
        chips.setdefault(place, []).append(at)
    places = list(chips)
    if len({len(c) for c in chips.values()}) != 1:
        return [[at] for at in range(len(line))]
    used = [k for k in range(len(places[0])) if len({p[k] for p in places}) > 1]
    if len(used) == 2:
        sizes = [len({p[k] for p in places}) for k in used]
        if 2 in sizes and sizes[0] * sizes[1] == len(places):
            short = used[sizes.index(2)]
            long = used[0] if short == used[1] else used[1]
            low = min(p[short] for p in places)
            up = sorted((p for p in places if p[short] == low), key=lambda p: p[long])
            down = sorted((p for p in places if p[short] != low), key=lambda p: -p[long])
            places = up + down
    return [chips[p] for p in places]


def labels_onehot(adapter_labels, count):
    return adapter_labels[:, None] == jnp.arange(count, dtype=jnp.int32)[None, :]


def select_both(project_rows, adapter_labels, count, rank):
    choose = labels_onehot(adapter_labels, count).astype(jnp.float32)
    total = project_rows.shape[0]
    own = jnp.sum(project_rows.reshape(total, count, rank) * choose[:, :, None], axis=1)
    return jnp.concatenate([own, project_rows[:, :rank]], axis=1)


def expand_factor(shrunk_rows, adapter_labels, adapter_output_weight):
    count, rank, width = adapter_output_weight.shape
    total = shrunk_rows.shape[0]
    choose = labels_onehot(adapter_labels, count).astype(jnp.float32)
    spread = (choose[:, :, None] * shrunk_rows[:, None, :rank].astype(jnp.float32)).reshape(
        total, count * rank
    )
    operand = jnp.concatenate([spread.astype(jnp.bfloat16), shrunk_rows[:, rank:]], axis=1)
    stacked = jnp.concatenate(
        [adapter_output_weight.reshape(count * rank, width), -adapter_output_weight[0]], axis=0
    )
    return jnp.dot(operand, stacked, preferred_element_type=jnp.float32)


def sum_over_row(summand, axis_size):
    rows, cols = summand.shape
    if rows % axis_size:
        return lax.psum(summand, "row")
    parts = lax.all_to_all(summand, "row", 0, 0, tiled=True)
    mine = jnp.sum(parts.reshape(axis_size, rows // axis_size, cols), axis=0)
    spread = jnp.broadcast_to(mine[None], (axis_size,) + mine.shape).reshape(rows, cols)
    return lax.all_to_all(spread, "row", 0, 0, tiled=True)


def chunk_matmul(chunks, starts, first, weight, before, extra, out_dtype):
    count = len(chunks)
    rows, units = chunks[0].shape
    features = weight.shape[0]
    added = [a for a in (before, extra) if a is not None]

    def body(starts_ref, *refs):
        x_refs = refs[:count]
        w_ref = refs[count]
        add_refs = refs[count + 1 : count + 1 + len(added)]
        out_ref, x_buf, w_buf, x_sem, w_sem = refs[count + 1 + len(added) :]
        copies = []
        for k in range(count):
            start = pl.multiple_of(starts_ref[first + k] * LANES, LANES)
            cx = pltpu.make_async_copy(x_refs[k], x_buf.at[k], x_sem.at[k])
            cw = pltpu.make_async_copy(w_ref.at[:, pl.ds(start, units)], w_buf.at[k], w_sem.at[k])
            cw.start()
            cx.start()
            copies.append((cx, cw))
        total = None
        for k in range(count):
            copies[k][1].wait()
            copies[k][0].wait()
            part = lax.dot_general(
                x_buf[k], w_buf[k], (((1,), (1,)), ((), ())), preferred_element_type=jnp.float32
            )
            total = part if total is None else total + part
        for ref in add_refs:
            total = total + ref[...]
        out_ref[...] = total.astype(out_dtype)

    anywhere = pl.BlockSpec(memory_space=pl.ANY)
    vmem = pl.BlockSpec(memory_space=pltpu.VMEM)
    return pl.pallas_call(
        body,
        out_shape=jax.ShapeDtypeStruct((rows, features), out_dtype),
        in_specs=[pl.BlockSpec(memory_space=pltpu.SMEM)]
        + [anywhere] * (count + 1)
        + [vmem] * len(added),
        out_specs=vmem,
        scratch_shapes=[
            pltpu.VMEM((count, rows, units), jnp.bfloat16),
            pltpu.VMEM((count, features, units), jnp.bfloat16),
            pltpu.SemaphoreType.DMA((count,)),
            pltpu.SemaphoreType.DMA((count,)),
        ],
        cost_estimate=pl.CostEstimate(
            flops=2 * count * rows * units * features,
            transcendentals=0,
            bytes_accessed=2 * count * units * (rows + features) + 8 * rows * features,
        ),
        compiler_params=pltpu.CompilerParams(vmem_limit_bytes=48 << 20),
    )(starts, *chunks, weight, *added)


def solution(mesh):
    axis_size = mesh.shape["row"]
    ring = chip_ring(mesh)
    chips, cores = len(ring), len(ring[0])
    forward = [(ring[p][c], ring[(p + 1) % chips][c]) for p in range(chips) for c in range(cores)]
    backward = [(b, a) for a, b in forward]
    partner = [(members[c], members[1 - c]) for members in ring for c in range(cores)] if cores == 2 else []

    def local(
        gated_hidden_rows,
        down_base_weight,
        adapter_input_factor,
        adapter_output_weight,
        request_adapter_index,
    ):
        steps, requests, device_units = gated_hidden_rows.shape
        count, rank, _ = adapter_input_factor.shape
        features = down_base_weight.shape[0]
        total = steps * requests
        flat = gated_hidden_rows.reshape(total, device_units)
        adapter_labels = request_adapter_index.reshape(total)
        project_rows = jnp.dot(
            flat,
            adapter_input_factor.reshape(count * rank, device_units).T,
            preferred_element_type=jnp.float32,
        )
        summed = sum_over_row(
            select_both(project_rows, adapter_labels, count, rank), axis_size
        )
        keep = (adapter_labels != 0).astype(jnp.float32)[:, None]
        shrunk_rows = (summed * keep).astype(jnp.bfloat16)
        extra = jnp.dot(
            summed[:, rank:],
            adapter_output_weight[0].astype(jnp.float32),
            precision=lax.Precision.HIGHEST,
        ) + expand_factor(shrunk_rows, adapter_labels, adapter_output_weight)

        if cores != 2 or chips < 2 or chips % 2 or device_units % (2 * LANES):
            base = lax.dot_general(
                lax.all_gather(flat, "row", axis=1, tiled=True),
                down_base_weight,
                (((1,), (1,)), ((), ())),
                preferred_element_type=jnp.float32,
            )
            return (base + extra).astype(jnp.bfloat16).reshape(steps, requests, features)

        half = device_units // 2
        where = []

        def start_of(offset, other, part):
            where.append((offset, other, part))
            return len(where) - 1

        own = [flat[:, :half], flat[:, half:]]
        hops = 2 * (chips // 2) - 1
        ups, downs = list(own), list(own)
        found = []
        for part in range(2):
            other = lax.ppermute(own[part], "row", partner)
            found += [(own[part], start_of(0, False, part)), (other, start_of(0, True, part))]
        batches = [found]
        for s in range(hops):
            up_part, down_part, d = s % 2, 1 - s % 2, s // 2 + 1
            ups[up_part] = lax.ppermute(ups[up_part], "row", forward)
            downs[down_part] = lax.ppermute(downs[down_part], "row", backward)
            found = []
            for data, offset, part in (
                (ups[up_part], -d, up_part), (downs[down_part], d, down_part)
            ):
                other = lax.ppermute(data, "row", partner)
                found.append((data, start_of(offset, False, part)))
                found.append((other, start_of(offset, True, part)))
            batches.append(found)
        order = [where[at] for found in batches for _, at in found]
        table = np.zeros((axis_size, len(order)), np.int32)
        for p, members in enumerate(ring):
            for c, at in enumerate(members):
                for k, (offset, other, part) in enumerate(order):
                    source = ring[(p + offset) % chips][1 - c if other else c]
                    table[at, k] = (source * 2 + part) * (half // LANES)
        starts = jnp.asarray(table)[lax.axis_index("row")]
        acc = None
        done = 0
        for k, found in enumerate(batches):
            last = k == len(batches) - 1
            acc = chunk_matmul(
                [data for data, _ in found],
                starts,
                done,
                down_base_weight,
                acc,
                extra if last else None,
                jnp.bfloat16 if last else jnp.float32,
            )
            done += len(found)
        return acc.reshape(steps, requests, features)

    placed = (
        P(None, "groups", "row"),
        P("row", None),
        P(None, None, "row"),
        P(None, None, "row"),
        P(None, "groups"),
    )

    return jax.shard_map(
        local, mesh=mesh, in_specs=placed, out_specs=P(None, "groups", "row"), check_vma=False
    )
```

time: 250 us -> 166 us (0.66)
  waiting for transfers between devices: 206 us -> 77.6 us
  Pallas kernels: 0 us -> 35.3 us
  starting transfers between devices: 0.04 us -> 30.7 us
  matrix products: 26.2 us -> 6.08 us
  between operations: 13.5 us -> 0.43 us
  local copies, waits for them, and re-layouts: 1.52 us -> 10.3 us
    all_gather x1 -> x0, waiting for transfers between devices: 113 us -> none  [local(): lax.all_gather(flattened_rows, 'row', axis=1, tiled=True)]
    psum x1 -> x0, waiting for transfers between devices: 92.2 us -> none  [local(): summed = lax.psum(summand, 'row')]
    ppermute x0 -> x30, waiting for transfers between devices: none -> 62.3 us  [the longest x7 56.9 us: local(): ups[up_part] = lax.ppermute(ups[up_part], 'row', forward)]
    pallas_call x0 -> x8, Pallas kernels: none -> 35.3 us  [chunk_matmul(): pl.pallas_call(body, out_shape=jax.ShapeDtypeStruct((rows, features), out...]
    dot_general x4 -> x3, matrix products: 26.2 us -> 6.08 us  [the longest x1 3.14 us: local(): jnp.dot(flat, adapter_input_factor.reshape(count * rank, device_units).T,...]
    ppermute x0 -> x30, starting transfers between devices: none -> 18.2 us  [the longest x7 11.4 us: local(): ups[up_part] = lax.ppermute(ups[up_part], 'row', forward)]
    all_to_all x0 -> x2, waiting for transfers between devices: none -> 15.3 us  [the longest x1 15.3 us: sum_over_row(): parts = lax.all_to_all(summand, 'row', 0, 0, tiled=True)]
    all_to_all x0 -> x2, starting transfers between devices: none -> 12.5 us  [the longest x1 6.55 us: sum_over_row(): parts = lax.all_to_all(summand, 'row', 0, 0, tiled=True)]
  transfers between devices with their start and end apart: 2 -> 32, of which waited for: 2 -> 11; matrix products, arithmetic and copies ran while one was open for 1% -> 9% of each run, Pallas kernels for 0% -> 18%
where the time goes in v1:
time: 166 us; the launch traced here: 165 us
  waiting for transfers between devices  77.6 us (47%)
  Pallas kernels  35.3 us (21%)
  starting transfers between devices  30.7 us (18%)
  local copies, waits for them, and re-layouts  10.3 us (6%)
  matrix products  6.08 us (4%)
  other arithmetic  4.51 us (3%)
    ppermute x7, waiting for transfers between devices, local(): ups[up_part] = lax.ppermute(ups[up_part], 'row', forward)  56.9 us
    pallas_call x8, Pallas kernels, chunk_matmul(): pl.pallas_call(body, out_shape=jax.ShapeDtypeStruct((rows, features), out...  35.3 us
    all_to_all x1, waiting for transfers between devices, sum_over_row(): parts = lax.all_to_all(summand, 'row', 0, 0, tiled=True)  15.3 us
    ppermute x7, starting transfers between devices, local(): ups[up_part] = lax.ppermute(ups[up_part], 'row', forward)  11.4 us
    all_to_all x1, starting transfers between devices, sum_over_row(): parts = lax.all_to_all(summand, 'row', 0, 0, tiled=True)  6.55 us
    all_to_all x1, starting transfers between devices, sum_over_row(): return lax.all_to_all(spread, 'row', 0, 0, tiled=True)  5.93 us
    ppermute x7, waiting for transfers between devices, local(): downs[down_part] = lax.ppermute(downs[down_part], 'row', backward)  5.34 us
    ppermute x7, starting transfers between devices, local(): downs[down_part] = lax.ppermute(downs[down_part], 'row', backward)  4.76 us
  transfers between devices with their start and end apart: 32, of which 11 were waited for; matrix products, arithmetic and copies ran while one was open for 9% of the time, Pallas kernels for 18%

profile of v1, /device:TPU:0, one launch (start us, length us, event | category | flops | bytes accessed | tf_op | source)
XLA Modules:
  0.0 164.9 jit_solution(1479214893922863785)
XLA Ops:
  0.0 1.6 fusion.12
  1.6 0.6 collective-permute-start.28
  2.1 2.6 %collective-permute-start = (bf16[384,896]{1,0:T(8,128)(2,1)S(1)}, bf16[384,896]{1,0:T(8,128)(2,1)}, u32[]{:S(2)}, u32[]{:S(2)}) collective-permute-start(bf16[384,896]{1,0:T(8,128)(2,1)S(1)} %get-tuple-element.6.refs_0_), channel_id=1, source_target_pairs={{0,4},{1,5},{4,8},{5,9},{8,12},{9,13},{12,14},{13,15},{14,10},{15,... | collective-permute-start | bytes 2064392 | tf_op jit(solution)/shard_map/ppermute | solution.py:188
  4.9 1.9 %collective-permute-start.10 = (bf16[384,896]{1,0:T(8,128)(2,1)S(1)}, bf16[384,896]{1,0:T(8,128)(2,1)}, u32[]{:S(2)}, u32[]{:S(2)}) collective-permute-start(bf16[384,896]{1,0:T(8,128)(2,1)S(1)} %get-tuple-element.5.refs_2_), channel_id=1, source_target_pairs={{0,4},{1,5},{4,8},{5,9},{8,12},{9,13},{12,14},{13,15},{14,10},{15,... | collective-permute-start | bytes 2064392 | tf_op jit(solution)/shard_map/ppermute | solution.py:188
  6.8 0.9 copy-done.5
  7.8 13.3 %collective-permute-done.refs_0_ = bf16[384,896]{1,0:T(8,128)(2,1)} collective-permute-done((bf16[384,896]{1,0:T(8,128)(2,1)S(1)}, bf16[384,896]{1,0:T(8,128)(2,1)}, u32[]{:S(2)}, u32[]{:S(2)}) %collective-permute-start) | collective-permute-done | bytes 688160 | tf_op jit(solution)/shard_map/ppermute | solution.py:188
  21.1 2.1 %collective-permute-done.5.refs_2_ = bf16[384,896]{1,0:T(8,128)(2,1)} collective-permute-done((bf16[384,896]{1,0:T(8,128)(2,1)S(1)}, bf16[384,896]{1,0:T(8,128)(2,1)}, u32[]{:S(2)}, u32[]{:S(2)}) %collective-permute-start.5) | collective-permute-done | bytes 688160 | tf_op jit(solution)/shard_map/ppermute | solution.py:189
  23.3 1.6 collective-permute-start.1
  24.8 11.0 %collective-permute-done.10.refs_0_ = bf16[384,896]{1,0:T(8,128)(2,1)} collective-permute-done((bf16[384,896]{1,0:T(8,128)(2,1)S(1)}, bf16[384,896]{1,0:T(8,128)(2,1)}, u32[]{:S(2)}, u32[]{:S(2)}) %collective-permute-start.10) | collective-permute-done | bytes 688160 | tf_op jit(solution)/shard_map/ppermute | solution.py:188
  35.9 3.1 %fusion.13 = f32[384,512]{1,0:T(8,128)} fusion(bf16[384,1792]{1,0:T(8,128)(2,1)} %bitcast.21, bf16[512,1792]{1,0:T(8,128)(2,1)S(1)} %bitcast.16), kind=kOutput, calls=%fused_computation.23 | convolution fusion | flops 704643072 | bytes 3997696 | tf_op jit(solution)/shard_map/dot_general | solution.py:146
  39.0 2.0 %collective-permute-start.6 = (bf16[384,896]{1,0:T(8,128)(2,1)}, bf16[384,896]{1,0:T(8,128)(2,1)}, u32[]{:S(2)}, u32[]{:S(2)}) collective-permute-start(bf16[384,896]{1,0:T(8,128)(2,1)} %collective-permute-done.5.refs_2_), channel_id=1, source_target_pairs={{4,0},{5,1},{8,4},{9,5},{12,8},{13,9},{14,12},{15,13},{10,14},{11,... | collective-permute-start | bytes 2064392 | tf_op jit(solution)/shard_map/ppermute | solution.py:189
  41.4 2.4 %copy.15 = f32[384,512]{0,1:T(8,128)} copy(f32[384,512]{1,0:T(8,128)} %fusion.13) | data formatting | bytes 1572864 | tf_op jit(solution)/shard_map/dot_general | solution.py:146
  43.7 1.2 multiply_reduce_fusion
  44.9 0.8 copy.16
  45.8 1.7 %collective-permute-start.15 = (bf16[384,896]{1,0:T(8,128)(2,1)}, bf16[384,896]{1,0:T(8,128)(2,1)}, u32[]{:S(2)}, u32[]{:S(2)}) collective-permute-start(bf16[384,896]{1,0:T(8,128)(2,1)} %collective-permute-done.14.refs_2_), channel_id=1, source_target_pairs={{4,0},{5,1},{8,4},{9,5},{12,8},{13,9},{14,12},{15,13},{10,14},{11,... | collective-permute-start | bytes 2064392 | tf_op jit(solution)/shard_map/ppermute | solution.py:189
  47.4 3.1 %collective-permute-done.1.refs_0_ = bf16[384,896]{1,0:T(8,128)(2,1)} collective-permute-done((bf16[384,896]{1,0:T(8,128)(2,1)}, bf16[384,896]{1,0:T(8,128)(2,1)}, u32[]{:S(2)}, u32[]{:S(2)}) %collective-permute-start.1) | collective-permute-done | bytes 688160 | tf_op jit(solution)/shard_map/ppermute | solution.py:188
  50.6 1.7 %pad_maximum_fusion = f32[384,128]{1,0:T(8,128)} fusion(f32[384,64]{1,0:T(8,128)S(1)} %slice-done, f32[384,64]{1,0:T(8,128)} %copy.16), kind=kLoop, calls=%fused_computation.11 | loop fusion | flops 49152 | bytes 393216 | tf_op jit(solution)/shard_map/concatenate | solution.py:43
  52.3 6.5 %all-to-all-start = ((f32[16,24,128]{2,1,0:T(8,128)}), f32[16,24,128]{2,1,0:T(8,128)S(1)}, u32[]{:S(2)}, u32[]{:S(2)}) async-start(f32[16,24,128]{2,1,0:T(8,128)} %bitcast.22), calls=%async_computation | async-start | bytes 393216 | tf_op jit(solution)/shard_map/all_to_all | solution.py:64
  58.9 1.5 bitcast_negate_fusion
  60.4 15.3 %all-to-all-done = f32[16,24,128]{2,1,0:T(8,128)S(1)} async-done(((f32[16,24,128]{2,1,0:T(8,128)}), f32[16,24,128]{2,1,0:T(8,128)S(1)}, u32[]{:S(2)}, u32[]{:S(2)}) %all-to-all-start) | async-done | bytes 196640 | tf_op jit(solution)/shard_map/all_to_all | solution.py:64
  75.7 0.7 broadcast_in_dim.2
  76.4 5.9 %all-to-all-start.1 = ((f32[16,24,128]{2,1,0:T(8,128)}), f32[16,24,128]{2,1,0:T(8,128)S(1)}, u32[]{:S(2)}, u32[]{:S(2)}) async-start(f32[16,24,128]{2,1,0:T(8,128)} %broadcast_in_dim.2), calls=%async_computation.1 | async-start | bytes 393216 | tf_op jit(solution)/shard_map/all_to_all | solution.py:67
  82.4 0.8 copy-done.3
  83.2 1.9 %collective-permute-start.2 = (bf16[384,896]{1,0:T(8,128)(2,1)}, bf16[384,896]{1,0:T(8,128)(2,1)}, u32[]{:S(2)}, u32[]{:S(2)}) collective-permute-start(bf16[384,896]{1,0:T(8,128)(2,1)} %collective-permute-done.1.refs_0_), channel_id=1, source_target_pairs={{0,4},{1,5},{4,8},{5,9},{8,12},{9,13},{12,14},{13,15},{14,10},{15,... | collective-permute-start | bytes 2064392 | tf_op jit(solution)/shard_map/ppermute | solution.py:188
  85.2 0.5 collective-permute-start.20
  85.9 0.7 dynamic-slice_bitcast_fusion.starts_ref
  86.5 1.1 copy-done.2
  87.6 1.1 copy-done.6
  88.7 4.1 %shard_map.64.refs_5_ = f32[384,512]{1,0:T(8,128)S(1)} custom-call(s32[32]{0:T(128)S(1)} %dynamic-slice_bitcast_fusion.starts_ref, bf16[384,896]{1,0:T(8,128)(2,1)S(1)} %copy-done.2, bf16[384,896]{1,0:T(8,128)(2,1)S(1)} %copy-done.6, bf16[384,896]{1,0:T(8,128)(2,1)S(1)} %get-tuple-element.5.refs_2_, bf16[384,896]{1,0:T(8,128)(2,1)} %collective-permute-done.29.refs_3_, ...), custom_call_target="tpu_custom_call" | custom-call | flops 1409286144 | bytes 7995392 | tf_op jit(solution)/shard_map/pallas_call | solution.py:103
  93.0 1.9 %collective-permute-start.12 = (bf16[384,896]{1,0:T(8,128)(2,1)}, bf16[384,896]{1,0:T(8,128)(2,1)S(1)}, u32[]{:S(2)}, u32[]{:S(2)}) collective-permute-start(bf16[384,896]{1,0:T(8,128)(2,1)} %collective-permute-done.11.refs_0_), channel_id=1, source_target_pairs={{0,4},{1,5},{4,8},{5,9},{8,12},{9,13},{12,14},{13,15},{14,10},{15,... | collective-permute-start | bytes 2064392 | tf_op jit(solution)/shard_map/ppermute | solution.py:188
  95.1 8.0 %collective-permute-done.2.refs_0_ = bf16[384,896]{1,0:T(8,128)(2,1)} collective-permute-done((bf16[384,896]{1,0:T(8,128)(2,1)}, bf16[384,896]{1,0:T(8,128)(2,1)}, u32[]{:S(2)}, u32[]{:S(2)}) %collective-permute-start.2) | collective-permute-done | bytes 688160 | tf_op jit(solution)/shard_map/ppermute | solution.py:188
  103.1 1.4 collective-permute-start.3
  104.5 0.3 collective-permute-done.7.refs_2_
  104.8 0.6 collective-permute-start.8
  105.5 1.4 fusion.6
  106.8 10.9 %collective-permute-done.12.refs_0_ = bf16[384,896]{1,0:T(8,128)(2,1)S(1)} collective-permute-done((bf16[384,896]{1,0:T(8,128)(2,1)}, bf16[384,896]{1,0:T(8,128)(2,1)S(1)}, u32[]{:S(2)}, u32[]{:S(2)}) %collective-permute-start.12) | collective-permute-done | bytes 688160 | tf_op jit(solution)/shard_map/ppermute | solution.py:188
  117.7 1.7 %collective-permute-done.16.refs_2_ = bf16[384,896]{1,0:T(8,128)(2,1)S(1)} collective-permute-done((bf16[384,896]{1,0:T(8,128)(2,1)}, bf16[384,896]{1,0:T(8,128)(2,1)S(1)}, u32[]{:S(2)}, u32[]{:S(2)}) %collective-permute-start.16) | collective-permute-done | bytes 688160 | tf_op jit(solution)/shard_map/ppermute | solution.py:189
  119.4 0.5 collective-permute-start.17
  120.0 1.6 convolution_add_fusion.refs_6_
  121.6 10.6 %collective-permute-done.3.refs_0_ = bf16[384,896]{1,0:T(8,128)(2,1)S(1)} collective-permute-done((bf16[384,896]{1,0:T(8,128)(2,1)}, bf16[384,896]{1,0:T(8,128)(2,1)S(1)}, u32[]{:S(2)}, u32[]{:S(2)}) %collective-permute-start.3) | collective-permute-done | bytes 688160 | tf_op jit(solution)/shard_map/ppermute | solution.py:188
  132.2 1.3 collective-permute-done.8.refs_2_
  133.4 4.5 %shard_map.65.refs_5_ = f32[384,512]{1,0:T(8,128)S(1)} custom-call(s32[32]{0:T(128)S(1)} %dynamic-slice_bitcast_fusion.starts_ref, bf16[384,896]{1,0:T(8,128)(2,1)} %collective-permute-done.refs_0_, bf16[384,896]{1,0:T(8,128)(2,1)} %collective-permute-done.26.refs_1_, bf16[384,896]{1,0:T(8,128)(2,1)} %collective-permute-done.5.refs_2_, ...), custom_call_target="tpu_custom_call" | custom-call | flops 1409286144 | bytes 7995392 | tf_op jit(solution)/shard_map/pallas_call | solution.py:103
  137.9 4.5 %shard_map.66.refs_5_ = f32[384,512]{1,0:T(8,128)S(1)} custom-call(s32[32]{0:T(128)S(1)} %dynamic-slice_bitcast_fusion.starts_ref, bf16[384,896]{1,0:T(8,128)(2,1)} %collective-permute-done.10.refs_0_, bf16[384,896]{1,0:T(8,128)(2,1)} %collective-permute-done.24.refs_1_, bf16[384,896]{1,0:T(8,128)(2,1)} %collective-permute-done.14.refs_2_, ...), custom_call_target="tpu_custom_call" | custom-call | flops 1409286144 | bytes 7995392 | tf_op jit(solution)/shard_map/pallas_call | solution.py:103
  142.4 4.5 %shard_map.67.refs_5_ = f32[384,512]{1,0:T(8,128)S(1)} custom-call(s32[32]{0:T(128)S(1)} %dynamic-slice_bitcast_fusion.starts_ref, bf16[384,896]{1,0:T(8,128)(2,1)} %collective-permute-done.1.refs_0_, bf16[384,896]{1,0:T(8,128)(2,1)} %collective-permute-done.22.refs_1_, bf16[384,896]{1,0:T(8,128)(2,1)} %collective-permute-done.6.refs_2_, ...), custom_call_target="tpu_custom_call" | custom-call | flops 1409286144 | bytes 7995392 | tf_op jit(solution)/shard_map/pallas_call | solution.py:103
  146.9 4.5 %shard_map.68.refs_5_ = f32[384,512]{1,0:T(8,128)S(1)} custom-call(s32[32]{0:T(128)S(1)} %dynamic-slice_bitcast_fusion.starts_ref, bf16[384,896]{1,0:T(8,128)(2,1)} %collective-permute-done.11.refs_0_, bf16[384,896]{1,0:T(8,128)(2,1)} %collective-permute-done.20.refs_1_, bf16[384,896]{1,0:T(8,128)(2,1)} %collective-permute-done.15.refs_2_, ...), custom_call_target="tpu_custom_call" | custom-call | flops 1409286144 | bytes 7995392 | tf_op jit(solution)/shard_map/pallas_call | solution.py:103
  151.4 4.3 %shard_map.69.refs_5_ = f32[384,512]{1,0:T(8,128)S(1)} custom-call(s32[32]{0:T(128)S(1)} %dynamic-slice_bitcast_fusion.starts_ref, bf16[384,896]{1,0:T(8,128)(2,1)} %collective-permute-done.2.refs_0_, bf16[384,896]{1,0:T(8,128)(2,1)S(1)} %collective-permute-done.18.refs_1_, bf16[384,896]{1,0:T(8,128)(2,1)} %collective-permute-done.7.refs_2_, ...), custom_call_target="tpu_custom_call" | custom-call | flops 1409286144 | bytes 7995392 | tf_op jit(solution)/shard_map/pallas_call | solution.py:103
  155.7 4.1 %shard_map.70.refs_5_ = f32[384,512]{1,0:T(8,128)S(1)} custom-call(s32[32]{0:T(128)S(1)} %dynamic-slice_bitcast_fusion.starts_ref, bf16[384,896]{1,0:T(8,128)(2,1)S(1)} %collective-permute-done.12.refs_0_, bf16[384,896]{1,0:T(8,128)(2,1)S(1)} %collective-permute-done.13.refs_1_, bf16[384,896]{1,0:T(8,128)(2,1)S(1)} %collective-permute-done.16.refs_2_, ...), custom_call_target="tpu_custom_call" | custom-call | flops 1409286144 | bytes 7995392 | tf_op jit(solution)/shard_map/pallas_call | solution.py:103
  159.8 4.9 %shard_map.71 = bf16[384,512]{1,0:T(8,128)(2,1)} custom-call(s32[32]{0:T(128)S(1)} %dynamic-slice_bitcast_fusion.starts_ref, bf16[384,896]{1,0:T(8,128)(2,1)S(1)} %collective-permute-done.3.refs_0_, bf16[384,896]{1,0:T(8,128)(2,1)S(1)} %collective-permute-done.4.refs_1_, bf16[384,896]{1,0:T(8,128)(2,1)S(1)} %collective-permute-done.8.refs_2_, ...), custom_call_target="tpu_custom_call" | custom-call | flops 1409286144 | bytes 7995392 | tf_op jit(solution)/shard_map/pallas_call | solution.py:103
  (61 shorter events, 1.5 us)
Async XLA Ops:
  0.0 35.9 %copy-start = (bf16[8,64,1792]{2,1,0:T(8,128)(2,1)S(1)}, bf16[8,64,1792]{2,1,0:T(8,128)(2,1)}, u32[]{:S(2)}) copy-start(bf16[8,64,1792]{2,1,0:T(8,128)(2,1)} %param.8) | copy-start | bytes 5505028
  0.0 23.2 %copy-start.7 = (s32[2,192]{1,0:T(2,128)S(1)}, s32[2,192]{1,0:T(2,128)}, u32[]{:S(2)}) copy-start(s32[2,192]{1,0:T(2,128)} %param.10) | copy-start | bytes 4612
  1.6 37.4 %copy-start.1 = (bf16[384,896]{1,0:T(8,128)(2,1)}, bf16[384,896]{1,0:T(8,128)(2,1)S(1)}, u32[]{:S(2)}) copy-start(bf16[384,896]{1,0:T(8,128)(2,1)S(1)} %get-tuple-element.6.refs_0_) | copy-start | bytes 2064388
  1.6 5.2 %collective-permute-start.28 = (bf16[384,896]{1,0:T(8,128)(2,1)S(1)}, bf16[384,896]{1,0:T(8,128)(2,1)S(1)}, u32[]{:S(2)}, u32[]{:S(2)}) collective-permute-start(bf16[384,896]{1,0:T(8,128)(2,1)S(1)} %get-tuple-element.6.refs_0_), channel_id=1, source_target_pairs={{0,1},{1,0},{4,5},{5,4},{8,9},{9,8},{12,13},{13,12},{14,15},{15,14... | collective-permute-start | bytes 2064392 | tf_op jit(solution)/shard_map/ppermute | solution.py:183
  2.1 19.0 %collective-permute-start = (bf16[384,896]{1,0:T(8,128)(2,1)S(1)}, bf16[384,896]{1,0:T(8,128)(2,1)}, u32[]{:S(2)}, u32[]{:S(2)}) collective-permute-start(bf16[384,896]{1,0:T(8,128)(2,1)S(1)} %get-tuple-element.6.refs_0_), channel_id=1, source_target_pairs={{0,4},{1,5},{4,8},{5,9},{8,12},{9,13},{12,14},{13,15},{14,10},{15,... | collective-permute-start | bytes 2064392 | tf_op jit(solution)/shard_map/ppermute | solution.py:188
  4.8 18.4 %collective-permute-start.5 = (bf16[384,896]{1,0:T(8,128)(2,1)S(1)}, bf16[384,896]{1,0:T(8,128)(2,1)}, u32[]{:S(2)}, u32[]{:S(2)}) collective-permute-start(bf16[384,896]{1,0:T(8,128)(2,1)S(1)} %get-tuple-element.5.refs_2_), channel_id=1, source_target_pairs={{4,0},{5,1},{8,4},{9,5},{12,8},{13,9},{14,12},{15,13},{10,14},{11,... | collective-permute-start | bytes 2064392 | tf_op jit(solution)/shard_map/ppermute | solution.py:189
  4.8 18.5 %collective-permute-start.29 = (bf16[384,896]{1,0:T(8,128)(2,1)S(1)}, bf16[384,896]{1,0:T(8,128)(2,1)}, u32[]{:S(2)}, u32[]{:S(2)}) collective-permute-start(bf16[384,896]{1,0:T(8,128)(2,1)S(1)} %get-tuple-element.5.refs_2_), channel_id=1, source_target_pairs={{0,1},{1,0},{4,5},{5,4},{8,9},{9,8},{12,13},{13,12},{14,15},{15,14... | collective-permute-start | bytes 2064392 | tf_op jit(solution)/shard_map/ppermute | solution.py:183
  4.9 30.9 %collective-permute-start.10 = (bf16[384,896]{1,0:T(8,128)(2,1)S(1)}, bf16[384,896]{1,0:T(8,128)(2,1)}, u32[]{:S(2)}, u32[]{:S(2)}) collective-permute-start(bf16[384,896]{1,0:T(8,128)(2,1)S(1)} %get-tuple-element.5.refs_2_), channel_id=1, source_target_pairs={{0,4},{1,5},{4,8},{5,9},{8,12},{9,13},{12,14},{13,15},{14,10},{15,... | collective-permute-start | bytes 2064392 | tf_op jit(solution)/shard_map/ppermute | solution.py:188
  6.8 0.9 copy-start.5
  7.7 31.3 %collective-permute-start.14 = (bf16[384,896]{1,0:T(8,128)(2,1)S(1)}, bf16[384,896]{1,0:T(8,128)(2,1)}, u32[]{:S(2)}, u32[]{:S(2)}) collective-permute-start(bf16[384,896]{1,0:T(8,128)(2,1)S(1)} %get-tuple-element.6.refs_0_), channel_id=1, source_target_pairs={{4,0},{5,1},{8,4},{9,5},{12,8},{13,9},{14,12},{15,13},{10,14},{11,... | collective-permute-start | bytes 2064392 | tf_op jit(solution)/shard_map/ppermute | solution.py:189
  21.1 19.9 %collective-permute-start.26 = (bf16[384,896]{1,0:T(8,128)(2,1)}, bf16[384,896]{1,0:T(8,128)(2,1)}, u32[]{:S(2)}, u32[]{:S(2)}) collective-permute-start(bf16[384,896]{1,0:T(8,128)(2,1)} %collective-permute-done.refs_0_), channel_id=1, source_target_pairs={{0,1},{1,0},{4,5},{5,4},{8,9},{9,8},{12,13},{13,12},{14,15},{15,14... | collective-permute-start | bytes 2064392 | tf_op jit(solution)/shard_map/ppermute | solution.py:194
  23.2 18.0 %collective-permute-start.27 = (bf16[384,896]{1,0:T(8,128)(2,1)}, bf16[384,896]{1,0:T(8,128)(2,1)}, u32[]{:S(2)}, u32[]{:S(2)}) collective-permute-start(bf16[384,896]{1,0:T(8,128)(2,1)} %collective-permute-done.5.refs_2_), channel_id=1, source_target_pairs={{0,1},{1,0},{4,5},{5,4},{8,9},{9,8},{12,13},{13,12},{14,15},{15,14... | collective-permute-start | bytes 2064392 | tf_op jit(solution)/shard_map/ppermute | solution.py:194
  23.3 27.3 %collective-permute-start.1 = (bf16[384,896]{1,0:T(8,128)(2,1)}, bf16[384,896]{1,0:T(8,128)(2,1)}, u32[]{:S(2)}, u32[]{:S(2)}) collective-permute-start(bf16[384,896]{1,0:T(8,128)(2,1)} %collective-permute-done.refs_0_), channel_id=1, source_target_pairs={{0,4},{1,5},{4,8},{5,9},{8,12},{9,13},{12,14},{13,15},{14,10},{15,... | collective-permute-start | bytes 2064392 | tf_op jit(solution)/shard_map/ppermute | solution.py:188
  35.8 9.9 %collective-permute-start.24 = (bf16[384,896]{1,0:T(8,128)(2,1)}, bf16[384,896]{1,0:T(8,128)(2,1)}, u32[]{:S(2)}, u32[]{:S(2)}) collective-permute-start(bf16[384,896]{1,0:T(8,128)(2,1)} %collective-permute-done.10.refs_0_), channel_id=1, source_target_pairs={{0,1},{1,0},{4,5},{5,4},{8,9},{9,8},{12,13},{13,12},{14,15},{15,14... | collective-permute-start | bytes 2064392 | tf_op jit(solution)/shard_map/ppermute | solution.py:194
  39.0 46.1 %collective-permute-start.6 = (bf16[384,896]{1,0:T(8,128)(2,1)}, bf16[384,896]{1,0:T(8,128)(2,1)}, u32[]{:S(2)}, u32[]{:S(2)}) collective-permute-start(bf16[384,896]{1,0:T(8,128)(2,1)} %collective-permute-done.5.refs_2_), channel_id=1, source_target_pairs={{4,0},{5,1},{8,4},{9,5},{12,8},{13,9},{14,12},{15,13},{10,14},{11,... | collective-permute-start | bytes 2064392 | tf_op jit(solution)/shard_map/ppermute | solution.py:189
  41.0 44.1 %collective-permute-start.11 = (bf16[384,896]{1,0:T(8,128)(2,1)}, bf16[384,896]{1,0:T(8,128)(2,1)}, u32[]{:S(2)}, u32[]{:S(2)}) collective-permute-start(bf16[384,896]{1,0:T(8,128)(2,1)} %collective-permute-done.10.refs_0_), channel_id=1, source_target_pairs={{0,4},{1,5},{4,8},{5,9},{8,12},{9,13},{12,14},{13,15},{14,10},{15,... | collective-permute-start | bytes 2064392 | tf_op jit(solution)/shard_map/ppermute | solution.py:188
  41.2 41.2 %collective-permute-start.25 = (bf16[384,896]{1,0:T(8,128)(2,1)}, bf16[384,896]{1,0:T(8,128)(2,1)S(1)}, u32[]{:S(2)}, u32[]{:S(2)}) collective-permute-start(bf16[384,896]{1,0:T(8,128)(2,1)} %collective-permute-done.14.refs_2_), channel_id=1, source_target_pairs={{0,1},{1,0},{4,5},{5,4},{8,9},{9,8},{12,13},{13,12},{14,15},{15,14... | collective-permute-start | bytes 2064392 | tf_op jit(solution)/shard_map/ppermute | solution.py:194
  41.4 9.2 %slice-start = ((f32[384,512]{1,0:T(8,128)}), f32[384,64]{1,0:T(8,128)S(1)}, s32[]{:S(2)}) async-start(f32[384,512]{1,0:T(8,128)} %fusion.13), calls=%async_computation.2 | async-start | bytes 393216 | tf_op jit(solution)/shard_map/slice | solution.py:43
  45.8 39.9 %collective-permute-start.15 = (bf16[384,896]{1,0:T(8,128)(2,1)}, bf16[384,896]{1,0:T(8,128)(2,1)}, u32[]{:S(2)}, u32[]{:S(2)}) collective-permute-start(bf16[384,896]{1,0:T(8,128)(2,1)} %collective-permute-done.14.refs_2_), channel_id=1, source_target_pairs={{4,0},{5,1},{8,4},{9,5},{12,8},{13,9},{14,12},{15,13},{10,14},{11,... | collective-permute-start | bytes 2064392 | tf_op jit(solution)/shard_map/ppermute | solution.py:189
  50.6 35.2 %collective-permute-start.22 = (bf16[384,896]{1,0:T(8,128)(2,1)}, bf16[384,896]{1,0:T(8,128)(2,1)}, u32[]{:S(2)}, u32[]{:S(2)}) collective-permute-start(bf16[384,896]{1,0:T(8,128)(2,1)} %collective-permute-done.1.refs_0_), channel_id=1, source_target_pairs={{0,1},{1,0},{4,5},{5,4},{8,9},{9,8},{12,13},{13,12},{14,15},{15,14... | collective-permute-start | bytes 2064392 | tf_op jit(solution)/shard_map/ppermute | solution.py:194
  52.3 23.4 %all-to-all-start = ((f32[16,24,128]{2,1,0:T(8,128)}), f32[16,24,128]{2,1,0:T(8,128)S(1)}, u32[]{:S(2)}, u32[]{:S(2)}) async-start(f32[16,24,128]{2,1,0:T(8,128)} %bitcast.22), calls=%async_computation | async-start | bytes 393216 | tf_op jit(solution)/shard_map/all_to_all | solution.py:64
  76.4 16.5 %all-to-all-start.1 = ((f32[16,24,128]{2,1,0:T(8,128)}), f32[16,24,128]{2,1,0:T(8,128)S(1)}, u32[]{:S(2)}, u32[]{:S(2)}) async-start(f32[16,24,128]{2,1,0:T(8,128)} %broadcast_in_dim.2), calls=%async_computation.1 | async-start | bytes 393216 | tf_op jit(solution)/shard_map/all_to_all | solution.py:67
  82.4 0.9 copy-start.3
  83.2 19.9 %collective-permute-start.2 = (bf16[384,896]{1,0:T(8,128)(2,1)}, bf16[384,896]{1,0:T(8,128)(2,1)}, u32[]{:S(2)}, u32[]{:S(2)}) collective-permute-start(bf16[384,896]{1,0:T(8,128)(2,1)} %collective-permute-done.1.refs_0_), channel_id=1, source_target_pairs={{0,4},{1,5},{4,8},{5,9},{8,12},{9,13},{12,14},{13,15},{14,10},{15,... | collective-permute-start | bytes 2064392 | tf_op jit(solution)/shard_map/ppermute | solution.py:188
  85.1 7.9 %collective-permute-start.23 = (bf16[384,896]{1,0:T(8,128)(2,1)}, bf16[384,896]{1,0:T(8,128)(2,1)}, u32[]{:S(2)}, u32[]{:S(2)}) collective-permute-start(bf16[384,896]{1,0:T(8,128)(2,1)} %collective-permute-done.6.refs_2_), channel_id=1, source_target_pairs={{0,1},{1,0},{4,5},{5,4},{8,9},{9,8},{12,13},{13,12},{14,15},{15,14... | collective-permute-start | bytes 2064392 | tf_op jit(solution)/shard_map/ppermute | solution.py:194
  85.2 9.8 %collective-permute-start.20 = (bf16[384,896]{1,0:T(8,128)(2,1)}, bf16[384,896]{1,0:T(8,128)(2,1)}, u32[]{:S(2)}, u32[]{:S(2)}) collective-permute-start(bf16[384,896]{1,0:T(8,128)(2,1)} %collective-permute-done.11.refs_0_), channel_id=1, source_target_pairs={{0,1},{1,0},{4,5},{5,4},{8,9},{9,8},{12,13},{13,12},{14,15},{15,14... | collective-permute-start | bytes 2064392 | tf_op jit(solution)/shard_map/ppermute | solution.py:194
  85.7 19.1 %collective-permute-start.7 = (bf16[384,896]{1,0:T(8,128)(2,1)}, bf16[384,896]{1,0:T(8,128)(2,1)}, u32[]{:S(2)}, u32[]{:S(2)}) collective-permute-start(bf16[384,896]{1,0:T(8,128)(2,1)} %collective-permute-done.6.refs_2_), channel_id=1, source_target_pairs={{4,0},{5,1},{8,4},{9,5},{12,8},{13,9},{14,12},{15,13},{10,14},{11,... | collective-permute-start | bytes 2064392 | tf_op jit(solution)/shard_map/ppermute | solution.py:189
  85.8 17.3 %collective-permute-start.21 = (bf16[384,896]{1,0:T(8,128)(2,1)}, bf16[384,896]{1,0:T(8,128)(2,1)}, u32[]{:S(2)}, u32[]{:S(2)}) collective-permute-start(bf16[384,896]{1,0:T(8,128)(2,1)} %collective-permute-done.15.refs_2_), channel_id=1, source_target_pairs={{0,1},{1,0},{4,5},{5,4},{8,9},{9,8},{12,13},{13,12},{14,15},{15,14... | collective-permute-start | bytes 2064392 | tf_op jit(solution)/shard_map/ppermute | solution.py:194
  86.5 1.1 copy-start.2
  87.6 1.1 copy-start.6
  93.0 24.7 %collective-permute-start.12 = (bf16[384,896]{1,0:T(8,128)(2,1)}, bf16[384,896]{1,0:T(8,128)(2,1)S(1)}, u32[]{:S(2)}, u32[]{:S(2)}) collective-permute-start(bf16[384,896]{1,0:T(8,128)(2,1)} %collective-permute-done.11.refs_0_), channel_id=1, source_target_pairs={{0,4},{1,5},{4,8},{5,9},{8,12},{9,13},{12,14},{13,15},{14,10},{15,... | collective-permute-start | bytes 2064392 | tf_op jit(solution)/shard_map/ppermute | solution.py:188
  95.0 24.5 %collective-permute-start.16 = (bf16[384,896]{1,0:T(8,128)(2,1)}, bf16[384,896]{1,0:T(8,128)(2,1)S(1)}, u32[]{:S(2)}, u32[]{:S(2)}) collective-permute-start(bf16[384,896]{1,0:T(8,128)(2,1)} %collective-permute-done.15.refs_2_), channel_id=1, source_target_pairs={{4,0},{5,1},{8,4},{9,5},{12,8},{13,9},{14,12},{15,13},{10,14},{11,... | collective-permute-start | bytes 2064392 | tf_op jit(solution)/shard_map/ppermute | solution.py:189
  103.1 16.4 %collective-permute-start.18 = (bf16[384,896]{1,0:T(8,128)(2,1)}, bf16[384,896]{1,0:T(8,128)(2,1)S(1)}, u32[]{:S(2)}, u32[]{:S(2)}) collective-permute-start(bf16[384,896]{1,0:T(8,128)(2,1)} %collective-permute-done.2.refs_0_), channel_id=1, source_target_pairs={{0,1},{1,0},{4,5},{5,4},{8,9},{9,8},{12,13},{13,12},{14,15},{15,14... | collective-permute-start | bytes 2064392 | tf_op jit(solution)/shard_map/ppermute | solution.py:194
  103.1 29.0 %collective-permute-start.3 = (bf16[384,896]{1,0:T(8,128)(2,1)}, bf16[384,896]{1,0:T(8,128)(2,1)S(1)}, u32[]{:S(2)}, u32[]{:S(2)}) collective-permute-start(bf16[384,896]{1,0:T(8,128)(2,1)} %collective-permute-done.2.refs_0_), channel_id=1, source_target_pairs={{0,4},{1,5},{4,8},{5,9},{8,12},{9,13},{12,14},{13,15},{14,10},{15,... | collective-permute-start | bytes 2064392 | tf_op jit(solution)/shard_map/ppermute | solution.py:188
  104.8 28.6 %collective-permute-start.8 = (bf16[384,896]{1,0:T(8,128)(2,1)}, bf16[384,896]{1,0:T(8,128)(2,1)S(1)}, u32[]{:S(2)}, u32[]{:S(2)}) collective-permute-start(bf16[384,896]{1,0:T(8,128)(2,1)} %collective-permute-done.7.refs_2_), channel_id=1, source_target_pairs={{4,0},{5,1},{8,4},{9,5},{12,8},{13,9},{14,12},{15,13},{10,14},{11,... | collective-permute-start | bytes 2064392 | tf_op jit(solution)/shard_map/ppermute | solution.py:189
  117.7 33.6 %collective-permute-start.19 = (bf16[384,896]{1,0:T(8,128)(2,1)}, bf16[384,896]{1,0:T(8,128)(2,1)S(1)}, u32[]{:S(2)}, u32[]{:S(2)}) collective-permute-start(bf16[384,896]{1,0:T(8,128)(2,1)} %collective-permute-done.7.refs_2_), channel_id=1, source_target_pairs={{0,1},{1,0},{4,5},{5,4},{8,9},{9,8},{12,13},{13,12},{14,15},{15,14... | collective-permute-start | bytes 2064392 | tf_op jit(solution)/shard_map/ppermute | solution.py:194
  119.4 36.2 %collective-permute-start.13 = (bf16[384,896]{1,0:T(8,128)(2,1)S(1)}, bf16[384,896]{1,0:T(8,128)(2,1)S(1)}, u32[]{:S(2)}, u32[]{:S(2)}) collective-permute-start(bf16[384,896]{1,0:T(8,128)(2,1)S(1)} %collective-permute-done.12.refs_0_), channel_id=1, source_target_pairs={{0,1},{1,0},{4,5},{5,4},{8,9},{9,8},{12,13},{13,12},{14,15},{15,14... | collective-permute-start | bytes 2064392 | tf_op jit(solution)/shard_map/ppermute | solution.py:194
  119.4 36.2 %collective-permute-start.17 = (bf16[384,896]{1,0:T(8,128)(2,1)S(1)}, bf16[384,896]{1,0:T(8,128)(2,1)S(1)}, u32[]{:S(2)}, u32[]{:S(2)}) collective-permute-start(bf16[384,896]{1,0:T(8,128)(2,1)S(1)} %collective-permute-done.16.refs_2_), channel_id=1, source_target_pairs={{0,1},{1,0},{4,5},{5,4},{8,9},{9,8},{12,13},{13,12},{14,15},{15,14... | collective-permute-start | bytes 2064392 | tf_op jit(solution)/shard_map/ppermute | solution.py:194
  121.5 16.4 %copy-start.4 = (bf16[384,896]{1,0:T(8,128)(2,1)S(1)}, bf16[384,896]{1,0:T(8,128)(2,1)}, u32[]{:S(2)}) copy-start(bf16[384,896]{1,0:T(8,128)(2,1)} %copy-done.3) | copy-start | bytes 2064388
  132.2 27.6 %collective-permute-start.4 = (bf16[384,896]{1,0:T(8,128)(2,1)S(1)}, bf16[384,896]{1,0:T(8,128)(2,1)S(1)}, u32[]{:S(2)}, u32[]{:S(2)}) collective-permute-start(bf16[384,896]{1,0:T(8,128)(2,1)S(1)} %collective-permute-done.3.refs_0_), channel_id=1, source_target_pairs={{0,1},{1,0},{4,5},{5,4},{8,9},{9,8},{12,13},{13,12},{14,15},{15,14... | collective-permute-start | bytes 2064392 | tf_op jit(solution)/shard_map/ppermute | solution.py:194
  133.4 26.4 %collective-permute-start.9 = (bf16[384,896]{1,0:T(8,128)(2,1)S(1)}, bf16[384,896]{1,0:T(8,128)(2,1)S(1)}, u32[]{:S(2)}, u32[]{:S(2)}) collective-permute-start(bf16[384,896]{1,0:T(8,128)(2,1)S(1)} %collective-permute-done.8.refs_2_), channel_id=1, source_target_pairs={{0,1},{1,0},{4,5},{5,4},{8,9},{9,8},{12,13},{13,12},{14,15},{15,14... | collective-permute-start | bytes 2064392 | tf_op jit(solution)/shard_map/ppermute | solution.py:194

commit v2 on v1

--- a/solution.py
+++ b/solution.py
@@ -32,15 +32,37 @@
     return [chips[p] for p in places]
 
 
+def project_selected(rows, labels, factors):
+    count, rank, units = factors.shape
+    total = rows.shape[0]
+    wide = count * rank
+
+    def body(x_ref, l_ref, a_ref, o_ref):
+        full = lax.dot_general(
+            x_ref[...], a_ref[...], (((1,), (1,)), ((), ())), preferred_element_type=jnp.float32
+        )
+        own = jnp.zeros((total, rank), jnp.float32)
+        for k in range(count):
+            own = own + jnp.where(l_ref[...] == k, full[:, k * rank : (k + 1) * rank], 0.0)
+        o_ref[...] = jnp.concatenate([own, full[:, :rank]], axis=1)
+
+    vmem = pl.BlockSpec(memory_space=pltpu.VMEM)
+    return pl.pallas_call(
+        body,
+        out_shape=jax.ShapeDtypeStruct((total, 2 * rank), jnp.float32),
+        in_specs=[vmem] * 3,
+        out_specs=vmem,
+        cost_estimate=pl.CostEstimate(
+            flops=2 * total * wide * units,
+            transcendentals=0,
+            bytes_accessed=2 * units * (total + wide) + 8 * total * rank,
+        ),
+        compiler_params=pltpu.CompilerParams(vmem_limit_bytes=32 << 20),
+    )(rows, labels[:, None], factors.reshape(wide, units))
+
+
 def labels_onehot(adapter_labels, count):
     return adapter_labels[:, None] == jnp.arange(count, dtype=jnp.int32)[None, :]
-
-
-def select_both(project_rows, adapter_labels, count, rank):
-    choose = labels_onehot(adapter_labels, count).astype(jnp.float32)
-    total = project_rows.shape[0]
-    own = jnp.sum(project_rows.reshape(total, count, rank) * choose[:, :, None], axis=1)
-    return jnp.concatenate([own, project_rows[:, :rank]], axis=1)
 
 
 def expand_factor(shrunk_rows, adapter_labels, adapter_output_weight):
@@ -138,19 +160,13 @@
         request_adapter_index,
     ):
         steps, requests, device_units = gated_hidden_rows.shape
-        count, rank, _ = adapter_input_factor.shape
+        _, rank, _ = adapter_input_factor.shape
         features = down_base_weight.shape[0]
         total = steps * requests
         flat = gated_hidden_rows.reshape(total, device_units)
         adapter_labels = request_adapter_index.reshape(total)
-        project_rows = jnp.dot(
-            flat,
-            adapter_input_factor.reshape(count * rank, device_units).T,
-            preferred_element_type=jnp.float32,
-        )
-        summed = sum_over_row(
-            select_both(project_rows, adapter_labels, count, rank), axis_size
-        )
+        summand = project_selected(flat, adapter_labels, adapter_input_factor)
+        summed = sum_over_row(summand, axis_size)
         keep = (adapter_labels != 0).astype(jnp.float32)[:, None]
         shrunk_rows = (summed * keep).astype(jnp.bfloat16)
         extra = jnp.dot(
@@ -194,7 +210,10 @@
                 other = lax.ppermute(data, "row", partner)
                 found.append((data, start_of(offset, False, part)))
                 found.append((other, start_of(offset, True, part)))
-            batches.append(found)
+            if s == hops - 1:
+                batches += [found[::2], found[1::2]]
+            else:
+                batches.append(found)
         order = [where[at] for found in batches for _, at in found]
         table = np.zeros((axis_size, len(order)), np.int32)
         for p, members in enumerate(ring):
@@ -213,7 +232,7 @@
                 done,
                 down_base_weight,
                 acc,
-                extra if last else None,
+                extra if k == hops - 1 else None,
                 jnp.bfloat16 if last else jnp.float32,
             )
             done += len(found)

time: 166 us -> 161 us (0.970)
  other arithmetic: 4.51 us -> 0.97 us
  Pallas kernels: 35.3 us -> 38.8 us
  matrix products: 6.08 us -> 2.9 us
  starting transfers between devices: 30.7 us -> 28.5 us
    ppermute x7, waiting for transfers between devices: 56.9 us -> 63.8 us  [local(): ups[up_part] = lax.ppermute(ups[up_part], 'row', forward)]
    all_to_all x1, waiting for transfers between devices: 15.3 us -> 10 us  [sum_over_row(): parts = lax.all_to_all(summand, 'row', 0, 0, tiled=True)]
    unnamed x16 -> x22, local copies, waits for them, and re-layouts: 3.93 us -> 7.22 us
    dot_general x1 -> x0, matrix products: 3.14 us -> none  [local(): jnp.dot(flat, adapter_input_factor.reshape(count * rank, device_units).T,...]
    ppermute x7, starting transfers between devices: 4.76 us -> 2.01 us  [local(): downs[down_part] = lax.ppermute(downs[down_part], 'row', backward)]
    dot_general x1 -> x0, local copies, waits for them, and re-layouts: 2.36 us -> none  [local(): jnp.dot(flat, adapter_input_factor.reshape(count * rank, device_units).T,...]
    ppermute x7, starting transfers between devices: 11.4 us -> 13.7 us  [local(): ups[up_part] = lax.ppermute(ups[up_part], 'row', forward)]
    pallas_call x0 -> x1, Pallas kernels: none -> 1.82 us  [project_selected(): pl.pallas_call(body, out_shape=jax.ShapeDtypeStruct((total, 2 * rank), jn...]
  transfers between devices with their start and end apart: 32 -> 32, of which waited for: 11 -> 10; matrix products, arithmetic and copies ran while one was open for 9% -> 4% of each run, Pallas kernels for 18% -> 22%
where the time goes in v2:
time: 161 us
  waiting for transfers between devices  78.3 us (49%)
  Pallas kernels  38.8 us (24%)
  starting transfers between devices  28.5 us (18%)
  local copies, waits for them, and re-layouts  10.5 us (7%)
  matrix products  2.9 us (2%)
    ppermute x7, waiting for transfers between devices, local(): ups[up_part] = lax.ppermute(ups[up_part], 'row', forward)  63.8 us
    pallas_call x9, Pallas kernels, chunk_matmul(): pl.pallas_call(body, out_shape=jax.ShapeDtypeStruct((rows, features), out...  37 us
    ppermute x7, starting transfers between devices, local(): ups[up_part] = lax.ppermute(ups[up_part], 'row', forward)  13.7 us
    all_to_all x1, waiting for transfers between devices, sum_over_row(): parts = lax.all_to_all(summand, 'row', 0, 0, tiled=True)  10 us
    unnamed x22, local copies, waits for them, and re-layouts  7.22 us
    all_to_all x1, starting transfers between devices, sum_over_row(): parts = lax.all_to_all(summand, 'row', 0, 0, tiled=True)  6.27 us
    all_to_all x1, starting transfers between devices, sum_over_row(): return lax.all_to_all(spread, 'row', 0, 0, tiled=True)  4.58 us
    ppermute x7, waiting for transfers between devices, local(): downs[down_part] = lax.ppermute(downs[down_part], 'row', backward)  4.49 us
  transfers between devices with their start and end apart: 32, of which 10 were waited for; matrix products, arithmetic and copies ran while one was open for 4% of the time, Pallas kernels for 22%

profile of v2, /device:TPU:0, one launch (start us, length us, event | category | flops | bytes accessed | tf_op | source)
XLA Modules:
  0.0 160.5 jit_solution(8044855379415602046)
XLA Ops:
  0.0 1.5 fusion.12
  1.5 0.6 collective-permute-start.28
  2.1 2.6 %collective-permute-start = (bf16[384,896]{1,0:T(8,128)(2,1)S(1)}, bf16[384,896]{1,0:T(8,128)(2,1)}, u32[]{:S(2)}, u32[]{:S(2)}) collective-permute-start(bf16[384,896]{1,0:T(8,128)(2,1)S(1)} %get-tuple-element.6.refs_0_), channel_id=1, source_target_pairs={{0,4},{1,5},{4,8},{5,9},{8,12},{9,13},{12,14},{13,15},{14,10},{15,... | collective-permute-start | bytes 2064392 | tf_op jit(solution)/shard_map/ppermute | solution.py:204
  4.7 2.0 %collective-permute-start.10 = (bf16[384,896]{1,0:T(8,128)(2,1)S(1)}, bf16[384,896]{1,0:T(8,128)(2,1)}, u32[]{:S(2)}, u32[]{:S(2)}) collective-permute-start(bf16[384,896]{1,0:T(8,128)(2,1)S(1)} %get-tuple-element.5.refs_2_), channel_id=1, source_target_pairs={{0,4},{1,5},{4,8},{5,9},{8,12},{9,13},{12,14},{13,15},{14,10},{15,... | collective-permute-start | bytes 2064392 | tf_op jit(solution)/shard_map/ppermute | solution.py:204
  6.8 0.9 copy-done.6
  7.6 13.4 %collective-permute-done.refs_0_ = bf16[384,896]{1,0:T(8,128)(2,1)} collective-permute-done((bf16[384,896]{1,0:T(8,128)(2,1)S(1)}, bf16[384,896]{1,0:T(8,128)(2,1)}, u32[]{:S(2)}, u32[]{:S(2)}) %collective-permute-start) | collective-permute-done | bytes 688160 | tf_op jit(solution)/shard_map/ppermute | solution.py:204
  21.1 2.1 %collective-permute-done.5.refs_2_ = bf16[384,896]{1,0:T(8,128)(2,1)} collective-permute-done((bf16[384,896]{1,0:T(8,128)(2,1)S(1)}, bf16[384,896]{1,0:T(8,128)(2,1)}, u32[]{:S(2)}, u32[]{:S(2)}) %collective-permute-start.5) | collective-permute-done | bytes 688160 | tf_op jit(solution)/shard_map/ppermute | solution.py:205
  23.1 12.4 %collective-permute-done.10.refs_0_ = bf16[384,896]{1,0:T(8,128)(2,1)} collective-permute-done((bf16[384,896]{1,0:T(8,128)(2,1)S(1)}, bf16[384,896]{1,0:T(8,128)(2,1)}, u32[]{:S(2)}, u32[]{:S(2)}) %collective-permute-start.10) | collective-permute-done | bytes 688160 | tf_op jit(solution)/shard_map/ppermute | solution.py:204
  35.6 0.8 copy-done.8
  36.4 1.8 %collective-permute-start.1 = (bf16[384,896]{1,0:T(8,128)(2,1)}, bf16[384,896]{1,0:T(8,128)(2,1)}, u32[]{:S(2)}, u32[]{:S(2)}) collective-permute-start(bf16[384,896]{1,0:T(8,128)(2,1)} %collective-permute-done.refs_0_), channel_id=1, source_target_pairs={{0,4},{1,5},{4,8},{5,9},{8,12},{9,13},{12,14},{13,15},{14,10},{15,... | collective-permute-start | bytes 2064392 | tf_op jit(solution)/shard_map/ppermute | solution.py:204
  38.2 0.2 collective-permute-start.25
  38.4 0.9 copy-done.2
  39.6 0.9 copy-done.4
  40.5 1.8 %collective-permute-start.11 = (bf16[384,896]{1,0:T(8,128)(2,1)}, bf16[384,896]{1,0:T(8,128)(2,1)}, u32[]{:S(2)}, u32[]{:S(2)}) collective-permute-start(bf16[384,896]{1,0:T(8,128)(2,1)} %collective-permute-done.10.refs_0_), channel_id=1, source_target_pairs={{0,4},{1,5},{4,8},{5,9},{8,12},{9,13},{12,14},{13,15},{14,10},{15,... | collective-permute-start | bytes 2064392 | tf_op jit(solution)/shard_map/ppermute | solution.py:204
  42.5 0.3 collective-permute-start.15
  42.8 12.3 %collective-permute-done.1.refs_0_ = bf16[384,896]{1,0:T(8,128)(2,1)} collective-permute-done((bf16[384,896]{1,0:T(8,128)(2,1)}, bf16[384,896]{1,0:T(8,128)(2,1)}, u32[]{:S(2)}, u32[]{:S(2)}) %collective-permute-start.1) | collective-permute-done | bytes 688160 | tf_op jit(solution)/shard_map/ppermute | solution.py:204
  55.0 1.5 copy-done.1
  56.5 1.8 %shard_map.70 = f32[384,128]{1,0:T(8,128)} custom-call(bf16[384,1792]{1,0:T(8,128)(2,1)S(1)} %bitcast.14, s32[384,1]{1,0:T(8,128)S(1)} %broadcast_in_dim_reshape.5.l_ref, bf16[512,1792]{1,0:T(8,128)(2,1)S(1)} %bitcast.15), custom_call_target="tpu_custom_call" | custom-call | flops 704643072 | bytes 3407872 | tf_op jit(solution)/shard_map/pallas_call | solution.py:50
  58.4 6.3 %all-to-all-start = ((f32[16,24,128]{2,1,0:T(8,128)}), f32[16,24,128]{2,1,0:T(8,128)S(1)}, u32[]{:S(2)}, u32[]{:S(2)}) async-start(f32[16,24,128]{2,1,0:T(8,128)} %bitcast.3), calls=%async_computation | async-start | bytes 393216 | tf_op jit(solution)/shard_map/all_to_all | solution.py:86
  64.7 0.8 bitcast_negate_fusion
  65.6 10.0 %all-to-all-done = f32[16,24,128]{2,1,0:T(8,128)S(1)} async-done(((f32[16,24,128]{2,1,0:T(8,128)}), f32[16,24,128]{2,1,0:T(8,128)S(1)}, u32[]{:S(2)}, u32[]{:S(2)}) %all-to-all-start) | async-done | bytes 196640 | tf_op jit(solution)/shard_map/all_to_all | solution.py:86
  75.6 0.7 broadcast_in_dim.2
  76.3 4.6 %all-to-all-start.1 = ((f32[16,24,128]{2,1,0:T(8,128)}), f32[16,24,128]{2,1,0:T(8,128)S(1)}, u32[]{:S(2)}, u32[]{:S(2)}) async-start(f32[16,24,128]{2,1,0:T(8,128)} %broadcast_in_dim.2), calls=%async_computation.1 | async-start | bytes 393216 | tf_op jit(solution)/shard_map/all_to_all | solution.py:89
  80.9 2.0 %collective-permute-start.2 = (bf16[384,896]{1,0:T(8,128)(2,1)}, bf16[384,896]{1,0:T(8,128)(2,1)S(1)}, u32[]{:S(2)}, u32[]{:S(2)}) collective-permute-start(bf16[384,896]{1,0:T(8,128)(2,1)} %collective-permute-done.1.refs_0_), channel_id=1, source_target_pairs={{0,4},{1,5},{4,8},{5,9},{8,12},{9,13},{12,14},{13,15},{14,10},{15,... | collective-permute-start | bytes 2064392 | tf_op jit(solution)/shard_map/ppermute | solution.py:204
  82.9 0.5 collective-permute-start.20
  83.6 0.7 dynamic-slice_bitcast_fusion.starts_ref
  84.3 1.1 copy-done.7
  85.4 1.1 copy-done.9
  86.5 4.1 %shard_map.64.refs_5_ = f32[384,512]{1,0:T(8,128)S(1)} custom-call(s32[32]{0:T(128)S(1)} %dynamic-slice_bitcast_fusion.starts_ref, bf16[384,896]{1,0:T(8,128)(2,1)S(1)} %get-tuple-element.6.refs_0_, bf16[384,896]{1,0:T(8,128)(2,1)S(1)} %copy-done.7, bf16[384,896]{1,0:T(8,128)(2,1)S(1)} %get-tuple-element.5.refs_2_, bf16[384,896]{1,0:T(8,128)(2,1)S(1)} %copy-done.9, ...), custom_call_target="tpu_custom_call" | custom-call | flops 1409286144 | bytes 7995392 | tf_op jit(solution)/shard_map/pallas_call | solution.py:125
  90.8 1.9 %collective-permute-start.12 = (bf16[384,896]{1,0:T(8,128)(2,1)}, bf16[384,896]{1,0:T(8,128)(2,1)S(1)}, u32[]{:S(2)}, u32[]{:S(2)}) collective-permute-start(bf16[384,896]{1,0:T(8,128)(2,1)} %collective-permute-done.11.refs_0_), channel_id=1, source_target_pairs={{0,4},{1,5},{4,8},{5,9},{8,12},{9,13},{12,14},{13,15},{14,10},{15,... | collective-permute-start | bytes 2064392 | tf_op jit(solution)/shard_map/ppermute | solution.py:204
  92.9 8.5 %collective-permute-done.2.refs_0_ = bf16[384,896]{1,0:T(8,128)(2,1)S(1)} collective-permute-done((bf16[384,896]{1,0:T(8,128)(2,1)}, bf16[384,896]{1,0:T(8,128)(2,1)S(1)}, u32[]{:S(2)}, u32[]{:S(2)}) %collective-permute-start.2) | collective-permute-done | bytes 688160 | tf_op jit(solution)/shard_map/ppermute | solution.py:204
  101.4 1.6 %collective-permute-start.3 = (bf16[384,896]{1,0:T(8,128)(2,1)S(1)}, bf16[384,896]{1,0:T(8,128)(2,1)S(1)}, u32[]{:S(2)}, u32[]{:S(2)}) collective-permute-start(bf16[384,896]{1,0:T(8,128)(2,1)S(1)} %collective-permute-done.2.refs_0_), channel_id=1, source_target_pairs={{0,4},{1,5},{4,8},{5,9},{8,12},{9,13},{12,14},{13,15},{14,10},{15,... | collective-permute-start | bytes 2064392 | tf_op jit(solution)/shard_map/ppermute | solution.py:204
  103.0 1.2 collective-permute-start.8
  104.3 1.4 fusion.6
  105.7 10.4 %collective-permute-done.12.refs_0_ = bf16[384,896]{1,0:T(8,128)(2,1)S(1)} collective-permute-done((bf16[384,896]{1,0:T(8,128)(2,1)}, bf16[384,896]{1,0:T(8,128)(2,1)S(1)}, u32[]{:S(2)}, u32[]{:S(2)}) %collective-permute-start.12) | collective-permute-done | bytes 688160 | tf_op jit(solution)/shard_map/ppermute | solution.py:204
  116.2 1.1 collective-permute-done.16.refs_2_
  117.3 0.5 collective-permute-start.17
  117.8 1.5 convolution_add_fusion.refs_6_
  119.3 4.3 %shard_map.65.refs_5_ = f32[384,512]{1,0:T(8,128)S(1)} custom-call(s32[32]{0:T(128)S(1)} %dynamic-slice_bitcast_fusion.starts_ref, bf16[384,896]{1,0:T(8,128)(2,1)} %collective-permute-done.refs_0_, bf16[384,896]{1,0:T(8,128)(2,1)S(1)} %copy-done.3, bf16[384,896]{1,0:T(8,128)(2,1)} %collective-permute-done.5.refs_2_, bf16[384,896]{1,0:T(8,128)(2,1)S(1)} %copy-done.5, ...), custom_call_target="tpu_custom_call" | custom-call | flops 1409286144 | bytes 7995392 | tf_op jit(solution)/shard_map/pallas_call | solution.py:125
  123.6 6.7 %collective-permute-done.3.refs_0_ = bf16[384,896]{1,0:T(8,128)(2,1)S(1)} collective-permute-done((bf16[384,896]{1,0:T(8,128)(2,1)S(1)}, bf16[384,896]{1,0:T(8,128)(2,1)S(1)}, u32[]{:S(2)}, u32[]{:S(2)}) %collective-permute-start.3) | collective-permute-done | bytes 688160 | tf_op jit(solution)/shard_map/ppermute | solution.py:204
  130.3 1.3 collective-permute-done.8.refs_1_
  131.6 4.5 %shard_map.66.refs_5_ = f32[384,512]{1,0:T(8,128)S(1)} custom-call(s32[32]{0:T(128)S(1)} %dynamic-slice_bitcast_fusion.starts_ref, bf16[384,896]{1,0:T(8,128)(2,1)} %collective-permute-done.10.refs_0_, bf16[384,896]{1,0:T(8,128)(2,1)} %collective-permute-done.24.refs_1_, bf16[384,896]{1,0:T(8,128)(2,1)} %collective-permute-done.14.refs_2_, ...), custom_call_target="tpu_custom_call" | custom-call | flops 1409286144 | bytes 7995392 | tf_op jit(solution)/shard_map/pallas_call | solution.py:125
  136.1 4.5 %shard_map.67.refs_5_ = f32[384,512]{1,0:T(8,128)S(1)} custom-call(s32[32]{0:T(128)S(1)} %dynamic-slice_bitcast_fusion.starts_ref, bf16[384,896]{1,0:T(8,128)(2,1)} %collective-permute-done.1.refs_0_, bf16[384,896]{1,0:T(8,128)(2,1)} %collective-permute-done.22.refs_1_, bf16[384,896]{1,0:T(8,128)(2,1)} %collective-permute-done.6.refs_2_, ...), custom_call_target="tpu_custom_call" | custom-call | flops 1409286144 | bytes 7995392 | tf_op jit(solution)/shard_map/pallas_call | solution.py:125
  140.6 4.5 %shard_map.68.refs_5_ = f32[384,512]{1,0:T(8,128)S(1)} custom-call(s32[32]{0:T(128)S(1)} %dynamic-slice_bitcast_fusion.starts_ref, bf16[384,896]{1,0:T(8,128)(2,1)} %collective-permute-done.11.refs_0_, bf16[384,896]{1,0:T(8,128)(2,1)} %collective-permute-done.20.refs_1_, bf16[384,896]{1,0:T(8,128)(2,1)} %collective-permute-done.15.refs_2_, ...), custom_call_target="tpu_custom_call" | custom-call | flops 1409286144 | bytes 7995392 | tf_op jit(solution)/shard_map/pallas_call | solution.py:125
  145.1 4.1 %shard_map.69.refs_5_ = f32[384,512]{1,0:T(8,128)S(1)} custom-call(s32[32]{0:T(128)S(1)} %dynamic-slice_bitcast_fusion.starts_ref, bf16[384,896]{1,0:T(8,128)(2,1)S(1)} %collective-permute-done.2.refs_0_, bf16[384,896]{1,0:T(8,128)(2,1)S(1)} %collective-permute-done.18.refs_1_, bf16[384,896]{1,0:T(8,128)(2,1)} %collective-permute-done.7.refs_2_, ...), custom_call_target="tpu_custom_call" | custom-call | flops 1409286144 | bytes 7995392 | tf_op jit(solution)/shard_map/pallas_call | solution.py:125
  149.2 4.1 %shard_map.71.refs_3_ = f32[384,512]{1,0:T(8,128)S(1)} custom-call(s32[32]{0:T(128)S(1)} %dynamic-slice_bitcast_fusion.starts_ref, bf16[384,896]{1,0:T(8,128)(2,1)S(1)} %collective-permute-done.12.refs_0_, bf16[384,896]{1,0:T(8,128)(2,1)S(1)} %collective-permute-done.13.refs_1_, bf16[384,896]{1,0:T(8,128)(2,1)S(1)} %collective-permute-done.16.refs_2_, ...), custom_call_target="tpu_custom_call" | custom-call | flops 1409286144 | bytes 7995392 | tf_op jit(solution)/shard_map/pallas_call | solution.py:125
  153.4 3.1 %shard_map.72.refs_3_ = f32[384,512]{1,0:T(8,128)S(1)} custom-call(s32[32]{0:T(128)S(1)} %dynamic-slice_bitcast_fusion.starts_ref, bf16[384,896]{1,0:T(8,128)(2,1)S(1)} %collective-permute-done.3.refs_0_, bf16[384,896]{1,0:T(8,128)(2,1)S(1)} %collective-permute-done.8.refs_1_, bf16[512,28672]{1,0:T(8,128)(2,1)} %refs_2_.3, f32[384,512]{1,0:T(8,128)S(1)} %shard_map.71.refs_3_), custom_call_target="tpu_custom_call" | custom-call | flops 704643072 | bytes 4784128 | tf_op jit(solution)/shard_map/pallas_call | solution.py:125
  156.5 3.9 %shard_map.73 = bf16[384,512]{1,0:T(8,128)(2,1)} custom-call(s32[32]{0:T(128)S(1)} %dynamic-slice_bitcast_fusion.starts_ref, bf16[384,896]{1,0:T(8,128)(2,1)S(1)} %collective-permute-done.4.refs_0_, bf16[384,896]{1,0:T(8,128)(2,1)S(1)} %collective-permute-done.9.refs_1_, bf16[512,28672]{1,0:T(8,128)(2,1)} %refs_2_.3, f32[384,512]{1,0:T(8,128)S(1)} %shard_map.72.refs_3_), custom_call_target="tpu_custom_call" | custom-call | flops 704643072 | bytes 4784128 | tf_op jit(solution)/shard_map/pallas_call | solution.py:125
  (63 shorter events, 1.2 us)
Async XLA Ops:
  0.0 42.3 %copy-start.10 = (s32[2,192]{1,0:T(2,128)S(1)}, s32[2,192]{1,0:T(2,128)}, u32[]{:S(2)}) copy-start(s32[2,192]{1,0:T(2,128)} %param.10) | copy-start | bytes 4612
  0.0 55.0 %copy-start = (bf16[2,192,1792]{2,1,0:T(8,128)(2,1)S(1)}, bf16[2,192,1792]{2,1,0:T(8,128)(2,1)}, u32[]{:S(2)}) copy-start(bf16[2,192,1792]{2,1,0:T(8,128)(2,1)} %param.6) | copy-start | bytes 4128772
  1.5 5.2 %collective-permute-start.28 = (bf16[384,896]{1,0:T(8,128)(2,1)S(1)}, bf16[384,896]{1,0:T(8,128)(2,1)S(1)}, u32[]{:S(2)}, u32[]{:S(2)}) collective-permute-start(bf16[384,896]{1,0:T(8,128)(2,1)S(1)} %get-tuple-element.6.refs_0_), channel_id=1, source_target_pairs={{0,1},{1,0},{4,5},{5,4},{8,9},{9,8},{12,13},{13,12},{14,15},{15,14... | collective-permute-start | bytes 2064392 | tf_op jit(solution)/shard_map/ppermute | solution.py:199
  2.1 19.0 %collective-permute-start = (bf16[384,896]{1,0:T(8,128)(2,1)S(1)}, bf16[384,896]{1,0:T(8,128)(2,1)}, u32[]{:S(2)}, u32[]{:S(2)}) collective-permute-start(bf16[384,896]{1,0:T(8,128)(2,1)S(1)} %get-tuple-element.6.refs_0_), channel_id=1, source_target_pairs={{0,4},{1,5},{4,8},{5,9},{8,12},{9,13},{12,14},{13,15},{14,10},{15,... | collective-permute-start | bytes 2064392 | tf_op jit(solution)/shard_map/ppermute | solution.py:204
  4.7 18.4 %collective-permute-start.5 = (bf16[384,896]{1,0:T(8,128)(2,1)S(1)}, bf16[384,896]{1,0:T(8,128)(2,1)}, u32[]{:S(2)}, u32[]{:S(2)}) collective-permute-start(bf16[384,896]{1,0:T(8,128)(2,1)S(1)} %get-tuple-element.5.refs_2_), channel_id=1, source_target_pairs={{4,0},{5,1},{8,4},{9,5},{12,8},{13,9},{14,12},{15,13},{10,14},{11,... | collective-permute-start | bytes 2064392 | tf_op jit(solution)/shard_map/ppermute | solution.py:205
  4.7 30.8 %collective-permute-start.10 = (bf16[384,896]{1,0:T(8,128)(2,1)S(1)}, bf16[384,896]{1,0:T(8,128)(2,1)}, u32[]{:S(2)}, u32[]{:S(2)}) collective-permute-start(bf16[384,896]{1,0:T(8,128)(2,1)S(1)} %get-tuple-element.5.refs_2_), channel_id=1, source_target_pairs={{0,4},{1,5},{4,8},{5,9},{8,12},{9,13},{12,14},{13,15},{14,10},{15,... | collective-permute-start | bytes 2064392 | tf_op jit(solution)/shard_map/ppermute | solution.py:204
  6.7 28.8 %collective-permute-start.29 = (bf16[384,896]{1,0:T(8,128)(2,1)S(1)}, bf16[384,896]{1,0:T(8,128)(2,1)S(1)}, u32[]{:S(2)}, u32[]{:S(2)}) collective-permute-start(bf16[384,896]{1,0:T(8,128)(2,1)S(1)} %get-tuple-element.5.refs_2_), channel_id=1, source_target_pairs={{0,1},{1,0},{4,5},{5,4},{8,9},{9,8},{12,13},{13,12},{14,15},{15,14... | collective-permute-start | bytes 2064392 | tf_op jit(solution)/shard_map/ppermute | solution.py:199
  6.7 0.9 copy-start.6
  7.6 30.6 %collective-permute-start.14 = (bf16[384,896]{1,0:T(8,128)(2,1)S(1)}, bf16[384,896]{1,0:T(8,128)(2,1)}, u32[]{:S(2)}, u32[]{:S(2)}) collective-permute-start(bf16[384,896]{1,0:T(8,128)(2,1)S(1)} %get-tuple-element.6.refs_0_), channel_id=1, source_target_pairs={{4,0},{5,1},{8,4},{9,5},{12,8},{13,9},{14,12},{15,13},{10,14},{11,... | collective-permute-start | bytes 2064392 | tf_op jit(solution)/shard_map/ppermute | solution.py:205
  21.1 17.4 %collective-permute-start.26 = (bf16[384,896]{1,0:T(8,128)(2,1)}, bf16[384,896]{1,0:T(8,128)(2,1)S(1)}, u32[]{:S(2)}, u32[]{:S(2)}) collective-permute-start(bf16[384,896]{1,0:T(8,128)(2,1)} %collective-permute-done.refs_0_), channel_id=1, source_target_pairs={{0,1},{1,0},{4,5},{5,4},{8,9},{9,8},{12,13},{13,12},{14,15},{15,14... | collective-permute-start | bytes 2064392 | tf_op jit(solution)/shard_map/ppermute | solution.py:210
  23.1 16.4 %collective-permute-start.27 = (bf16[384,896]{1,0:T(8,128)(2,1)}, bf16[384,896]{1,0:T(8,128)(2,1)S(1)}, u32[]{:S(2)}, u32[]{:S(2)}) collective-permute-start(bf16[384,896]{1,0:T(8,128)(2,1)} %collective-permute-done.5.refs_2_), channel_id=1, source_target_pairs={{0,1},{1,0},{4,5},{5,4},{8,9},{9,8},{12,13},{13,12},{14,15},{15,14... | collective-permute-start | bytes 2064392 | tf_op jit(solution)/shard_map/ppermute | solution.py:210
  35.6 6.9 %collective-permute-start.24 = (bf16[384,896]{1,0:T(8,128)(2,1)}, bf16[384,896]{1,0:T(8,128)(2,1)}, u32[]{:S(2)}, u32[]{:S(2)}) collective-permute-start(bf16[384,896]{1,0:T(8,128)(2,1)} %collective-permute-done.10.refs_0_), channel_id=1, source_target_pairs={{0,1},{1,0},{4,5},{5,4},{8,9},{9,8},{12,13},{13,12},{14,15},{15,14... | collective-permute-start | bytes 2064392 | tf_op jit(solution)/shard_map/ppermute | solution.py:210
  35.6 0.8 copy-start.8
  36.4 18.6 %collective-permute-start.1 = (bf16[384,896]{1,0:T(8,128)(2,1)}, bf16[384,896]{1,0:T(8,128)(2,1)}, u32[]{:S(2)}, u32[]{:S(2)}) collective-permute-start(bf16[384,896]{1,0:T(8,128)(2,1)} %collective-permute-done.refs_0_), channel_id=1, source_target_pairs={{0,4},{1,5},{4,8},{5,9},{8,12},{9,13},{12,14},{13,15},{14,10},{15,... | collective-permute-start | bytes 2064392 | tf_op jit(solution)/shard_map/ppermute | solution.py:204
  38.2 42.7 %collective-permute-start.25 = (bf16[384,896]{1,0:T(8,128)(2,1)}, bf16[384,896]{1,0:T(8,128)(2,1)}, u32[]{:S(2)}, u32[]{:S(2)}) collective-permute-start(bf16[384,896]{1,0:T(8,128)(2,1)} %collective-permute-done.14.refs_2_), channel_id=1, source_target_pairs={{0,1},{1,0},{4,5},{5,4},{8,9},{9,8},{12,13},{13,12},{14,15},{15,14... | collective-permute-start | bytes 2064392 | tf_op jit(solution)/shard_map/ppermute | solution.py:210
  38.4 0.9 copy-start.2
  39.3 43.5 %collective-permute-start.6 = (bf16[384,896]{1,0:T(8,128)(2,1)}, bf16[384,896]{1,0:T(8,128)(2,1)}, u32[]{:S(2)}, u32[]{:S(2)}) collective-permute-start(bf16[384,896]{1,0:T(8,128)(2,1)} %collective-permute-done.5.refs_2_), channel_id=1, source_target_pairs={{4,0},{5,1},{8,4},{9,5},{12,8},{13,9},{14,12},{15,13},{10,14},{11,... | collective-permute-start | bytes 2064392 | tf_op jit(solution)/shard_map/ppermute | solution.py:205
  39.6 0.9 copy-start.4
  40.5 42.4 %collective-permute-start.11 = (bf16[384,896]{1,0:T(8,128)(2,1)}, bf16[384,896]{1,0:T(8,128)(2,1)}, u32[]{:S(2)}, u32[]{:S(2)}) collective-permute-start(bf16[384,896]{1,0:T(8,128)(2,1)} %collective-permute-done.10.refs_0_), channel_id=1, source_target_pairs={{0,4},{1,5},{4,8},{5,9},{8,12},{9,13},{12,14},{13,15},{14,10},{15,... | collective-permute-start | bytes 2064392 | tf_op jit(solution)/shard_map/ppermute | solution.py:204
  42.5 40.9 %collective-permute-start.15 = (bf16[384,896]{1,0:T(8,128)(2,1)}, bf16[384,896]{1,0:T(8,128)(2,1)}, u32[]{:S(2)}, u32[]{:S(2)}) collective-permute-start(bf16[384,896]{1,0:T(8,128)(2,1)} %collective-permute-done.14.refs_2_), channel_id=1, source_target_pairs={{4,0},{5,1},{8,4},{9,5},{12,8},{13,9},{14,12},{15,13},{10,14},{11,... | collective-permute-start | bytes 2064392 | tf_op jit(solution)/shard_map/ppermute | solution.py:205
  55.0 28.5 %collective-permute-start.22 = (bf16[384,896]{1,0:T(8,128)(2,1)}, bf16[384,896]{1,0:T(8,128)(2,1)}, u32[]{:S(2)}, u32[]{:S(2)}) collective-permute-start(bf16[384,896]{1,0:T(8,128)(2,1)} %collective-permute-done.1.refs_0_), channel_id=1, source_target_pairs={{0,1},{1,0},{4,5},{5,4},{8,9},{9,8},{12,13},{13,12},{14,15},{15,14... | collective-permute-start | bytes 2064392 | tf_op jit(solution)/shard_map/ppermute | solution.py:210
  55.0 1.5 copy-start.1
  58.4 17.2 %all-to-all-start = ((f32[16,24,128]{2,1,0:T(8,128)}), f32[16,24,128]{2,1,0:T(8,128)S(1)}, u32[]{:S(2)}, u32[]{:S(2)}) async-start(f32[16,24,128]{2,1,0:T(8,128)} %bitcast.3), calls=%async_computation | async-start | bytes 393216 | tf_op jit(solution)/shard_map/all_to_all | solution.py:86
  76.3 14.3 %all-to-all-start.1 = ((f32[16,24,128]{2,1,0:T(8,128)}), f32[16,24,128]{2,1,0:T(8,128)S(1)}, u32[]{:S(2)}, u32[]{:S(2)}) async-start(f32[16,24,128]{2,1,0:T(8,128)} %broadcast_in_dim.2), calls=%async_computation.1 | async-start | bytes 393216 | tf_op jit(solution)/shard_map/all_to_all | solution.py:89
  80.9 20.5 %collective-permute-start.2 = (bf16[384,896]{1,0:T(8,128)(2,1)}, bf16[384,896]{1,0:T(8,128)(2,1)S(1)}, u32[]{:S(2)}, u32[]{:S(2)}) collective-permute-start(bf16[384,896]{1,0:T(8,128)(2,1)} %collective-permute-done.1.refs_0_), channel_id=1, source_target_pairs={{0,4},{1,5},{4,8},{5,9},{8,12},{9,13},{12,14},{13,15},{14,10},{15,... | collective-permute-start | bytes 2064392 | tf_op jit(solution)/shard_map/ppermute | solution.py:204
  82.9 7.9 %collective-permute-start.23 = (bf16[384,896]{1,0:T(8,128)(2,1)}, bf16[384,896]{1,0:T(8,128)(2,1)}, u32[]{:S(2)}, u32[]{:S(2)}) collective-permute-start(bf16[384,896]{1,0:T(8,128)(2,1)} %collective-permute-done.6.refs_2_), channel_id=1, source_target_pairs={{0,1},{1,0},{4,5},{5,4},{8,9},{9,8},{12,13},{13,12},{14,15},{15,14... | collective-permute-start | bytes 2064392 | tf_op jit(solution)/shard_map/ppermute | solution.py:210
  82.9 9.8 %collective-permute-start.20 = (bf16[384,896]{1,0:T(8,128)(2,1)}, bf16[384,896]{1,0:T(8,128)(2,1)}, u32[]{:S(2)}, u32[]{:S(2)}) collective-permute-start(bf16[384,896]{1,0:T(8,128)(2,1)} %collective-permute-done.11.refs_0_), channel_id=1, source_target_pairs={{0,1},{1,0},{4,5},{5,4},{8,9},{9,8},{12,13},{13,12},{14,15},{15,14... | collective-permute-start | bytes 2064392 | tf_op jit(solution)/shard_map/ppermute | solution.py:210
  83.4 19.7 %collective-permute-start.7 = (bf16[384,896]{1,0:T(8,128)(2,1)}, bf16[384,896]{1,0:T(8,128)(2,1)}, u32[]{:S(2)}, u32[]{:S(2)}) collective-permute-start(bf16[384,896]{1,0:T(8,128)(2,1)} %collective-permute-done.6.refs_2_), channel_id=1, source_target_pairs={{4,0},{5,1},{8,4},{9,5},{12,8},{13,9},{14,12},{15,13},{10,14},{11,... | collective-permute-start | bytes 2064392 | tf_op jit(solution)/shard_map/ppermute | solution.py:205
  83.5 17.9 %collective-permute-start.21 = (bf16[384,896]{1,0:T(8,128)(2,1)}, bf16[384,896]{1,0:T(8,128)(2,1)}, u32[]{:S(2)}, u32[]{:S(2)}) collective-permute-start(bf16[384,896]{1,0:T(8,128)(2,1)} %collective-permute-done.15.refs_2_), channel_id=1, source_target_pairs={{0,1},{1,0},{4,5},{5,4},{8,9},{9,8},{12,13},{13,12},{14,15},{15,14... | collective-permute-start | bytes 2064392 | tf_op jit(solution)/shard_map/ppermute | solution.py:210
  84.3 1.1 copy-start.7
  85.4 1.1 copy-start.9
  90.8 25.4 %collective-permute-start.12 = (bf16[384,896]{1,0:T(8,128)(2,1)}, bf16[384,896]{1,0:T(8,128)(2,1)S(1)}, u32[]{:S(2)}, u32[]{:S(2)}) collective-permute-start(bf16[384,896]{1,0:T(8,128)(2,1)} %collective-permute-done.11.refs_0_), channel_id=1, source_target_pairs={{0,4},{1,5},{4,8},{5,9},{8,12},{9,13},{12,14},{13,15},{14,10},{15,... | collective-permute-start | bytes 2064392 | tf_op jit(solution)/shard_map/ppermute | solution.py:204
  92.7 24.6 %collective-permute-start.16 = (bf16[384,896]{1,0:T(8,128)(2,1)}, bf16[384,896]{1,0:T(8,128)(2,1)S(1)}, u32[]{:S(2)}, u32[]{:S(2)}) collective-permute-start(bf16[384,896]{1,0:T(8,128)(2,1)} %collective-permute-done.15.refs_2_), channel_id=1, source_target_pairs={{4,0},{5,1},{8,4},{9,5},{12,8},{13,9},{14,12},{15,13},{10,14},{11,... | collective-permute-start | bytes 2064392 | tf_op jit(solution)/shard_map/ppermute | solution.py:205
  101.4 15.9 %collective-permute-start.18 = (bf16[384,896]{1,0:T(8,128)(2,1)S(1)}, bf16[384,896]{1,0:T(8,128)(2,1)S(1)}, u32[]{:S(2)}, u32[]{:S(2)}) collective-permute-start(bf16[384,896]{1,0:T(8,128)(2,1)S(1)} %collective-permute-done.2.refs_0_), channel_id=1, source_target_pairs={{0,1},{1,0},{4,5},{5,4},{8,9},{9,8},{12,13},{13,12},{14,15},{15,14... | collective-permute-start | bytes 2064392 | tf_op jit(solution)/shard_map/ppermute | solution.py:210
  101.4 28.9 %collective-permute-start.3 = (bf16[384,896]{1,0:T(8,128)(2,1)S(1)}, bf16[384,896]{1,0:T(8,128)(2,1)S(1)}, u32[]{:S(2)}, u32[]{:S(2)}) collective-permute-start(bf16[384,896]{1,0:T(8,128)(2,1)S(1)} %collective-permute-done.2.refs_0_), channel_id=1, source_target_pairs={{0,4},{1,5},{4,8},{5,9},{8,12},{9,13},{12,14},{13,15},{14,10},{15,... | collective-permute-start | bytes 2064392 | tf_op jit(solution)/shard_map/ppermute | solution.py:204
  103.0 28.6 %collective-permute-start.8 = (bf16[384,896]{1,0:T(8,128)(2,1)}, bf16[384,896]{1,0:T(8,128)(2,1)S(1)}, u32[]{:S(2)}, u32[]{:S(2)}) collective-permute-start(bf16[384,896]{1,0:T(8,128)(2,1)} %collective-permute-done.7.refs_2_), channel_id=1, source_target_pairs={{4,0},{5,1},{8,4},{9,5},{12,8},{13,9},{14,12},{15,13},{10,14},{11,... | collective-permute-start | bytes 2064392 | tf_op jit(solution)/shard_map/ppermute | solution.py:205
  105.7 13.6 %copy-start.3 = (bf16[384,896]{1,0:T(8,128)(2,1)S(1)}, bf16[384,896]{1,0:T(8,128)(2,1)}, u32[]{:S(2)}) copy-start(bf16[384,896]{1,0:T(8,128)(2,1)} %copy-done.2) | copy-start | bytes 2064388
  105.7 13.6 %copy-start.5 = (bf16[384,896]{1,0:T(8,128)(2,1)S(1)}, bf16[384,896]{1,0:T(8,128)(2,1)}, u32[]{:S(2)}) copy-start(bf16[384,896]{1,0:T(8,128)(2,1)} %copy-done.4) | copy-start | bytes 2064388
  116.2 28.9 %collective-permute-start.19 = (bf16[384,896]{1,0:T(8,128)(2,1)}, bf16[384,896]{1,0:T(8,128)(2,1)S(1)}, u32[]{:S(2)}, u32[]{:S(2)}) collective-permute-start(bf16[384,896]{1,0:T(8,128)(2,1)} %collective-permute-done.7.refs_2_), channel_id=1, source_target_pairs={{0,1},{1,0},{4,5},{5,4},{8,9},{9,8},{12,13},{13,12},{14,15},{15,14... | collective-permute-start | bytes 2064392 | tf_op jit(solution)/shard_map/ppermute | solution.py:210
  117.3 32.0 %collective-permute-start.13 = (bf16[384,896]{1,0:T(8,128)(2,1)S(1)}, bf16[384,896]{1,0:T(8,128)(2,1)S(1)}, u32[]{:S(2)}, u32[]{:S(2)}) collective-permute-start(bf16[384,896]{1,0:T(8,128)(2,1)S(1)} %collective-permute-done.12.refs_0_), channel_id=1, source_target_pairs={{0,1},{1,0},{4,5},{5,4},{8,9},{9,8},{12,13},{13,12},{14,15},{15,14... | collective-permute-start | bytes 2064392 | tf_op jit(solution)/shard_map/ppermute | solution.py:210
  117.3 32.0 %collective-permute-start.17 = (bf16[384,896]{1,0:T(8,128)(2,1)S(1)}, bf16[384,896]{1,0:T(8,128)(2,1)S(1)}, u32[]{:S(2)}, u32[]{:S(2)}) collective-permute-start(bf16[384,896]{1,0:T(8,128)(2,1)S(1)} %collective-permute-done.16.refs_2_), channel_id=1, source_target_pairs={{0,1},{1,0},{4,5},{5,4},{8,9},{9,8},{12,13},{13,12},{14,15},{15,14... | collective-permute-start | bytes 2064392 | tf_op jit(solution)/shard_map/ppermute | solution.py:210
  130.3 26.2 %collective-permute-start.4 = (bf16[384,896]{1,0:T(8,128)(2,1)S(1)}, bf16[384,896]{1,0:T(8,128)(2,1)S(1)}, u32[]{:S(2)}, u32[]{:S(2)}) collective-permute-start(bf16[384,896]{1,0:T(8,128)(2,1)S(1)} %collective-permute-done.3.refs_0_), channel_id=1, source_target_pairs={{0,1},{1,0},{4,5},{5,4},{8,9},{9,8},{12,13},{13,12},{14,15},{15,14... | collective-permute-start | bytes 2064392 | tf_op jit(solution)/shard_map/ppermute | solution.py:210
  131.6 24.9 %collective-permute-start.9 = (bf16[384,896]{1,0:T(8,128)(2,1)S(1)}, bf16[384,896]{1,0:T(8,128)(2,1)S(1)}, u32[]{:S(2)}, u32[]{:S(2)}) collective-permute-start(bf16[384,896]{1,0:T(8,128)(2,1)S(1)} %collective-permute-done.8.refs_1_), channel_id=1, source_target_pairs={{0,1},{1,0},{4,5},{5,4},{8,9},{9,8},{12,13},{13,12},{14,15},{15,14... | collective-permute-start | bytes 2064392 | tf_op jit(solution)/shard_map/ppermute | solution.py:210

commit v3 on v2

v3 whole, which is shorter than its diff:
```python
import jax
import jax.numpy as jnp
import numpy as np
from jax import lax
from jax.experimental import pallas as pl
from jax.experimental.pallas import tpu as pltpu
from jax.sharding import PartitionSpec as P


LANES = 128


def chip_ring(mesh):
    line = mesh.devices.reshape(mesh.devices.shape[0], -1)[0]
    chips = {}
    for at, device in enumerate(line):
        place = tuple(getattr(device, "coords", (at, 0, 0)))
        chips.setdefault(place, []).append(at)
    places = list(chips)
    if len({len(c) for c in chips.values()}) != 1:
        return [[at] for at in range(len(line))], False
    used = [k for k in range(len(places[0])) if len({p[k] for p in places}) > 1]
    if len(used) == 2:
        sizes = [len({p[k] for p in places}) for k in used]
        if 2 in sizes and sizes[0] * sizes[1] == len(places):
            short = used[sizes.index(2)]
            long = used[0] if short == used[1] else used[1]
            low = min(p[short] for p in places)
            up = sorted((p for p in places if p[short] == low), key=lambda p: p[long])
            down = sorted((p for p in places if p[short] != low), key=lambda p: -p[long])
            places = up + down
            return [chips[p] for p in places], True
    return [chips[p] for p in places], False


def project_selected(rows, labels, factors, first):
    count, rank, units = factors.shape
    total = rows.shape[0]
    wide = count * rank
    part = total // 2

    def body(f_ref, x_ref, l_ref, a_ref, mine_ref, other_ref, s_ref):
        full = lax.dot_general(
            x_ref[...], a_ref[...], (((1,), (1,)), ((), ())), preferred_element_type=jnp.float32
        )
        own = jnp.zeros((total, rank), jnp.float32)
        for k in range(count):
            own = own + jnp.where(l_ref[...] == k, full[:, k * rank : (k + 1) * rank], 0.0)
        s_ref[...] = jnp.concatenate([own, full[:, :rank]], axis=1)
        at = f_ref[0]
        mine_ref[...] = s_ref[pl.ds(pl.multiple_of(at * part, 8), part), :]
        other_ref[...] = s_ref[pl.ds(pl.multiple_of((1 - at) * part, 8), part), :]

    vmem = pl.BlockSpec(memory_space=pltpu.VMEM)
    shape = jax.ShapeDtypeStruct((part, 2 * rank), jnp.float32)
    return pl.pallas_call(
        body,
        out_shape=(shape, shape),
        in_specs=[pl.BlockSpec(memory_space=pltpu.SMEM)] + [vmem] * 3,
        out_specs=(vmem, vmem),
        scratch_shapes=[pltpu.VMEM((total, 2 * rank), jnp.float32)],
        cost_estimate=pl.CostEstimate(
            flops=2 * total * wide * units,
            transcendentals=0,
            bytes_accessed=2 * units * (total + wide) + 8 * total * rank,
        ),
        compiler_params=pltpu.CompilerParams(vmem_limit_bytes=32 << 20),
    )(first.reshape(1), rows, labels[:, None], factors.reshape(wide, units))


def labels_onehot(adapter_labels, count):
    return adapter_labels[:, None] == jnp.arange(count, dtype=jnp.int32)[None, :]


def select_both(project_rows, adapter_labels, count, rank):
    choose = labels_onehot(adapter_labels, count).astype(jnp.float32)
    total = project_rows.shape[0]
    own = jnp.sum(project_rows.reshape(total, count, rank) * choose[:, :, None], axis=1)
    return jnp.concatenate([own, project_rows[:, :rank]], axis=1)


def expand_factor(shrunk_rows, adapter_labels, adapter_output_weight):
    count, rank, width = adapter_output_weight.shape
    total = shrunk_rows.shape[0]
    choose = labels_onehot(adapter_labels, count).astype(jnp.float32)
    spread = (choose[:, :, None] * shrunk_rows[:, None, :rank].astype(jnp.float32)).reshape(
        total, count * rank
    )
    operand = jnp.concatenate([spread.astype(jnp.bfloat16), shrunk_rows[:, rank:]], axis=1)
    stacked = jnp.concatenate(
        [adapter_output_weight.reshape(count * rank, width), -adapter_output_weight[0]], axis=0
    )
    return jnp.dot(operand, stacked, preferred_element_type=jnp.float32)


def adapter_terms(summed, labels, outputs):
    rank = outputs.shape[1]
    keep = (labels != 0).astype(jnp.float32)[:, None]
    shrunk_rows = (summed * keep).astype(jnp.bfloat16)
    resident = jnp.dot(
        summed[:, rank:], outputs[0].astype(jnp.float32), precision=lax.Precision.HIGHEST
    )
    return resident + expand_factor(shrunk_rows, labels, outputs)


def sum_over_row(summand, axis_size):
    rows, cols = summand.shape
    if rows % axis_size:
        return lax.psum(summand, "row")
    parts = lax.all_to_all(summand, "row", 0, 0, tiled=True)
    mine = jnp.sum(parts.reshape(axis_size, rows // axis_size, cols), axis=0)
    spread = jnp.broadcast_to(mine[None], (axis_size,) + mine.shape).reshape(rows, cols)
    return lax.all_to_all(spread, "row", 0, 0, tiled=True)


def swap(rows, at, pairs):
    part = rows.shape[0] // 2
    low, high = rows[:part], rows[part:]
    got = lax.ppermute(jnp.where(at == 0, high, low), "row", pairs)
    return jnp.where(at == 0, low, high) + got


def join(part, at, pairs):
    got = lax.ppermute(part, "row", pairs)
    return jnp.concatenate([jnp.where(at == 0, part, got), jnp.where(at == 0, got, part)], axis=0)


def sum_by_stages(mine, other, core, side, partner, across, lines):
    got = lax.ppermute(other, "row", partner)
    rows = swap(mine + got, side, across)
    size = len(lines[0])
    piece = rows.shape[0] // size
    parts = lax.all_to_all(rows, "row", 0, 0, axis_index_groups=lines, tiled=True)
    total = jnp.sum(parts.reshape(size, piece, rows.shape[1]), axis=0)
    spread = jnp.broadcast_to(total[None], (size,) + total.shape).reshape(rows.shape)
    whole = lax.all_to_all(spread, "row", 0, 0, axis_index_groups=lines, tiled=True)
    return join(join(whole, side, across), core, partner)


def chunk_matmul(chunks, starts, first, weight, before, extra, out_dtype):
    count = len(chunks)
    rows = chunks[0].shape[0]
    widths = [c.shape[1] for c in chunks]
    features = weight.shape[0]
    added = [a for a in (before, extra) if a is not None]

    def body(starts_ref, *refs):
        x_refs = refs[:count]
        w_ref = refs[count]
        add_refs = refs[count + 1 : count + 1 + len(added)]
        rest = refs[count + 1 + len(added) :]
        out_ref, x_bufs, w_bufs = rest[0], rest[1 : 1 + count], rest[1 + count : 1 + 2 * count]
        x_sem, w_sem = rest[1 + 2 * count :]
        copies = []
        for k in range(count):
            start = pl.multiple_of(starts_ref[first + k] * LANES, LANES)
            cx = pltpu.make_async_copy(x_refs[k], x_bufs[k], x_sem.at[k])
            cw = pltpu.make_async_copy(w_ref.at[:, pl.ds(start, widths[k])], w_bufs[k], w_sem.at[k])
            cw.start()
            cx.start()
            copies.append((cx, cw))
        total = None
        for k in range(count):
            copies[k][1].wait()
            copies[k][0].wait()
            part = lax.dot_general(
                x_bufs[k][...], w_bufs[k][...], (((1,), (1,)), ((), ())), preferred_element_type=jnp.float32
            )
            total = part if total is None else total + part
        for ref in add_refs:
            total = total + ref[...]
        out_ref[...] = total.astype(out_dtype)

    anywhere = pl.BlockSpec(memory_space=pl.ANY)
    vmem = pl.BlockSpec(memory_space=pltpu.VMEM)
    return pl.pallas_call(
        body,
        out_shape=jax.ShapeDtypeStruct((rows, features), out_dtype),
        in_specs=[pl.BlockSpec(memory_space=pltpu.SMEM)]
        + [anywhere] * (count + 1)
        + [vmem] * len(added),
        out_specs=vmem,
        scratch_shapes=[pltpu.VMEM((rows, w), jnp.bfloat16) for w in widths]
        + [pltpu.VMEM((features, w), jnp.bfloat16) for w in widths]
        + [
            pltpu.SemaphoreType.DMA((count,)),
            pltpu.SemaphoreType.DMA((count,)),
        ],
        cost_estimate=pl.CostEstimate(
            flops=2 * rows * sum(widths) * features,
            transcendentals=0,
            bytes_accessed=2 * sum(widths) * (rows + features) + 8 * rows * features,
        ),
        compiler_params=pltpu.CompilerParams(vmem_limit_bytes=48 << 20),
    )(starts, *chunks, weight, *added)


def solution(mesh):
    axis_size = mesh.shape["row"]
    ring, snake = chip_ring(mesh)
    chips, cores = len(ring), len(ring[0])
    forward = [(ring[p][c], ring[(p + 1) % chips][c]) for p in range(chips) for c in range(cores)]
    backward = [(b, a) for a, b in forward]
    partner = [(members[c], members[1 - c]) for members in ring for c in range(cores)] if cores == 2 else []

    long = chips // 2
    across = [(ring[p][c], ring[chips - 1 - p][c]) for p in range(chips) for c in range(cores)]
    lines = [
        [ring[p][c] for p in range(lo, lo + long)] for lo in (0, long) for c in range(cores)
    ]
    place = np.zeros((axis_size, 2), np.int32)
    for p, members in enumerate(ring):
        for c, at in enumerate(members):
            place[at] = c, int(p >= long)

    def plain(flat, weight, factors, outputs, labels):
        count, rank, units = factors.shape
        project_rows = jnp.dot(
            flat, factors.reshape(count * rank, units).T, preferred_element_type=jnp.float32
        )
        summed = sum_over_row(select_both(project_rows, labels, count, rank), axis_size)
        base = lax.dot_general(
            lax.all_gather(flat, "row", axis=1, tiled=True),
            weight,
            (((1,), (1,)), ((), ())),
            preferred_element_type=jnp.float32,
        )
        return (base + adapter_terms(summed, labels, outputs)).astype(jnp.bfloat16)

    def ringed(flat, weight, factors, outputs, labels):
        device_units = flat.shape[1]
        half = device_units // 2
        tiles = half // LANES
        cut = (tiles - tiles * 3 // 7) * LANES
        me = lax.axis_index("row")
        core, side = [jnp.asarray(place)[me][k] for k in range(2)]
        mine, other = project_selected(flat, labels, factors, core)
        summed = sum_by_stages(mine, other, core, side, partner, across, lines)
        extra = adapter_terms(summed, labels, outputs)

        plan = [(s // 2 + 1, s % 2, 0, half) for s in range(2 * long - 2)]
        plan += [(long, 0, 0, cut), (long, 0, cut, half - cut)]
        own = [flat[:, :half], flat[:, half:]]
        beside = lax.ppermute(flat, "row", partner)
        batches = [[(flat, 0, False, 0, 0), (beside, 0, True, 0, 0)]]
        held = {"up": list(own), "down": list(own)}
        for distance, turn, column, width in plan:
            found = []
            for way, pairs, part in (("up", forward, turn), ("down", backward, 1 - turn)):
                send = held[way][part]
                if width < half:
                    send = send[:, column : column + width]
                data = lax.ppermute(send, "row", pairs)
                if width == half:
                    held[way][part] = data
                beside = lax.ppermute(data, "row", partner)
                offset = -distance if way == "up" else distance
                found.append((data, offset, False, part, column))
                found.append((beside, offset, True, part, column))
            batches.append(found)
        batches[-1:] = [batches[-1][::2], batches[-1][1::2]]
        order = [entry[1:] for found in batches for entry in found]
        table = np.zeros((axis_size, len(order)), np.int32)
        for p, members in enumerate(ring):
            for c, at in enumerate(members):
                for k, (offset, beside, part, column) in enumerate(order):
                    source = ring[(p + offset) % chips][1 - c if beside else c]
                    table[at, k] = (source * device_units + part * half + column) // LANES
        starts = jnp.asarray(table)[me]
        acc = None
        done = 0
        for k, found in enumerate(batches):
            last = k == len(batches) - 1
            acc = chunk_matmul(
                [entry[0] for entry in found],
                starts,
                done,
                weight,
                acc,
                extra if k == len(batches) - 4 else None,
                jnp.bfloat16 if last else jnp.float32,
            )
            done += len(found)
        return acc

    def local(
        gated_hidden_rows,
        down_base_weight,
        adapter_input_factor,
        adapter_output_weight,
        request_adapter_index,
    ):
        steps, requests, device_units = gated_hidden_rows.shape
        total = steps * requests
        fits = device_units % (2 * LANES) == 0 and total % (32 * max(long, 1)) == 0
        run = ringed if snake and cores == 2 and long > 1 and fits else plain
        out = run(
            gated_hidden_rows.reshape(total, device_units),
            down_base_weight,
            adapter_input_factor,
            adapter_output_weight,
            request_adapter_index.reshape(total),
        )
        return out.reshape(steps, requests, out.shape[1])

    placed = (
        P(None, "groups", "row"),
        P("row", None),
        P(None, None, "row"),
        P(None, None, "row"),
        P(None, "groups"),
    )

    return jax.shard_map(
        local, mesh=mesh, in_specs=placed, out_specs=P(None, "groups", "row"), check_vma=False
    )
```

time: 161 us -> 185 us (1.15)
  blocking collectives: 0 us -> 27.2 us
  waiting for transfers between devices: 78.3 us -> 68.4 us
  local copies, waits for them, and re-layouts: 10.5 us -> 14.7 us
  starting transfers between devices: 28.5 us -> 24.8 us
  other arithmetic: 0.97 us -> 4.33 us
  Pallas kernels: 38.8 us -> 42 us
  matrix products: 2.9 us -> 1.02 us
    all_to_all x0 -> x2, blocking collectives: none -> 27.2 us  [the longest x1 15.7 us: sum_by_stages(): lax.all_to_all(rows, 'row', 0, 0, axis_index_groups=lines, tiled=True)]
    all_to_all x2 -> x0, starting transfers between devices: 10.9 us -> none  [the longest x1 6.27 us: sum_over_row(): parts = lax.all_to_all(summand, 'row', 0, 0, tiled=True)]
    all_to_all x2 -> x0, waiting for transfers between devices: 10 us -> none  [the longest x1 10 us: sum_over_row(): parts = lax.all_to_all(summand, 'row', 0, 0, tiled=True)]
    ppermute x30 -> x37, starting transfers between devices: 17.6 us -> 24.8 us  [the longest x16 19.5 us: ringed(): data = lax.ppermute(send, 'row', pairs)]
    slice x1 -> x7, local copies, waits for them, and re-layouts: 1.52 us -> 4.81 us  [the longest x1 2.5 us: ringed(): own = [flat[:, :half], flat[:, half:]]]
    pallas_call x9 -> x10, Pallas kernels: 37 us -> 38.8 us  [chunk_matmul(): pl.pallas_call(body, out_shape=jax.ShapeDtypeStruct((rows, features), out...]
    unnamed x22 -> x40, local copies, waits for them, and re-layouts: 7.22 us -> 5.85 us
    ppermute x30 -> x37, waiting for transfers between devices: 68.3 us -> 68.4 us  [the longest x16 65.6 us: ringed(): data = lax.ppermute(send, 'row', pairs)]
  transfers between devices with their start and end apart: 32 -> 37, of which waited for: 10 -> 14; matrix products, arithmetic and copies ran while one was open for 4% -> 7% of each run, Pallas kernels for 22% -> 19%
where the time goes in v3:
time: 185 us
  waiting for transfers between devices  68.4 us (37%)
  Pallas kernels  42 us (23%)
  blocking collectives  27.2 us (15%)
  starting transfers between devices  24.8 us (13%)
  local copies, waits for them, and re-layouts  14.7 us (8%)
  other arithmetic  4.33 us (2%)
  between operations  2.01 us (1%)
    ppermute x16, waiting for transfers between devices, ringed(): data = lax.ppermute(send, 'row', pairs)  65.6 us
    pallas_call x10, Pallas kernels, chunk_matmul(): pl.pallas_call(body, out_shape=jax.ShapeDtypeStruct((rows, features), out...  38.8 us
    ppermute x16, starting transfers between devices, ringed(): data = lax.ppermute(send, 'row', pairs)  19.5 us
    all_to_all x1, blocking collectives, sum_by_stages(): lax.all_to_all(rows, 'row', 0, 0, axis_index_groups=lines, tiled=True)  15.7 us
    all_to_all x1, blocking collectives, sum_by_stages(): lax.all_to_all(spread, 'row', 0, 0, axis_index_groups=lines, tiled=True)  11.5 us
    unnamed x40, local copies, waits for them, and re-layouts  5.85 us
  transfers between devices with their start and end apart: 37, of which 14 were waited for; matrix products, arithmetic and copies ran while one was open for 7% of the time, Pallas kernels for 19%

profile of v3, /device:TPU:0, one launch (start us, length us, event | category | flops | bytes accessed | tf_op | source)
XLA Modules:
  0.0 184.5 jit_solution(12460964714664374247)
XLA Ops:
  1.3 0.9 broadcast_in_dim_reshape.5.l_ref
  2.2 1.5 copy-done
  3.7 3.2 %shard_map.79 = (f32[192,128]{1,0:T(8,128)S(1)}, f32[192,128]{1,0:T(8,128)S(1)}) custom-call(s32[1]{0:T(128)} %bitcast.4.f_ref, bf16[384,1792]{1,0:T(8,128)(2,1)} %bitcast.1.refs_0_.x_ref, s32[384,1]{1,0:T(8,128)S(1)} %broadcast_in_dim_reshape.5.l_ref, bf16[512,1792]{1,0:T(8,128)(2,1)S(1)} %bitcast.18), custom_call_target="tpu_custom_call" | custom-call | flops 704643072 | bytes 3407872 | tf_op jit(solution)/shard_map/pallas_call | solution.py:56
  8.4 2.9 %collective-permute-start.34 = (f32[96,128]{1,0:T(8,128)S(1)}, f32[96,128]{1,0:T(8,128)S(1)}, u32[]{:S(2)}, u32[]{:S(2)}) collective-permute-start(f32[96,128]{1,0:T(8,128)S(1)} %slice_select_fusion), channel_id=1, source_target_pairs={{0,2},{1,3},{4,6},{5,7},{8,10},{9,11},{12,14},{13,15},{14,12},{15,... | collective-permute-start | bytes 147464 | tf_op jit(solution)/shard_map/ppermute | solution.py:119
  11.3 2.5 %fusion.16 = (bf16[384,896]{1,0:T(8,128)(2,1)}, bf16[384,896]{1,0:T(8,128)(2,1)}) fusion(bf16[384,1792]{1,0:T(8,128)(2,1)} %bitcast.1.refs_0_.x_ref), kind=kLoop, calls=%fused_computation.33 | loop fusion | bytes 2752512 | tf_op jit(solution)/shard_map/slice | solution.py:243
  13.8 1.6 collective-permute-start
  15.4 15.7 %all_to_all.18 = f32[4,24,128]{2,1,0:T(8,128)S(1)} all-to-all(f32[4,24,128]{2,1,0:T(8,128)S(1)} %bitcast.21), channel_id=1, replica_groups={{0,4,8,12},{1,5,9,13},{14,10,6,2},{15,11,7,3},{16,20,24,28},{17,21,25,2..., dimensions={0} | all-to-all | bytes 98304 | tf_op jit(solution)/shard_map/all_to_all | solution.py:133
  31.2 11.5 %all_to_all.19 = f32[4,24,128]{2,1,0:T(8,128)S(1)} all-to-all(f32[4,24,128]{2,1,0:T(8,128)S(1)} %broadcast_in_dim.2), channel_id=1, replica_groups={{0,4,8,12},{1,5,9,13},{14,10,6,2},{15,11,7,3},{16,20,24,28},{17,21,25,2..., dimensions={0} | all-to-all | bytes 98304 | tf_op jit(solution)/shard_map/all_to_all | solution.py:136
  42.7 2.0 %collective-permute-start.5 = (bf16[384,896]{1,0:T(8,128)(2,1)}, bf16[384,896]{1,0:T(8,128)(2,1)S(1)}, u32[]{:S(2)}, u32[]{:S(2)}) collective-permute-start(bf16[384,896]{1,0:T(8,128)(2,1)} %get-tuple-element.9), channel_id=1, source_target_pairs={{4,0},{5,1},{8,4},{9,5},{12,8},{13,9},{14,12},{15,13},{10,14},{11,... | collective-permute-start | bytes 2064392 | tf_op jit(solution)/shard_map/ppermute | solution.py:253
  44.7 2.1 %collective-permute-done.35 = f32[96,128]{1,0:T(8,128)S(1)} collective-permute-done((f32[96,128]{1,0:T(8,128)S(1)}, f32[96,128]{1,0:T(8,128)S(1)}, u32[]{:S(2)}, u32[]{:S(2)}) %collective-permute-start.35) | collective-permute-done | bytes 49184 | tf_op jit(solution)/shard_map/ppermute | solution.py:124
  46.9 0.9 collective-permute-start.14
  49.0 12.2 %collective-permute-done.5.refs_2_ = bf16[384,896]{1,0:T(8,128)(2,1)S(1)} collective-permute-done((bf16[384,896]{1,0:T(8,128)(2,1)}, bf16[384,896]{1,0:T(8,128)(2,1)S(1)}, u32[]{:S(2)}, u32[]{:S(2)}) %collective-permute-start.5) | collective-permute-done | bytes 688160 | tf_op jit(solution)/shard_map/ppermute | solution.py:253
  61.2 3.8 %collective-permute-done.14.refs_0_ = bf16[384,896]{1,0:T(8,128)(2,1)} collective-permute-done((bf16[384,896]{1,0:T(8,128)(2,1)}, bf16[384,896]{1,0:T(8,128)(2,1)}, u32[]{:S(2)}, u32[]{:S(2)}) %collective-permute-start.14) | collective-permute-done | bytes 688160 | tf_op jit(solution)/shard_map/ppermute | solution.py:253
  65.1 7.1 %collective-permute-done.18.refs_2_ = bf16[384,896]{1,0:T(8,128)(2,1)} collective-permute-done((bf16[384,896]{1,0:T(8,128)(2,1)}, bf16[384,896]{1,0:T(8,128)(2,1)}, u32[]{:S(2)}, u32[]{:S(2)}) %collective-permute-start.18) | collective-permute-done | bytes 688160 | tf_op jit(solution)/shard_map/ppermute | solution.py:253
  73.0 0.8 copy-done.3
  73.9 1.3 collective-permute-start.6
  75.2 0.8 copy-done.1
  76.1 0.9 copy-done.5
  77.7 1.4 collective-permute-start.19
  79.1 11.6 %collective-permute-done.1.refs_0_ = bf16[384,896]{1,0:T(8,128)(2,1)} collective-permute-done((bf16[384,896]{1,0:T(8,128)(2,1)S(1)}, bf16[384,896]{1,0:T(8,128)(2,1)}, u32[]{:S(2)}, u32[]{:S(2)}) %collective-permute-start.1) | collective-permute-done | bytes 688160 | tf_op jit(solution)/shard_map/ppermute | solution.py:253
  91.4 0.9 collective-permute-done.6.refs_2_
  93.7 1.5 bitcast_negate_fusion
  95.2 10.3 %collective-permute-done.15.refs_0_ = bf16[384,896]{1,0:T(8,128)(2,1)} collective-permute-done((bf16[384,896]{1,0:T(8,128)(2,1)}, bf16[384,896]{1,0:T(8,128)(2,1)}, u32[]{:S(2)}, u32[]{:S(2)}) %collective-permute-start.15) | collective-permute-done | bytes 688160 | tf_op jit(solution)/shard_map/ppermute | solution.py:253
  105.4 2.0 %collective-permute-start.7 = (bf16[384,896]{1,0:T(8,128)(2,1)}, bf16[384,896]{1,0:T(8,128)(2,1)S(1)}, u32[]{:S(2)}, u32[]{:S(2)}) collective-permute-start(bf16[384,896]{1,0:T(8,128)(2,1)} %collective-permute-done.6.refs_2_), channel_id=1, source_target_pairs={{4,0},{5,1},{8,4},{9,5},{12,8},{13,9},{14,12},{15,13},{10,14},{11,... | collective-permute-start | bytes 2064392 | tf_op jit(solution)/shard_map/ppermute | solution.py:253
  107.5 0.9 broadcast_select_fusion.1
  108.5 0.8 copy-done.7
  109.3 0.9 copy-done.9
  110.7 8.1 %collective-permute-done.2.refs_0_ = bf16[384,896]{1,0:T(8,128)(2,1)S(1)} collective-permute-done((bf16[384,896]{1,0:T(8,128)(2,1)}, bf16[384,896]{1,0:T(8,128)(2,1)S(1)}, u32[]{:S(2)}, u32[]{:S(2)}) %collective-permute-start.2) | collective-permute-done | bytes 688160 | tf_op jit(solution)/shard_map/ppermute | solution.py:253
  118.8 3.2 %collective-permute-start.20 = (bf16[384,896]{1,0:T(8,128)(2,1)}, bf16[384,896]{1,0:T(8,128)(2,1)}, u32[]{:S(2)}, u32[]{:S(2)}) collective-permute-start(bf16[384,896]{1,0:T(8,128)(2,1)} %collective-permute-done.19.refs_2_), channel_id=1, source_target_pairs={{4,0},{5,1},{8,4},{9,5},{12,8},{13,9},{14,12},{15,13},{10,14},{11,... | collective-permute-start | bytes 2064392 | tf_op jit(solution)/shard_map/ppermute | solution.py:253
  122.9 1.7 copy.12
  124.5 1.6 copy.13
  126.3 1.0 multiply_convert_fusion
  127.3 2.0 %collective-permute-start.8 = (bf16[384,384]{1,0:T(8,128)(2,1)S(1)}, bf16[384,384]{1,0:T(8,128)(2,1)S(1)}, u32[]{:S(2)}, u32[]{:S(2)}) collective-permute-start(bf16[384,384]{1,0:T(8,128)(2,1)S(1)} %slice.65), channel_id=1, source_target_pairs={{4,0},{5,1},{8,4},{9,5},{12,8},{13,9},{14,12},{15,13},{10,14},{11,... | collective-permute-start | bytes 884744 | tf_op jit(solution)/shard_map/ppermute | solution.py:253
  130.0 3.6 %collective-permute-done.16.refs_0_ = bf16[384,896]{1,0:T(8,128)(2,1)} collective-permute-done((bf16[384,896]{1,0:T(8,128)(2,1)}, bf16[384,896]{1,0:T(8,128)(2,1)}, u32[]{:S(2)}, u32[]{:S(2)}) %collective-permute-start.16) | collective-permute-done | bytes 688160 | tf_op jit(solution)/shard_map/ppermute | solution.py:253
  133.7 5.2 %collective-permute-done.20.refs_2_ = bf16[384,896]{1,0:T(8,128)(2,1)} collective-permute-done((bf16[384,896]{1,0:T(8,128)(2,1)}, bf16[384,896]{1,0:T(8,128)(2,1)}, u32[]{:S(2)}, u32[]{:S(2)}) %collective-permute-start.20) | collective-permute-done | bytes 688160 | tf_op jit(solution)/shard_map/ppermute | solution.py:253
  138.8 1.1 collective-permute-done.3.refs_0_
  140.4 1.8 collective-permute-done.8.refs_1_
  142.3 4.7 %shard_map.73.refs_5_ = f32[384,512]{1,0:T(8,128)S(1)} custom-call(s32[34]{0:T(128)S(1)} %dynamic-slice_bitcast_fusion.starts_ref, bf16[384,1792]{1,0:T(8,128)(2,1)} %bitcast.1.refs_0_.x_ref, bf16[384,1792]{1,0:T(8,128)(2,1)S(1)} %collective-permute-done.32.refs_1_, bf16[512,28672]{1,0:T(8,128)(2,1)} %refs_2_.5), custom_call_target="tpu_custom_call" | custom-call | flops 1409286144 | bytes 7995392 | tf_op jit(solution)/shard_map/pallas_call | solution.py:176
  147.0 1.8 %collective-permute-start.12 = (bf16[384,512]{1,0:T(8,128)(2,1)S(1)}, bf16[384,512]{1,0:T(8,128)(2,1)S(1)}, u32[]{:S(2)}, u32[]{:S(2)}) collective-permute-start(bf16[384,512]{1,0:T(8,128)(2,1)S(1)} %slice.67), channel_id=1, source_target_pairs={{4,0},{5,1},{8,4},{9,5},{12,8},{13,9},{14,12},{15,13},{10,14},{11,... | collective-permute-start | bytes 1179656 | tf_op jit(solution)/shard_map/ppermute | solution.py:253
  148.8 4.1 %shard_map.74.refs_5_ = f32[384,512]{1,0:T(8,128)S(1)} custom-call(s32[34]{0:T(128)S(1)} %dynamic-slice_bitcast_fusion.starts_ref, bf16[384,896]{1,0:T(8,128)(2,1)S(1)} %collective-permute-done.refs_0_, bf16[384,896]{1,0:T(8,128)(2,1)S(1)} %copy-done.4, bf16[384,896]{1,0:T(8,128)(2,1)S(1)} %copy-done.2, bf16[384,896]{1,0:T(8,128)(2,1)S(1)} %copy-done.6, ...), custom_call_target="tpu_custom_call" | custom-call | flops 1409286144 | bytes 7995392 | tf_op jit(solution)/shard_map/pallas_call | solution.py:176
  153.0 4.5 %shard_map.75.refs_5_ = f32[384,512]{1,0:T(8,128)S(1)} custom-call(s32[34]{0:T(128)S(1)} %dynamic-slice_bitcast_fusion.starts_ref, bf16[384,896]{1,0:T(8,128)(2,1)} %collective-permute-done.14.refs_0_, bf16[384,896]{1,0:T(8,128)(2,1)} %collective-permute-done.28.refs_1_, bf16[384,896]{1,0:T(8,128)(2,1)} %collective-permute-done.18.refs_2_, ...), custom_call_target="tpu_custom_call" | custom-call | flops 1409286144 | bytes 7995392 | tf_op jit(solution)/shard_map/pallas_call | solution.py:176
  157.5 4.3 %shard_map.76.refs_5_ = f32[384,512]{1,0:T(8,128)S(1)} custom-call(s32[34]{0:T(128)S(1)} %dynamic-slice_bitcast_fusion.starts_ref, bf16[384,896]{1,0:T(8,128)(2,1)} %collective-permute-done.1.refs_0_, bf16[384,896]{1,0:T(8,128)(2,1)S(1)} %copy-done.8, bf16[384,896]{1,0:T(8,128)(2,1)} %collective-permute-done.6.refs_2_, bf16[384,896]{1,0:T(8,128)(2,1)S(1)} %copy-done.10, ...), custom_call_target="tpu_custom_call" | custom-call | flops 1409286144 | bytes 7995392 | tf_op jit(solution)/shard_map/pallas_call | solution.py:176
  162.4 4.5 %shard_map.77.refs_5_ = f32[384,512]{1,0:T(8,128)S(1)} custom-call(s32[34]{0:T(128)S(1)} %dynamic-slice_bitcast_fusion.starts_ref, bf16[384,896]{1,0:T(8,128)(2,1)} %collective-permute-done.15.refs_0_, bf16[384,896]{1,0:T(8,128)(2,1)} %collective-permute-done.24.refs_1_, bf16[384,896]{1,0:T(8,128)(2,1)} %collective-permute-done.19.refs_2_, ...), custom_call_target="tpu_custom_call" | custom-call | flops 1409286144 | bytes 7995392 | tf_op jit(solution)/shard_map/pallas_call | solution.py:176
  167.4 4.1 %shard_map.78.refs_5_ = f32[384,512]{1,0:T(8,128)S(1)} custom-call(s32[34]{0:T(128)S(1)} %dynamic-slice_bitcast_fusion.starts_ref, bf16[384,896]{1,0:T(8,128)(2,1)S(1)} %collective-permute-done.2.refs_0_, bf16[384,896]{1,0:T(8,128)(2,1)S(1)} %collective-permute-done.22.refs_1_, bf16[384,896]{1,0:T(8,128)(2,1)S(1)} %collective-permute-done.7.refs_2_, ...), custom_call_target="tpu_custom_call" | custom-call | flops 1409286144 | bytes 7995392 | tf_op jit(solution)/shard_map/pallas_call | solution.py:176
  171.6 4.3 %shard_map.80.refs_5_ = f32[384,512]{1,0:T(8,128)S(1)} custom-call(s32[34]{0:T(128)S(1)} %dynamic-slice_bitcast_fusion.starts_ref, bf16[384,896]{1,0:T(8,128)(2,1)} %collective-permute-done.16.refs_0_, bf16[384,896]{1,0:T(8,128)(2,1)S(1)} %collective-permute-done.17.refs_1_, bf16[384,896]{1,0:T(8,128)(2,1)} %collective-permute-done.20.refs_2_, ...), custom_call_target="tpu_custom_call" | custom-call | flops 1409286144 | bytes 7995392 | tf_op jit(solution)/shard_map/pallas_call | solution.py:176
  175.9 3.1 %shard_map.81.refs_3_ = f32[384,512]{1,0:T(8,128)S(1)} custom-call(s32[34]{0:T(128)S(1)} %dynamic-slice_bitcast_fusion.starts_ref, bf16[384,512]{1,0:T(8,128)(2,1)S(1)} %collective-permute-done.10.refs_0_, bf16[384,512]{1,0:T(8,128)(2,1)S(1)} %collective-permute-done.11.refs_1_, bf16[384,512]{1,0:T(8,128)(2,1)S(1)} %collective-permute-done.12.refs_2_, ...), custom_call_target="tpu_custom_call" | custom-call | flops 805306368 | bytes 5242880 | tf_op jit(solution)/shard_map/pallas_call | solution.py:176
  178.9 2.3 %shard_map.82.refs_3_ = f32[384,512]{1,0:T(8,128)S(1)} custom-call(s32[34]{0:T(128)S(1)} %dynamic-slice_bitcast_fusion.starts_ref, bf16[384,384]{1,0:T(8,128)(2,1)S(1)} %collective-permute-done.3.refs_0_, bf16[384,384]{1,0:T(8,128)(2,1)S(1)} %collective-permute-done.8.refs_1_, bf16[512,28672]{1,0:T(8,128)(2,1)} %refs_2_.5, f32[384,512]{1,0:T(8,128)S(1)} %shard_map.81.refs_3_), custom_call_target="tpu_custom_call" | custom-call | flops 301989888 | bytes 2949120 | tf_op jit(solution)/shard_map/pallas_call | solution.py:176
  181.3 3.1 %shard_map.83 = bf16[384,512]{1,0:T(8,128)(2,1)} custom-call(s32[34]{0:T(128)S(1)} %dynamic-slice_bitcast_fusion.starts_ref, bf16[384,384]{1,0:T(8,128)(2,1)S(1)} %collective-permute-done.4.refs_0_, bf16[384,384]{1,0:T(8,128)(2,1)S(1)} %collective-permute-done.9.refs_1_, bf16[512,28672]{1,0:T(8,128)(2,1)} %refs_2_.5, f32[384,512]{1,0:T(8,128)S(1)} %shard_map.82.refs_3_), custom_call_target="tpu_custom_call" | custom-call | flops 301989888 | bytes 2949120 | tf_op jit(solution)/shard_map/pallas_call | solution.py:176
  (107 shorter events, 10.6 us)
Async XLA Ops:
  6.9 1.5 collective-permute-start.33
  7.4 65.6 %collective-permute-start.32 = (bf16[384,1792]{1,0:T(8,128)(2,1)}, bf16[384,1792]{1,0:T(8,128)(2,1)S(1)}, u32[]{:S(2)}, u32[]{:S(2)}) collective-permute-start(bf16[384,1792]{1,0:T(8,128)(2,1)} %bitcast.1.refs_0_.x_ref), channel_id=1, source_target_pairs={{0,1},{1,0},{4,5},{5,4},{8,9},{9,8},{12,13},{13,12},{14,15},{15,14... | collective-permute-start | bytes 4128776 | tf_op jit(solution)/shard_map/ppermute | solution.py:244
  8.4 67.6 %copy-start.19 = (s32[2,192]{1,0:T(2,128)S(1)}, s32[2,192]{1,0:T(2,128)}, u32[]{:S(2)}) copy-start(s32[2,192]{1,0:T(2,128)} %param.11) | copy-start | bytes 4612
  8.4 7.0 %collective-permute-start.34 = (f32[96,128]{1,0:T(8,128)S(1)}, f32[96,128]{1,0:T(8,128)S(1)}, u32[]{:S(2)}, u32[]{:S(2)}) collective-permute-start(f32[96,128]{1,0:T(8,128)S(1)} %slice_select_fusion), channel_id=1, source_target_pairs={{0,2},{1,3},{4,6},{5,7},{8,10},{9,11},{12,14},{13,15},{14,12},{15,... | collective-permute-start | bytes 147464 | tf_op jit(solution)/shard_map/ppermute | solution.py:119
  13.8 35.2 %collective-permute-start = (bf16[384,896]{1,0:T(8,128)(2,1)}, bf16[384,896]{1,0:T(8,128)(2,1)S(1)}, u32[]{:S(2)}, u32[]{:S(2)}) collective-permute-start(bf16[384,896]{1,0:T(8,128)(2,1)} %get-tuple-element.10), channel_id=1, source_target_pairs={{0,4},{1,5},{4,8},{5,9},{8,12},{9,13},{12,14},{13,15},{14,10},{15,... | collective-permute-start | bytes 2064392 | tf_op jit(solution)/shard_map/ppermute | solution.py:253
  42.7 4.1 %collective-permute-start.35 = (f32[96,128]{1,0:T(8,128)S(1)}, f32[96,128]{1,0:T(8,128)S(1)}, u32[]{:S(2)}, u32[]{:S(2)}) collective-permute-start(f32[96,128]{1,0:T(8,128)S(1)} %bitcast.20), channel_id=1, source_target_pairs={{0,2},{1,3},{4,6},{5,7},{8,10},{9,11},{12,14},{13,15},{14,12},{15,... | collective-permute-start | bytes 147464 | tf_op jit(solution)/shard_map/ppermute | solution.py:124
  42.7 18.5 %collective-permute-start.5 = (bf16[384,896]{1,0:T(8,128)(2,1)}, bf16[384,896]{1,0:T(8,128)(2,1)S(1)}, u32[]{:S(2)}, u32[]{:S(2)}) collective-permute-start(bf16[384,896]{1,0:T(8,128)(2,1)} %get-tuple-element.9), channel_id=1, source_target_pairs={{4,0},{5,1},{8,4},{9,5},{12,8},{13,9},{14,12},{15,13},{10,14},{11,... | collective-permute-start | bytes 2064392 | tf_op jit(solution)/shard_map/ppermute | solution.py:253
  46.8 26.2 %copy-start.13 = (f32[96,128]{1,0:T(8,128)}, f32[96,128]{1,0:T(8,128)S(1)}, u32[]{:S(2)}) copy-start(f32[96,128]{1,0:T(8,128)S(1)} %get-tuple-element.15) | copy-start | bytes 147460
  46.8 26.2 %copy-start.14 = (f32[96,128]{1,0:T(8,128)}, f32[96,128]{1,0:T(8,128)S(1)}, u32[]{:S(2)}) copy-start(f32[96,128]{1,0:T(8,128)S(1)} %get-tuple-element.16) | copy-start | bytes 147460
  46.8 1.4 collective-permute-start.36
  46.9 18.2 %collective-permute-start.14 = (bf16[384,896]{1,0:T(8,128)(2,1)}, bf16[384,896]{1,0:T(8,128)(2,1)}, u32[]{:S(2)}, u32[]{:S(2)}) collective-permute-start(bf16[384,896]{1,0:T(8,128)(2,1)} %get-tuple-element.9), channel_id=1, source_target_pairs={{0,4},{1,5},{4,8},{5,9},{8,12},{9,13},{12,14},{13,15},{14,10},{15,... | collective-permute-start | bytes 2064392 | tf_op jit(solution)/shard_map/ppermute | solution.py:253
  48.2 24.0 %collective-permute-start.18 = (bf16[384,896]{1,0:T(8,128)(2,1)}, bf16[384,896]{1,0:T(8,128)(2,1)}, u32[]{:S(2)}, u32[]{:S(2)}) collective-permute-start(bf16[384,896]{1,0:T(8,128)(2,1)} %get-tuple-element.10), channel_id=1, source_target_pairs={{4,0},{5,1},{8,4},{9,5},{12,8},{13,9},{14,12},{15,13},{10,14},{11,... | collective-permute-start | bytes 2064392 | tf_op jit(solution)/shard_map/ppermute | solution.py:253
  49.0 24.0 %collective-permute-start.30 = (bf16[384,896]{1,0:T(8,128)(2,1)S(1)}, bf16[384,896]{1,0:T(8,128)(2,1)S(1)}, u32[]{:S(2)}, u32[]{:S(2)}) collective-permute-start(bf16[384,896]{1,0:T(8,128)(2,1)S(1)} %collective-permute-done.refs_0_), channel_id=1, source_target_pairs={{0,1},{1,0},{4,5},{5,4},{8,9},{9,8},{12,13},{13,12},{14,15},{15,14... | collective-permute-start | bytes 2064392 | tf_op jit(solution)/shard_map/ppermute | solution.py:256
  61.2 14.9 %collective-permute-start.31 = (bf16[384,896]{1,0:T(8,128)(2,1)S(1)}, bf16[384,896]{1,0:T(8,128)(2,1)S(1)}, u32[]{:S(2)}, u32[]{:S(2)}) collective-permute-start(bf16[384,896]{1,0:T(8,128)(2,1)S(1)} %collective-permute-done.5.refs_2_), channel_id=1, source_target_pairs={{0,1},{1,0},{4,5},{5,4},{8,9},{9,8},{12,13},{13,12},{14,15},{15,14... | collective-permute-start | bytes 2064392 | tf_op jit(solution)/shard_map/ppermute | solution.py:256
  65.1 12.7 %collective-permute-start.28 = (bf16[384,896]{1,0:T(8,128)(2,1)}, bf16[384,896]{1,0:T(8,128)(2,1)}, u32[]{:S(2)}, u32[]{:S(2)}) collective-permute-start(bf16[384,896]{1,0:T(8,128)(2,1)} %collective-permute-done.14.refs_0_), channel_id=1, source_target_pairs={{0,1},{1,0},{4,5},{5,4},{8,9},{9,8},{12,13},{13,12},{14,15},{15,14... | collective-permute-start | bytes 2064392 | tf_op jit(solution)/shard_map/ppermute | solution.py:256
  72.2 18.5 %collective-permute-start.1 = (bf16[384,896]{1,0:T(8,128)(2,1)S(1)}, bf16[384,896]{1,0:T(8,128)(2,1)}, u32[]{:S(2)}, u32[]{:S(2)}) collective-permute-start(bf16[384,896]{1,0:T(8,128)(2,1)S(1)} %collective-permute-done.refs_0_), channel_id=1, source_target_pairs={{0,4},{1,5},{4,8},{5,9},{8,12},{9,13},{12,14},{13,15},{14,10},{15,... | collective-permute-start | bytes 2064392 | tf_op jit(solution)/shard_map/ppermute | solution.py:253
  73.0 17.7 %collective-permute-start.29 = (bf16[384,896]{1,0:T(8,128)(2,1)}, bf16[384,896]{1,0:T(8,128)(2,1)}, u32[]{:S(2)}, u32[]{:S(2)}) collective-permute-start(bf16[384,896]{1,0:T(8,128)(2,1)} %collective-permute-done.18.refs_2_), channel_id=1, source_target_pairs={{0,1},{1,0},{4,5},{5,4},{8,9},{9,8},{12,13},{13,12},{14,15},{15,14... | collective-permute-start | bytes 2064392 | tf_op jit(solution)/shard_map/ppermute | solution.py:256
  73.9 18.4 %collective-permute-start.6 = (bf16[384,896]{1,0:T(8,128)(2,1)S(1)}, bf16[384,896]{1,0:T(8,128)(2,1)}, u32[]{:S(2)}, u32[]{:S(2)}) collective-permute-start(bf16[384,896]{1,0:T(8,128)(2,1)S(1)} %collective-permute-done.5.refs_2_), channel_id=1, source_target_pairs={{4,0},{5,1},{8,4},{9,5},{12,8},{13,9},{14,12},{15,13},{10,14},{11,... | collective-permute-start | bytes 2064392 | tf_op jit(solution)/shard_map/ppermute | solution.py:253
  77.0 28.4 %collective-permute-start.15 = (bf16[384,896]{1,0:T(8,128)(2,1)}, bf16[384,896]{1,0:T(8,128)(2,1)}, u32[]{:S(2)}, u32[]{:S(2)}) collective-permute-start(bf16[384,896]{1,0:T(8,128)(2,1)} %collective-permute-done.14.refs_0_), channel_id=1, source_target_pairs={{0,4},{1,5},{4,8},{5,9},{8,12},{9,13},{12,14},{13,15},{14,10},{15,... | collective-permute-start | bytes 2064392 | tf_op jit(solution)/shard_map/ppermute | solution.py:253
  77.7 30.6 %collective-permute-start.19 = (bf16[384,896]{1,0:T(8,128)(2,1)}, bf16[384,896]{1,0:T(8,128)(2,1)}, u32[]{:S(2)}, u32[]{:S(2)}) collective-permute-start(bf16[384,896]{1,0:T(8,128)(2,1)} %collective-permute-done.18.refs_2_), channel_id=1, source_target_pairs={{4,0},{5,1},{8,4},{9,5},{12,8},{13,9},{14,12},{15,13},{10,14},{11,... | collective-permute-start | bytes 2064392 | tf_op jit(solution)/shard_map/ppermute | solution.py:253
  90.7 17.8 %collective-permute-start.26 = (bf16[384,896]{1,0:T(8,128)(2,1)}, bf16[384,896]{1,0:T(8,128)(2,1)S(1)}, u32[]{:S(2)}, u32[]{:S(2)}) collective-permute-start(bf16[384,896]{1,0:T(8,128)(2,1)} %collective-permute-done.1.refs_0_), channel_id=1, source_target_pairs={{0,1},{1,0},{4,5},{5,4},{8,9},{9,8},{12,13},{13,12},{14,15},{15,14... | collective-permute-start | bytes 2064392 | tf_op jit(solution)/shard_map/ppermute | solution.py:256
  90.7 28.1 %collective-permute-start.2 = (bf16[384,896]{1,0:T(8,128)(2,1)}, bf16[384,896]{1,0:T(8,128)(2,1)S(1)}, u32[]{:S(2)}, u32[]{:S(2)}) collective-permute-start(bf16[384,896]{1,0:T(8,128)(2,1)} %collective-permute-done.1.refs_0_), channel_id=1, source_target_pairs={{0,4},{1,5},{4,8},{5,9},{8,12},{9,13},{12,14},{13,15},{14,10},{15,... | collective-permute-start | bytes 2064392 | tf_op jit(solution)/shard_map/ppermute | solution.py:253
  92.3 17.0 %collective-permute-start.27 = (bf16[384,896]{1,0:T(8,128)(2,1)}, bf16[384,896]{1,0:T(8,128)(2,1)S(1)}, u32[]{:S(2)}, u32[]{:S(2)}) collective-permute-start(bf16[384,896]{1,0:T(8,128)(2,1)} %collective-permute-done.6.refs_2_), channel_id=1, source_target_pairs={{0,1},{1,0},{4,5},{5,4},{8,9},{9,8},{12,13},{13,12},{14,15},{15,14... | collective-permute-start | bytes 2064392 | tf_op jit(solution)/shard_map/ppermute | solution.py:256
  105.4 20.8 %collective-permute-start.7 = (bf16[384,896]{1,0:T(8,128)(2,1)}, bf16[384,896]{1,0:T(8,128)(2,1)S(1)}, u32[]{:S(2)}, u32[]{:S(2)}) collective-permute-start(bf16[384,896]{1,0:T(8,128)(2,1)} %collective-permute-done.6.refs_2_), channel_id=1, source_target_pairs={{4,0},{5,1},{8,4},{9,5},{12,8},{13,9},{14,12},{15,13},{10,14},{11,... | collective-permute-start | bytes 2064392 | tf_op jit(solution)/shard_map/ppermute | solution.py:253
  108.4 13.6 %copy-start.11 = (f32[192,128]{1,0:T(8,128)}, f32[192,128]{1,0:T(8,128)S(1)}, u32[]{:S(2)}) copy-start(f32[192,128]{1,0:T(8,128)S(1)} %get-tuple-element.12) | copy-start | bytes 294916
  108.4 19.0 %collective-permute-start.24 = (bf16[384,896]{1,0:T(8,128)(2,1)}, bf16[384,896]{1,0:T(8,128)(2,1)}, u32[]{:S(2)}, u32[]{:S(2)}) collective-permute-start(bf16[384,896]{1,0:T(8,128)(2,1)} %collective-permute-done.15.refs_0_), channel_id=1, source_target_pairs={{0,1},{1,0},{4,5},{5,4},{8,9},{9,8},{12,13},{13,12},{14,15},{15,14... | collective-permute-start | bytes 2064392 | tf_op jit(solution)/shard_map/ppermute | solution.py:256
  109.3 24.3 %collective-permute-start.16 = (bf16[384,896]{1,0:T(8,128)(2,1)}, bf16[384,896]{1,0:T(8,128)(2,1)}, u32[]{:S(2)}, u32[]{:S(2)}) collective-permute-start(bf16[384,896]{1,0:T(8,128)(2,1)} %collective-permute-done.15.refs_0_), channel_id=1, source_target_pairs={{0,4},{1,5},{4,8},{5,9},{8,12},{9,13},{12,14},{13,15},{14,10},{15,... | collective-permute-start | bytes 2064392 | tf_op jit(solution)/shard_map/ppermute | solution.py:253
  110.2 19.7 %collective-permute-start.25 = (bf16[384,896]{1,0:T(8,128)(2,1)}, bf16[384,896]{1,0:T(8,128)(2,1)}, u32[]{:S(2)}, u32[]{:S(2)}) collective-permute-start(bf16[384,896]{1,0:T(8,128)(2,1)} %collective-permute-done.19.refs_2_), channel_id=1, source_target_pairs={{0,1},{1,0},{4,5},{5,4},{8,9},{9,8},{12,13},{13,12},{14,15},{15,14... | collective-permute-start | bytes 2064392 | tf_op jit(solution)/shard_map/ppermute | solution.py:256
  118.8 20.0 %collective-permute-start.20 = (bf16[384,896]{1,0:T(8,128)(2,1)}, bf16[384,896]{1,0:T(8,128)(2,1)}, u32[]{:S(2)}, u32[]{:S(2)}) collective-permute-start(bf16[384,896]{1,0:T(8,128)(2,1)} %collective-permute-done.19.refs_2_), channel_id=1, source_target_pairs={{4,0},{5,1},{8,4},{9,5},{12,8},{13,9},{14,12},{15,13},{10,14},{11,... | collective-permute-start | bytes 2064392 | tf_op jit(solution)/shard_map/ppermute | solution.py:253
  126.2 3.2 %copy-start.18 = (bf16[8,64,512]{2,1,0:T(8,128)(2,1)S(1)}, bf16[8,64,512]{2,1,0:T(8,128)(2,1)}, u32[]{:S(2)}) copy-start(bf16[8,64,512]{2,1,0:T(8,128)(2,1)} %param.10) | copy-start | bytes 1572868
  126.2 13.7 %collective-permute-start.3 = (bf16[384,384]{1,0:T(8,128)(2,1)S(1)}, bf16[384,384]{1,0:T(8,128)(2,1)S(1)}, u32[]{:S(2)}, u32[]{:S(2)}) collective-permute-start(bf16[384,384]{1,0:T(8,128)(2,1)S(1)} %slice.63), channel_id=1, source_target_pairs={{0,4},{1,5},{4,8},{5,9},{8,12},{9,13},{12,14},{13,15},{14,10},{15,... | collective-permute-start | bytes 884744 | tf_op jit(solution)/shard_map/ppermute | solution.py:253
  127.3 14.9 %collective-permute-start.8 = (bf16[384,384]{1,0:T(8,128)(2,1)S(1)}, bf16[384,384]{1,0:T(8,128)(2,1)S(1)}, u32[]{:S(2)}, u32[]{:S(2)}) collective-permute-start(bf16[384,384]{1,0:T(8,128)(2,1)S(1)} %slice.65), channel_id=1, source_target_pairs={{4,0},{5,1},{8,4},{9,5},{12,8},{13,9},{14,12},{15,13},{10,14},{11,... | collective-permute-start | bytes 884744 | tf_op jit(solution)/shard_map/ppermute | solution.py:253
  129.3 10.5 %copy-start.12 = (f32[192,128]{1,0:T(8,128)S(1)}, f32[192,128]{1,0:T(8,128)}, u32[]{:S(2)}) copy-start(f32[192,128]{1,0:T(8,128)} %copy-done.11) | copy-start | bytes 294916
  129.9 17.1 %collective-permute-start.10 = (bf16[384,512]{1,0:T(8,128)(2,1)S(1)}, bf16[384,512]{1,0:T(8,128)(2,1)S(1)}, u32[]{:S(2)}, u32[]{:S(2)}) collective-permute-start(bf16[384,512]{1,0:T(8,128)(2,1)S(1)} %slice.66), channel_id=1, source_target_pairs={{0,4},{1,5},{4,8},{5,9},{8,12},{9,13},{12,14},{13,15},{14,10},{15,... | collective-permute-start | bytes 1179656 | tf_op jit(solution)/shard_map/ppermute | solution.py:253
  133.6 28.2 %collective-permute-start.22 = (bf16[384,896]{1,0:T(8,128)(2,1)S(1)}, bf16[384,896]{1,0:T(8,128)(2,1)S(1)}, u32[]{:S(2)}, u32[]{:S(2)}) collective-permute-start(bf16[384,896]{1,0:T(8,128)(2,1)S(1)} %collective-permute-done.2.refs_0_), channel_id=1, source_target_pairs={{0,1},{1,0},{4,5},{5,4},{8,9},{9,8},{12,13},{13,12},{14,15},{15,14... | collective-permute-start | bytes 2064392 | tf_op jit(solution)/shard_map/ppermute | solution.py:256
  138.8 28.0 %collective-permute-start.23 = (bf16[384,896]{1,0:T(8,128)(2,1)S(1)}, bf16[384,896]{1,0:T(8,128)(2,1)S(1)}, u32[]{:S(2)}, u32[]{:S(2)}) collective-permute-start(bf16[384,896]{1,0:T(8,128)(2,1)S(1)} %collective-permute-done.7.refs_2_), channel_id=1, source_target_pairs={{0,1},{1,0},{4,5},{5,4},{8,9},{9,8},{12,13},{13,12},{14,15},{15,14... | collective-permute-start | bytes 2064392 | tf_op jit(solution)/shard_map/ppermute | solution.py:256
  139.9 27.1 %collective-permute-start.17 = (bf16[384,896]{1,0:T(8,128)(2,1)}, bf16[384,896]{1,0:T(8,128)(2,1)S(1)}, u32[]{:S(2)}, u32[]{:S(2)}) collective-permute-start(bf16[384,896]{1,0:T(8,128)(2,1)} %collective-permute-done.16.refs_0_), channel_id=1, source_target_pairs={{0,1},{1,0},{4,5},{5,4},{8,9},{9,8},{12,13},{13,12},{14,15},{15,14... | collective-permute-start | bytes 2064392 | tf_op jit(solution)/shard_map/ppermute | solution.py:256
  140.4 8.4 %copy-start.2 = (bf16[384,896]{1,0:T(8,128)(2,1)S(1)}, bf16[384,896]{1,0:T(8,128)(2,1)}, u32[]{:S(2)}) copy-start(bf16[384,896]{1,0:T(8,128)(2,1)} %copy-done.1) | copy-start | bytes 2064388
  140.4 8.4 %copy-start.4 = (bf16[384,896]{1,0:T(8,128)(2,1)S(1)}, bf16[384,896]{1,0:T(8,128)(2,1)}, u32[]{:S(2)}) copy-start(bf16[384,896]{1,0:T(8,128)(2,1)} %copy-done.3) | copy-start | bytes 2064388
  140.4 8.4 %copy-start.6 = (bf16[384,896]{1,0:T(8,128)(2,1)S(1)}, bf16[384,896]{1,0:T(8,128)(2,1)}, u32[]{:S(2)}) copy-start(bf16[384,896]{1,0:T(8,128)(2,1)} %copy-done.5) | copy-start | bytes 2064388
  142.3 29.3 %collective-permute-start.21 = (bf16[384,896]{1,0:T(8,128)(2,1)}, bf16[384,896]{1,0:T(8,128)(2,1)S(1)}, u32[]{:S(2)}, u32[]{:S(2)}) collective-permute-start(bf16[384,896]{1,0:T(8,128)(2,1)} %collective-permute-done.20.refs_2_), channel_id=1, source_target_pairs={{0,1},{1,0},{4,5},{5,4},{8,9},{9,8},{12,13},{13,12},{14,15},{15,14... | collective-permute-start | bytes 2064392 | tf_op jit(solution)/shard_map/ppermute | solution.py:256
  147.0 14.8 %collective-permute-start.12 = (bf16[384,512]{1,0:T(8,128)(2,1)S(1)}, bf16[384,512]{1,0:T(8,128)(2,1)S(1)}, u32[]{:S(2)}, u32[]{:S(2)}) collective-permute-start(bf16[384,512]{1,0:T(8,128)(2,1)S(1)} %slice.67), channel_id=1, source_target_pairs={{4,0},{5,1},{8,4},{9,5},{12,8},{13,9},{14,12},{15,13},{10,14},{11,... | collective-permute-start | bytes 1179656 | tf_op jit(solution)/shard_map/ppermute | solution.py:253
  153.0 4.5 %copy-start.8 = (bf16[384,896]{1,0:T(8,128)(2,1)S(1)}, bf16[384,896]{1,0:T(8,128)(2,1)}, u32[]{:S(2)}) copy-start(bf16[384,896]{1,0:T(8,128)(2,1)} %copy-done.7) | copy-start | bytes 2064388
  153.0 4.5 %copy-start.10 = (bf16[384,896]{1,0:T(8,128)(2,1)S(1)}, bf16[384,896]{1,0:T(8,128)(2,1)}, u32[]{:S(2)}) copy-start(bf16[384,896]{1,0:T(8,128)(2,1)} %copy-done.9) | copy-start | bytes 2064388
  161.8 14.1 %collective-permute-start.11 = (bf16[384,512]{1,0:T(8,128)(2,1)S(1)}, bf16[384,512]{1,0:T(8,128)(2,1)S(1)}, u32[]{:S(2)}, u32[]{:S(2)}) collective-permute-start(bf16[384,512]{1,0:T(8,128)(2,1)S(1)} %collective-permute-done.10.refs_0_), channel_id=1, source_target_pairs={{0,1},{1,0},{4,5},{5,4},{8,9},{9,8},{12,13},{13,12},{14,15},{15,14... | collective-permute-start | bytes 1179656 | tf_op jit(solution)/shard_map/ppermute | solution.py:256
  161.9 14.0 %collective-permute-start.13 = (bf16[384,512]{1,0:T(8,128)(2,1)S(1)}, bf16[384,512]{1,0:T(8,128)(2,1)S(1)}, u32[]{:S(2)}, u32[]{:S(2)}) collective-permute-start(bf16[384,512]{1,0:T(8,128)(2,1)S(1)} %collective-permute-done.12.refs_2_), channel_id=1, source_target_pairs={{0,1},{1,0},{4,5},{5,4},{8,9},{9,8},{12,13},{13,12},{14,15},{15,14... | collective-permute-start | bytes 1179656 | tf_op jit(solution)/shard_map/ppermute | solution.py:256
  166.8 14.4 %collective-permute-start.4 = (bf16[384,384]{1,0:T(8,128)(2,1)S(1)}, bf16[384,384]{1,0:T(8,128)(2,1)S(1)}, u32[]{:S(2)}, u32[]{:S(2)}) collective-permute-start(bf16[384,384]{1,0:T(8,128)(2,1)S(1)} %collective-permute-done.3.refs_0_), channel_id=1, source_target_pairs={{0,1},{1,0},{4,5},{5,4},{8,9},{9,8},{12,13},{13,12},{14,15},{15,14... | collective-permute-start | bytes 884744 | tf_op jit(solution)/shard_map/ppermute | solution.py:256
  167.0 14.3 %collective-permute-start.9 = (bf16[384,384]{1,0:T(8,128)(2,1)S(1)}, bf16[384,384]{1,0:T(8,128)(2,1)S(1)}, u32[]{:S(2)}, u32[]{:S(2)}) collective-permute-start(bf16[384,384]{1,0:T(8,128)(2,1)S(1)} %collective-permute-done.8.refs_1_), channel_id=1, source_target_pairs={{0,1},{1,0},{4,5},{5,4},{8,9},{9,8},{12,13},{13,12},{14,15},{15,14... | collective-permute-start | bytes 884744 | tf_op jit(solution)/shard_map/ppermute | solution.py:256
  (9 other events, 13.0 us)

commit v4 on v3

--- a/solution.py
+++ b/solution.py
@@ -33,13 +33,20 @@
     return [chips[p] for p in places], False
 
 
+def in_hbm(array):
+    return pltpu.with_memory_space_constraint(array, pltpu.HBM)
+
+
 def project_selected(rows, labels, factors, first):
     count, rank, units = factors.shape
     total = rows.shape[0]
     wide = count * rank
     part = total // 2
 
-    def body(f_ref, x_ref, l_ref, a_ref, mine_ref, other_ref, s_ref):
+    def body(f_ref, x_ref, l_ref, a_any, mine_ref, other_ref, s_ref, a_ref, sem):
+        copy = pltpu.make_async_copy(a_any, a_ref, sem)
+        copy.start()
+        copy.wait()
         full = lax.dot_general(
             x_ref[...], a_ref[...], (((1,), (1,)), ((), ())), preferred_element_type=jnp.float32
         )
@@ -52,20 +59,25 @@
         other_ref[...] = s_ref[pl.ds(pl.multiple_of((1 - at) * part, 8), part), :]
 
     vmem = pl.BlockSpec(memory_space=pltpu.VMEM)
+    anywhere = pl.BlockSpec(memory_space=pltpu.HBM)
     shape = jax.ShapeDtypeStruct((part, 2 * rank), jnp.float32)
     return pl.pallas_call(
         body,
         out_shape=(shape, shape),
-        in_specs=[pl.BlockSpec(memory_space=pltpu.SMEM)] + [vmem] * 3,
+        in_specs=[pl.BlockSpec(memory_space=pltpu.SMEM), vmem, vmem, anywhere],
         out_specs=(vmem, vmem),
-        scratch_shapes=[pltpu.VMEM((total, 2 * rank), jnp.float32)],
+        scratch_shapes=[
+            pltpu.VMEM((total, 2 * rank), jnp.float32),
+            pltpu.VMEM((wide, units), jnp.bfloat16),
+            pltpu.SemaphoreType.DMA,
+        ],
         cost_estimate=pl.CostEstimate(
             flops=2 * total * wide * units,
             transcendentals=0,
             bytes_accessed=2 * units * (total + wide) + 8 * total * rank,
         ),
-        compiler_params=pltpu.CompilerParams(vmem_limit_bytes=32 << 20),
-    )(first.reshape(1), rows, labels[:, None], factors.reshape(wide, units))
+        compiler_params=pltpu.CompilerParams(vmem_limit_bytes=12 << 20),
+    )(first.reshape(1), rows, labels[:, None], in_hbm(factors.reshape(wide, units)))
 
 
 def labels_onehot(adapter_labels, count):
@@ -125,7 +137,7 @@
     return jnp.concatenate([jnp.where(at == 0, part, got), jnp.where(at == 0, got, part)], axis=0)
 
 
-def sum_by_stages(mine, other, core, side, partner, across, lines):
+def sum_by_stages(mine, other, side, partner, across, lines):
     got = lax.ppermute(other, "row", partner)
     rows = swap(mine + got, side, across)
     size = len(lines[0])
@@ -134,65 +146,134 @@
     total = jnp.sum(parts.reshape(size, piece, rows.shape[1]), axis=0)
     spread = jnp.broadcast_to(total[None], (size,) + total.shape).reshape(rows.shape)
     whole = lax.all_to_all(spread, "row", 0, 0, axis_index_groups=lines, tiled=True)
-    return join(join(whole, side, across), core, partner)
-
-
-def chunk_matmul(chunks, starts, first, weight, before, extra, out_dtype):
+    half = join(whole, side, across)
+    return half, lax.ppermute(half, "row", partner)
+
+
+def chunk_matmul(chunks, starts, first, weight, added, out_dtype, ready=None, ahead=()):
     count = len(chunks)
     rows = chunks[0].shape[0]
     widths = [c.shape[1] for c in chunks]
     features = weight.shape[0]
-    added = [a for a in (before, extra) if a is not None]
+    later = len(ahead)
 
     def body(starts_ref, *refs):
-        x_refs = refs[:count]
-        w_ref = refs[count]
-        add_refs = refs[count + 1 : count + 1 + len(added)]
-        rest = refs[count + 1 + len(added) :]
-        out_ref, x_bufs, w_bufs = rest[0], rest[1 : 1 + count], rest[1 + count : 1 + 2 * count]
-        x_sem, w_sem = rest[1 + 2 * count :]
+        x_refs, refs = refs[:count], refs[count:]
+        w_refs, refs = refs[: len(blocks)], refs[len(blocks) :]
+        add_refs, refs = refs[: len(added)], refs[len(added) :]
+        out_ref, ahead_refs, refs = refs[0], refs[1 : 1 + later], refs[1 + later :]
+
+        def block(at, units):
+            start = pl.multiple_of(starts_ref[at] * LANES, LANES)
+            return w_refs[0].at[:, pl.ds(start, units)]
+
         copies = []
-        for k in range(count):
-            start = pl.multiple_of(starts_ref[first + k] * LANES, LANES)
-            cx = pltpu.make_async_copy(x_refs[k], x_bufs[k], x_sem.at[k])
-            cw = pltpu.make_async_copy(w_ref.at[:, pl.ds(start, widths[k])], w_bufs[k], w_sem.at[k])
-            cw.start()
-            cx.start()
-            copies.append((cx, cw))
+        w_bufs = w_refs
+        if ready is None:
+            w_bufs, w_sem = refs[:count], refs[count]
+            for k in range(count):
+                copy = pltpu.make_async_copy(block(first + k, widths[k]), w_bufs[k], w_sem.at[k])
+                copy.start()
+                copies.append(copy)
+        fetches = [
+            pltpu.make_async_copy(block(at, units), ahead_refs[k], refs[-1].at[k])
+            for k, (at, units) in enumerate(ahead)
+        ]
+        for fetch in fetches:
+            fetch.start()
         total = None
         for k in range(count):
-            copies[k][1].wait()
-            copies[k][0].wait()
+            if copies:
+                copies[k].wait()
             part = lax.dot_general(
-                x_bufs[k][...], w_bufs[k][...], (((1,), (1,)), ((), ())), preferred_element_type=jnp.float32
+                x_refs[k][...],
+                w_bufs[k][...],
+                (((1,), (1,)), ((), ())),
+                preferred_element_type=jnp.float32,
             )
             total = part if total is None else total + part
         for ref in add_refs:
             total = total + ref[...]
         out_ref[...] = total.astype(out_dtype)
-
-    anywhere = pl.BlockSpec(memory_space=pl.ANY)
+        for fetch in fetches:
+            fetch.wait()
+
+    anywhere = pl.BlockSpec(memory_space=pltpu.HBM)
+    vmem = pl.BlockSpec(memory_space=pltpu.VMEM)
+    blocks = [in_hbm(weight)] if ready is None else list(ready)
+    held = anywhere if ready is None else vmem
+    scratch = []
+    if ready is None:
+        scratch += [pltpu.VMEM((features, w), jnp.bfloat16) for w in widths]
+        scratch += [pltpu.SemaphoreType.DMA((count,))]
+    if later:
+        scratch += [pltpu.SemaphoreType.DMA((later,))]
+    room = 2 * sum(widths) * (rows + features) + 2 * features * sum(u for _, u in ahead)
+    room += 4 * rows * features * (1 + len(added))
+    moved = sum(widths) * (rows + features) + features * sum(units for _, units in ahead)
+    out = pl.pallas_call(
+        body,
+        out_shape=[jax.ShapeDtypeStruct((rows, features), out_dtype)]
+        + [jax.ShapeDtypeStruct((features, units), jnp.bfloat16) for _, units in ahead],
+        in_specs=[pl.BlockSpec(memory_space=pltpu.SMEM)]
+        + [vmem] * count
+        + [held] * len(blocks)
+        + [vmem] * len(added),
+        out_specs=[vmem] * (1 + later),
+        scratch_shapes=scratch,
+        cost_estimate=pl.CostEstimate(
+            flops=2 * rows * sum(widths) * features,
+            transcendentals=0,
+            bytes_accessed=2 * moved + 8 * rows * features,
+        ),
+        compiler_params=pltpu.CompilerParams(vmem_limit_bytes=room + (5 << 20)),
+    )(starts, *chunks, *blocks, *added)
+    return out[0], out[1:]
+
+
+def adapter_kernel(mine, other, core, labels, outputs):
+    count, rank, width = outputs.shape
+    part, cols = mine.shape
+    total = 2 * part
+
+    def body(core_ref, mine_ref, other_ref, l_ref, w_ref, o_ref, s_ref):
+        at = core_ref[0]
+        s_ref[pl.ds(pl.multiple_of(at * part, 8), part), :] = mine_ref[...]
+        s_ref[pl.ds(pl.multiple_of((1 - at) * part, 8), part), :] = other_ref[...]
+        summed = s_ref[...]
+        label = l_ref[...]
+        shrunk = jnp.where(label != 0, summed, 0.0).astype(jnp.bfloat16).astype(jnp.float32)
+        own = shrunk[:, :rank]
+        spread = jnp.concatenate([jnp.where(label == k, own, 0.0) for k in range(count)], axis=1)
+        update = jnp.dot(
+            spread.astype(jnp.bfloat16), w_ref[...], preferred_element_type=jnp.float32
+        )
+        resident = summed[:, rank:]
+        high = resident.astype(jnp.bfloat16)
+        left = resident - high.astype(jnp.float32)
+        middle = left.astype(jnp.bfloat16)
+        low = (left - middle.astype(jnp.float32)).astype(jnp.bfloat16)
+        first = w_ref[:rank, :]
+        taken = shrunk[:, rank:].astype(jnp.bfloat16)
+        base = jnp.dot(low, first, preferred_element_type=jnp.float32)
+        base = base + jnp.dot(middle, first, preferred_element_type=jnp.float32)
+        base = base + jnp.dot(high, first, preferred_element_type=jnp.float32)
+        o_ref[...] = base + (update - jnp.dot(taken, first, preferred_element_type=jnp.float32))
+
     vmem = pl.BlockSpec(memory_space=pltpu.VMEM)
     return pl.pallas_call(
         body,
-        out_shape=jax.ShapeDtypeStruct((rows, features), out_dtype),
-        in_specs=[pl.BlockSpec(memory_space=pltpu.SMEM)]
-        + [anywhere] * (count + 1)
-        + [vmem] * len(added),
+        out_shape=jax.ShapeDtypeStruct((total, width), jnp.float32),
+        in_specs=[pl.BlockSpec(memory_space=pltpu.SMEM)] + [vmem] * 4,
         out_specs=vmem,
-        scratch_shapes=[pltpu.VMEM((rows, w), jnp.bfloat16) for w in widths]
-        + [pltpu.VMEM((features, w), jnp.bfloat16) for w in widths]
-        + [
-            pltpu.SemaphoreType.DMA((count,)),
-            pltpu.SemaphoreType.DMA((count,)),
-        ],
+        scratch_shapes=[pltpu.VMEM((total, cols), jnp.float32)],
         cost_estimate=pl.CostEstimate(
-            flops=2 * rows * sum(widths) * features,
+            flops=2 * total * (count + 4) * rank * width,
             transcendentals=0,
-            bytes_accessed=2 * sum(widths) * (rows + features) + 8 * rows * features,
+            bytes_accessed=2 * count * rank * width + 4 * total * (cols + width),
         ),
-        compiler_params=pltpu.CompilerParams(vmem_limit_bytes=48 << 20),
-    )(starts, *chunks, weight, *added)
+        compiler_params=pltpu.CompilerParams(vmem_limit_bytes=12 << 20),
+    )(core.reshape(1), mine, other, labels[:, None], outputs.reshape(count * rank, width))
 
 
 def solution(mesh):
@@ -235,8 +316,8 @@
         me = lax.axis_index("row")
         core, side = [jnp.asarray(place)[me][k] for k in range(2)]
         mine, other = project_selected(flat, labels, factors, core)
-        summed = sum_by_stages(mine, other, core, side, partner, across, lines)
-        extra = adapter_terms(summed, labels, outputs)
+        halves = sum_by_stages(mine, other, side, partner, across, lines)
+        extra = adapter_kernel(*halves, core, labels, outputs)
 
         plan = [(s // 2 + 1, s % 2, 0, half) for s in range(2 * long - 2)]
         plan += [(long, 0, 0, cut), (long, 0, cut, half - cut)]
@@ -267,21 +348,32 @@
                     source = ring[(p + offset) % chips][1 - c if beside else c]
                     table[at, k] = (source * device_units + part * half + column) // LANES
         starts = jnp.asarray(table)[me]
-        acc = None
+        acc = []
         done = 0
+        ends = len(batches) - 2
+        tail = len(order) - sum(len(found) for found in batches[ends:])
+        ahead = [(tail + k, found[0].shape[1]) for k, found in enumerate(batches[ends] + batches[-1])]
+        ready = None
         for k, found in enumerate(batches):
             last = k == len(batches) - 1
-            acc = chunk_matmul(
+            held = None
+            if k >= ends:
+                held, ready = ready[: len(found)], ready[len(found) :]
+            out, fetched = chunk_matmul(
                 [entry[0] for entry in found],
                 starts,
                 done,
                 weight,
-                acc,
-                extra if k == len(batches) - 4 else None,
+                acc + ([extra] if k == ends - 2 else []),
                 jnp.bfloat16 if last else jnp.float32,
+                held,
+                ahead if k == ends - 1 else (),
             )
+            if k == ends - 1:
+                ready = fetched
+            acc = [out]
             done += len(found)
-        return acc
+        return acc[0]
 
     def local(
         gated_hidden_rows,

time: 185 us -> 180 us (0.973)
  waiting for transfers between devices: 68.4 us -> 98.6 us
  blocking collectives: 27.2 us -> 10.9 us
  local copies, waits for them, and re-layouts: 14.7 us -> 5.05 us
  other arithmetic: 4.33 us -> 0.06 us
  Pallas kernels: 42 us -> 40 us
    ppermute x16, waiting for transfers between devices: 65.6 us -> 87.3 us  [ringed(): data = lax.ppermute(send, 'row', pairs)]
    all_to_all x1 -> x0, blocking collectives: 11.5 us -> none  [sum_by_stages(): lax.all_to_all(spread, 'row', 0, 0, axis_index_groups=lines, tiled=True)]
    all_to_all x0 -> x1, waiting for transfers between devices: none -> 5.58 us  [sum_by_stages(): lax.all_to_all(spread, 'row', 0, 0, axis_index_groups=lines, tiled=True)]
    ppermute x16, starting transfers between devices: 19.5 us -> 14.5 us  [ringed(): data = lax.ppermute(send, 'row', pairs)]
    all_to_all x1, blocking collectives: 15.7 us -> 10.9 us  [sum_by_stages(): lax.all_to_all(rows, 'row', 0, 0, axis_index_groups=lines, tiled=True)]
    unnamed x40 -> x6, local copies, waits for them, and re-layouts: 5.85 us -> 1.34 us
    all_to_all x0 -> x1, starting transfers between devices: none -> 3.27 us  [sum_by_stages(): lax.all_to_all(spread, 'row', 0, 0, axis_index_groups=lines, tiled=True)]
    slice x1, local copies, waits for them, and re-layouts: 2.5 us -> 0.11 us  [ringed(): own = [flat[:, :half], flat[:, half:]]]
  transfers between devices with their start and end apart: 37 -> 38, of which waited for: 14 -> 16; matrix products, arithmetic and copies ran while one was open for 7% -> 1% of each run, Pallas kernels for 19% -> 19%
where the time goes in v4:
time: 180 us; the launch traced here: 179 us
  waiting for transfers between devices  98.6 us (55%)
  Pallas kernels  40 us (22%)
  starting transfers between devices  23.9 us (13%)
  blocking collectives  10.9 us (6%)
  local copies, waits for them, and re-layouts  5.05 us (3%)
    ppermute x16, waiting for transfers between devices, ringed(): data = lax.ppermute(send, 'row', pairs)  87.3 us
    pallas_call x10, Pallas kernels, chunk_matmul(): pl.pallas_call(body, out_shape=[jax.ShapeDtypeStruct((rows, features), ou...  34.6 us
    ppermute x16, starting transfers between devices, ringed(): data = lax.ppermute(send, 'row', pairs)  14.5 us
    all_to_all x1, blocking collectives, sum_by_stages(): lax.all_to_all(rows, 'row', 0, 0, axis_index_groups=lines, tiled=True)  10.9 us
    all_to_all x1, waiting for transfers between devices, sum_by_stages(): lax.all_to_all(spread, 'row', 0, 0, axis_index_groups=lines, tiled=True)  5.58 us
  transfers between devices with their start and end apart: 38, of which 16 were waited for; matrix products, arithmetic and copies ran while one was open for 1% of the time, Pallas kernels for 19%

profile of v4, /device:TPU:0, one launch (start us, length us, event | category | flops | bytes accessed | tf_op | source)
XLA Modules:
  0.0 179.4 jit_solution(8604271416522526841)
XLA Ops:
  0.0 0.7 constant_dynamic-slice_fusion
  0.7 0.6 fusion.1
  1.3 0.9 broadcast_in_dim_reshape.5.l_ref
  2.2 1.3 copy-done
  3.5 3.4 %shard_map.79 = (f32[192,128]{1,0:T(8,128)S(1)}, f32[192,128]{1,0:T(8,128)S(1)}) custom-call(s32[1]{0:T(128)} %bitcast.2.f_ref.core_ref, bf16[384,1792]{1,0:T(8,128)(2,1)S(1)} %bitcast.12, s32[384,1]{1,0:T(8,128)S(1)} %broadcast_in_dim_reshape.5.l_ref, bf16[512,1792]{1,0:T(8,128)(2,1)} %bitcast.17), custom_call_target="tpu_custom_call" | custom-call | flops 704643072 | bytes 3407872 | tf_op jit(solution)/shard_map/pallas_call | solution.py:64
  6.9 0.6 collective-permute-start.33
  8.4 2.9 %collective-permute-start.34 = (f32[96,128]{1,0:T(8,128)S(1)}, f32[96,128]{1,0:T(8,128)S(1)}, u32[]{:S(2)}, u32[]{:S(2)}) collective-permute-start(f32[96,128]{1,0:T(8,128)S(1)} %slice_select_fusion), channel_id=1, source_target_pairs={{0,2},{1,3},{4,6},{5,7},{8,10},{9,11},{12,14},{13,15},{14,12},{15,... | collective-permute-start | bytes 147464 | tf_op jit(solution)/shard_map/ppermute | solution.py:131
  11.4 2.1 %collective-permute-done.34 = f32[96,128]{1,0:T(8,128)S(1)} collective-permute-done((f32[96,128]{1,0:T(8,128)S(1)}, f32[96,128]{1,0:T(8,128)S(1)}, u32[]{:S(2)}, u32[]{:S(2)}) %collective-permute-start.34) | collective-permute-done | bytes 49184 | tf_op jit(solution)/shard_map/ppermute | solution.py:131
  13.5 10.9 %all_to_all.18 = f32[4,24,128]{2,1,0:T(8,128)S(1)} all-to-all(f32[4,24,128]{2,1,0:T(8,128)S(1)} %bitcast.19), channel_id=1, replica_groups={{0,4,8,12},{1,5,9,13},{14,10,6,2},{15,11,7,3},{16,20,24,28},{17,21,25,2..., dimensions={0} | all-to-all | bytes 98304 | tf_op jit(solution)/shard_map/all_to_all | solution.py:145
  24.3 0.6 broadcast_in_dim.2
  25.0 3.3 %all-to-all-start.1 = ((f32[4,24,128]{2,1,0:T(8,128)}), f32[4,24,128]{2,1,0:T(8,128)S(1)}, u32[]{:S(2)}, u32[]{:S(2)}) async-start(f32[4,24,128]{2,1,0:T(8,128)} %broadcast_in_dim.2), calls=%async_computation.1 | async-start | bytes 98304 | tf_op jit(solution)/shard_map/all_to_all | solution.py:148
  28.3 5.6 %all-to-all-done.1 = f32[4,24,128]{2,1,0:T(8,128)S(1)} async-done(((f32[4,24,128]{2,1,0:T(8,128)}), f32[4,24,128]{2,1,0:T(8,128)S(1)}, u32[]{:S(2)}, u32[]{:S(2)}) %all-to-all-start.1) | async-done | bytes 49184 | tf_op jit(solution)/shard_map/all_to_all | solution.py:148
  34.0 1.2 collective-permute-start
  35.2 3.3 %collective-permute-done.35 = f32[96,128]{1,0:T(8,128)S(1)} collective-permute-done((f32[96,128]{1,0:T(8,128)S(1)}, f32[96,128]{1,0:T(8,128)S(1)}, u32[]{:S(2)}, u32[]{:S(2)}) %collective-permute-start.35) | collective-permute-done | bytes 49184 | tf_op jit(solution)/shard_map/ppermute | solution.py:136
  38.7 2.0 %collective-permute-start.14 = (bf16[384,896]{1,0:T(8,128)(2,1)S(1)}, bf16[384,896]{1,0:T(8,128)(2,1)S(1)}, u32[]{:S(2)}, u32[]{:S(2)}) collective-permute-start(bf16[384,896]{1,0:T(8,128)(2,1)S(1)} %get-tuple-element.19), channel_id=1, source_target_pairs={{0,4},{1,5},{4,8},{5,9},{8,12},{9,13},{12,14},{13,15},{14,10},{15,... | collective-permute-start | bytes 2064392 | tf_op jit(solution)/shard_map/ppermute | solution.py:334
  40.8 12.5 %collective-permute-done.refs_0_ = bf16[384,896]{1,0:T(8,128)(2,1)S(1)} collective-permute-done((bf16[384,896]{1,0:T(8,128)(2,1)S(1)}, bf16[384,896]{1,0:T(8,128)(2,1)S(1)}, u32[]{:S(2)}, u32[]{:S(2)}) %collective-permute-start) | collective-permute-done | bytes 688160 | tf_op jit(solution)/shard_map/ppermute | solution.py:334
  53.3 3.7 %collective-permute-done.5.refs_2_ = bf16[384,896]{1,0:T(8,128)(2,1)S(1)} collective-permute-done((bf16[384,896]{1,0:T(8,128)(2,1)S(1)}, bf16[384,896]{1,0:T(8,128)(2,1)S(1)}, u32[]{:S(2)}, u32[]{:S(2)}) %collective-permute-start.5) | collective-permute-done | bytes 688160 | tf_op jit(solution)/shard_map/ppermute | solution.py:334
  57.0 7.1 %collective-permute-done.14.refs_0_ = bf16[384,896]{1,0:T(8,128)(2,1)S(1)} collective-permute-done((bf16[384,896]{1,0:T(8,128)(2,1)S(1)}, bf16[384,896]{1,0:T(8,128)(2,1)S(1)}, u32[]{:S(2)}, u32[]{:S(2)}) %collective-permute-start.14) | collective-permute-done | bytes 688160 | tf_op jit(solution)/shard_map/ppermute | solution.py:334
  64.1 7.2 %collective-permute-done.18.refs_2_ = bf16[384,896]{1,0:T(8,128)(2,1)S(1)} collective-permute-done((bf16[384,896]{1,0:T(8,128)(2,1)S(1)}, bf16[384,896]{1,0:T(8,128)(2,1)S(1)}, u32[]{:S(2)}, u32[]{:S(2)}) %collective-permute-start.18) | collective-permute-done | bytes 688160 | tf_op jit(solution)/shard_map/ppermute | solution.py:334
  71.5 1.7 collective-permute-start.6
  73.3 0.4 collective-permute-start.15
  73.6 1.7 collective-permute-start.19
  75.3 14.2 %collective-permute-done.1.refs_0_ = bf16[384,896]{1,0:T(8,128)(2,1)S(1)} collective-permute-done((bf16[384,896]{1,0:T(8,128)(2,1)S(1)}, bf16[384,896]{1,0:T(8,128)(2,1)S(1)}, u32[]{:S(2)}, u32[]{:S(2)}) %collective-permute-start.1) | collective-permute-done | bytes 688160 | tf_op jit(solution)/shard_map/ppermute | solution.py:334
  90.3 13.9 %collective-permute-done.15.refs_0_ = bf16[384,896]{1,0:T(8,128)(2,1)S(1)} collective-permute-done((bf16[384,896]{1,0:T(8,128)(2,1)S(1)}, bf16[384,896]{1,0:T(8,128)(2,1)S(1)}, u32[]{:S(2)}, u32[]{:S(2)}) %collective-permute-start.15) | collective-permute-done | bytes 688160 | tf_op jit(solution)/shard_map/ppermute | solution.py:334
  104.6 0.5 collective-permute-start.25
  105.1 1.7 collective-permute-start.16
  106.8 12.2 %collective-permute-done.2.refs_0_ = bf16[384,896]{1,0:T(8,128)(2,1)S(1)} collective-permute-done((bf16[384,896]{1,0:T(8,128)(2,1)S(1)}, bf16[384,896]{1,0:T(8,128)(2,1)S(1)}, u32[]{:S(2)}, u32[]{:S(2)}) %collective-permute-start.2) | collective-permute-done | bytes 688160 | tf_op jit(solution)/shard_map/ppermute | solution.py:334
  119.3 1.8 %collective-permute-start.3 = (bf16[384,384]{1,0:T(8,128)(2,1)S(1)}, bf16[384,384]{1,0:T(8,128)(2,1)S(1)}, u32[]{:S(2)}, u32[]{:S(2)}) collective-permute-start(bf16[384,384]{1,0:T(8,128)(2,1)S(1)} %slice.46), channel_id=1, source_target_pairs={{0,4},{1,5},{4,8},{5,9},{8,12},{9,13},{12,14},{13,15},{14,10},{15,... | collective-permute-start | bytes 884744 | tf_op jit(solution)/shard_map/ppermute | solution.py:334
  121.6 1.8 %collective-permute-start.10 = (bf16[384,512]{1,0:T(8,128)(2,1)S(1)}, bf16[384,512]{1,0:T(8,128)(2,1)S(1)}, u32[]{:S(2)}, u32[]{:S(2)}) collective-permute-start(bf16[384,512]{1,0:T(8,128)(2,1)S(1)} %slice.49), channel_id=1, source_target_pairs={{0,4},{1,5},{4,8},{5,9},{8,12},{9,13},{12,14},{13,15},{14,10},{15,... | collective-permute-start | bytes 1179656 | tf_op jit(solution)/shard_map/ppermute | solution.py:334
  123.4 10.4 %collective-permute-done.16.refs_0_ = bf16[384,896]{1,0:T(8,128)(2,1)S(1)} collective-permute-done((bf16[384,896]{1,0:T(8,128)(2,1)S(1)}, bf16[384,896]{1,0:T(8,128)(2,1)S(1)}, u32[]{:S(2)}, u32[]{:S(2)}) %collective-permute-start.16) | collective-permute-done | bytes 688160 | tf_op jit(solution)/shard_map/ppermute | solution.py:334
  133.8 0.7 dynamic-slice_bitcast_fusion.starts_ref
  134.5 2.4 %collective-permute-done.20.refs_2_ = bf16[384,896]{1,0:T(8,128)(2,1)S(1)} collective-permute-done((bf16[384,896]{1,0:T(8,128)(2,1)S(1)}, bf16[384,896]{1,0:T(8,128)(2,1)S(1)}, u32[]{:S(2)}, u32[]{:S(2)}) %collective-permute-start.20) | collective-permute-done | bytes 688160 | tf_op jit(solution)/shard_map/ppermute | solution.py:334
  136.9 3.2 %collective-permute-done.3.refs_0_ = bf16[384,384]{1,0:T(8,128)(2,1)S(1)} collective-permute-done((bf16[384,384]{1,0:T(8,128)(2,1)S(1)}, bf16[384,384]{1,0:T(8,128)(2,1)S(1)}, u32[]{:S(2)}, u32[]{:S(2)}) %collective-permute-start.3) | collective-permute-done | bytes 294944 | tf_op jit(solution)/shard_map/ppermute | solution.py:334
  140.1 1.9 %shard_map.80.refs_6_ = f32[384,512]{1,0:T(8,128)S(1)} custom-call(s32[1]{0:T(128)} %bitcast.2.f_ref.core_ref, f32[192,128]{1,0:T(8,128)S(1)} %pad_maximum_fusion.mine_ref, f32[192,128]{1,0:T(8,128)S(1)} %collective-permute-done.36.other_ref, s32[384,1]{1,0:T(8,128)S(1)} %broadcast_in_dim_reshape.5.l_ref, bf16[512,512]{1,0:T(8,128)(2,1)S(1)} %bitcast.16), custom_call_target="tpu_custom_call" | custom-call | flops 301989888 | bytes 1507328 | tf_op jit(solution)/shard_map/pallas_call | solution.py:264
  142.1 0.6 collective-permute-start.21
  142.6 4.2 %shard_map.73.refs_5_ = f32[384,512]{1,0:T(8,128)S(1)} custom-call(s32[34]{0:T(128)S(1)} %dynamic-slice_bitcast_fusion.starts_ref, bf16[384,1792]{1,0:T(8,128)(2,1)S(1)} %bitcast.15, bf16[384,1792]{1,0:T(8,128)(2,1)S(1)} %collective-permute-done.32.refs_1_, bf16[512,28672]{1,0:T(8,128)(2,1)} %refs_4_.13), custom_call_target="tpu_custom_call" | custom-call | flops 1409286144 | bytes 7995392 | tf_op jit(solution)/shard_map/pallas_call | solution.py:214
  147.1 0.6 collective-permute-start.12
  147.7 4.0 %shard_map.74.refs_5_ = f32[384,512]{1,0:T(8,128)S(1)} custom-call(s32[34]{0:T(128)S(1)} %dynamic-slice_bitcast_fusion.starts_ref, bf16[384,896]{1,0:T(8,128)(2,1)S(1)} %collective-permute-done.refs_0_, bf16[384,896]{1,0:T(8,128)(2,1)S(1)} %collective-permute-done.30.refs_1_, bf16[384,896]{1,0:T(8,128)(2,1)S(1)} %collective-permute-done.5.refs_2_, ...), custom_call_target="tpu_custom_call" | custom-call | flops 1409286144 | bytes 7995392 | tf_op jit(solution)/shard_map/pallas_call | solution.py:214
  151.7 4.0 %shard_map.75.refs_5_ = f32[384,512]{1,0:T(8,128)S(1)} custom-call(s32[34]{0:T(128)S(1)} %dynamic-slice_bitcast_fusion.starts_ref, bf16[384,896]{1,0:T(8,128)(2,1)S(1)} %collective-permute-done.14.refs_0_, bf16[384,896]{1,0:T(8,128)(2,1)S(1)} %collective-permute-done.28.refs_1_, bf16[384,896]{1,0:T(8,128)(2,1)S(1)} %collective-permute-done.18.refs_2_, ...), custom_call_target="tpu_custom_call" | custom-call | flops 1409286144 | bytes 7995392 | tf_op jit(solution)/shard_map/pallas_call | solution.py:214
  155.8 4.0 %shard_map.76.refs_5_ = f32[384,512]{1,0:T(8,128)S(1)} custom-call(s32[34]{0:T(128)S(1)} %dynamic-slice_bitcast_fusion.starts_ref, bf16[384,896]{1,0:T(8,128)(2,1)S(1)} %collective-permute-done.1.refs_0_, bf16[384,896]{1,0:T(8,128)(2,1)S(1)} %collective-permute-done.26.refs_1_, bf16[384,896]{1,0:T(8,128)(2,1)S(1)} %collective-permute-done.6.refs_2_, ...), custom_call_target="tpu_custom_call" | custom-call | flops 1409286144 | bytes 7995392 | tf_op jit(solution)/shard_map/pallas_call | solution.py:214
  159.9 0.5 collective-permute-start.13
  160.4 4.0 %shard_map.77.refs_5_ = f32[384,512]{1,0:T(8,128)S(1)} custom-call(s32[34]{0:T(128)S(1)} %dynamic-slice_bitcast_fusion.starts_ref, bf16[384,896]{1,0:T(8,128)(2,1)S(1)} %collective-permute-done.15.refs_0_, bf16[384,896]{1,0:T(8,128)(2,1)S(1)} %collective-permute-done.24.refs_1_, bf16[384,896]{1,0:T(8,128)(2,1)S(1)} %collective-permute-done.19.refs_2_, ...), custom_call_target="tpu_custom_call" | custom-call | flops 1409286144 | bytes 7995392 | tf_op jit(solution)/shard_map/pallas_call | solution.py:214
  164.6 0.4 collective-permute-start.9
  165.1 4.0 %shard_map.78.refs_5_ = f32[384,512]{1,0:T(8,128)S(1)} custom-call(s32[34]{0:T(128)S(1)} %dynamic-slice_bitcast_fusion.starts_ref, bf16[384,896]{1,0:T(8,128)(2,1)S(1)} %collective-permute-done.2.refs_0_, bf16[384,896]{1,0:T(8,128)(2,1)S(1)} %collective-permute-done.22.refs_1_, bf16[384,896]{1,0:T(8,128)(2,1)S(1)} %collective-permute-done.7.refs_2_, ...), custom_call_target="tpu_custom_call" | custom-call | flops 1409286144 | bytes 7995392 | tf_op jit(solution)/shard_map/pallas_call | solution.py:214
  169.1 4.0 %shard_map.81.refs_5_ = f32[384,512]{1,0:T(8,128)S(1)} custom-call(s32[34]{0:T(128)S(1)} %dynamic-slice_bitcast_fusion.starts_ref, bf16[384,896]{1,0:T(8,128)(2,1)S(1)} %collective-permute-done.16.refs_0_, bf16[384,896]{1,0:T(8,128)(2,1)S(1)} %collective-permute-done.17.refs_1_, bf16[384,896]{1,0:T(8,128)(2,1)S(1)} %collective-permute-done.20.refs_2_, ...), custom_call_target="tpu_custom_call" | custom-call | flops 1409286144 | bytes 7995392 | tf_op jit(solution)/shard_map/pallas_call | solution.py:214
  173.2 3.1 %shard_map.82 = (f32[384,512]{1,0:T(8,128)S(1)}, bf16[512,384]{1,0:T(8,128)(2,1)S(1)}, bf16[512,384]{1,0:T(8,128)(2,1)S(1)}, bf16[512,384]{1,0:T(8,128)(2,1)S(1)}, bf16[512,384]{1,0:T(8,128)(2,1)S(1)}) custom-call(s32[34]{0:T(128)S(1)} %dynamic-slice_bitcast_fusion.starts_ref, bf16[384,512]{1,0:T(8,128)(2,1)S(1)} %collective-permute-done.10.refs_0_, ...), custom_call_target="tpu_custom_call" | custom-call | flops 805306368 | bytes 6815744 | tf_op jit(solution)/shard_map/pallas_call | solution.py:214
  176.3 1.1 shard_map.83.refs_4_
  177.5 1.9 %shard_map.84 = bf16[384,512]{1,0:T(8,128)(2,1)} custom-call(s32[34]{0:T(128)S(1)} %dynamic-slice_bitcast_fusion.starts_ref, bf16[384,384]{1,0:T(8,128)(2,1)S(1)} %collective-permute-done.4.refs_0_, bf16[384,384]{1,0:T(8,128)(2,1)S(1)} %collective-permute-done.9.refs_1_, bf16[512,384]{1,0:T(8,128)(2,1)S(1)} %get-tuple-element.14.refs_2_, ...), custom_call_target="tpu_custom_call" | custom-call | flops 301989888 | bytes 2949120 | tf_op jit(solution)/shard_map/pallas_call | solution.py:214
  (63 shorter events, 3.4 us)
Async XLA Ops:
  2.2 1.3 copy-start
  3.5 24.7 %copy-start.1 = (bf16[2,192,1792]{2,1,0:T(8,128)(2,1)S(1)}, bf16[2,192,1792]{2,1,0:T(8,128)(2,1)}, u32[]{:S(2)}) copy-start(bf16[2,192,1792]{2,1,0:T(8,128)(2,1)} %param.7) | copy-start | bytes 4128772
  6.9 1.5 collective-permute-start.33
  8.4 5.0 %collective-permute-start.34 = (f32[96,128]{1,0:T(8,128)S(1)}, f32[96,128]{1,0:T(8,128)S(1)}, u32[]{:S(2)}, u32[]{:S(2)}) collective-permute-start(f32[96,128]{1,0:T(8,128)S(1)} %slice_select_fusion), channel_id=1, source_target_pairs={{0,2},{1,3},{4,6},{5,7},{8,10},{9,11},{12,14},{13,15},{14,12},{15,... | collective-permute-start | bytes 147464 | tf_op jit(solution)/shard_map/ppermute | solution.py:131
  25.0 8.9 %all-to-all-start.1 = ((f32[4,24,128]{2,1,0:T(8,128)}), f32[4,24,128]{2,1,0:T(8,128)S(1)}, u32[]{:S(2)}, u32[]{:S(2)}) async-start(f32[4,24,128]{2,1,0:T(8,128)} %broadcast_in_dim.2), calls=%async_computation.1 | async-start | bytes 98304 | tf_op jit(solution)/shard_map/all_to_all | solution.py:148
  28.3 43.3 %collective-permute-start.32 = (bf16[384,1792]{1,0:T(8,128)(2,1)S(1)}, bf16[384,1792]{1,0:T(8,128)(2,1)S(1)}, u32[]{:S(2)}, u32[]{:S(2)}) collective-permute-start(bf16[384,1792]{1,0:T(8,128)(2,1)S(1)} %bitcast.13), channel_id=1, source_target_pairs={{0,1},{1,0},{4,5},{5,4},{8,9},{9,8},{12,13},{13,12},{14,15},{15,14... | collective-permute-start | bytes 4128776 | tf_op jit(solution)/shard_map/ppermute | solution.py:325
  33.9 4.6 %collective-permute-start.35 = (f32[96,128]{1,0:T(8,128)S(1)}, f32[96,128]{1,0:T(8,128)S(1)}, u32[]{:S(2)}, u32[]{:S(2)}) collective-permute-start(f32[96,128]{1,0:T(8,128)S(1)} %bitcast.18), channel_id=1, source_target_pairs={{0,2},{1,3},{4,6},{5,7},{8,10},{9,11},{12,14},{13,15},{14,12},{15,... | collective-permute-start | bytes 147464 | tf_op jit(solution)/shard_map/ppermute | solution.py:136
  34.0 106.1 %copy-start.2 = (bf16[8,64,512]{2,1,0:T(8,128)(2,1)S(1)}, bf16[8,64,512]{2,1,0:T(8,128)(2,1)}, u32[]{:S(2)}) copy-start(bf16[8,64,512]{2,1,0:T(8,128)(2,1)} %param.10) | copy-start | bytes 1572868
  34.0 19.2 %collective-permute-start = (bf16[384,896]{1,0:T(8,128)(2,1)S(1)}, bf16[384,896]{1,0:T(8,128)(2,1)S(1)}, u32[]{:S(2)}, u32[]{:S(2)}) collective-permute-start(bf16[384,896]{1,0:T(8,128)(2,1)S(1)} %get-tuple-element.20), channel_id=1, source_target_pairs={{0,4},{1,5},{4,8},{5,9},{8,12},{9,13},{12,14},{13,15},{14,10},{15,... | collective-permute-start | bytes 2064392 | tf_op jit(solution)/shard_map/ppermute | solution.py:334
  38.6 2.2 %collective-permute-start.36 = (f32[192,128]{1,0:T(8,128)S(1)}, f32[192,128]{1,0:T(8,128)S(1)}, u32[]{:S(2)}, u32[]{:S(2)}) collective-permute-start(f32[192,128]{1,0:T(8,128)S(1)} %pad_maximum_fusion.mine_ref), channel_id=1, source_target_pairs={{0,1},{1,0},{4,5},{5,4},{8,9},{9,8},{12,13},{13,12},{14,15},{15,14... | collective-permute-start | bytes 294920 | tf_op jit(solution)/shard_map/ppermute | solution.py:150
  38.6 18.4 %collective-permute-start.5 = (bf16[384,896]{1,0:T(8,128)(2,1)S(1)}, bf16[384,896]{1,0:T(8,128)(2,1)S(1)}, u32[]{:S(2)}, u32[]{:S(2)}) collective-permute-start(bf16[384,896]{1,0:T(8,128)(2,1)S(1)} %get-tuple-element.19), channel_id=1, source_target_pairs={{4,0},{5,1},{8,4},{9,5},{12,8},{13,9},{14,12},{15,13},{10,14},{11,... | collective-permute-start | bytes 2064392 | tf_op jit(solution)/shard_map/ppermute | solution.py:334
  38.7 25.4 %collective-permute-start.14 = (bf16[384,896]{1,0:T(8,128)(2,1)S(1)}, bf16[384,896]{1,0:T(8,128)(2,1)S(1)}, u32[]{:S(2)}, u32[]{:S(2)}) collective-permute-start(bf16[384,896]{1,0:T(8,128)(2,1)S(1)} %get-tuple-element.19), channel_id=1, source_target_pairs={{0,4},{1,5},{4,8},{5,9},{8,12},{9,13},{12,14},{13,15},{14,10},{15,... | collective-permute-start | bytes 2064392 | tf_op jit(solution)/shard_map/ppermute | solution.py:334
  40.7 30.5 %collective-permute-start.18 = (bf16[384,896]{1,0:T(8,128)(2,1)S(1)}, bf16[384,896]{1,0:T(8,128)(2,1)S(1)}, u32[]{:S(2)}, u32[]{:S(2)}) collective-permute-start(bf16[384,896]{1,0:T(8,128)(2,1)S(1)} %get-tuple-element.20), channel_id=1, source_target_pairs={{4,0},{5,1},{8,4},{9,5},{12,8},{13,9},{14,12},{15,13},{10,14},{11,... | collective-permute-start | bytes 2064392 | tf_op jit(solution)/shard_map/ppermute | solution.py:334
  53.3 20.0 %collective-permute-start.30 = (bf16[384,896]{1,0:T(8,128)(2,1)S(1)}, bf16[384,896]{1,0:T(8,128)(2,1)S(1)}, u32[]{:S(2)}, u32[]{:S(2)}) collective-permute-start(bf16[384,896]{1,0:T(8,128)(2,1)S(1)} %collective-permute-done.refs_0_), channel_id=1, source_target_pairs={{0,1},{1,0},{4,5},{5,4},{8,9},{9,8},{12,13},{13,12},{14,15},{15,14... | collective-permute-start | bytes 2064392 | tf_op jit(solution)/shard_map/ppermute | solution.py:337
  57.0 16.3 %collective-permute-start.31 = (bf16[384,896]{1,0:T(8,128)(2,1)S(1)}, bf16[384,896]{1,0:T(8,128)(2,1)S(1)}, u32[]{:S(2)}, u32[]{:S(2)}) collective-permute-start(bf16[384,896]{1,0:T(8,128)(2,1)S(1)} %collective-permute-done.5.refs_2_), channel_id=1, source_target_pairs={{0,1},{1,0},{4,5},{5,4},{8,9},{9,8},{12,13},{13,12},{14,15},{15,14... | collective-permute-start | bytes 2064392 | tf_op jit(solution)/shard_map/ppermute | solution.py:337
  64.0 9.6 %collective-permute-start.28 = (bf16[384,896]{1,0:T(8,128)(2,1)S(1)}, bf16[384,896]{1,0:T(8,128)(2,1)S(1)}, u32[]{:S(2)}, u32[]{:S(2)}) collective-permute-start(bf16[384,896]{1,0:T(8,128)(2,1)S(1)} %collective-permute-done.14.refs_0_), channel_id=1, source_target_pairs={{0,1},{1,0},{4,5},{5,4},{8,9},{9,8},{12,13},{13,12},{14,15},{15,14... | collective-permute-start | bytes 2064392 | tf_op jit(solution)/shard_map/ppermute | solution.py:337
  71.2 18.3 %collective-permute-start.1 = (bf16[384,896]{1,0:T(8,128)(2,1)S(1)}, bf16[384,896]{1,0:T(8,128)(2,1)S(1)}, u32[]{:S(2)}, u32[]{:S(2)}) collective-permute-start(bf16[384,896]{1,0:T(8,128)(2,1)S(1)} %collective-permute-done.refs_0_), channel_id=1, source_target_pairs={{0,4},{1,5},{4,8},{5,9},{8,12},{9,13},{12,14},{13,15},{14,10},{15,... | collective-permute-start | bytes 2064392 | tf_op jit(solution)/shard_map/ppermute | solution.py:334
  71.5 18.3 %collective-permute-start.6 = (bf16[384,896]{1,0:T(8,128)(2,1)S(1)}, bf16[384,896]{1,0:T(8,128)(2,1)S(1)}, u32[]{:S(2)}, u32[]{:S(2)}) collective-permute-start(bf16[384,896]{1,0:T(8,128)(2,1)S(1)} %collective-permute-done.5.refs_2_), channel_id=1, source_target_pairs={{4,0},{5,1},{8,4},{9,5},{12,8},{13,9},{14,12},{15,13},{10,14},{11,... | collective-permute-start | bytes 2064392 | tf_op jit(solution)/shard_map/ppermute | solution.py:334
  73.2 16.8 %collective-permute-start.29 = (bf16[384,896]{1,0:T(8,128)(2,1)S(1)}, bf16[384,896]{1,0:T(8,128)(2,1)S(1)}, u32[]{:S(2)}, u32[]{:S(2)}) collective-permute-start(bf16[384,896]{1,0:T(8,128)(2,1)S(1)} %collective-permute-done.18.refs_2_), channel_id=1, source_target_pairs={{0,1},{1,0},{4,5},{5,4},{8,9},{9,8},{12,13},{13,12},{14,15},{15,14... | collective-permute-start | bytes 2064392 | tf_op jit(solution)/shard_map/ppermute | solution.py:337
  73.3 31.0 %collective-permute-start.15 = (bf16[384,896]{1,0:T(8,128)(2,1)S(1)}, bf16[384,896]{1,0:T(8,128)(2,1)S(1)}, u32[]{:S(2)}, u32[]{:S(2)}) collective-permute-start(bf16[384,896]{1,0:T(8,128)(2,1)S(1)} %collective-permute-done.14.refs_0_), channel_id=1, source_target_pairs={{0,4},{1,5},{4,8},{5,9},{8,12},{9,13},{12,14},{13,15},{14,10},{15,... | collective-permute-start | bytes 2064392 | tf_op jit(solution)/shard_map/ppermute | solution.py:334
  73.6 30.9 %collective-permute-start.19 = (bf16[384,896]{1,0:T(8,128)(2,1)S(1)}, bf16[384,896]{1,0:T(8,128)(2,1)S(1)}, u32[]{:S(2)}, u32[]{:S(2)}) collective-permute-start(bf16[384,896]{1,0:T(8,128)(2,1)S(1)} %collective-permute-done.18.refs_2_), channel_id=1, source_target_pairs={{4,0},{5,1},{8,4},{9,5},{12,8},{13,9},{14,12},{15,13},{10,14},{11,... | collective-permute-start | bytes 2064392 | tf_op jit(solution)/shard_map/ppermute | solution.py:334
  89.5 15.0 %collective-permute-start.26 = (bf16[384,896]{1,0:T(8,128)(2,1)S(1)}, bf16[384,896]{1,0:T(8,128)(2,1)S(1)}, u32[]{:S(2)}, u32[]{:S(2)}) collective-permute-start(bf16[384,896]{1,0:T(8,128)(2,1)S(1)} %collective-permute-done.1.refs_0_), channel_id=1, source_target_pairs={{0,1},{1,0},{4,5},{5,4},{8,9},{9,8},{12,13},{13,12},{14,15},{15,14... | collective-permute-start | bytes 2064392 | tf_op jit(solution)/shard_map/ppermute | solution.py:337
  89.8 15.2 %collective-permute-start.27 = (bf16[384,896]{1,0:T(8,128)(2,1)S(1)}, bf16[384,896]{1,0:T(8,128)(2,1)S(1)}, u32[]{:S(2)}, u32[]{:S(2)}) collective-permute-start(bf16[384,896]{1,0:T(8,128)(2,1)S(1)} %collective-permute-done.6.refs_2_), channel_id=1, source_target_pairs={{0,1},{1,0},{4,5},{5,4},{8,9},{9,8},{12,13},{13,12},{14,15},{15,14... | collective-permute-start | bytes 2064392 | tf_op jit(solution)/shard_map/ppermute | solution.py:337
  90.0 29.0 %collective-permute-start.2 = (bf16[384,896]{1,0:T(8,128)(2,1)S(1)}, bf16[384,896]{1,0:T(8,128)(2,1)S(1)}, u32[]{:S(2)}, u32[]{:S(2)}) collective-permute-start(bf16[384,896]{1,0:T(8,128)(2,1)S(1)} %collective-permute-done.1.refs_0_), channel_id=1, source_target_pairs={{0,4},{1,5},{4,8},{5,9},{8,12},{9,13},{12,14},{13,15},{14,10},{15,... | collective-permute-start | bytes 2064392 | tf_op jit(solution)/shard_map/ppermute | solution.py:334
  104.3 15.1 %collective-permute-start.7 = (bf16[384,896]{1,0:T(8,128)(2,1)S(1)}, bf16[384,896]{1,0:T(8,128)(2,1)S(1)}, u32[]{:S(2)}, u32[]{:S(2)}) collective-permute-start(bf16[384,896]{1,0:T(8,128)(2,1)S(1)} %collective-permute-done.6.refs_2_), channel_id=1, source_target_pairs={{4,0},{5,1},{8,4},{9,5},{12,8},{13,9},{14,12},{15,13},{10,14},{11,... | collective-permute-start | bytes 2064392 | tf_op jit(solution)/shard_map/ppermute | solution.py:334
  104.6 16.6 %collective-permute-start.24 = (bf16[384,896]{1,0:T(8,128)(2,1)S(1)}, bf16[384,896]{1,0:T(8,128)(2,1)S(1)}, u32[]{:S(2)}, u32[]{:S(2)}) collective-permute-start(bf16[384,896]{1,0:T(8,128)(2,1)S(1)} %collective-permute-done.15.refs_0_), channel_id=1, source_target_pairs={{0,1},{1,0},{4,5},{5,4},{8,9},{9,8},{12,13},{13,12},{14,15},{15,14... | collective-permute-start | bytes 2064392 | tf_op jit(solution)/shard_map/ppermute | solution.py:337
  104.6 17.0 %collective-permute-start.25 = (bf16[384,896]{1,0:T(8,128)(2,1)S(1)}, bf16[384,896]{1,0:T(8,128)(2,1)S(1)}, u32[]{:S(2)}, u32[]{:S(2)}) collective-permute-start(bf16[384,896]{1,0:T(8,128)(2,1)S(1)} %collective-permute-done.19.refs_2_), channel_id=1, source_target_pairs={{0,1},{1,0},{4,5},{5,4},{8,9},{9,8},{12,13},{13,12},{14,15},{15,14... | collective-permute-start | bytes 2064392 | tf_op jit(solution)/shard_map/ppermute | solution.py:337
  105.1 28.7 %collective-permute-start.16 = (bf16[384,896]{1,0:T(8,128)(2,1)S(1)}, bf16[384,896]{1,0:T(8,128)(2,1)S(1)}, u32[]{:S(2)}, u32[]{:S(2)}) collective-permute-start(bf16[384,896]{1,0:T(8,128)(2,1)S(1)} %collective-permute-done.15.refs_0_), channel_id=1, source_target_pairs={{0,4},{1,5},{4,8},{5,9},{8,12},{9,13},{12,14},{13,15},{14,10},{15,... | collective-permute-start | bytes 2064392 | tf_op jit(solution)/shard_map/ppermute | solution.py:334
  119.0 17.9 %collective-permute-start.20 = (bf16[384,896]{1,0:T(8,128)(2,1)S(1)}, bf16[384,896]{1,0:T(8,128)(2,1)S(1)}, u32[]{:S(2)}, u32[]{:S(2)}) collective-permute-start(bf16[384,896]{1,0:T(8,128)(2,1)S(1)} %collective-permute-done.19.refs_2_), channel_id=1, source_target_pairs={{4,0},{5,1},{8,4},{9,5},{12,8},{13,9},{14,12},{15,13},{10,14},{11,... | collective-permute-start | bytes 2064392 | tf_op jit(solution)/shard_map/ppermute | solution.py:334
  119.3 20.7 %collective-permute-start.3 = (bf16[384,384]{1,0:T(8,128)(2,1)S(1)}, bf16[384,384]{1,0:T(8,128)(2,1)S(1)}, u32[]{:S(2)}, u32[]{:S(2)}) collective-permute-start(bf16[384,384]{1,0:T(8,128)(2,1)S(1)} %slice.46), channel_id=1, source_target_pairs={{0,4},{1,5},{4,8},{5,9},{8,12},{9,13},{12,14},{13,15},{14,10},{15,... | collective-permute-start | bytes 884744 | tf_op jit(solution)/shard_map/ppermute | solution.py:334
  121.2 20.9 %collective-permute-start.8 = (bf16[384,384]{1,0:T(8,128)(2,1)S(1)}, bf16[384,384]{1,0:T(8,128)(2,1)S(1)}, u32[]{:S(2)}, u32[]{:S(2)}) collective-permute-start(bf16[384,384]{1,0:T(8,128)(2,1)S(1)} %slice.48), channel_id=1, source_target_pairs={{4,0},{5,1},{8,4},{9,5},{12,8},{13,9},{14,12},{15,13},{10,14},{11,... | collective-permute-start | bytes 884744 | tf_op jit(solution)/shard_map/ppermute | solution.py:334
  121.6 25.6 %collective-permute-start.10 = (bf16[384,512]{1,0:T(8,128)(2,1)S(1)}, bf16[384,512]{1,0:T(8,128)(2,1)S(1)}, u32[]{:S(2)}, u32[]{:S(2)}) collective-permute-start(bf16[384,512]{1,0:T(8,128)(2,1)S(1)} %slice.49), channel_id=1, source_target_pairs={{0,4},{1,5},{4,8},{5,9},{8,12},{9,13},{12,14},{13,15},{14,10},{15,... | collective-permute-start | bytes 1179656 | tf_op jit(solution)/shard_map/ppermute | solution.py:334
  133.8 26.2 %collective-permute-start.22 = (bf16[384,896]{1,0:T(8,128)(2,1)S(1)}, bf16[384,896]{1,0:T(8,128)(2,1)S(1)}, u32[]{:S(2)}, u32[]{:S(2)}) collective-permute-start(bf16[384,896]{1,0:T(8,128)(2,1)S(1)} %collective-permute-done.2.refs_0_), channel_id=1, source_target_pairs={{0,1},{1,0},{4,5},{5,4},{8,9},{9,8},{12,13},{13,12},{14,15},{15,14... | collective-permute-start | bytes 2064392 | tf_op jit(solution)/shard_map/ppermute | solution.py:337
  136.9 27.6 %collective-permute-start.23 = (bf16[384,896]{1,0:T(8,128)(2,1)S(1)}, bf16[384,896]{1,0:T(8,128)(2,1)S(1)}, u32[]{:S(2)}, u32[]{:S(2)}) collective-permute-start(bf16[384,896]{1,0:T(8,128)(2,1)S(1)} %collective-permute-done.7.refs_2_), channel_id=1, source_target_pairs={{0,1},{1,0},{4,5},{5,4},{8,9},{9,8},{12,13},{13,12},{14,15},{15,14... | collective-permute-start | bytes 2064392 | tf_op jit(solution)/shard_map/ppermute | solution.py:337
  140.1 24.6 %collective-permute-start.17 = (bf16[384,896]{1,0:T(8,128)(2,1)S(1)}, bf16[384,896]{1,0:T(8,128)(2,1)S(1)}, u32[]{:S(2)}, u32[]{:S(2)}) collective-permute-start(bf16[384,896]{1,0:T(8,128)(2,1)S(1)} %collective-permute-done.16.refs_0_), channel_id=1, source_target_pairs={{0,1},{1,0},{4,5},{5,4},{8,9},{9,8},{12,13},{13,12},{14,15},{15,14... | collective-permute-start | bytes 2064392 | tf_op jit(solution)/shard_map/ppermute | solution.py:337
  142.1 27.1 %collective-permute-start.21 = (bf16[384,896]{1,0:T(8,128)(2,1)S(1)}, bf16[384,896]{1,0:T(8,128)(2,1)S(1)}, u32[]{:S(2)}, u32[]{:S(2)}) collective-permute-start(bf16[384,896]{1,0:T(8,128)(2,1)S(1)} %collective-permute-done.20.refs_2_), channel_id=1, source_target_pairs={{0,1},{1,0},{4,5},{5,4},{8,9},{9,8},{12,13},{13,12},{14,15},{15,14... | collective-permute-start | bytes 2064392 | tf_op jit(solution)/shard_map/ppermute | solution.py:337
  147.1 12.7 %collective-permute-start.12 = (bf16[384,512]{1,0:T(8,128)(2,1)S(1)}, bf16[384,512]{1,0:T(8,128)(2,1)S(1)}, u32[]{:S(2)}, u32[]{:S(2)}) collective-permute-start(bf16[384,512]{1,0:T(8,128)(2,1)S(1)} %slice.50), channel_id=1, source_target_pairs={{4,0},{5,1},{8,4},{9,5},{12,8},{13,9},{14,12},{15,13},{10,14},{11,... | collective-permute-start | bytes 1179656 | tf_op jit(solution)/shard_map/ppermute | solution.py:334
  159.8 13.3 %collective-permute-start.11 = (bf16[384,512]{1,0:T(8,128)(2,1)S(1)}, bf16[384,512]{1,0:T(8,128)(2,1)S(1)}, u32[]{:S(2)}, u32[]{:S(2)}) collective-permute-start(bf16[384,512]{1,0:T(8,128)(2,1)S(1)} %collective-permute-done.10.refs_0_), channel_id=1, source_target_pairs={{0,1},{1,0},{4,5},{5,4},{8,9},{9,8},{12,13},{13,12},{14,15},{15,14... | collective-permute-start | bytes 1179656 | tf_op jit(solution)/shard_map/ppermute | solution.py:337
  159.9 13.2 %collective-permute-start.13 = (bf16[384,512]{1,0:T(8,128)(2,1)S(1)}, bf16[384,512]{1,0:T(8,128)(2,1)S(1)}, u32[]{:S(2)}, u32[]{:S(2)}) collective-permute-start(bf16[384,512]{1,0:T(8,128)(2,1)S(1)} %collective-permute-done.12.refs_2_), channel_id=1, source_target_pairs={{0,1},{1,0},{4,5},{5,4},{8,9},{9,8},{12,13},{13,12},{14,15},{15,14... | collective-permute-start | bytes 1179656 | tf_op jit(solution)/shard_map/ppermute | solution.py:337
  164.5 13.0 %collective-permute-start.4 = (bf16[384,384]{1,0:T(8,128)(2,1)S(1)}, bf16[384,384]{1,0:T(8,128)(2,1)S(1)}, u32[]{:S(2)}, u32[]{:S(2)}) collective-permute-start(bf16[384,384]{1,0:T(8,128)(2,1)S(1)} %collective-permute-done.3.refs_0_), channel_id=1, source_target_pairs={{0,1},{1,0},{4,5},{5,4},{8,9},{9,8},{12,13},{13,12},{14,15},{15,14... | collective-permute-start | bytes 884744 | tf_op jit(solution)/shard_map/ppermute | solution.py:337
  164.6 12.8 %collective-permute-start.9 = (bf16[384,384]{1,0:T(8,128)(2,1)S(1)}, bf16[384,384]{1,0:T(8,128)(2,1)S(1)}, u32[]{:S(2)}, u32[]{:S(2)}) collective-permute-start(bf16[384,384]{1,0:T(8,128)(2,1)S(1)} %collective-permute-done.8.refs_1_), channel_id=1, source_target_pairs={{0,1},{1,0},{4,5},{5,4},{8,9},{9,8},{12,13},{13,12},{14,15},{15,14... | collective-permute-start | bytes 884744 | tf_op jit(solution)/shard_map/ppermute | solution.py:337

commit v5 on v4

--- a/solution.py
+++ b/solution.py
@@ -37,18 +37,48 @@
     return pltpu.with_memory_space_constraint(array, pltpu.HBM)
 
 
+def cut_block(block, half):
+    def body(x_ref, a_ref, b_ref, sem):
+        copies = [
+            pltpu.make_async_copy(x_ref.at[:, pl.ds(k * half, half)], out, sem.at[k])
+            for k, out in enumerate((a_ref, b_ref))
+        ]
+        for copy in copies:
+            copy.start()
+        for copy in copies:
+            copy.wait()
+
+    vmem = pl.BlockSpec(memory_space=pltpu.VMEM)
+    shape = jax.ShapeDtypeStruct((block.shape[0], half), block.dtype)
+    return pl.pallas_call(
+        body,
+        out_shape=(shape, shape),
+        in_specs=[pl.BlockSpec(memory_space=pltpu.HBM)],
+        out_specs=(vmem, vmem),
+        scratch_shapes=[pltpu.SemaphoreType.DMA((2,))],
+        compiler_params=pltpu.CompilerParams(vmem_limit_bytes=4 << 20),
+    )(in_hbm(block))
+
+
 def project_selected(rows, labels, factors, first):
     count, rank, units = factors.shape
-    total = rows.shape[0]
+    total = rows[0].shape[0]
+    half = units // 2
     wide = count * rank
     part = total // 2
 
-    def body(f_ref, x_ref, l_ref, a_any, mine_ref, other_ref, s_ref, a_ref, sem):
+    def body(f_ref, low_ref, high_ref, l_ref, a_any, mine_ref, other_ref, s_ref, a_ref, sem):
         copy = pltpu.make_async_copy(a_any, a_ref, sem)
         copy.start()
         copy.wait()
-        full = lax.dot_general(
-            x_ref[...], a_ref[...], (((1,), (1,)), ((), ())), preferred_element_type=jnp.float32
+        full = sum(
+            lax.dot_general(
+                x_ref[...],
+                a_ref[:, k * half : (k + 1) * half],
+                (((1,), (1,)), ((), ())),
+                preferred_element_type=jnp.float32,
+            )
+            for k, x_ref in enumerate((low_ref, high_ref))
         )
         own = jnp.zeros((total, rank), jnp.float32)
         for k in range(count):
@@ -64,7 +94,7 @@
     return pl.pallas_call(
         body,
         out_shape=(shape, shape),
-        in_specs=[pl.BlockSpec(memory_space=pltpu.SMEM), vmem, vmem, anywhere],
+        in_specs=[pl.BlockSpec(memory_space=pltpu.SMEM), vmem, vmem, vmem, anywhere],
         out_specs=(vmem, vmem),
         scratch_shapes=[
             pltpu.VMEM((total, 2 * rank), jnp.float32),
@@ -77,7 +107,7 @@
             bytes_accessed=2 * units * (total + wide) + 8 * total * rank,
         ),
         compiler_params=pltpu.CompilerParams(vmem_limit_bytes=12 << 20),
-    )(first.reshape(1), rows, labels[:, None], in_hbm(factors.reshape(wide, units)))
+    )(first.reshape(1), *rows, labels[:, None], in_hbm(factors.reshape(wide, units)))
 
 
 def labels_onehot(adapter_labels, count):
@@ -150,7 +180,7 @@
     return half, lax.ppermute(half, "row", partner)
 
 
-def chunk_matmul(chunks, starts, first, weight, added, out_dtype, ready=None, ahead=()):
+def chunk_matmul(chunks, starts, first, weight, added, out_dtype, ready, ahead):
     count = len(chunks)
     rows = chunks[0].shape[0]
     widths = [c.shape[1] for c in chunks]
@@ -159,20 +189,20 @@
 
     def body(starts_ref, *refs):
         x_refs, refs = refs[:count], refs[count:]
-        w_refs, refs = refs[: len(blocks)], refs[len(blocks) :]
+        w_any, refs = refs[0], refs[1:]
+        w_refs, refs = refs[: len(ready)], refs[len(ready) :]
         add_refs, refs = refs[: len(added)], refs[len(added) :]
         out_ref, ahead_refs, refs = refs[0], refs[1 : 1 + later], refs[1 + later :]
 
         def block(at, units):
             start = pl.multiple_of(starts_ref[at] * LANES, LANES)
-            return w_refs[0].at[:, pl.ds(start, units)]
+            return w_any.at[:, pl.ds(start, units)]
 
         copies = []
-        w_bufs = w_refs
-        if ready is None:
-            w_bufs, w_sem = refs[:count], refs[count]
+        if not ready:
+            w_refs, w_sem = refs[:count], refs[count]
             for k in range(count):
-                copy = pltpu.make_async_copy(block(first + k, widths[k]), w_bufs[k], w_sem.at[k])
+                copy = pltpu.make_async_copy(block(first + k, widths[k]), w_refs[k], w_sem.at[k])
                 copy.start()
                 copies.append(copy)
         fetches = [
@@ -187,7 +217,7 @@
                 copies[k].wait()
             part = lax.dot_general(
                 x_refs[k][...],
-                w_bufs[k][...],
+                w_refs[k][...],
                 (((1,), (1,)), ((), ())),
                 preferred_element_type=jnp.float32,
             )
@@ -200,10 +230,8 @@
 
     anywhere = pl.BlockSpec(memory_space=pltpu.HBM)
     vmem = pl.BlockSpec(memory_space=pltpu.VMEM)
-    blocks = [in_hbm(weight)] if ready is None else list(ready)
-    held = anywhere if ready is None else vmem
     scratch = []
-    if ready is None:
+    if not ready:
         scratch += [pltpu.VMEM((features, w), jnp.bfloat16) for w in widths]
         scratch += [pltpu.SemaphoreType.DMA((count,))]
     if later:
@@ -217,8 +245,8 @@
         + [jax.ShapeDtypeStruct((features, units), jnp.bfloat16) for _, units in ahead],
         in_specs=[pl.BlockSpec(memory_space=pltpu.SMEM)]
         + [vmem] * count
-        + [held] * len(blocks)
-        + [vmem] * len(added),
+        + [anywhere]
+        + [vmem] * (len(ready) + len(added)),
         out_specs=[vmem] * (1 + later),
         scratch_shapes=scratch,
         cost_estimate=pl.CostEstimate(
@@ -227,7 +255,7 @@
             bytes_accessed=2 * moved + 8 * rows * features,
         ),
         compiler_params=pltpu.CompilerParams(vmem_limit_bytes=room + (5 << 20)),
-    )(starts, *chunks, *blocks, *added)
+    )(starts, *chunks, in_hbm(weight), *ready, *added)
     return out[0], out[1:]
 
 
@@ -312,18 +340,18 @@
         device_units = flat.shape[1]
         half = device_units // 2
         tiles = half // LANES
-        cut = (tiles - tiles * 3 // 7) * LANES
+        cut = (tiles - tiles * 2 // 7) * LANES
         me = lax.axis_index("row")
         core, side = [jnp.asarray(place)[me][k] for k in range(2)]
-        mine, other = project_selected(flat, labels, factors, core)
+        own = cut_block(flat, half)
+        mine, other = project_selected(own, labels, factors, core)
         halves = sum_by_stages(mine, other, side, partner, across, lines)
         extra = adapter_kernel(*halves, core, labels, outputs)
 
         plan = [(s // 2 + 1, s % 2, 0, half) for s in range(2 * long - 2)]
         plan += [(long, 0, 0, cut), (long, 0, cut, half - cut)]
-        own = [flat[:, :half], flat[:, half:]]
         beside = lax.ppermute(flat, "row", partner)
-        batches = [[(flat, 0, False, 0, 0), (beside, 0, True, 0, 0)]]
+        batches = [[(own[part], 0, False, part, 0) for part in range(2)] + [(beside, 0, True, 0, 0)]]
         held = {"up": list(own), "down": list(own)}
         for distance, turn, column, width in plan:
             found = []
@@ -348,17 +376,16 @@
                     source = ring[(p + offset) % chips][1 - c if beside else c]
                     table[at, k] = (source * device_units + part * half + column) // LANES
         starts = jnp.asarray(table)[me]
-        acc = []
-        done = 0
+        acc, ready, done = [], [], 0
         ends = len(batches) - 2
-        tail = len(order) - sum(len(found) for found in batches[ends:])
-        ahead = [(tail + k, found[0].shape[1]) for k, found in enumerate(batches[ends] + batches[-1])]
-        ready = None
+        settled = min(3, ends - 2)
         for k, found in enumerate(batches):
             last = k == len(batches) - 1
-            held = None
-            if k >= ends:
-                held, ready = ready[: len(found)], ready[len(found) :]
+            coming = []
+            if settled <= k <= ends - 2:
+                coming = batches[k + 1] if k < ends - 2 else sum(batches[k + 1 :], [])
+            at = done + len(found)
+            ahead = [(at + j, entry[0].shape[1]) for j, entry in enumerate(coming)]
             out, fetched = chunk_matmul(
                 [entry[0] for entry in found],
                 starts,
@@ -366,11 +393,10 @@
                 weight,
                 acc + ([extra] if k == ends - 2 else []),
                 jnp.bfloat16 if last else jnp.float32,
-                held,
-                ahead if k == ends - 1 else (),
+                ready[: len(found)],
+                ahead,
             )
-            if k == ends - 1:
-                ready = fetched
+            ready = ready[len(found) :] + list(fetched)
             acc = [out]
             done += len(found)
         return acc[0]

time: 180 us -> 181 us (level)
  starting transfers between devices: 23.9 us -> 34.1 us
  waiting for transfers between devices: 98.6 us -> 91 us
  local copies, waits for them, and re-layouts: 5.05 us -> 2.98 us
    ppermute x16, waiting for transfers between devices: 87.3 us -> 81.9 us  [ringed(): data = lax.ppermute(send, 'row', pairs)]
    ppermute x1, starting transfers between devices: 0.01 us -> 4.63 us  [join(): got = lax.ppermute(part, 'row', pairs)]
    ppermute x16, starting transfers between devices: 14.5 us -> 18.4 us  [ringed(): data = lax.ppermute(send, 'row', pairs)]
    all_to_all x1, starting transfers between devices: 3.27 us -> 5.37 us  [sum_by_stages(): lax.all_to_all(rows, 'row', 0, 0, axis_index_groups=lines, tiled=True)]
    all_to_all x1, waiting for transfers between devices: 5.58 us -> 3.68 us  [sum_by_stages(): lax.all_to_all(rows, 'row', 0, 0, axis_index_groups=lines, tiled=True)]
where the time goes in v5:
time: 181 us
  waiting for transfers between devices  91 us (50%)
  Pallas kernels  40.4 us (22%)
  starting transfers between devices  34.1 us (19%)
  blocking collectives  10.8 us (6%)
  local copies, waits for them, and re-layouts  2.98 us (2%)
    ppermute x16, waiting for transfers between devices, ringed(): data = lax.ppermute(send, 'row', pairs)  81.9 us
    pallas_call x10, Pallas kernels, chunk_matmul(): pl.pallas_call(body, out_shape=[jax.ShapeDtypeStruct((rows, features), ou...  33.8 us
    ppermute x16, starting transfers between devices, ringed(): data = lax.ppermute(send, 'row', pairs)  18.4 us
    all_to_all x1, blocking collectives, sum_by_stages(): lax.all_to_all(spread, 'row', 0, 0, axis_index_groups=lines, tiled=True)  10.8 us
    all_to_all x1, starting transfers between devices, sum_by_stages(): lax.all_to_all(rows, 'row', 0, 0, axis_index_groups=lines, tiled=True)  5.37 us
    ppermute x1, starting transfers between devices, join(): got = lax.ppermute(part, 'row', pairs)  4.63 us
    all_to_all x1, waiting for transfers between devices, sum_by_stages(): lax.all_to_all(rows, 'row', 0, 0, axis_index_groups=lines, tiled=True)  3.68 us
  transfers between devices with their start and end apart: 38, of which 16 were waited for; matrix products, arithmetic and copies ran while one was open for 1% of the time, Pallas kernels for 19%

profile of v5, /device:TPU:0, one launch (start us, length us, event | category | flops | bytes accessed | tf_op | source)
XLA Modules:
  0.0 180.9 jit_solution(2439200274516016214)
XLA Ops:
  0.0 0.7 constant_dynamic-slice_fusion
  1.3 1.3 shard_map.73
  2.6 0.9 broadcast_in_dim_reshape.5.l_ref
  3.5 3.4 %shard_map.80 = (f32[192,128]{1,0:T(8,128)S(1)}, f32[192,128]{1,0:T(8,128)S(1)}) custom-call(s32[1]{0:T(128)} %bitcast.2.f_ref.core_ref, bf16[384,896]{1,0:T(8,128)(2,1)S(1)} %get-tuple-element.33.refs_0_.low_ref, bf16[384,896]{1,0:T(8,128)(2,1)S(1)} %get-tuple-element.34.refs_1_.high_ref, s32[384,1]{1,0:T(8,128)S(1)} %broadcast_in_dim_reshape.5.l_ref, ...), custom_call_target="tpu_custom_call" | custom-call | flops 704643072 | bytes 3407872 | tf_op jit(solution)/shard_map/pallas_call | solution.py:94
  8.4 2.9 %collective-permute-start.30 = (f32[96,128]{1,0:T(8,128)S(1)}, f32[96,128]{1,0:T(8,128)S(1)}, u32[]{:S(2)}, u32[]{:S(2)}) collective-permute-start(f32[96,128]{1,0:T(8,128)S(1)} %slice_select_fusion), channel_id=1, source_target_pairs={{0,2},{1,3},{4,6},{5,7},{8,10},{9,11},{12,14},{13,15},{14,12},{15,... | collective-permute-start | bytes 147464 | tf_op jit(solution)/shard_map/ppermute | solution.py:161
  11.4 2.1 %collective-permute-done.30 = f32[96,128]{1,0:T(8,128)S(1)} collective-permute-done((f32[96,128]{1,0:T(8,128)S(1)}, f32[96,128]{1,0:T(8,128)S(1)}, u32[]{:S(2)}, u32[]{:S(2)}) %collective-permute-start.30) | collective-permute-done | bytes 49184 | tf_op jit(solution)/shard_map/ppermute | solution.py:161
  13.4 0.6 select_add_fusion
  14.1 5.4 %all-to-all-start = ((f32[4,24,128]{2,1,0:T(8,128)}), f32[4,24,128]{2,1,0:T(8,128)S(1)}, u32[]{:S(2)}, u32[]{:S(2)}) async-start(f32[4,24,128]{2,1,0:T(8,128)} %bitcast.15), calls=%async_computation | async-start | bytes 98304 | tf_op jit(solution)/shard_map/all_to_all | solution.py:175
  19.4 2.0 %collective-permute-start = (bf16[384,896]{1,0:T(8,128)(2,1)S(1)}, bf16[384,896]{1,0:T(8,128)(2,1)}, u32[]{:S(2)}, u32[]{:S(2)}) collective-permute-start(bf16[384,896]{1,0:T(8,128)(2,1)S(1)} %get-tuple-element.33.refs_0_.low_ref), channel_id=1, source_target_pairs={{0,4},{1,5},{4,8},{5,9},{8,12},{9,13},{12,14},{13,15},{14,10},{15,... | collective-permute-start | bytes 2064392 | tf_op jit(solution)/shard_map/ppermute | solution.py:362
  21.5 3.7 %all-to-all-done = f32[4,24,128]{2,1,0:T(8,128)S(1)} async-done(((f32[4,24,128]{2,1,0:T(8,128)}), f32[4,24,128]{2,1,0:T(8,128)S(1)}, u32[]{:S(2)}, u32[]{:S(2)}) %all-to-all-start) | async-done | bytes 49184 | tf_op jit(solution)/shard_map/all_to_all | solution.py:175
  25.1 10.8 %all_to_all.18 = f32[4,24,128]{2,1,0:T(8,128)S(1)} all-to-all(f32[4,24,128]{2,1,0:T(8,128)S(1)} %broadcast_in_dim.2), channel_id=1, replica_groups={{0,4,8,12},{1,5,9,13},{14,10,6,2},{15,11,7,3},{16,20,24,28},{17,21,25,2..., dimensions={0} | all-to-all | bytes 98304 | tf_op jit(solution)/shard_map/all_to_all | solution.py:178
  35.9 4.6 %collective-permute-start.31 = (f32[96,128]{1,0:T(8,128)S(1)}, f32[96,128]{1,0:T(8,128)S(1)}, u32[]{:S(2)}, u32[]{:S(2)}) collective-permute-start(f32[96,128]{1,0:T(8,128)S(1)} %bitcast.14), channel_id=1, source_target_pairs={{0,2},{1,3},{4,6},{5,7},{8,10},{9,11},{12,14},{13,15},{14,12},{15,... | collective-permute-start | bytes 147464 | tf_op jit(solution)/shard_map/ppermute | solution.py:166
  40.6 2.1 %collective-permute-done.31 = f32[96,128]{1,0:T(8,128)S(1)} collective-permute-done((f32[96,128]{1,0:T(8,128)S(1)}, f32[96,128]{1,0:T(8,128)S(1)}, u32[]{:S(2)}, u32[]{:S(2)}) %collective-permute-start.31) | collective-permute-done | bytes 49184 | tf_op jit(solution)/shard_map/ppermute | solution.py:166
  43.2 0.9 collective-permute-done.32.other_ref
  44.1 2.5 %collective-permute-start.14 = (bf16[384,896]{1,0:T(8,128)(2,1)S(1)}, bf16[384,896]{1,0:T(8,128)(2,1)S(1)}, u32[]{:S(2)}, u32[]{:S(2)}) collective-permute-start(bf16[384,896]{1,0:T(8,128)(2,1)S(1)} %get-tuple-element.33.refs_0_.low_ref), channel_id=1, source_target_pairs={{4,0},{5,1},{8,4},{9,5},{12,8},{13,9},{14,12},{15,13},{10,14},{11,... | collective-permute-start | bytes 2064392 | tf_op jit(solution)/shard_map/ppermute | solution.py:362
  46.6 12.3 %collective-permute-done.5.refs_2_ = bf16[384,896]{1,0:T(8,128)(2,1)S(1)} collective-permute-done((bf16[384,896]{1,0:T(8,128)(2,1)S(1)}, bf16[384,896]{1,0:T(8,128)(2,1)S(1)}, u32[]{:S(2)}, u32[]{:S(2)}) %collective-permute-start.5) | collective-permute-done | bytes 688160 | tf_op jit(solution)/shard_map/ppermute | solution.py:362
  58.9 2.5 %collective-permute-done.10.refs_0_ = bf16[384,896]{1,0:T(8,128)(2,1)S(1)} collective-permute-done((bf16[384,896]{1,0:T(8,128)(2,1)S(1)}, bf16[384,896]{1,0:T(8,128)(2,1)S(1)}, u32[]{:S(2)}, u32[]{:S(2)}) %collective-permute-start.10) | collective-permute-done | bytes 688160 | tf_op jit(solution)/shard_map/ppermute | solution.py:362
  61.4 8.8 %collective-permute-done.14.refs_2_ = bf16[384,896]{1,0:T(8,128)(2,1)S(1)} collective-permute-done((bf16[384,896]{1,0:T(8,128)(2,1)S(1)}, bf16[384,896]{1,0:T(8,128)(2,1)S(1)}, u32[]{:S(2)}, u32[]{:S(2)}) %collective-permute-start.14) | collective-permute-done | bytes 688160 | tf_op jit(solution)/shard_map/ppermute | solution.py:362
  70.2 1.1 collective-permute-start.1
  71.3 0.9 collective-permute-start.6
  72.3 1.2 collective-permute-start.11
  73.4 0.9 collective-permute-start.15
  74.4 14.4 %collective-permute-done.1.refs_0_ = bf16[384,896]{1,0:T(8,128)(2,1)S(1)} collective-permute-done((bf16[384,896]{1,0:T(8,128)(2,1)}, bf16[384,896]{1,0:T(8,128)(2,1)S(1)}, u32[]{:S(2)}, u32[]{:S(2)}) %collective-permute-start.1) | collective-permute-done | bytes 688160 | tf_op jit(solution)/shard_map/ppermute | solution.py:362
  88.8 0.9 collective-permute-done.6.refs_2_
  89.7 0.7 collective-permute-start.2
  90.4 13.1 %collective-permute-done.11.refs_0_ = bf16[384,896]{1,0:T(8,128)(2,1)S(1)} collective-permute-done((bf16[384,896]{1,0:T(8,128)(2,1)S(1)}, bf16[384,896]{1,0:T(8,128)(2,1)S(1)}, u32[]{:S(2)}, u32[]{:S(2)}) %collective-permute-start.11) | collective-permute-done | bytes 688160 | tf_op jit(solution)/shard_map/ppermute | solution.py:362
  104.0 1.6 collective-permute-start.7
  106.1 12.2 %collective-permute-done.2.refs_0_ = bf16[384,896]{1,0:T(8,128)(2,1)S(1)} collective-permute-done((bf16[384,896]{1,0:T(8,128)(2,1)S(1)}, bf16[384,896]{1,0:T(8,128)(2,1)S(1)}, u32[]{:S(2)}, u32[]{:S(2)}) %collective-permute-start.2) | collective-permute-done | bytes 688160 | tf_op jit(solution)/shard_map/ppermute | solution.py:362
  118.2 1.6 collective-permute-start.16
  120.4 1.9 %collective-permute-done.7.refs_2_ = bf16[384,896]{1,0:T(8,128)(2,1)S(1)} collective-permute-done((bf16[384,896]{1,0:T(8,128)(2,1)S(1)}, bf16[384,896]{1,0:T(8,128)(2,1)S(1)}, u32[]{:S(2)}, u32[]{:S(2)}) %collective-permute-start.7) | collective-permute-done | bytes 688160 | tf_op jit(solution)/shard_map/ppermute | solution.py:362
  122.3 1.1 collective-permute-start.3
  123.4 9.6 %collective-permute-done.12.refs_0_ = bf16[384,896]{1,0:T(8,128)(2,1)S(1)} collective-permute-done((bf16[384,896]{1,0:T(8,128)(2,1)S(1)}, bf16[384,896]{1,0:T(8,128)(2,1)S(1)}, u32[]{:S(2)}, u32[]{:S(2)}) %collective-permute-start.12) | collective-permute-done | bytes 688160 | tf_op jit(solution)/shard_map/ppermute | solution.py:362
  133.0 3.1 %collective-permute-done.16.refs_2_ = bf16[384,896]{1,0:T(8,128)(2,1)S(1)} collective-permute-done((bf16[384,896]{1,0:T(8,128)(2,1)S(1)}, bf16[384,896]{1,0:T(8,128)(2,1)S(1)}, u32[]{:S(2)}, u32[]{:S(2)}) %collective-permute-start.16) | collective-permute-done | bytes 688160 | tf_op jit(solution)/shard_map/ppermute | solution.py:362
  136.2 1.6 collective-permute-start.35
  137.8 0.7 dynamic-slice_bitcast_fusion.starts_ref
  138.5 1.9 %shard_map.81.refs_10_ = f32[384,512]{1,0:T(8,128)S(1)} custom-call(s32[1]{0:T(128)} %bitcast.2.f_ref.core_ref, f32[192,128]{1,0:T(8,128)S(1)} %pad_maximum_fusion.mine_ref, f32[192,128]{1,0:T(8,128)S(1)} %collective-permute-done.32.other_ref, s32[384,1]{1,0:T(8,128)S(1)} %broadcast_in_dim_reshape.5.l_ref, bf16[512,512]{1,0:T(8,128)(2,1)S(1)} %bitcast.12), custom_call_target="tpu_custom_call" | custom-call | flops 301989888 | bytes 1507328 | tf_op jit(solution)/shard_map/pallas_call | solution.py:292
  140.4 3.0 %collective-permute-done.3.refs_0_ = bf16[384,256]{1,0:T(8,128)(2,1)S(1)} collective-permute-done((bf16[384,256]{1,0:T(8,128)(2,1)S(1)}, bf16[384,256]{1,0:T(8,128)(2,1)S(1)}, u32[]{:S(2)}, u32[]{:S(2)}) %collective-permute-start.3) | collective-permute-done | bytes 196640 | tf_op jit(solution)/shard_map/ppermute | solution.py:362
  144.0 3.8 %shard_map.74.refs_5_ = f32[384,512]{1,0:T(8,128)S(1)} custom-call(s32[35]{0:T(128)S(1)} %dynamic-slice_bitcast_fusion.starts_ref, bf16[384,896]{1,0:T(8,128)(2,1)S(1)} %get-tuple-element.33.refs_0_.low_ref, bf16[384,896]{1,0:T(8,128)(2,1)S(1)} %get-tuple-element.34.refs_1_.high_ref, bf16[384,1792]{1,0:T(8,128)(2,1)S(1)} %collective-permute-done.28.refs_2_, ...), custom_call_target="tpu_custom_call" | custom-call | flops 1409286144 | bytes 7995392 | tf_op jit(solution)/shard_map/pallas_call | solution.py:242
  147.8 4.6 %shard_map.75.refs_5_ = f32[384,512]{1,0:T(8,128)S(1)} custom-call(s32[35]{0:T(128)S(1)} %dynamic-slice_bitcast_fusion.starts_ref, bf16[384,896]{1,0:T(8,128)(2,1)} %collective-permute-done.refs_0_, bf16[384,896]{1,0:T(8,128)(2,1)S(1)} %collective-permute-done.26.refs_1_, bf16[384,896]{1,0:T(8,128)(2,1)S(1)} %collective-permute-done.5.refs_2_, ...), custom_call_target="tpu_custom_call" | custom-call | flops 1409286144 | bytes 7995392 | tf_op jit(solution)/shard_map/pallas_call | solution.py:242
  152.4 4.0 %shard_map.76.refs_5_ = f32[384,512]{1,0:T(8,128)S(1)} custom-call(s32[35]{0:T(128)S(1)} %dynamic-slice_bitcast_fusion.starts_ref, bf16[384,896]{1,0:T(8,128)(2,1)S(1)} %collective-permute-done.10.refs_0_, bf16[384,896]{1,0:T(8,128)(2,1)S(1)} %collective-permute-done.24.refs_1_, bf16[384,896]{1,0:T(8,128)(2,1)S(1)} %collective-permute-done.14.refs_2_, ...), custom_call_target="tpu_custom_call" | custom-call | flops 1409286144 | bytes 7995392 | tf_op jit(solution)/shard_map/pallas_call | solution.py:242
  157.1 4.4 %shard_map.77 = (f32[384,512]{1,0:T(8,128)S(1)}, bf16[512,896]{1,0:T(8,128)(2,1)S(1)}, bf16[512,896]{1,0:T(8,128)(2,1)S(1)}, bf16[512,896]{1,0:T(8,128)(2,1)S(1)}, bf16[512,896]{1,0:T(8,128)(2,1)S(1)}) custom-call(s32[35]{0:T(128)S(1)} %dynamic-slice_bitcast_fusion.starts_ref, bf16[384,896]{1,0:T(8,128)(2,1)S(1)} %collective-permute-done.1.refs_0_, ...), custom_call_target="tpu_custom_call" | custom-call | flops 1409286144 | bytes 11665408 | tf_op jit(solution)/shard_map/pallas_call | solution.py:242
  161.4 1.8 %collective-permute-start.8 = (bf16[384,256]{1,0:T(8,128)(2,1)S(1)}, bf16[384,256]{1,0:T(8,128)(2,1)S(1)}, u32[]{:S(2)}, u32[]{:S(2)}) collective-permute-start(bf16[384,256]{1,0:T(8,128)(2,1)S(1)} %slice.38), channel_id=1, source_target_pairs={{4,0},{5,1},{8,4},{9,5},{12,8},{13,9},{14,12},{15,13},{10,14},{11,... | collective-permute-start | bytes 589832 | tf_op jit(solution)/shard_map/ppermute | solution.py:362
  163.3 4.1 %shard_map.78 = (f32[384,512]{1,0:T(8,128)S(1)}, bf16[512,896]{1,0:T(8,128)(2,1)S(1)}, bf16[512,896]{1,0:T(8,128)(2,1)S(1)}, bf16[512,896]{1,0:T(8,128)(2,1)S(1)}, bf16[512,896]{1,0:T(8,128)(2,1)S(1)}) custom-call(s32[35]{0:T(128)S(1)} %dynamic-slice_bitcast_fusion.starts_ref, bf16[384,896]{1,0:T(8,128)(2,1)S(1)} %collective-permute-done.11.refs_0_, ...), custom_call_target="tpu_custom_call" | custom-call | flops 1409286144 | bytes 11665408 | tf_op jit(solution)/shard_map/pallas_call | solution.py:242
  167.4 4.1 %shard_map.79 = (f32[384,512]{1,0:T(8,128)S(1)}, bf16[512,896]{1,0:T(8,128)(2,1)S(1)}, bf16[512,896]{1,0:T(8,128)(2,1)S(1)}, bf16[512,896]{1,0:T(8,128)(2,1)S(1)}, bf16[512,896]{1,0:T(8,128)(2,1)S(1)}) custom-call(s32[35]{0:T(128)S(1)} %dynamic-slice_bitcast_fusion.starts_ref, bf16[384,896]{1,0:T(8,128)(2,1)S(1)} %collective-permute-done.2.refs_0_, ...), custom_call_target="tpu_custom_call" | custom-call | flops 1409286144 | bytes 11665408 | tf_op jit(solution)/shard_map/pallas_call | solution.py:242
  172.1 4.1 %shard_map.82 = (f32[384,512]{1,0:T(8,128)S(1)}, bf16[512,640]{1,0:T(8,128)(2,1)S(1)}, bf16[512,640]{1,0:T(8,128)(2,1)S(1)}, bf16[512,640]{1,0:T(8,128)(2,1)S(1)...) custom-call(s32[35]{0:T(128)S(1)} %dynamic-slice_bitcast_fusion.star, ...), custom_call_target="tpu_custom_call" | custom-call | flops 1409286144 | bytes 11665408 | tf_op jit(solution)/shard_map/pallas_call | solution.py:242
  176.3 1.9 %shard_map.83.refs_5_ = f32[384,512]{1,0:T(8,128)S(1)} custom-call(s32[35]{0:T(128)S(1)} %dynamic-slice_bitcast_fusion.starts_ref, bf16[384,640]{1,0:T(8,128)(2,1)S(1)} %collective-permute-done.33.refs_0_, bf16[384,640]{1,0:T(8,128)(2,1)S(1)} %collective-permute-done.34.refs_1_, bf16[384,640]{1,0:T(8,128)(2,1)S(1)} %collective-permute-done.35.refs_2_, ...), custom_call_target="tpu_custom_call" | custom-call | flops 1006632960 | bytes 6160384 | tf_op jit(solution)/shard_map/pallas_call | solution.py:242
  178.3 0.9 shard_map.84.refs_5_
  179.2 1.7 shard_map.85
  (59 shorter events, 5.3 us)
Async XLA Ops:
  6.9 1.5 collective-permute-start.29
  8.4 130.1 %copy-start = (bf16[8,64,512]{2,1,0:T(8,128)(2,1)S(1)}, bf16[8,64,512]{2,1,0:T(8,128)(2,1)}, u32[]{:S(2)}) copy-start(bf16[8,64,512]{2,1,0:T(8,128)(2,1)} %param.10) | copy-start | bytes 1572868
  8.4 5.0 %collective-permute-start.30 = (f32[96,128]{1,0:T(8,128)S(1)}, f32[96,128]{1,0:T(8,128)S(1)}, u32[]{:S(2)}, u32[]{:S(2)}) collective-permute-start(f32[96,128]{1,0:T(8,128)S(1)} %slice_select_fusion), channel_id=1, source_target_pairs={{0,2},{1,3},{4,6},{5,7},{8,10},{9,11},{12,14},{13,15},{14,12},{15,... | collective-permute-start | bytes 147464 | tf_op jit(solution)/shard_map/ppermute | solution.py:161
  11.4 60.0 %collective-permute-start.28 = (bf16[384,1792]{1,0:T(8,128)(2,1)}, bf16[384,1792]{1,0:T(8,128)(2,1)S(1)}, u32[]{:S(2)}, u32[]{:S(2)}) collective-permute-start(bf16[384,1792]{1,0:T(8,128)(2,1)} %bitcast.1.x_ref), channel_id=1, source_target_pairs={{0,1},{1,0},{4,5},{5,4},{8,9},{9,8},{12,13},{13,12},{14,15},{15,14... | collective-permute-start | bytes 4128776 | tf_op jit(solution)/shard_map/ppermute | solution.py:353
  14.1 11.1 %all-to-all-start = ((f32[4,24,128]{2,1,0:T(8,128)}), f32[4,24,128]{2,1,0:T(8,128)S(1)}, u32[]{:S(2)}, u32[]{:S(2)}) async-start(f32[4,24,128]{2,1,0:T(8,128)} %bitcast.15), calls=%async_computation | async-start | bytes 98304 | tf_op jit(solution)/shard_map/all_to_all | solution.py:175
  19.4 27.2 %collective-permute-start = (bf16[384,896]{1,0:T(8,128)(2,1)S(1)}, bf16[384,896]{1,0:T(8,128)(2,1)}, u32[]{:S(2)}, u32[]{:S(2)}) collective-permute-start(bf16[384,896]{1,0:T(8,128)(2,1)S(1)} %get-tuple-element.33.refs_0_.low_ref), channel_id=1, source_target_pairs={{0,4},{1,5},{4,8},{5,9},{8,12},{9,13},{12,14},{13,15},{14,10},{15,... | collective-permute-start | bytes 2064392 | tf_op jit(solution)/shard_map/ppermute | solution.py:362
  35.9 6.8 %collective-permute-start.31 = (f32[96,128]{1,0:T(8,128)S(1)}, f32[96,128]{1,0:T(8,128)S(1)}, u32[]{:S(2)}, u32[]{:S(2)}) collective-permute-start(f32[96,128]{1,0:T(8,128)S(1)} %bitcast.14), channel_id=1, source_target_pairs={{0,2},{1,3},{4,6},{5,7},{8,10},{9,11},{12,14},{13,15},{14,12},{15,... | collective-permute-start | bytes 147464 | tf_op jit(solution)/shard_map/ppermute | solution.py:166
  40.6 18.3 %collective-permute-start.5 = (bf16[384,896]{1,0:T(8,128)(2,1)S(1)}, bf16[384,896]{1,0:T(8,128)(2,1)S(1)}, u32[]{:S(2)}, u32[]{:S(2)}) collective-permute-start(bf16[384,896]{1,0:T(8,128)(2,1)S(1)} %get-tuple-element.34.refs_1_.high_ref), channel_id=1, source_target_pairs={{4,0},{5,1},{8,4},{9,5},{12,8},{13,9},{14,12},{15,13},{10,14},{11,... | collective-permute-start | bytes 2064392 | tf_op jit(solution)/shard_map/ppermute | solution.py:362
  42.7 1.4 collective-permute-start.32
  42.8 18.6 %collective-permute-start.10 = (bf16[384,896]{1,0:T(8,128)(2,1)S(1)}, bf16[384,896]{1,0:T(8,128)(2,1)S(1)}, u32[]{:S(2)}, u32[]{:S(2)}) collective-permute-start(bf16[384,896]{1,0:T(8,128)(2,1)S(1)} %get-tuple-element.34.refs_1_.high_ref), channel_id=1, source_target_pairs={{0,4},{1,5},{4,8},{5,9},{8,12},{9,13},{12,14},{13,15},{14,10},{15,... | collective-permute-start | bytes 2064392 | tf_op jit(solution)/shard_map/ppermute | solution.py:362
  44.1 26.1 %collective-permute-start.14 = (bf16[384,896]{1,0:T(8,128)(2,1)S(1)}, bf16[384,896]{1,0:T(8,128)(2,1)S(1)}, u32[]{:S(2)}, u32[]{:S(2)}) collective-permute-start(bf16[384,896]{1,0:T(8,128)(2,1)S(1)} %get-tuple-element.33.refs_0_.low_ref), channel_id=1, source_target_pairs={{4,0},{5,1},{8,4},{9,5},{12,8},{13,9},{14,12},{15,13},{10,14},{11,... | collective-permute-start | bytes 2064392 | tf_op jit(solution)/shard_map/ppermute | solution.py:362
  46.6 25.7 %collective-permute-start.26 = (bf16[384,896]{1,0:T(8,128)(2,1)}, bf16[384,896]{1,0:T(8,128)(2,1)S(1)}, u32[]{:S(2)}, u32[]{:S(2)}) collective-permute-start(bf16[384,896]{1,0:T(8,128)(2,1)} %collective-permute-done.refs_0_), channel_id=1, source_target_pairs={{0,1},{1,0},{4,5},{5,4},{8,9},{9,8},{12,13},{13,12},{14,15},{15,14... | collective-permute-start | bytes 2064392 | tf_op jit(solution)/shard_map/ppermute | solution.py:365
  58.9 13.4 %collective-permute-start.27 = (bf16[384,896]{1,0:T(8,128)(2,1)S(1)}, bf16[384,896]{1,0:T(8,128)(2,1)S(1)}, u32[]{:S(2)}, u32[]{:S(2)}) collective-permute-start(bf16[384,896]{1,0:T(8,128)(2,1)S(1)} %collective-permute-done.5.refs_2_), channel_id=1, source_target_pairs={{0,1},{1,0},{4,5},{5,4},{8,9},{9,8},{12,13},{13,12},{14,15},{15,14... | collective-permute-start | bytes 2064392 | tf_op jit(solution)/shard_map/ppermute | solution.py:365
  61.4 12.0 %collective-permute-start.24 = (bf16[384,896]{1,0:T(8,128)(2,1)S(1)}, bf16[384,896]{1,0:T(8,128)(2,1)S(1)}, u32[]{:S(2)}, u32[]{:S(2)}) collective-permute-start(bf16[384,896]{1,0:T(8,128)(2,1)S(1)} %collective-permute-done.10.refs_0_), channel_id=1, source_target_pairs={{0,1},{1,0},{4,5},{5,4},{8,9},{9,8},{12,13},{13,12},{14,15},{15,14... | collective-permute-start | bytes 2064392 | tf_op jit(solution)/shard_map/ppermute | solution.py:365
  70.2 18.5 %collective-permute-start.1 = (bf16[384,896]{1,0:T(8,128)(2,1)}, bf16[384,896]{1,0:T(8,128)(2,1)S(1)}, u32[]{:S(2)}, u32[]{:S(2)}) collective-permute-start(bf16[384,896]{1,0:T(8,128)(2,1)} %collective-permute-done.refs_0_), channel_id=1, source_target_pairs={{0,4},{1,5},{4,8},{5,9},{8,12},{9,13},{12,14},{13,15},{14,10},{15,... | collective-permute-start | bytes 2064392 | tf_op jit(solution)/shard_map/ppermute | solution.py:362
  71.3 18.3 %collective-permute-start.6 = (bf16[384,896]{1,0:T(8,128)(2,1)S(1)}, bf16[384,896]{1,0:T(8,128)(2,1)S(1)}, u32[]{:S(2)}, u32[]{:S(2)}) collective-permute-start(bf16[384,896]{1,0:T(8,128)(2,1)S(1)} %collective-permute-done.5.refs_2_), channel_id=1, source_target_pairs={{4,0},{5,1},{8,4},{9,5},{12,8},{13,9},{14,12},{15,13},{10,14},{11,... | collective-permute-start | bytes 2064392 | tf_op jit(solution)/shard_map/ppermute | solution.py:362
  72.3 17.4 %collective-permute-start.25 = (bf16[384,896]{1,0:T(8,128)(2,1)S(1)}, bf16[384,896]{1,0:T(8,128)(2,1)S(1)}, u32[]{:S(2)}, u32[]{:S(2)}) collective-permute-start(bf16[384,896]{1,0:T(8,128)(2,1)S(1)} %collective-permute-done.14.refs_2_), channel_id=1, source_target_pairs={{0,1},{1,0},{4,5},{5,4},{8,9},{9,8},{12,13},{13,12},{14,15},{15,14... | collective-permute-start | bytes 2064392 | tf_op jit(solution)/shard_map/ppermute | solution.py:365
  72.3 31.2 %collective-permute-start.11 = (bf16[384,896]{1,0:T(8,128)(2,1)S(1)}, bf16[384,896]{1,0:T(8,128)(2,1)S(1)}, u32[]{:S(2)}, u32[]{:S(2)}) collective-permute-start(bf16[384,896]{1,0:T(8,128)(2,1)S(1)} %collective-permute-done.10.refs_0_), channel_id=1, source_target_pairs={{0,4},{1,5},{4,8},{5,9},{8,12},{9,13},{12,14},{13,15},{14,10},{15,... | collective-permute-start | bytes 2064392 | tf_op jit(solution)/shard_map/ppermute | solution.py:362
  73.4 30.1 %collective-permute-start.15 = (bf16[384,896]{1,0:T(8,128)(2,1)S(1)}, bf16[384,896]{1,0:T(8,128)(2,1)S(1)}, u32[]{:S(2)}, u32[]{:S(2)}) collective-permute-start(bf16[384,896]{1,0:T(8,128)(2,1)S(1)} %collective-permute-done.14.refs_2_), channel_id=1, source_target_pairs={{4,0},{5,1},{8,4},{9,5},{12,8},{13,9},{14,12},{15,13},{10,14},{11,... | collective-permute-start | bytes 2064392 | tf_op jit(solution)/shard_map/ppermute | solution.py:362
  88.8 15.3 %collective-permute-start.22 = (bf16[384,896]{1,0:T(8,128)(2,1)S(1)}, bf16[384,896]{1,0:T(8,128)(2,1)S(1)}, u32[]{:S(2)}, u32[]{:S(2)}) collective-permute-start(bf16[384,896]{1,0:T(8,128)(2,1)S(1)} %collective-permute-done.1.refs_0_), channel_id=1, source_target_pairs={{0,1},{1,0},{4,5},{5,4},{8,9},{9,8},{12,13},{13,12},{14,15},{15,14... | collective-permute-start | bytes 2064392 | tf_op jit(solution)/shard_map/ppermute | solution.py:365
  89.6 16.0 %collective-permute-start.23 = (bf16[384,896]{1,0:T(8,128)(2,1)S(1)}, bf16[384,896]{1,0:T(8,128)(2,1)S(1)}, u32[]{:S(2)}, u32[]{:S(2)}) collective-permute-start(bf16[384,896]{1,0:T(8,128)(2,1)S(1)} %collective-permute-done.6.refs_2_), channel_id=1, source_target_pairs={{0,1},{1,0},{4,5},{5,4},{8,9},{9,8},{12,13},{13,12},{14,15},{15,14... | collective-permute-start | bytes 2064392 | tf_op jit(solution)/shard_map/ppermute | solution.py:365
  89.7 28.6 %collective-permute-start.2 = (bf16[384,896]{1,0:T(8,128)(2,1)S(1)}, bf16[384,896]{1,0:T(8,128)(2,1)S(1)}, u32[]{:S(2)}, u32[]{:S(2)}) collective-permute-start(bf16[384,896]{1,0:T(8,128)(2,1)S(1)} %collective-permute-done.1.refs_0_), channel_id=1, source_target_pairs={{0,4},{1,5},{4,8},{5,9},{8,12},{9,13},{12,14},{13,15},{14,10},{15,... | collective-permute-start | bytes 2064392 | tf_op jit(solution)/shard_map/ppermute | solution.py:362
  103.5 16.4 %collective-permute-start.20 = (bf16[384,896]{1,0:T(8,128)(2,1)S(1)}, bf16[384,896]{1,0:T(8,128)(2,1)S(1)}, u32[]{:S(2)}, u32[]{:S(2)}) collective-permute-start(bf16[384,896]{1,0:T(8,128)(2,1)S(1)} %collective-permute-done.11.refs_0_), channel_id=1, source_target_pairs={{0,1},{1,0},{4,5},{5,4},{8,9},{9,8},{12,13},{13,12},{14,15},{15,14... | collective-permute-start | bytes 2064392 | tf_op jit(solution)/shard_map/ppermute | solution.py:365
  103.5 16.9 %collective-permute-start.21 = (bf16[384,896]{1,0:T(8,128)(2,1)S(1)}, bf16[384,896]{1,0:T(8,128)(2,1)S(1)}, u32[]{:S(2)}, u32[]{:S(2)}) collective-permute-start(bf16[384,896]{1,0:T(8,128)(2,1)S(1)} %collective-permute-done.15.refs_2_), channel_id=1, source_target_pairs={{0,1},{1,0},{4,5},{5,4},{8,9},{9,8},{12,13},{13,12},{14,15},{15,14... | collective-permute-start | bytes 2064392 | tf_op jit(solution)/shard_map/ppermute | solution.py:365
  104.0 18.3 %collective-permute-start.7 = (bf16[384,896]{1,0:T(8,128)(2,1)S(1)}, bf16[384,896]{1,0:T(8,128)(2,1)S(1)}, u32[]{:S(2)}, u32[]{:S(2)}) collective-permute-start(bf16[384,896]{1,0:T(8,128)(2,1)S(1)} %collective-permute-done.6.refs_2_), channel_id=1, source_target_pairs={{4,0},{5,1},{8,4},{9,5},{12,8},{13,9},{14,12},{15,13},{10,14},{11,... | collective-permute-start | bytes 2064392 | tf_op jit(solution)/shard_map/ppermute | solution.py:362
  105.6 27.4 %collective-permute-start.12 = (bf16[384,896]{1,0:T(8,128)(2,1)S(1)}, bf16[384,896]{1,0:T(8,128)(2,1)S(1)}, u32[]{:S(2)}, u32[]{:S(2)}) collective-permute-start(bf16[384,896]{1,0:T(8,128)(2,1)S(1)} %collective-permute-done.11.refs_0_), channel_id=1, source_target_pairs={{0,4},{1,5},{4,8},{5,9},{8,12},{9,13},{12,14},{13,15},{14,10},{15,... | collective-permute-start | bytes 2064392 | tf_op jit(solution)/shard_map/ppermute | solution.py:362
  118.2 17.9 %collective-permute-start.16 = (bf16[384,896]{1,0:T(8,128)(2,1)S(1)}, bf16[384,896]{1,0:T(8,128)(2,1)S(1)}, u32[]{:S(2)}, u32[]{:S(2)}) collective-permute-start(bf16[384,896]{1,0:T(8,128)(2,1)S(1)} %collective-permute-done.15.refs_2_), channel_id=1, source_target_pairs={{4,0},{5,1},{8,4},{9,5},{12,8},{13,9},{14,12},{15,13},{10,14},{11,... | collective-permute-start | bytes 2064392 | tf_op jit(solution)/shard_map/ppermute | solution.py:362
  119.9 23.5 %collective-permute-start.33 = (bf16[384,640]{1,0:T(8,128)(2,1)S(1)}, bf16[384,640]{1,0:T(8,128)(2,1)S(1)}, u32[]{:S(2)}, u32[]{:S(2)}) collective-permute-start(bf16[384,640]{1,0:T(8,128)(2,1)S(1)} %slice.41), channel_id=1, source_target_pairs={{0,4},{1,5},{4,8},{5,9},{8,12},{9,13},{12,14},{13,15},{14,10},{15,... | collective-permute-start | bytes 1474568 | tf_op jit(solution)/shard_map/ppermute | solution.py:362
  120.4 36.2 %collective-permute-start.18 = (bf16[384,896]{1,0:T(8,128)(2,1)S(1)}, bf16[384,896]{1,0:T(8,128)(2,1)S(1)}, u32[]{:S(2)}, u32[]{:S(2)}) collective-permute-start(bf16[384,896]{1,0:T(8,128)(2,1)S(1)} %collective-permute-done.2.refs_0_), channel_id=1, source_target_pairs={{0,1},{1,0},{4,5},{5,4},{8,9},{9,8},{12,13},{13,12},{14,15},{15,14... | collective-permute-start | bytes 2064392 | tf_op jit(solution)/shard_map/ppermute | solution.py:365
  122.3 21.1 %collective-permute-start.3 = (bf16[384,256]{1,0:T(8,128)(2,1)S(1)}, bf16[384,256]{1,0:T(8,128)(2,1)S(1)}, u32[]{:S(2)}, u32[]{:S(2)}) collective-permute-start(bf16[384,256]{1,0:T(8,128)(2,1)S(1)} %slice.37), channel_id=1, source_target_pairs={{0,4},{1,5},{4,8},{5,9},{8,12},{9,13},{12,14},{13,15},{14,10},{15,... | collective-permute-start | bytes 589832 | tf_op jit(solution)/shard_map/ppermute | solution.py:362
  133.0 28.4 %collective-permute-start.19 = (bf16[384,896]{1,0:T(8,128)(2,1)S(1)}, bf16[384,896]{1,0:T(8,128)(2,1)S(1)}, u32[]{:S(2)}, u32[]{:S(2)}) collective-permute-start(bf16[384,896]{1,0:T(8,128)(2,1)S(1)} %collective-permute-done.7.refs_2_), channel_id=1, source_target_pairs={{0,1},{1,0},{4,5},{5,4},{8,9},{9,8},{12,13},{13,12},{14,15},{15,14... | collective-permute-start | bytes 2064392 | tf_op jit(solution)/shard_map/ppermute | solution.py:365
  136.2 20.3 %collective-permute-start.35 = (bf16[384,640]{1,0:T(8,128)(2,1)S(1)}, bf16[384,640]{1,0:T(8,128)(2,1)S(1)}, u32[]{:S(2)}, u32[]{:S(2)}) collective-permute-start(bf16[384,640]{1,0:T(8,128)(2,1)S(1)} %slice.42), channel_id=1, source_target_pairs={{4,0},{5,1},{8,4},{9,5},{12,8},{13,9},{14,12},{15,13},{10,14},{11,... | collective-permute-start | bytes 1474568 | tf_op jit(solution)/shard_map/ppermute | solution.py:362
  143.4 28.2 %collective-permute-start.13 = (bf16[384,896]{1,0:T(8,128)(2,1)S(1)}, bf16[384,896]{1,0:T(8,128)(2,1)S(1)}, u32[]{:S(2)}, u32[]{:S(2)}) collective-permute-start(bf16[384,896]{1,0:T(8,128)(2,1)S(1)} %collective-permute-done.12.refs_0_), channel_id=1, source_target_pairs={{0,1},{1,0},{4,5},{5,4},{8,9},{9,8},{12,13},{13,12},{14,15},{15,14... | collective-permute-start | bytes 2064392 | tf_op jit(solution)/shard_map/ppermute | solution.py:365
  143.5 28.7 %collective-permute-start.17 = (bf16[384,896]{1,0:T(8,128)(2,1)S(1)}, bf16[384,896]{1,0:T(8,128)(2,1)S(1)}, u32[]{:S(2)}, u32[]{:S(2)}) collective-permute-start(bf16[384,896]{1,0:T(8,128)(2,1)S(1)} %collective-permute-done.16.refs_2_), channel_id=1, source_target_pairs={{0,1},{1,0},{4,5},{5,4},{8,9},{9,8},{12,13},{13,12},{14,15},{15,14... | collective-permute-start | bytes 2064392 | tf_op jit(solution)/shard_map/ppermute | solution.py:365
  156.5 19.8 %collective-permute-start.34 = (bf16[384,640]{1,0:T(8,128)(2,1)S(1)}, bf16[384,640]{1,0:T(8,128)(2,1)S(1)}, u32[]{:S(2)}, u32[]{:S(2)}) collective-permute-start(bf16[384,640]{1,0:T(8,128)(2,1)S(1)} %collective-permute-done.33.refs_0_), channel_id=1, source_target_pairs={{0,1},{1,0},{4,5},{5,4},{8,9},{9,8},{12,13},{13,12},{14,15},{15,14... | collective-permute-start | bytes 1474568 | tf_op jit(solution)/shard_map/ppermute | solution.py:365
  156.6 19.7 %collective-permute-start.36 = (bf16[384,640]{1,0:T(8,128)(2,1)S(1)}, bf16[384,640]{1,0:T(8,128)(2,1)S(1)}, u32[]{:S(2)}, u32[]{:S(2)}) collective-permute-start(bf16[384,640]{1,0:T(8,128)(2,1)S(1)} %collective-permute-done.35.refs_2_), channel_id=1, source_target_pairs={{0,1},{1,0},{4,5},{5,4},{8,9},{9,8},{12,13},{13,12},{14,15},{15,14... | collective-permute-start | bytes 1474568 | tf_op jit(solution)/shard_map/ppermute | solution.py:365
  161.4 10.1 %collective-permute-start.8 = (bf16[384,256]{1,0:T(8,128)(2,1)S(1)}, bf16[384,256]{1,0:T(8,128)(2,1)S(1)}, u32[]{:S(2)}, u32[]{:S(2)}) collective-permute-start(bf16[384,256]{1,0:T(8,128)(2,1)S(1)} %slice.38), channel_id=1, source_target_pairs={{4,0},{5,1},{8,4},{9,5},{12,8},{13,9},{14,12},{15,13},{10,14},{11,... | collective-permute-start | bytes 589832 | tf_op jit(solution)/shard_map/ppermute | solution.py:362
  171.5 7.7 %collective-permute-start.4 = (bf16[384,256]{1,0:T(8,128)(2,1)S(1)}, bf16[384,256]{1,0:T(8,128)(2,1)S(1)}, u32[]{:S(2)}, u32[]{:S(2)}) collective-permute-start(bf16[384,256]{1,0:T(8,128)(2,1)S(1)} %collective-permute-done.3.refs_0_), channel_id=1, source_target_pairs={{0,1},{1,0},{4,5},{5,4},{8,9},{9,8},{12,13},{13,12},{14,15},{15,14... | collective-permute-start | bytes 589832 | tf_op jit(solution)/shard_map/ppermute | solution.py:365
  171.6 7.6 %collective-permute-start.9 = (bf16[384,256]{1,0:T(8,128)(2,1)S(1)}, bf16[384,256]{1,0:T(8,128)(2,1)S(1)}, u32[]{:S(2)}, u32[]{:S(2)}) collective-permute-start(bf16[384,256]{1,0:T(8,128)(2,1)S(1)} %collective-permute-done.8.refs_1_), channel_id=1, source_target_pairs={{0,1},{1,0},{4,5},{5,4},{8,9},{9,8},{12,13},{13,12},{14,15},{15,14... | collective-permute-start | bytes 589832 | tf_op jit(solution)/shard_map/ppermute | solution.py:365

commit v6 on v5

--- a/solution.py
+++ b/solution.py
@@ -308,7 +308,10 @@
     axis_size = mesh.shape["row"]
     ring, snake = chip_ring(mesh)
     chips, cores = len(ring), len(ring[0])
-    forward = [(ring[p][c], ring[(p + 1) % chips][c]) for p in range(chips) for c in range(cores)]
+    turn_of = [1, -1]
+    forward = [
+        (ring[p][c], ring[(p + turn_of[c % 2]) % chips][c]) for p in range(chips) for c in range(cores)
+    ]
     backward = [(b, a) for a, b in forward]
     partner = [(members[c], members[1 - c]) for members in ring for c in range(cores)] if cores == 2 else []
 
@@ -373,7 +376,8 @@
         for p, members in enumerate(ring):
             for c, at in enumerate(members):
                 for k, (offset, beside, part, column) in enumerate(order):
-                    source = ring[(p + offset) % chips][1 - c if beside else c]
+                    its = 1 - c if beside else c
+                    source = ring[(p + offset * turn_of[its]) % chips][its]
                     table[at, k] = (source * device_units + part * half + column) // LANES
         starts = jnp.asarray(table)[me]
         acc, ready, done = [], [], 0

time: 181 us -> 168 us (0.928)
  waiting for transfers between devices: 91 us -> 84.7 us
  starting transfers between devices: 34.1 us -> 30.1 us
  blocking collectives: 10.8 us -> 8.06 us
    ppermute x16, waiting for transfers between devices: 81.9 us -> 75 us  [ringed(): data = lax.ppermute(send, 'row', pairs)]
    ppermute x1, starting transfers between devices: 4.63 us -> 1.58 us  [join(): got = lax.ppermute(part, 'row', pairs)]
    all_to_all x1, blocking collectives: 10.8 us -> 8.06 us  [sum_by_stages(): lax.all_to_all(spread, 'row', 0, 0, axis_index_groups=lines, tiled=True)]
  transfers between devices with their start and end apart: 38 -> 38, of which waited for: 16 -> 15; matrix products, arithmetic and copies ran while one was open for 1% -> 1% of each run, Pallas kernels for 19% -> 20%
where the time goes in v6:
time: 168 us
  waiting for transfers between devices  84.7 us (50%)
  Pallas kernels  40.4 us (24%)
  starting transfers between devices  30.1 us (18%)
  blocking collectives  8.06 us (5%)
  local copies, waits for them, and re-layouts  2.98 us (2%)
    ppermute x16, waiting for transfers between devices, ringed(): data = lax.ppermute(send, 'row', pairs)  75 us
    pallas_call x10, Pallas kernels, chunk_matmul(): pl.pallas_call(body, out_shape=[jax.ShapeDtypeStruct((rows, features), ou...  33.8 us
    ppermute x16, starting transfers between devices, ringed(): data = lax.ppermute(send, 'row', pairs)  17.4 us
    all_to_all x1, blocking collectives, sum_by_stages(): lax.all_to_all(spread, 'row', 0, 0, axis_index_groups=lines, tiled=True)  8.06 us
    all_to_all x1, starting transfers between devices, sum_by_stages(): lax.all_to_all(rows, 'row', 0, 0, axis_index_groups=lines, tiled=True)  5.37 us
    all_to_all x1, waiting for transfers between devices, sum_by_stages(): lax.all_to_all(rows, 'row', 0, 0, axis_index_groups=lines, tiled=True)  3.81 us
    pallas_call x1, Pallas kernels, project_selected(): pl.pallas_call(body, out_shape=(shape, shape), in_specs=[pl.BlockSpec(mem...  3.39 us
  transfers between devices with their start and end apart: 38, of which 15 were waited for; matrix products, arithmetic and copies ran while one was open for 1% of the time, Pallas kernels for 20%

profile of v6, /device:TPU:0, one launch (start us, length us, event | category | flops | bytes accessed | tf_op | source)
XLA Modules:
  0.0 167.9 jit_solution(17863770261424069870)
XLA Ops:
  0.0 0.7 constant_dynamic-slice_fusion
  0.7 0.6 fusion
  1.3 1.3 shard_map.73
  2.6 0.9 broadcast_in_dim_reshape.5.l_ref
  3.5 3.4 %shard_map.80 = (f32[192,128]{1,0:T(8,128)S(1)}, f32[192,128]{1,0:T(8,128)S(1)}) custom-call(s32[1]{0:T(128)} %bitcast.2.f_ref.core_ref, bf16[384,896]{1,0:T(8,128)(2,1)S(1)} %get-tuple-element.33.refs_0_.low_ref, bf16[384,896]{1,0:T(8,128)(2,1)S(1)} %get-tuple-element.34.refs_1_.high_ref, s32[384,1]{1,0:T(8,128)S(1)} %broadcast_in_dim_reshape.5.l_ref, ...), custom_call_target="tpu_custom_call" | custom-call | flops 704643072 | bytes 3407872 | tf_op jit(solution)/shard_map/pallas_call | solution.py:94
  6.9 0.6 collective-permute-start.29
  8.4 2.9 %collective-permute-start.30 = (f32[96,128]{1,0:T(8,128)S(1)}, f32[96,128]{1,0:T(8,128)S(1)}, u32[]{:S(2)}, u32[]{:S(2)}) collective-permute-start(f32[96,128]{1,0:T(8,128)S(1)} %slice_select_fusion), channel_id=1, source_target_pairs={{0,2},{1,3},{4,6},{5,7},{8,10},{9,11},{12,14},{13,15},{14,12},{15,... | collective-permute-start | bytes 147464 | tf_op jit(solution)/shard_map/ppermute | solution.py:161
  11.4 2.1 %collective-permute-done.30 = f32[96,128]{1,0:T(8,128)S(1)} collective-permute-done((f32[96,128]{1,0:T(8,128)S(1)}, f32[96,128]{1,0:T(8,128)S(1)}, u32[]{:S(2)}, u32[]{:S(2)}) %collective-permute-start.30) | collective-permute-done | bytes 49184 | tf_op jit(solution)/shard_map/ppermute | solution.py:161
  13.4 0.6 select_add_fusion
  14.1 5.4 %all-to-all-start = ((f32[4,24,128]{2,1,0:T(8,128)}), f32[4,24,128]{2,1,0:T(8,128)S(1)}, u32[]{:S(2)}, u32[]{:S(2)}) async-start(f32[4,24,128]{2,1,0:T(8,128)} %bitcast.15), calls=%async_computation | async-start | bytes 98304 | tf_op jit(solution)/shard_map/all_to_all | solution.py:175
  19.4 2.0 %collective-permute-start = (bf16[384,896]{1,0:T(8,128)(2,1)S(1)}, bf16[384,896]{1,0:T(8,128)(2,1)}, u32[]{:S(2)}, u32[]{:S(2)}) collective-permute-start(bf16[384,896]{1,0:T(8,128)(2,1)S(1)} %get-tuple-element.33.refs_0_.low_ref), channel_id=1, source_target_pairs={{0,4},{1,3},{4,8},{5,1},{8,12},{9,5},{12,14},{13,9},{14,10},{15,13... | collective-permute-start | bytes 2064392 | tf_op jit(solution)/shard_map/ppermute | solution.py:365
  21.5 3.8 %all-to-all-done = f32[4,24,128]{2,1,0:T(8,128)S(1)} async-done(((f32[4,24,128]{2,1,0:T(8,128)}), f32[4,24,128]{2,1,0:T(8,128)S(1)}, u32[]{:S(2)}, u32[]{:S(2)}) %all-to-all-start) | async-done | bytes 49184 | tf_op jit(solution)/shard_map/all_to_all | solution.py:175
  25.3 8.1 %all_to_all.18 = f32[4,24,128]{2,1,0:T(8,128)S(1)} all-to-all(f32[4,24,128]{2,1,0:T(8,128)S(1)} %broadcast_in_dim.2), channel_id=1, replica_groups={{0,4,8,12},{1,5,9,13},{14,10,6,2},{15,11,7,3},{16,20,24,28},{17,21,25,2..., dimensions={0} | all-to-all | bytes 98304 | tf_op jit(solution)/shard_map/all_to_all | solution.py:178
  33.3 1.6 collective-permute-start.31
  35.4 2.6 %collective-permute-done.31 = f32[96,128]{1,0:T(8,128)S(1)} collective-permute-done((f32[96,128]{1,0:T(8,128)S(1)}, f32[96,128]{1,0:T(8,128)S(1)}, u32[]{:S(2)}, u32[]{:S(2)}) %collective-permute-start.31) | collective-permute-done | bytes 49184 | tf_op jit(solution)/shard_map/ppermute | solution.py:166
  38.4 0.9 collective-permute-done.32.other_ref
  39.4 1.1 collective-permute-start.14
  40.4 10.1 %collective-permute-done.5.refs_2_ = bf16[384,896]{1,0:T(8,128)(2,1)S(1)} collective-permute-done((bf16[384,896]{1,0:T(8,128)(2,1)S(1)}, bf16[384,896]{1,0:T(8,128)(2,1)S(1)}, u32[]{:S(2)}, u32[]{:S(2)}) %collective-permute-start.5) | collective-permute-done | bytes 688160 | tf_op jit(solution)/shard_map/ppermute | solution.py:365
  50.6 5.9 %collective-permute-done.10.refs_0_ = bf16[384,896]{1,0:T(8,128)(2,1)S(1)} collective-permute-done((bf16[384,896]{1,0:T(8,128)(2,1)S(1)}, bf16[384,896]{1,0:T(8,128)(2,1)S(1)}, u32[]{:S(2)}, u32[]{:S(2)}) %collective-permute-start.10) | collective-permute-done | bytes 688160 | tf_op jit(solution)/shard_map/ppermute | solution.py:365
  56.4 5.0 %collective-permute-done.14.refs_2_ = bf16[384,896]{1,0:T(8,128)(2,1)S(1)} collective-permute-done((bf16[384,896]{1,0:T(8,128)(2,1)S(1)}, bf16[384,896]{1,0:T(8,128)(2,1)S(1)}, u32[]{:S(2)}, u32[]{:S(2)}) %collective-permute-start.14) | collective-permute-done | bytes 688160 | tf_op jit(solution)/shard_map/ppermute | solution.py:365
  61.5 2.0 %collective-permute-start.6 = (bf16[384,896]{1,0:T(8,128)(2,1)S(1)}, bf16[384,896]{1,0:T(8,128)(2,1)S(1)}, u32[]{:S(2)}, u32[]{:S(2)}) collective-permute-start(bf16[384,896]{1,0:T(8,128)(2,1)S(1)} %collective-permute-done.5.refs_2_), channel_id=1, source_target_pairs={{4,0},{3,1},{8,4},{1,5},{12,8},{5,9},{14,12},{9,13},{10,14},{13,15... | collective-permute-start | bytes 2064392 | tf_op jit(solution)/shard_map/ppermute | solution.py:365
  63.6 2.0 %collective-permute-start.15 = (bf16[384,896]{1,0:T(8,128)(2,1)S(1)}, bf16[384,896]{1,0:T(8,128)(2,1)S(1)}, u32[]{:S(2)}, u32[]{:S(2)}) collective-permute-start(bf16[384,896]{1,0:T(8,128)(2,1)S(1)} %collective-permute-done.14.refs_2_), channel_id=1, source_target_pairs={{4,0},{3,1},{8,4},{1,5},{12,8},{5,9},{14,12},{9,13},{10,14},{13,15... | collective-permute-start | bytes 2064392 | tf_op jit(solution)/shard_map/ppermute | solution.py:365
  65.6 14.4 %collective-permute-done.1.refs_0_ = bf16[384,896]{1,0:T(8,128)(2,1)S(1)} collective-permute-done((bf16[384,896]{1,0:T(8,128)(2,1)}, bf16[384,896]{1,0:T(8,128)(2,1)S(1)}, u32[]{:S(2)}, u32[]{:S(2)}) %collective-permute-start.1) | collective-permute-done | bytes 688160 | tf_op jit(solution)/shard_map/ppermute | solution.py:365
  80.0 0.5 collective-permute-start.23
  80.5 0.8 collective-permute-start.2
  81.3 8.1 %collective-permute-done.11.refs_0_ = bf16[384,896]{1,0:T(8,128)(2,1)S(1)} collective-permute-done((bf16[384,896]{1,0:T(8,128)(2,1)S(1)}, bf16[384,896]{1,0:T(8,128)(2,1)S(1)}, u32[]{:S(2)}, u32[]{:S(2)}) %collective-permute-start.11) | collective-permute-done | bytes 688160 | tf_op jit(solution)/shard_map/ppermute | solution.py:365
  89.4 5.1 %collective-permute-done.15.refs_2_ = bf16[384,896]{1,0:T(8,128)(2,1)S(1)} collective-permute-done((bf16[384,896]{1,0:T(8,128)(2,1)S(1)}, bf16[384,896]{1,0:T(8,128)(2,1)S(1)}, u32[]{:S(2)}, u32[]{:S(2)}) %collective-permute-start.15) | collective-permute-done | bytes 688160 | tf_op jit(solution)/shard_map/ppermute | solution.py:365
  94.5 1.8 %collective-permute-start.7 = (bf16[384,896]{1,0:T(8,128)(2,1)S(1)}, bf16[384,896]{1,0:T(8,128)(2,1)S(1)}, u32[]{:S(2)}, u32[]{:S(2)}) collective-permute-start(bf16[384,896]{1,0:T(8,128)(2,1)S(1)} %collective-permute-done.6.refs_2_), channel_id=1, source_target_pairs={{4,0},{3,1},{8,4},{1,5},{12,8},{5,9},{14,12},{9,13},{10,14},{13,15... | collective-permute-start | bytes 2064392 | tf_op jit(solution)/shard_map/ppermute | solution.py:365
  96.8 1.6 collective-permute-start.16
  98.9 13.2 %collective-permute-done.7.refs_2_ = bf16[384,896]{1,0:T(8,128)(2,1)S(1)} collective-permute-done((bf16[384,896]{1,0:T(8,128)(2,1)S(1)}, bf16[384,896]{1,0:T(8,128)(2,1)S(1)}, u32[]{:S(2)}, u32[]{:S(2)}) %collective-permute-start.7) | collective-permute-done | bytes 688160 | tf_op jit(solution)/shard_map/ppermute | solution.py:365
  112.2 1.7 %collective-permute-start.3 = (bf16[384,256]{1,0:T(8,128)(2,1)S(1)}, bf16[384,256]{1,0:T(8,128)(2,1)S(1)}, u32[]{:S(2)}, u32[]{:S(2)}) collective-permute-start(bf16[384,256]{1,0:T(8,128)(2,1)S(1)} %slice.37), channel_id=1, source_target_pairs={{0,4},{1,3},{4,8},{5,1},{8,12},{9,5},{12,14},{13,9},{14,10},{15,13... | collective-permute-start | bytes 589832 | tf_op jit(solution)/shard_map/ppermute | solution.py:365
  113.9 0.8 collective-permute-done.12.refs_0_
  114.7 12.1 %collective-permute-done.16.refs_2_ = bf16[384,896]{1,0:T(8,128)(2,1)S(1)} collective-permute-done((bf16[384,896]{1,0:T(8,128)(2,1)S(1)}, bf16[384,896]{1,0:T(8,128)(2,1)S(1)}, u32[]{:S(2)}, u32[]{:S(2)}) %collective-permute-start.16) | collective-permute-done | bytes 688160 | tf_op jit(solution)/shard_map/ppermute | solution.py:365
  126.8 2.2 %collective-permute-start.35 = (bf16[384,640]{1,0:T(8,128)(2,1)S(1)}, bf16[384,640]{1,0:T(8,128)(2,1)S(1)}, u32[]{:S(2)}, u32[]{:S(2)}) collective-permute-start(bf16[384,640]{1,0:T(8,128)(2,1)S(1)} %slice.42), channel_id=1, source_target_pairs={{4,0},{3,1},{8,4},{1,5},{12,8},{5,9},{14,12},{9,13},{10,14},{13,15... | collective-permute-start | bytes 1474568 | tf_op jit(solution)/shard_map/ppermute | solution.py:365
  129.0 0.7 dynamic-slice_bitcast_fusion.starts_ref
  129.7 1.9 %shard_map.81.refs_10_ = f32[384,512]{1,0:T(8,128)S(1)} custom-call(s32[1]{0:T(128)} %bitcast.2.f_ref.core_ref, f32[192,128]{1,0:T(8,128)S(1)} %pad_maximum_fusion.mine_ref, f32[192,128]{1,0:T(8,128)S(1)} %collective-permute-done.32.other_ref, s32[384,1]{1,0:T(8,128)S(1)} %broadcast_in_dim_reshape.5.l_ref, bf16[512,512]{1,0:T(8,128)(2,1)S(1)} %bitcast.12), custom_call_target="tpu_custom_call" | custom-call | flops 301989888 | bytes 1507328 | tf_op jit(solution)/shard_map/pallas_call | solution.py:292
  131.7 0.5 collective-permute-start.17
  132.2 3.8 %shard_map.74.refs_5_ = f32[384,512]{1,0:T(8,128)S(1)} custom-call(s32[35]{0:T(128)S(1)} %dynamic-slice_bitcast_fusion.starts_ref, bf16[384,896]{1,0:T(8,128)(2,1)S(1)} %get-tuple-element.33.refs_0_.low_ref, bf16[384,896]{1,0:T(8,128)(2,1)S(1)} %get-tuple-element.34.refs_1_.high_ref, bf16[384,1792]{1,0:T(8,128)(2,1)S(1)} %collective-permute-done.28.refs_2_, ...), custom_call_target="tpu_custom_call" | custom-call | flops 1409286144 | bytes 7995392 | tf_op jit(solution)/shard_map/pallas_call | solution.py:242
  136.1 4.6 %shard_map.75.refs_5_ = f32[384,512]{1,0:T(8,128)S(1)} custom-call(s32[35]{0:T(128)S(1)} %dynamic-slice_bitcast_fusion.starts_ref, bf16[384,896]{1,0:T(8,128)(2,1)} %collective-permute-done.refs_0_, bf16[384,896]{1,0:T(8,128)(2,1)S(1)} %collective-permute-done.26.refs_1_, bf16[384,896]{1,0:T(8,128)(2,1)S(1)} %collective-permute-done.5.refs_2_, ...), custom_call_target="tpu_custom_call" | custom-call | flops 1409286144 | bytes 7995392 | tf_op jit(solution)/shard_map/pallas_call | solution.py:242
  140.7 4.0 %shard_map.76.refs_5_ = f32[384,512]{1,0:T(8,128)S(1)} custom-call(s32[35]{0:T(128)S(1)} %dynamic-slice_bitcast_fusion.starts_ref, bf16[384,896]{1,0:T(8,128)(2,1)S(1)} %collective-permute-done.10.refs_0_, bf16[384,896]{1,0:T(8,128)(2,1)S(1)} %collective-permute-done.24.refs_1_, bf16[384,896]{1,0:T(8,128)(2,1)S(1)} %collective-permute-done.14.refs_2_, ...), custom_call_target="tpu_custom_call" | custom-call | flops 1409286144 | bytes 7995392 | tf_op jit(solution)/shard_map/pallas_call | solution.py:242
  145.3 4.4 %shard_map.77 = (f32[384,512]{1,0:T(8,128)S(1)}, bf16[512,896]{1,0:T(8,128)(2,1)S(1)}, bf16[512,896]{1,0:T(8,128)(2,1)S(1)}, bf16[512,896]{1,0:T(8,128)(2,1)S(1)}, bf16[512,896]{1,0:T(8,128)(2,1)S(1)}) custom-call(s32[35]{0:T(128)S(1)} %dynamic-slice_bitcast_fusion.starts_ref, bf16[384,896]{1,0:T(8,128)(2,1)S(1)} %collective-permute-done.1.refs_0_, ...), custom_call_target="tpu_custom_call" | custom-call | flops 1409286144 | bytes 11665408 | tf_op jit(solution)/shard_map/pallas_call | solution.py:242
  149.7 0.6 collective-permute-start.8
  150.3 4.1 %shard_map.78 = (f32[384,512]{1,0:T(8,128)S(1)}, bf16[512,896]{1,0:T(8,128)(2,1)S(1)}, bf16[512,896]{1,0:T(8,128)(2,1)S(1)}, bf16[512,896]{1,0:T(8,128)(2,1)S(1)}, bf16[512,896]{1,0:T(8,128)(2,1)S(1)}) custom-call(s32[35]{0:T(128)S(1)} %dynamic-slice_bitcast_fusion.starts_ref, bf16[384,896]{1,0:T(8,128)(2,1)S(1)} %collective-permute-done.11.refs_0_, ...), custom_call_target="tpu_custom_call" | custom-call | flops 1409286144 | bytes 11665408 | tf_op jit(solution)/shard_map/pallas_call | solution.py:242
  154.4 4.1 %shard_map.79 = (f32[384,512]{1,0:T(8,128)S(1)}, bf16[512,896]{1,0:T(8,128)(2,1)S(1)}, bf16[512,896]{1,0:T(8,128)(2,1)S(1)}, bf16[512,896]{1,0:T(8,128)(2,1)S(1)}, bf16[512,896]{1,0:T(8,128)(2,1)S(1)}) custom-call(s32[35]{0:T(128)S(1)} %dynamic-slice_bitcast_fusion.starts_ref, bf16[384,896]{1,0:T(8,128)(2,1)S(1)} %collective-permute-done.2.refs_0_, ...), custom_call_target="tpu_custom_call" | custom-call | flops 1409286144 | bytes 11665408 | tf_op jit(solution)/shard_map/pallas_call | solution.py:242
  159.1 4.1 %shard_map.82 = (f32[384,512]{1,0:T(8,128)S(1)}, bf16[512,640]{1,0:T(8,128)(2,1)S(1)}, bf16[512,640]{1,0:T(8,128)(2,1)S(1)}, bf16[512,640]{1,0:T(8,128)(2,1)S(1)...) custom-call(s32[35]{0:T(128)S(1)} %dynamic-slice_bitcast_fusion.star, ...), custom_call_target="tpu_custom_call" | custom-call | flops 1409286144 | bytes 11665408 | tf_op jit(solution)/shard_map/pallas_call | solution.py:242
  163.3 2.0 %shard_map.83.refs_5_ = f32[384,512]{1,0:T(8,128)S(1)} custom-call(s32[35]{0:T(128)S(1)} %dynamic-slice_bitcast_fusion.starts_ref, bf16[384,640]{1,0:T(8,128)(2,1)S(1)} %collective-permute-done.33.refs_0_, bf16[384,640]{1,0:T(8,128)(2,1)S(1)} %collective-permute-done.34.refs_1_, bf16[384,640]{1,0:T(8,128)(2,1)S(1)} %collective-permute-done.35.refs_2_, ...), custom_call_target="tpu_custom_call" | custom-call | flops 1006632960 | bytes 6160384 | tf_op jit(solution)/shard_map/pallas_call | solution.py:242
  165.2 0.9 shard_map.84.refs_5_
  166.2 1.7 %shard_map.85 = bf16[384,512]{1,0:T(8,128)(2,1)} custom-call(s32[35]{0:T(128)S(1)} %dynamic-slice_bitcast_fusion.starts_ref, bf16[384,256]{1,0:T(8,128)(2,1)S(1)} %collective-permute-done.4.refs_0_, bf16[384,256]{1,0:T(8,128)(2,1)S(1)} %collective-permute-done.9.refs_1_, bf16[512,28672]{1,0:T(8,128)(2,1)} %refs_2_.3, ...), custom_call_target="tpu_custom_call" | custom-call | flops 201326592 | bytes 2490368 | tf_op jit(solution)/shard_map/pallas_call | solution.py:242
  (59 shorter events, 3.6 us)
Async XLA Ops:
  6.9 1.5 collective-permute-start.29
  8.4 121.3 %copy-start = (bf16[8,64,512]{2,1,0:T(8,128)(2,1)S(1)}, bf16[8,64,512]{2,1,0:T(8,128)(2,1)}, u32[]{:S(2)}) copy-start(bf16[8,64,512]{2,1,0:T(8,128)(2,1)} %param.10) | copy-start | bytes 1572868
  8.4 5.0 %collective-permute-start.30 = (f32[96,128]{1,0:T(8,128)S(1)}, f32[96,128]{1,0:T(8,128)S(1)}, u32[]{:S(2)}, u32[]{:S(2)}) collective-permute-start(f32[96,128]{1,0:T(8,128)S(1)} %slice_select_fusion), channel_id=1, source_target_pairs={{0,2},{1,3},{4,6},{5,7},{8,10},{9,11},{12,14},{13,15},{14,12},{15,... | collective-permute-start | bytes 147464 | tf_op jit(solution)/shard_map/ppermute | solution.py:161
  11.4 50.1 %collective-permute-start.28 = (bf16[384,1792]{1,0:T(8,128)(2,1)}, bf16[384,1792]{1,0:T(8,128)(2,1)S(1)}, u32[]{:S(2)}, u32[]{:S(2)}) collective-permute-start(bf16[384,1792]{1,0:T(8,128)(2,1)} %bitcast.1.x_ref), channel_id=1, source_target_pairs={{0,1},{1,0},{4,5},{5,4},{8,9},{9,8},{12,13},{13,12},{14,15},{15,14... | collective-permute-start | bytes 4128776 | tf_op jit(solution)/shard_map/ppermute | solution.py:356
  14.1 11.2 %all-to-all-start = ((f32[4,24,128]{2,1,0:T(8,128)}), f32[4,24,128]{2,1,0:T(8,128)S(1)}, u32[]{:S(2)}, u32[]{:S(2)}) async-start(f32[4,24,128]{2,1,0:T(8,128)} %bitcast.15), calls=%async_computation | async-start | bytes 98304 | tf_op jit(solution)/shard_map/all_to_all | solution.py:175
  19.4 21.0 %collective-permute-start = (bf16[384,896]{1,0:T(8,128)(2,1)S(1)}, bf16[384,896]{1,0:T(8,128)(2,1)}, u32[]{:S(2)}, u32[]{:S(2)}) collective-permute-start(bf16[384,896]{1,0:T(8,128)(2,1)S(1)} %get-tuple-element.33.refs_0_.low_ref), channel_id=1, source_target_pairs={{0,4},{1,3},{4,8},{5,1},{8,12},{9,5},{12,14},{13,9},{14,10},{15,13... | collective-permute-start | bytes 2064392 | tf_op jit(solution)/shard_map/ppermute | solution.py:365
  33.3 4.6 %collective-permute-start.31 = (f32[96,128]{1,0:T(8,128)S(1)}, f32[96,128]{1,0:T(8,128)S(1)}, u32[]{:S(2)}, u32[]{:S(2)}) collective-permute-start(f32[96,128]{1,0:T(8,128)S(1)} %bitcast.14), channel_id=1, source_target_pairs={{0,2},{1,3},{4,6},{5,7},{8,10},{9,11},{12,14},{13,15},{14,12},{15,... | collective-permute-start | bytes 147464 | tf_op jit(solution)/shard_map/ppermute | solution.py:166
  34.9 15.6 %collective-permute-start.5 = (bf16[384,896]{1,0:T(8,128)(2,1)S(1)}, bf16[384,896]{1,0:T(8,128)(2,1)S(1)}, u32[]{:S(2)}, u32[]{:S(2)}) collective-permute-start(bf16[384,896]{1,0:T(8,128)(2,1)S(1)} %get-tuple-element.34.refs_1_.high_ref), channel_id=1, source_target_pairs={{4,0},{3,1},{8,4},{1,5},{12,8},{5,9},{14,12},{9,13},{10,14},{13,15... | collective-permute-start | bytes 2064392 | tf_op jit(solution)/shard_map/ppermute | solution.py:365
  38.0 1.4 collective-permute-start.32
  38.1 18.4 %collective-permute-start.10 = (bf16[384,896]{1,0:T(8,128)(2,1)S(1)}, bf16[384,896]{1,0:T(8,128)(2,1)S(1)}, u32[]{:S(2)}, u32[]{:S(2)}) collective-permute-start(bf16[384,896]{1,0:T(8,128)(2,1)S(1)} %get-tuple-element.34.refs_1_.high_ref), channel_id=1, source_target_pairs={{0,4},{1,3},{4,8},{5,1},{8,12},{9,5},{12,14},{13,9},{14,10},{15,13... | collective-permute-start | bytes 2064392 | tf_op jit(solution)/shard_map/ppermute | solution.py:365
  39.4 22.1 %collective-permute-start.14 = (bf16[384,896]{1,0:T(8,128)(2,1)S(1)}, bf16[384,896]{1,0:T(8,128)(2,1)S(1)}, u32[]{:S(2)}, u32[]{:S(2)}) collective-permute-start(bf16[384,896]{1,0:T(8,128)(2,1)S(1)} %get-tuple-element.33.refs_0_.low_ref), channel_id=1, source_target_pairs={{4,0},{3,1},{8,4},{1,5},{12,8},{5,9},{14,12},{9,13},{10,14},{13,15... | collective-permute-start | bytes 2064392 | tf_op jit(solution)/shard_map/ppermute | solution.py:365
  40.4 23.1 %collective-permute-start.26 = (bf16[384,896]{1,0:T(8,128)(2,1)}, bf16[384,896]{1,0:T(8,128)(2,1)S(1)}, u32[]{:S(2)}, u32[]{:S(2)}) collective-permute-start(bf16[384,896]{1,0:T(8,128)(2,1)} %collective-permute-done.refs_0_), channel_id=1, source_target_pairs={{0,1},{1,0},{4,5},{5,4},{8,9},{9,8},{12,13},{13,12},{14,15},{15,14... | collective-permute-start | bytes 2064392 | tf_op jit(solution)/shard_map/ppermute | solution.py:368
  50.5 12.9 %collective-permute-start.27 = (bf16[384,896]{1,0:T(8,128)(2,1)S(1)}, bf16[384,896]{1,0:T(8,128)(2,1)S(1)}, u32[]{:S(2)}, u32[]{:S(2)}) collective-permute-start(bf16[384,896]{1,0:T(8,128)(2,1)S(1)} %collective-permute-done.5.refs_2_), channel_id=1, source_target_pairs={{0,1},{1,0},{4,5},{5,4},{8,9},{9,8},{12,13},{13,12},{14,15},{15,14... | collective-permute-start | bytes 2064392 | tf_op jit(solution)/shard_map/ppermute | solution.py:368
  56.4 7.1 %collective-permute-start.24 = (bf16[384,896]{1,0:T(8,128)(2,1)S(1)}, bf16[384,896]{1,0:T(8,128)(2,1)S(1)}, u32[]{:S(2)}, u32[]{:S(2)}) collective-permute-start(bf16[384,896]{1,0:T(8,128)(2,1)S(1)} %collective-permute-done.10.refs_0_), channel_id=1, source_target_pairs={{0,1},{1,0},{4,5},{5,4},{8,9},{9,8},{12,13},{13,12},{14,15},{15,14... | collective-permute-start | bytes 2064392 | tf_op jit(solution)/shard_map/ppermute | solution.py:368
  61.5 18.5 %collective-permute-start.1 = (bf16[384,896]{1,0:T(8,128)(2,1)}, bf16[384,896]{1,0:T(8,128)(2,1)S(1)}, u32[]{:S(2)}, u32[]{:S(2)}) collective-permute-start(bf16[384,896]{1,0:T(8,128)(2,1)} %collective-permute-done.refs_0_), channel_id=1, source_target_pairs={{0,4},{1,3},{4,8},{5,1},{8,12},{9,5},{12,14},{13,9},{14,10},{15,13... | collective-permute-start | bytes 2064392 | tf_op jit(solution)/shard_map/ppermute | solution.py:365
  61.5 18.5 %collective-permute-start.6 = (bf16[384,896]{1,0:T(8,128)(2,1)S(1)}, bf16[384,896]{1,0:T(8,128)(2,1)S(1)}, u32[]{:S(2)}, u32[]{:S(2)}) collective-permute-start(bf16[384,896]{1,0:T(8,128)(2,1)S(1)} %collective-permute-done.5.refs_2_), channel_id=1, source_target_pairs={{4,0},{3,1},{8,4},{1,5},{12,8},{5,9},{14,12},{9,13},{10,14},{13,15... | collective-permute-start | bytes 2064392 | tf_op jit(solution)/shard_map/ppermute | solution.py:365
  63.5 17.0 %collective-permute-start.25 = (bf16[384,896]{1,0:T(8,128)(2,1)S(1)}, bf16[384,896]{1,0:T(8,128)(2,1)S(1)}, u32[]{:S(2)}, u32[]{:S(2)}) collective-permute-start(bf16[384,896]{1,0:T(8,128)(2,1)S(1)} %collective-permute-done.14.refs_2_), channel_id=1, source_target_pairs={{0,1},{1,0},{4,5},{5,4},{8,9},{9,8},{12,13},{13,12},{14,15},{15,14... | collective-permute-start | bytes 2064392 | tf_op jit(solution)/shard_map/ppermute | solution.py:368
  63.5 25.9 %collective-permute-start.11 = (bf16[384,896]{1,0:T(8,128)(2,1)S(1)}, bf16[384,896]{1,0:T(8,128)(2,1)S(1)}, u32[]{:S(2)}, u32[]{:S(2)}) collective-permute-start(bf16[384,896]{1,0:T(8,128)(2,1)S(1)} %collective-permute-done.10.refs_0_), channel_id=1, source_target_pairs={{0,4},{1,3},{4,8},{5,1},{8,12},{9,5},{12,14},{13,9},{14,10},{15,13... | collective-permute-start | bytes 2064392 | tf_op jit(solution)/shard_map/ppermute | solution.py:365
  63.6 30.9 %collective-permute-start.15 = (bf16[384,896]{1,0:T(8,128)(2,1)S(1)}, bf16[384,896]{1,0:T(8,128)(2,1)S(1)}, u32[]{:S(2)}, u32[]{:S(2)}) collective-permute-start(bf16[384,896]{1,0:T(8,128)(2,1)S(1)} %collective-permute-done.14.refs_2_), channel_id=1, source_target_pairs={{4,0},{3,1},{8,4},{1,5},{12,8},{5,9},{14,12},{9,13},{10,14},{13,15... | collective-permute-start | bytes 2064392 | tf_op jit(solution)/shard_map/ppermute | solution.py:365
  80.0 14.6 %collective-permute-start.22 = (bf16[384,896]{1,0:T(8,128)(2,1)S(1)}, bf16[384,896]{1,0:T(8,128)(2,1)S(1)}, u32[]{:S(2)}, u32[]{:S(2)}) collective-permute-start(bf16[384,896]{1,0:T(8,128)(2,1)S(1)} %collective-permute-done.1.refs_0_), channel_id=1, source_target_pairs={{0,1},{1,0},{4,5},{5,4},{8,9},{9,8},{12,13},{13,12},{14,15},{15,14... | collective-permute-start | bytes 2064392 | tf_op jit(solution)/shard_map/ppermute | solution.py:368
  80.0 16.4 %collective-permute-start.23 = (bf16[384,896]{1,0:T(8,128)(2,1)S(1)}, bf16[384,896]{1,0:T(8,128)(2,1)S(1)}, u32[]{:S(2)}, u32[]{:S(2)}) collective-permute-start(bf16[384,896]{1,0:T(8,128)(2,1)S(1)} %collective-permute-done.6.refs_2_), channel_id=1, source_target_pairs={{0,1},{1,0},{4,5},{5,4},{8,9},{9,8},{12,13},{13,12},{14,15},{15,14... | collective-permute-start | bytes 2064392 | tf_op jit(solution)/shard_map/ppermute | solution.py:368
  80.5 16.3 %collective-permute-start.2 = (bf16[384,896]{1,0:T(8,128)(2,1)S(1)}, bf16[384,896]{1,0:T(8,128)(2,1)S(1)}, u32[]{:S(2)}, u32[]{:S(2)}) collective-permute-start(bf16[384,896]{1,0:T(8,128)(2,1)S(1)} %collective-permute-done.1.refs_0_), channel_id=1, source_target_pairs={{0,4},{1,3},{4,8},{5,1},{8,12},{9,5},{12,14},{13,9},{14,10},{15,13... | collective-permute-start | bytes 2064392 | tf_op jit(solution)/shard_map/ppermute | solution.py:365
  89.4 9.0 %collective-permute-start.20 = (bf16[384,896]{1,0:T(8,128)(2,1)S(1)}, bf16[384,896]{1,0:T(8,128)(2,1)S(1)}, u32[]{:S(2)}, u32[]{:S(2)}) collective-permute-start(bf16[384,896]{1,0:T(8,128)(2,1)S(1)} %collective-permute-done.11.refs_0_), channel_id=1, source_target_pairs={{0,1},{1,0},{4,5},{5,4},{8,9},{9,8},{12,13},{13,12},{14,15},{15,14... | collective-permute-start | bytes 2064392 | tf_op jit(solution)/shard_map/ppermute | solution.py:368
  94.5 4.4 %collective-permute-start.21 = (bf16[384,896]{1,0:T(8,128)(2,1)S(1)}, bf16[384,896]{1,0:T(8,128)(2,1)S(1)}, u32[]{:S(2)}, u32[]{:S(2)}) collective-permute-start(bf16[384,896]{1,0:T(8,128)(2,1)S(1)} %collective-permute-done.15.refs_2_), channel_id=1, source_target_pairs={{0,1},{1,0},{4,5},{5,4},{8,9},{9,8},{12,13},{13,12},{14,15},{15,14... | collective-permute-start | bytes 2064392 | tf_op jit(solution)/shard_map/ppermute | solution.py:368
  94.5 17.6 %collective-permute-start.7 = (bf16[384,896]{1,0:T(8,128)(2,1)S(1)}, bf16[384,896]{1,0:T(8,128)(2,1)S(1)}, u32[]{:S(2)}, u32[]{:S(2)}) collective-permute-start(bf16[384,896]{1,0:T(8,128)(2,1)S(1)} %collective-permute-done.6.refs_2_), channel_id=1, source_target_pairs={{4,0},{3,1},{8,4},{1,5},{12,8},{5,9},{14,12},{9,13},{10,14},{13,15... | collective-permute-start | bytes 2064392 | tf_op jit(solution)/shard_map/ppermute | solution.py:365
  96.3 18.3 %collective-permute-start.12 = (bf16[384,896]{1,0:T(8,128)(2,1)S(1)}, bf16[384,896]{1,0:T(8,128)(2,1)S(1)}, u32[]{:S(2)}, u32[]{:S(2)}) collective-permute-start(bf16[384,896]{1,0:T(8,128)(2,1)S(1)} %collective-permute-done.11.refs_0_), channel_id=1, source_target_pairs={{0,4},{1,3},{4,8},{5,1},{8,12},{9,5},{12,14},{13,9},{14,10},{15,13... | collective-permute-start | bytes 2064392 | tf_op jit(solution)/shard_map/ppermute | solution.py:365
  96.8 30.0 %collective-permute-start.16 = (bf16[384,896]{1,0:T(8,128)(2,1)S(1)}, bf16[384,896]{1,0:T(8,128)(2,1)S(1)}, u32[]{:S(2)}, u32[]{:S(2)}) collective-permute-start(bf16[384,896]{1,0:T(8,128)(2,1)S(1)} %collective-permute-done.15.refs_2_), channel_id=1, source_target_pairs={{4,0},{3,1},{8,4},{1,5},{12,8},{5,9},{14,12},{9,13},{10,14},{13,15... | collective-permute-start | bytes 2064392 | tf_op jit(solution)/shard_map/ppermute | solution.py:365
  98.4 33.3 %collective-permute-start.33 = (bf16[384,640]{1,0:T(8,128)(2,1)S(1)}, bf16[384,640]{1,0:T(8,128)(2,1)S(1)}, u32[]{:S(2)}, u32[]{:S(2)}) collective-permute-start(bf16[384,640]{1,0:T(8,128)(2,1)S(1)} %slice.41), channel_id=1, source_target_pairs={{0,4},{1,3},{4,8},{5,1},{8,12},{9,5},{12,14},{13,9},{14,10},{15,13... | collective-permute-start | bytes 1474568 | tf_op jit(solution)/shard_map/ppermute | solution.py:365
  98.9 46.0 %collective-permute-start.18 = (bf16[384,896]{1,0:T(8,128)(2,1)S(1)}, bf16[384,896]{1,0:T(8,128)(2,1)S(1)}, u32[]{:S(2)}, u32[]{:S(2)}) collective-permute-start(bf16[384,896]{1,0:T(8,128)(2,1)S(1)} %collective-permute-done.2.refs_0_), channel_id=1, source_target_pairs={{0,1},{1,0},{4,5},{5,4},{8,9},{9,8},{12,13},{13,12},{14,15},{15,14... | collective-permute-start | bytes 2064392 | tf_op jit(solution)/shard_map/ppermute | solution.py:368
  112.2 19.5 %collective-permute-start.3 = (bf16[384,256]{1,0:T(8,128)(2,1)S(1)}, bf16[384,256]{1,0:T(8,128)(2,1)S(1)}, u32[]{:S(2)}, u32[]{:S(2)}) collective-permute-start(bf16[384,256]{1,0:T(8,128)(2,1)S(1)} %slice.37), channel_id=1, source_target_pairs={{0,4},{1,3},{4,8},{5,1},{8,12},{9,5},{12,14},{13,9},{14,10},{15,13... | collective-permute-start | bytes 589832 | tf_op jit(solution)/shard_map/ppermute | solution.py:365
  114.7 35.0 %collective-permute-start.19 = (bf16[384,896]{1,0:T(8,128)(2,1)S(1)}, bf16[384,896]{1,0:T(8,128)(2,1)S(1)}, u32[]{:S(2)}, u32[]{:S(2)}) collective-permute-start(bf16[384,896]{1,0:T(8,128)(2,1)S(1)} %collective-permute-done.7.refs_2_), channel_id=1, source_target_pairs={{0,1},{1,0},{4,5},{5,4},{8,9},{9,8},{12,13},{13,12},{14,15},{15,14... | collective-permute-start | bytes 2064392 | tf_op jit(solution)/shard_map/ppermute | solution.py:368
  126.8 17.9 %collective-permute-start.35 = (bf16[384,640]{1,0:T(8,128)(2,1)S(1)}, bf16[384,640]{1,0:T(8,128)(2,1)S(1)}, u32[]{:S(2)}, u32[]{:S(2)}) collective-permute-start(bf16[384,640]{1,0:T(8,128)(2,1)S(1)} %slice.42), channel_id=1, source_target_pairs={{4,0},{3,1},{8,4},{1,5},{12,8},{5,9},{14,12},{9,13},{10,14},{13,15... | collective-permute-start | bytes 1474568 | tf_op jit(solution)/shard_map/ppermute | solution.py:365
  131.7 27.0 %collective-permute-start.13 = (bf16[384,896]{1,0:T(8,128)(2,1)S(1)}, bf16[384,896]{1,0:T(8,128)(2,1)S(1)}, u32[]{:S(2)}, u32[]{:S(2)}) collective-permute-start(bf16[384,896]{1,0:T(8,128)(2,1)S(1)} %collective-permute-done.12.refs_0_), channel_id=1, source_target_pairs={{0,1},{1,0},{4,5},{5,4},{8,9},{9,8},{12,13},{13,12},{14,15},{15,14... | collective-permute-start | bytes 2064392 | tf_op jit(solution)/shard_map/ppermute | solution.py:368
  131.7 27.4 %collective-permute-start.17 = (bf16[384,896]{1,0:T(8,128)(2,1)S(1)}, bf16[384,896]{1,0:T(8,128)(2,1)S(1)}, u32[]{:S(2)}, u32[]{:S(2)}) collective-permute-start(bf16[384,896]{1,0:T(8,128)(2,1)S(1)} %collective-permute-done.16.refs_2_), channel_id=1, source_target_pairs={{0,1},{1,0},{4,5},{5,4},{8,9},{9,8},{12,13},{13,12},{14,15},{15,14... | collective-permute-start | bytes 2064392 | tf_op jit(solution)/shard_map/ppermute | solution.py:368
  144.7 18.5 %collective-permute-start.34 = (bf16[384,640]{1,0:T(8,128)(2,1)S(1)}, bf16[384,640]{1,0:T(8,128)(2,1)S(1)}, u32[]{:S(2)}, u32[]{:S(2)}) collective-permute-start(bf16[384,640]{1,0:T(8,128)(2,1)S(1)} %collective-permute-done.33.refs_0_), channel_id=1, source_target_pairs={{0,1},{1,0},{4,5},{5,4},{8,9},{9,8},{12,13},{13,12},{14,15},{15,14... | collective-permute-start | bytes 1474568 | tf_op jit(solution)/shard_map/ppermute | solution.py:368
  144.9 18.4 %collective-permute-start.36 = (bf16[384,640]{1,0:T(8,128)(2,1)S(1)}, bf16[384,640]{1,0:T(8,128)(2,1)S(1)}, u32[]{:S(2)}, u32[]{:S(2)}) collective-permute-start(bf16[384,640]{1,0:T(8,128)(2,1)S(1)} %collective-permute-done.35.refs_2_), channel_id=1, source_target_pairs={{0,1},{1,0},{4,5},{5,4},{8,9},{9,8},{12,13},{13,12},{14,15},{15,14... | collective-permute-start | bytes 1474568 | tf_op jit(solution)/shard_map/ppermute | solution.py:368
  149.7 8.8 %collective-permute-start.8 = (bf16[384,256]{1,0:T(8,128)(2,1)S(1)}, bf16[384,256]{1,0:T(8,128)(2,1)S(1)}, u32[]{:S(2)}, u32[]{:S(2)}) collective-permute-start(bf16[384,256]{1,0:T(8,128)(2,1)S(1)} %slice.38), channel_id=1, source_target_pairs={{4,0},{3,1},{8,4},{1,5},{12,8},{5,9},{14,12},{9,13},{10,14},{13,15... | collective-permute-start | bytes 589832 | tf_op jit(solution)/shard_map/ppermute | solution.py:365
  158.5 7.7 %collective-permute-start.4 = (bf16[384,256]{1,0:T(8,128)(2,1)S(1)}, bf16[384,256]{1,0:T(8,128)(2,1)S(1)}, u32[]{:S(2)}, u32[]{:S(2)}) collective-permute-start(bf16[384,256]{1,0:T(8,128)(2,1)S(1)} %collective-permute-done.3.refs_0_), channel_id=1, source_target_pairs={{0,1},{1,0},{4,5},{5,4},{8,9},{9,8},{12,13},{13,12},{14,15},{15,14... | collective-permute-start | bytes 589832 | tf_op jit(solution)/shard_map/ppermute | solution.py:368
  158.6 7.6 %collective-permute-start.9 = (bf16[384,256]{1,0:T(8,128)(2,1)S(1)}, bf16[384,256]{1,0:T(8,128)(2,1)S(1)}, u32[]{:S(2)}, u32[]{:S(2)}) collective-permute-start(bf16[384,256]{1,0:T(8,128)(2,1)S(1)} %collective-permute-done.8.refs_1_), channel_id=1, source_target_pairs={{0,1},{1,0},{4,5},{5,4},{8,9},{9,8},{12,13},{13,12},{14,15},{15,14... | collective-permute-start | bytes 589832 | tf_op jit(solution)/shard_map/ppermute | solution.py:368

commit v7 on v6

--- a/solution.py
+++ b/solution.py
@@ -259,6 +259,49 @@
     return out[0], out[1:]
 
 
+def row_cuts(total):
+    unit = total // 24
+    return [(0, 14 * unit), (14 * unit, 10 * unit)]
+
+
+def rows_matmul(chunks, blocks, acc, row, out, final):
+    count = len(chunks)
+    rows = chunks[0].shape[0]
+    features = blocks[0].shape[0]
+    total = acc.shape[0] if out is None else out.shape[0]
+
+    def body(*refs):
+        x_refs, w_refs, a_ref, refs = refs[:count], refs[count : 2 * count], refs[2 * count], refs[2 * count + 1 :]
+        value = a_ref[...] if a_ref.shape[0] == rows else a_ref[row : row + rows, :]
+        for x_ref, w_ref in zip(x_refs, w_refs):
+            value = value + lax.dot_general(
+                x_ref[...], w_ref[...], (((1,), (1,)), ((), ())), preferred_element_type=jnp.float32
+            )
+        if final:
+            o_ref, s_ref, sem = refs[-3:]
+            s_ref[...] = value.astype(jnp.bfloat16)
+            copy = pltpu.make_async_copy(s_ref, o_ref.at[pl.ds(row, rows)], sem)
+            copy.start()
+            copy.wait()
+        else:
+            refs[0][...] = value
+
+    anywhere = pl.BlockSpec(memory_space=pltpu.HBM)
+    vmem = pl.BlockSpec(memory_space=pltpu.VMEM)
+    shape = jax.ShapeDtypeStruct((total, features), jnp.bfloat16)
+    if not final:
+        shape = jax.ShapeDtypeStruct((rows, features), jnp.float32)
+    return pl.pallas_call(
+        body,
+        out_shape=shape,
+        in_specs=[vmem] * (2 * count + 1) + ([] if out is None else [anywhere]),
+        out_specs=anywhere if final else vmem,
+        scratch_shapes=[pltpu.VMEM((rows, features), jnp.bfloat16), pltpu.SemaphoreType.DMA] if final else [],
+        input_output_aliases={} if out is None else {2 * count + 1: 0},
+        compiler_params=pltpu.CompilerParams(vmem_limit_bytes=16 << 20),
+    )(*chunks, *blocks, acc, *([] if out is None else [out]))
+
+
 def adapter_kernel(mine, other, core, labels, outputs):
     count, rank, width = outputs.shape
     part, cols = mine.shape
@@ -342,8 +385,8 @@
     def ringed(flat, weight, factors, outputs, labels):
         device_units = flat.shape[1]
         half = device_units // 2
-        tiles = half // LANES
-        cut = (tiles - tiles * 2 // 7) * LANES
+        total = flat.shape[0]
+        cuts = row_cuts(total)
         me = lax.axis_index("row")
         core, side = [jnp.asarray(place)[me][k] for k in range(2)]
         own = cut_block(flat, half)
@@ -351,59 +394,61 @@
         halves = sum_by_stages(mine, other, side, partner, across, lines)
         extra = adapter_kernel(*halves, core, labels, outputs)
 
-        plan = [(s // 2 + 1, s % 2, 0, half) for s in range(2 * long - 2)]
-        plan += [(long, 0, 0, cut), (long, 0, cut, half - cut)]
+        plan = [(s // 2 + 1, s % 2, 0, total) for s in range(2 * long - 2)]
+        plan += [(long, 0, row, rows) for row, rows in cuts]
         beside = lax.ppermute(flat, "row", partner)
-        batches = [[(own[part], 0, False, part, 0) for part in range(2)] + [(beside, 0, True, 0, 0)]]
+        batches = [[(own[part], 0, False, part) for part in range(2)] + [(beside, 0, True, 0)]]
         held = {"up": list(own), "down": list(own)}
-        for distance, turn, column, width in plan:
+        for distance, turn, row, rows in plan:
             found = []
             for way, pairs, part in (("up", forward, turn), ("down", backward, 1 - turn)):
                 send = held[way][part]
-                if width < half:
-                    send = send[:, column : column + width]
+                if rows < total:
+                    send = send[row : row + rows]
                 data = lax.ppermute(send, "row", pairs)
-                if width == half:
+                if rows == total:
                     held[way][part] = data
                 beside = lax.ppermute(data, "row", partner)
                 offset = -distance if way == "up" else distance
-                found.append((data, offset, False, part, column))
-                found.append((beside, offset, True, part, column))
+                found.append((data, offset, False, part))
+                found.append((beside, offset, True, part))
             batches.append(found)
-        batches[-1:] = [batches[-1][::2], batches[-1][1::2]]
         order = [entry[1:] for found in batches for entry in found]
         table = np.zeros((axis_size, len(order)), np.int32)
         for p, members in enumerate(ring):
             for c, at in enumerate(members):
-                for k, (offset, beside, part, column) in enumerate(order):
+                for k, (offset, beside, part) in enumerate(order):
                     its = 1 - c if beside else c
                     source = ring[(p + offset * turn_of[its]) % chips][its]
-                    table[at, k] = (source * device_units + part * half + column) // LANES
+                    table[at, k] = (source * device_units + part * half) // LANES
         starts = jnp.asarray(table)[me]
         acc, ready, done = [], [], 0
-        ends = len(batches) - 2
-        settled = min(3, ends - 2)
-        for k, found in enumerate(batches):
-            last = k == len(batches) - 1
-            coming = []
-            if settled <= k <= ends - 2:
-                coming = batches[k + 1] if k < ends - 2 else sum(batches[k + 1 :], [])
+        ends = len(batches) - len(cuts)
+        settled = min(3, ends - 1)
+        for k, found in enumerate(batches[:ends]):
+            coming = batches[k + 1] if k >= settled else []
             at = done + len(found)
-            ahead = [(at + j, entry[0].shape[1]) for j, entry in enumerate(coming)]
-            out, fetched = chunk_matmul(
+            ahead = [(at + j, half) for j, _ in enumerate(coming)]
+            out, ready_next = chunk_matmul(
                 [entry[0] for entry in found],
                 starts,
                 done,
                 weight,
-                acc + ([extra] if k == ends - 2 else []),
-                jnp.bfloat16 if last else jnp.float32,
-                ready[: len(found)],
+                acc + ([extra] if k == ends - 1 else []),
+                jnp.float32,
+                ready,
                 ahead,
             )
-            ready = ready[len(found) :] + list(fetched)
-            acc = [out]
-            done += len(found)
-        return acc[0]
+            acc, ready, done = [out], list(ready_next), at
+        out = None
+        for k, ((row, _), found) in enumerate(zip(cuts, batches[ends:])):
+            chunks = [entry[0] for entry in found]
+            rest = acc[0]
+            if k == len(cuts) - 1:
+                rest = rows_matmul(chunks[::2], ready[::2], rest, row, None, False)
+                chunks, ready = chunks[1::2], ready[1::2]
+            out = rows_matmul(chunks, ready, rest, row, out, True)
+        return out
 
     def local(
         gated_hidden_rows,
@@ -414,7 +459,7 @@
     ):
         steps, requests, device_units = gated_hidden_rows.shape
         total = steps * requests
-        fits = device_units % (2 * LANES) == 0 and total % (32 * max(long, 1)) == 0
+        fits = device_units % (2 * LANES) == 0 and total % 384 == 0 and total % (32 * max(long, 1)) == 0
         run = ringed if snake and cores == 2 and long > 1 and fits else plain
         out = run(
             gated_hidden_rows.reshape(total, device_units),
@@ -433,6 +478,4 @@
         P(None, "groups"),
     )
 
-    return jax.shard_map(
-        local, mesh=mesh, in_specs=placed, out_specs=P(None, "groups", "row"), check_vma=False
-    )
+    return jax.shard_map(local, mesh=mesh, in_specs=placed, out_specs=P(None, "groups", "row"), check_vma=False)

time: 168 us -> 176 us (1.048)
  waiting for transfers between devices: 84.7 us -> 94 us
  starting transfers between devices: 30.1 us -> 26.2 us
  blocking collectives: 8.06 us -> 10.9 us
    ppermute x1, waiting for transfers between devices: 2.59 us -> 11.8 us  [join(): got = lax.ppermute(part, 'row', pairs)]
    pallas_call x10 -> x7, Pallas kernels: 33.8 us -> 29.2 us  [chunk_matmul(): pl.pallas_call(body, out_shape=[jax.ShapeDtypeStruct((rows, features), ou...]
    pallas_call x0 -> x3, Pallas kernels: none -> 4.21 us  [rows_matmul(): pl.pallas_call(body, out_shape=shape, in_specs=[vmem] * (2 * count + 1) +...]
    all_to_all x1, blocking collectives: 8.06 us -> 10.9 us  [sum_by_stages(): lax.all_to_all(rows, 'row', 0, 0, axis_index_groups=lines, tiled=True)]
    all_to_all x1, starting transfers between devices: 5.37 us -> 3.27 us  [sum_by_stages(): lax.all_to_all(spread, 'row', 0, 0, axis_index_groups=lines, tiled=True)]
  transfers between devices with their start and end apart: 38 -> 38, of which waited for: 15 -> 14; matrix products, arithmetic and copies ran while one was open for 1% -> 1% of each run, Pallas kernels for 20% -> 19%
where the time goes in v7:
time: 176 us
  waiting for transfers between devices  94 us (53%)
  Pallas kernels  40 us (23%)
  starting transfers between devices  26.2 us (15%)
  blocking collectives  10.9 us (6%)
  local copies, waits for them, and re-layouts  3.6 us (2%)
    ppermute x16, waiting for transfers between devices, ringed(): data = lax.ppermute(send, 'row', pairs)  74.7 us
    pallas_call x7, Pallas kernels, chunk_matmul(): pl.pallas_call(body, out_shape=[jax.ShapeDtypeStruct((rows, features), ou...  29.2 us
    ppermute x16, starting transfers between devices, ringed(): data = lax.ppermute(send, 'row', pairs)  16.6 us
    ppermute x1, waiting for transfers between devices, join(): got = lax.ppermute(part, 'row', pairs)  11.8 us
    all_to_all x1, blocking collectives, sum_by_stages(): lax.all_to_all(rows, 'row', 0, 0, axis_index_groups=lines, tiled=True)  10.9 us
    pallas_call x3, Pallas kernels, rows_matmul(): pl.pallas_call(body, out_shape=shape, in_specs=[vmem] * (2 * count + 1) +...  4.21 us
    all_to_all x1, waiting for transfers between devices, sum_by_stages(): lax.all_to_all(spread, 'row', 0, 0, axis_index_groups=lines, tiled=True)  3.82 us
  transfers between devices with their start and end apart: 38, of which 14 were waited for; matrix products, arithmetic and copies ran while one was open for 1% of the time, Pallas kernels for 19%

profile of v7, /device:TPU:0, one launch (start us, length us, event | category | flops | bytes accessed | tf_op | source)
XLA Modules:
  0.0 175.9 jit_solution(16924934902123679596)
XLA Ops:
  0.0 0.7 constant_dynamic-slice_fusion
  0.7 0.6 fusion
  1.3 1.3 shard_map.73
  2.6 0.9 broadcast_in_dim_reshape.5.l_ref
  3.5 3.4 %shard_map.80 = (f32[192,128]{1,0:T(8,128)S(1)}, f32[192,128]{1,0:T(8,128)S(1)}) custom-call(s32[1]{0:T(128)} %bitcast.2.f_ref.core_ref, bf16[384,896]{1,0:T(8,128)(2,1)S(1)} %get-tuple-element.29.refs_0_.low_ref, bf16[384,896]{1,0:T(8,128)(2,1)S(1)} %get-tuple-element.30.refs_1_.high_ref, s32[384,1]{1,0:T(8,128)S(1)} %broadcast_in_dim_reshape.5.l_ref, ...), custom_call_target="tpu_custom_call" | custom-call | flops 704643072 | bytes 3407872 | tf_op jit(solution)/shard_map/pallas_call | solution.py:94
  6.9 0.6 collective-permute-start.29
  8.4 2.9 %collective-permute-start.30 = (f32[96,128]{1,0:T(8,128)S(1)}, f32[96,128]{1,0:T(8,128)S(1)}, u32[]{:S(2)}, u32[]{:S(2)}) collective-permute-start(f32[96,128]{1,0:T(8,128)S(1)} %slice_select_fusion), channel_id=1, source_target_pairs={{0,2},{1,3},{4,6},{5,7},{8,10},{9,11},{12,14},{13,15},{14,12},{15,... | collective-permute-start | bytes 147464 | tf_op jit(solution)/shard_map/ppermute | solution.py:161
  11.4 2.1 %collective-permute-done.30 = f32[96,128]{1,0:T(8,128)S(1)} collective-permute-done((f32[96,128]{1,0:T(8,128)S(1)}, f32[96,128]{1,0:T(8,128)S(1)}, u32[]{:S(2)}, u32[]{:S(2)}) %collective-permute-start.30) | collective-permute-done | bytes 49184 | tf_op jit(solution)/shard_map/ppermute | solution.py:161
  13.5 10.9 %all_to_all.18 = f32[4,24,128]{2,1,0:T(8,128)S(1)} all-to-all(f32[4,24,128]{2,1,0:T(8,128)S(1)} %bitcast.15), channel_id=1, replica_groups={{0,4,8,12},{1,5,9,13},{14,10,6,2},{15,11,7,3},{16,20,24,28},{17,21,25,2..., dimensions={0} | all-to-all | bytes 98304 | tf_op jit(solution)/shard_map/all_to_all | solution.py:175
  24.3 0.6 broadcast_in_dim.2
  25.0 3.3 %all-to-all-start.1 = ((f32[4,24,128]{2,1,0:T(8,128)}), f32[4,24,128]{2,1,0:T(8,128)S(1)}, u32[]{:S(2)}, u32[]{:S(2)}) async-start(f32[4,24,128]{2,1,0:T(8,128)} %broadcast_in_dim.2), calls=%async_computation.1 | async-start | bytes 98304 | tf_op jit(solution)/shard_map/all_to_all | solution.py:178
  28.2 2.0 %collective-permute-start = (bf16[384,896]{1,0:T(8,128)(2,1)S(1)}, bf16[384,896]{1,0:T(8,128)(2,1)}, u32[]{:S(2)}, u32[]{:S(2)}) collective-permute-start(bf16[384,896]{1,0:T(8,128)(2,1)S(1)} %get-tuple-element.29.refs_0_.low_ref), channel_id=1, source_target_pairs={{0,4},{1,3},{4,8},{5,1},{8,12},{9,5},{12,14},{13,9},{14,10},{15,13... | collective-permute-start | bytes 2064392 | tf_op jit(solution)/shard_map/ppermute | solution.py:408
  30.2 3.8 %all-to-all-done.1 = f32[4,24,128]{2,1,0:T(8,128)S(1)} async-done(((f32[4,24,128]{2,1,0:T(8,128)}), f32[4,24,128]{2,1,0:T(8,128)S(1)}, u32[]{:S(2)}, u32[]{:S(2)}) %all-to-all-start.1) | async-done | bytes 49184 | tf_op jit(solution)/shard_map/all_to_all | solution.py:178
  34.1 2.0 %collective-permute-start.5 = (bf16[384,896]{1,0:T(8,128)(2,1)S(1)}, bf16[384,896]{1,0:T(8,128)(2,1)S(1)}, u32[]{:S(2)}, u32[]{:S(2)}) collective-permute-start(bf16[384,896]{1,0:T(8,128)(2,1)S(1)} %get-tuple-element.30.refs_1_.high_ref), channel_id=1, source_target_pairs={{4,0},{3,1},{8,4},{1,5},{12,8},{5,9},{14,12},{9,13},{10,14},{13,15... | collective-permute-start | bytes 2064392 | tf_op jit(solution)/shard_map/ppermute | solution.py:408
  36.1 11.8 %collective-permute-done.31 = f32[96,128]{1,0:T(8,128)S(1)} collective-permute-done((f32[96,128]{1,0:T(8,128)S(1)}, f32[96,128]{1,0:T(8,128)S(1)}, u32[]{:S(2)}, u32[]{:S(2)}) %collective-permute-start.31) | collective-permute-done | bytes 49184 | tf_op jit(solution)/shard_map/ppermute | solution.py:166
  48.1 1.2 collective-permute-done.32.other_ref
  49.3 0.8 collective-permute-start.14
  50.1 0.5 collective-permute-start.27
  50.6 15.3 %collective-permute-done.10.refs_0_ = bf16[384,896]{1,0:T(8,128)(2,1)S(1)} collective-permute-done((bf16[384,896]{1,0:T(8,128)(2,1)S(1)}, bf16[384,896]{1,0:T(8,128)(2,1)S(1)}, u32[]{:S(2)}, u32[]{:S(2)}) %collective-permute-start.10) | collective-permute-done | bytes 688160 | tf_op jit(solution)/shard_map/ppermute | solution.py:408
  66.0 2.0 %collective-permute-start.6 = (bf16[384,896]{1,0:T(8,128)(2,1)S(1)}, bf16[384,896]{1,0:T(8,128)(2,1)S(1)}, u32[]{:S(2)}, u32[]{:S(2)}) collective-permute-start(bf16[384,896]{1,0:T(8,128)(2,1)S(1)} %collective-permute-done.5.refs_2_), channel_id=1, source_target_pairs={{4,0},{3,1},{8,4},{1,5},{12,8},{5,9},{14,12},{9,13},{10,14},{13,15... | collective-permute-start | bytes 2064392 | tf_op jit(solution)/shard_map/ppermute | solution.py:408
  68.3 1.8 %collective-permute-start.15 = (bf16[384,896]{1,0:T(8,128)(2,1)S(1)}, bf16[384,896]{1,0:T(8,128)(2,1)S(1)}, u32[]{:S(2)}, u32[]{:S(2)}) collective-permute-start(bf16[384,896]{1,0:T(8,128)(2,1)S(1)} %collective-permute-done.14.refs_2_), channel_id=1, source_target_pairs={{4,0},{3,1},{8,4},{1,5},{12,8},{5,9},{14,12},{9,13},{10,14},{13,15... | collective-permute-start | bytes 2064392 | tf_op jit(solution)/shard_map/ppermute | solution.py:408
  70.1 14.4 %collective-permute-done.1.refs_0_ = bf16[384,896]{1,0:T(8,128)(2,1)S(1)} collective-permute-done((bf16[384,896]{1,0:T(8,128)(2,1)}, bf16[384,896]{1,0:T(8,128)(2,1)S(1)}, u32[]{:S(2)}, u32[]{:S(2)}) %collective-permute-start.1) | collective-permute-done | bytes 688160 | tf_op jit(solution)/shard_map/ppermute | solution.py:408
  84.5 0.5 collective-permute-start.23
  85.0 0.7 collective-permute-start.2
  85.7 12.9 %collective-permute-done.11.refs_0_ = bf16[384,896]{1,0:T(8,128)(2,1)S(1)} collective-permute-done((bf16[384,896]{1,0:T(8,128)(2,1)S(1)}, bf16[384,896]{1,0:T(8,128)(2,1)S(1)}, u32[]{:S(2)}, u32[]{:S(2)}) %collective-permute-start.11) | collective-permute-done | bytes 688160 | tf_op jit(solution)/shard_map/ppermute | solution.py:408
  99.1 2.0 %collective-permute-start.7 = (bf16[384,896]{1,0:T(8,128)(2,1)S(1)}, bf16[384,896]{1,0:T(8,128)(2,1)S(1)}, u32[]{:S(2)}, u32[]{:S(2)}) collective-permute-start(bf16[384,896]{1,0:T(8,128)(2,1)S(1)} %collective-permute-done.6.refs_2_), channel_id=1, source_target_pairs={{4,0},{3,1},{8,4},{1,5},{12,8},{5,9},{14,12},{9,13},{10,14},{13,15... | collective-permute-start | bytes 2064392 | tf_op jit(solution)/shard_map/ppermute | solution.py:408
  101.2 9.1 %collective-permute-done.2.refs_0_ = bf16[384,896]{1,0:T(8,128)(2,1)S(1)} collective-permute-done((bf16[384,896]{1,0:T(8,128)(2,1)S(1)}, bf16[384,896]{1,0:T(8,128)(2,1)S(1)}, u32[]{:S(2)}, u32[]{:S(2)}) %collective-permute-start.2) | collective-permute-done | bytes 688160 | tf_op jit(solution)/shard_map/ppermute | solution.py:408
  110.3 2.1 %collective-permute-start.3 = (bf16[160,896]{1,0:T(8,128)(2,1)S(1)}, bf16[160,896]{1,0:T(8,128)(2,1)S(1)}, u32[]{:S(2)}, u32[]{:S(2)}) collective-permute-start(bf16[160,896]{1,0:T(8,128)(2,1)S(1)} %slice.37), channel_id=1, source_target_pairs={{0,4},{1,3},{4,8},{5,1},{8,12},{9,5},{12,14},{13,9},{14,10},{15,13... | collective-permute-start | bytes 860168 | tf_op jit(solution)/shard_map/ppermute | solution.py:408
  112.4 5.0 %collective-permute-done.7.refs_2_ = bf16[384,896]{1,0:T(8,128)(2,1)S(1)} collective-permute-done((bf16[384,896]{1,0:T(8,128)(2,1)S(1)}, bf16[384,896]{1,0:T(8,128)(2,1)S(1)}, u32[]{:S(2)}, u32[]{:S(2)}) %collective-permute-start.7) | collective-permute-done | bytes 688160 | tf_op jit(solution)/shard_map/ppermute | solution.py:408
  117.6 1.9 %collective-permute-start.8 = (bf16[160,896]{1,0:T(8,128)(2,1)S(1)}, bf16[160,896]{1,0:T(8,128)(2,1)S(1)}, u32[]{:S(2)}, u32[]{:S(2)}) collective-permute-start(bf16[160,896]{1,0:T(8,128)(2,1)S(1)} %slice.38), channel_id=1, source_target_pairs={{4,0},{3,1},{8,4},{1,5},{12,8},{5,9},{14,12},{9,13},{10,14},{13,15... | collective-permute-start | bytes 860168 | tf_op jit(solution)/shard_map/ppermute | solution.py:408
  119.5 5.5 %collective-permute-done.12.refs_0_ = bf16[384,896]{1,0:T(8,128)(2,1)S(1)} collective-permute-done((bf16[384,896]{1,0:T(8,128)(2,1)S(1)}, bf16[384,896]{1,0:T(8,128)(2,1)S(1)}, u32[]{:S(2)}, u32[]{:S(2)}) %collective-permute-start.12) | collective-permute-done | bytes 688160 | tf_op jit(solution)/shard_map/ppermute | solution.py:408
  125.0 7.1 %collective-permute-done.16.refs_2_ = bf16[384,896]{1,0:T(8,128)(2,1)S(1)} collective-permute-done((bf16[384,896]{1,0:T(8,128)(2,1)S(1)}, bf16[384,896]{1,0:T(8,128)(2,1)S(1)}, u32[]{:S(2)}, u32[]{:S(2)}) %collective-permute-start.16) | collective-permute-done | bytes 688160 | tf_op jit(solution)/shard_map/ppermute | solution.py:408
  132.1 0.5 collective-permute-start.13
  132.6 0.7 dynamic-slice_bitcast_fusion.starts_ref
  133.4 4.9 %collective-permute-done.8.refs_1_ = bf16[160,896]{1,0:T(8,128)(2,1)S(1)} collective-permute-done((bf16[160,896]{1,0:T(8,128)(2,1)S(1)}, bf16[160,896]{1,0:T(8,128)(2,1)S(1)}, u32[]{:S(2)}, u32[]{:S(2)}) %collective-permute-start.8) | collective-permute-done | bytes 286752 | tf_op jit(solution)/shard_map/ppermute | solution.py:408
  138.3 0.7 collective-permute-start.35
  139.0 1.9 %shard_map.81.refs_10_ = f32[384,512]{1,0:T(8,128)S(1)} custom-call(s32[1]{0:T(128)} %bitcast.2.f_ref.core_ref, f32[192,128]{1,0:T(8,128)S(1)} %pad_maximum_fusion.mine_ref, f32[192,128]{1,0:T(8,128)S(1)} %collective-permute-done.32.other_ref, s32[384,1]{1,0:T(8,128)S(1)} %broadcast_in_dim_reshape.5.l_ref, bf16[512,512]{1,0:T(8,128)(2,1)S(1)} %bitcast.12), custom_call_target="tpu_custom_call" | custom-call | flops 301989888 | bytes 1507328 | tf_op jit(solution)/shard_map/pallas_call | solution.py:335
  141.0 3.8 %shard_map.74.refs_5_ = f32[384,512]{1,0:T(8,128)S(1)} custom-call(s32[35]{0:T(128)S(1)} %dynamic-slice_bitcast_fusion.starts_ref, bf16[384,896]{1,0:T(8,128)(2,1)S(1)} %get-tuple-element.29.refs_0_.low_ref, bf16[384,896]{1,0:T(8,128)(2,1)S(1)} %get-tuple-element.30.refs_1_.high_ref, bf16[384,1792]{1,0:T(8,128)(2,1)S(1)} %collective-permute-done.28.refs_2_, ...), custom_call_target="tpu_custom_call" | custom-call | flops 1409286144 | bytes 7995392 | tf_op jit(solution)/shard_map/pallas_call | solution.py:242
  144.8 4.6 %shard_map.75.refs_5_ = f32[384,512]{1,0:T(8,128)S(1)} custom-call(s32[35]{0:T(128)S(1)} %dynamic-slice_bitcast_fusion.starts_ref, bf16[384,896]{1,0:T(8,128)(2,1)} %collective-permute-done.refs_0_, bf16[384,896]{1,0:T(8,128)(2,1)S(1)} %collective-permute-done.26.refs_1_, bf16[384,896]{1,0:T(8,128)(2,1)S(1)} %collective-permute-done.5.refs_2_, ...), custom_call_target="tpu_custom_call" | custom-call | flops 1409286144 | bytes 7995392 | tf_op jit(solution)/shard_map/pallas_call | solution.py:242
  149.4 4.0 %shard_map.76.refs_5_ = f32[384,512]{1,0:T(8,128)S(1)} custom-call(s32[35]{0:T(128)S(1)} %dynamic-slice_bitcast_fusion.starts_ref, bf16[384,896]{1,0:T(8,128)(2,1)S(1)} %collective-permute-done.10.refs_0_, bf16[384,896]{1,0:T(8,128)(2,1)S(1)} %collective-permute-done.24.refs_1_, bf16[384,896]{1,0:T(8,128)(2,1)S(1)} %collective-permute-done.14.refs_2_, ...), custom_call_target="tpu_custom_call" | custom-call | flops 1409286144 | bytes 7995392 | tf_op jit(solution)/shard_map/pallas_call | solution.py:242
  153.5 0.6 collective-permute-start.34
  154.2 4.4 %shard_map.77 = (f32[384,512]{1,0:T(8,128)S(1)}, bf16[512,896]{1,0:T(8,128)(2,1)S(1)}, bf16[512,896]{1,0:T(8,128)(2,1)S(1)}, bf16[512,896]{1,0:T(8,128)(2,1)S(1)}, bf16[512,896]{1,0:T(8,128)(2,1)S(1)}) custom-call(s32[35]{0:T(128)S(1)} %dynamic-slice_bitcast_fusion.starts_ref, bf16[384,896]{1,0:T(8,128)(2,1)S(1)} %collective-permute-done.1.refs_0_, ...), custom_call_target="tpu_custom_call" | custom-call | flops 1409286144 | bytes 11665408 | tf_op jit(solution)/shard_map/pallas_call | solution.py:242
  159.1 4.1 %shard_map.78 = (f32[384,512]{1,0:T(8,128)S(1)}, bf16[512,896]{1,0:T(8,128)(2,1)S(1)}, bf16[512,896]{1,0:T(8,128)(2,1)S(1)}, bf16[512,896]{1,0:T(8,128)(2,1)S(1)}, bf16[512,896]{1,0:T(8,128)(2,1)S(1)}) custom-call(s32[35]{0:T(128)S(1)} %dynamic-slice_bitcast_fusion.starts_ref, bf16[384,896]{1,0:T(8,128)(2,1)S(1)} %collective-permute-done.11.refs_0_, ...), custom_call_target="tpu_custom_call" | custom-call | flops 1409286144 | bytes 11665408 | tf_op jit(solution)/shard_map/pallas_call | solution.py:242
  163.2 4.1 %shard_map.79 = (f32[384,512]{1,0:T(8,128)S(1)}, bf16[512,896]{1,0:T(8,128)(2,1)S(1)}, bf16[512,896]{1,0:T(8,128)(2,1)S(1)}, bf16[512,896]{1,0:T(8,128)(2,1)S(1)}, bf16[512,896]{1,0:T(8,128)(2,1)S(1)}) custom-call(s32[35]{0:T(128)S(1)} %dynamic-slice_bitcast_fusion.starts_ref, bf16[384,896]{1,0:T(8,128)(2,1)S(1)} %collective-permute-done.2.refs_0_, ...), custom_call_target="tpu_custom_call" | custom-call | flops 1409286144 | bytes 11665408 | tf_op jit(solution)/shard_map/pallas_call | solution.py:242
  167.4 4.1 %shard_map.82 = (f32[384,512]{1,0:T(8,128)S(1)}, bf16[512,896]{1,0:T(8,128)(2,1)S(1)}, bf16[512,896]{1,0:T(8,128)(2,1)S(1)}, bf16[512,896]{1,0:T(8,128)(2,1)S(1)}, bf16[512,896]{1,0:T(8,128)(2,1)S(1)}) custom-call(s32[35]{0:T(128)S(1)} %dynamic-slice_bitcast_fusion.starts_ref, bf16[384,896]{1,0:T(8,128)(2,1)S(1)} %collective-permute-done.12.refs_0_, ...), custom_call_target="tpu_custom_call" | custom-call | flops 1409286144 | bytes 11665408 | tf_op jit(solution)/shard_map/pallas_call | solution.py:242
  171.5 0.8 shard_map.83.refs_4_
  172.3 2.0 %shard_map.84.refs_5_ = bf16[384,512]{1,0:T(8,128)(2,1)} custom-call(bf16[224,896]{1,0:T(8,128)(2,1)S(1)} %collective-permute-done.33.refs_0_, bf16[224,896]{1,0:T(8,128)(2,1)S(1)} %collective-permute-done.34.refs_1_, bf16[224,896]{1,0:T(8,128)(2,1)S(1)} %collective-permute-done.35.refs_2_, bf16[224,896]{1,0:T(8,128)(2,1)S(1)} %collective-permute-done.36.refs_3_, ...), custom_call_target="tpu_custom_call" | custom-call | tf_op jit(solution)/shard_map/pallas_call | solution.py:294
  174.3 1.4 shard_map.85
  (59 shorter events, 2.5 us)
Async XLA Ops:
  6.9 1.5 collective-permute-start.29
  8.4 130.5 %copy-start = (bf16[8,64,512]{2,1,0:T(8,128)(2,1)S(1)}, bf16[8,64,512]{2,1,0:T(8,128)(2,1)}, u32[]{:S(2)}) copy-start(bf16[8,64,512]{2,1,0:T(8,128)(2,1)} %param.10) | copy-start | bytes 1572868
  8.4 5.0 %collective-permute-start.30 = (f32[96,128]{1,0:T(8,128)S(1)}, f32[96,128]{1,0:T(8,128)S(1)}, u32[]{:S(2)}, u32[]{:S(2)}) collective-permute-start(f32[96,128]{1,0:T(8,128)S(1)} %slice_select_fusion), channel_id=1, source_target_pairs={{0,2},{1,3},{4,6},{5,7},{8,10},{9,11},{12,14},{13,15},{14,12},{15,... | collective-permute-start | bytes 147464 | tf_op jit(solution)/shard_map/ppermute | solution.py:161
  11.4 54.6 %collective-permute-start.28 = (bf16[384,1792]{1,0:T(8,128)(2,1)}, bf16[384,1792]{1,0:T(8,128)(2,1)S(1)}, u32[]{:S(2)}, u32[]{:S(2)}) collective-permute-start(bf16[384,1792]{1,0:T(8,128)(2,1)} %bitcast.x_ref), channel_id=1, source_target_pairs={{0,1},{1,0},{4,5},{5,4},{8,9},{9,8},{12,13},{13,12},{14,15},{15,14... | collective-permute-start | bytes 4128776 | tf_op jit(solution)/shard_map/ppermute | solution.py:399
  25.0 9.1 %all-to-all-start.1 = ((f32[4,24,128]{2,1,0:T(8,128)}), f32[4,24,128]{2,1,0:T(8,128)S(1)}, u32[]{:S(2)}, u32[]{:S(2)}) async-start(f32[4,24,128]{2,1,0:T(8,128)} %broadcast_in_dim.2), calls=%async_computation.1 | async-start | bytes 98304 | tf_op jit(solution)/shard_map/all_to_all | solution.py:178
  28.2 21.8 %collective-permute-start = (bf16[384,896]{1,0:T(8,128)(2,1)S(1)}, bf16[384,896]{1,0:T(8,128)(2,1)}, u32[]{:S(2)}, u32[]{:S(2)}) collective-permute-start(bf16[384,896]{1,0:T(8,128)(2,1)S(1)} %get-tuple-element.29.refs_0_.low_ref), channel_id=1, source_target_pairs={{0,4},{1,3},{4,8},{5,1},{8,12},{9,5},{12,14},{13,9},{14,10},{15,13... | collective-permute-start | bytes 2064392 | tf_op jit(solution)/shard_map/ppermute | solution.py:408
  34.0 13.8 %collective-permute-start.31 = (f32[96,128]{1,0:T(8,128)S(1)}, f32[96,128]{1,0:T(8,128)S(1)}, u32[]{:S(2)}, u32[]{:S(2)}) collective-permute-start(f32[96,128]{1,0:T(8,128)S(1)} %bitcast.14), channel_id=1, source_target_pairs={{0,2},{1,3},{4,6},{5,7},{8,10},{9,11},{12,14},{13,15},{14,12},{15,... | collective-permute-start | bytes 147464 | tf_op jit(solution)/shard_map/ppermute | solution.py:166
  34.1 16.0 %collective-permute-start.5 = (bf16[384,896]{1,0:T(8,128)(2,1)S(1)}, bf16[384,896]{1,0:T(8,128)(2,1)S(1)}, u32[]{:S(2)}, u32[]{:S(2)}) collective-permute-start(bf16[384,896]{1,0:T(8,128)(2,1)S(1)} %get-tuple-element.30.refs_1_.high_ref), channel_id=1, source_target_pairs={{4,0},{3,1},{8,4},{1,5},{12,8},{5,9},{14,12},{9,13},{10,14},{13,15... | collective-permute-start | bytes 2064392 | tf_op jit(solution)/shard_map/ppermute | solution.py:408
  47.9 1.4 collective-permute-start.32
  48.0 17.9 %collective-permute-start.10 = (bf16[384,896]{1,0:T(8,128)(2,1)S(1)}, bf16[384,896]{1,0:T(8,128)(2,1)S(1)}, u32[]{:S(2)}, u32[]{:S(2)}) collective-permute-start(bf16[384,896]{1,0:T(8,128)(2,1)S(1)} %get-tuple-element.30.refs_1_.high_ref), channel_id=1, source_target_pairs={{0,4},{1,3},{4,8},{5,1},{8,12},{9,5},{12,14},{13,9},{14,10},{15,13... | collective-permute-start | bytes 2064392 | tf_op jit(solution)/shard_map/ppermute | solution.py:408
  49.3 16.7 %collective-permute-start.14 = (bf16[384,896]{1,0:T(8,128)(2,1)S(1)}, bf16[384,896]{1,0:T(8,128)(2,1)S(1)}, u32[]{:S(2)}, u32[]{:S(2)}) collective-permute-start(bf16[384,896]{1,0:T(8,128)(2,1)S(1)} %get-tuple-element.29.refs_0_.low_ref), channel_id=1, source_target_pairs={{4,0},{3,1},{8,4},{1,5},{12,8},{5,9},{14,12},{9,13},{10,14},{13,15... | collective-permute-start | bytes 2064392 | tf_op jit(solution)/shard_map/ppermute | solution.py:408
  50.1 17.9 %collective-permute-start.26 = (bf16[384,896]{1,0:T(8,128)(2,1)}, bf16[384,896]{1,0:T(8,128)(2,1)S(1)}, u32[]{:S(2)}, u32[]{:S(2)}) collective-permute-start(bf16[384,896]{1,0:T(8,128)(2,1)} %collective-permute-done.refs_0_), channel_id=1, source_target_pairs={{0,1},{1,0},{4,5},{5,4},{8,9},{9,8},{12,13},{13,12},{14,15},{15,14... | collective-permute-start | bytes 2064392 | tf_op jit(solution)/shard_map/ppermute | solution.py:411
  50.1 17.9 %collective-permute-start.27 = (bf16[384,896]{1,0:T(8,128)(2,1)S(1)}, bf16[384,896]{1,0:T(8,128)(2,1)S(1)}, u32[]{:S(2)}, u32[]{:S(2)}) collective-permute-start(bf16[384,896]{1,0:T(8,128)(2,1)S(1)} %collective-permute-done.5.refs_2_), channel_id=1, source_target_pairs={{0,1},{1,0},{4,5},{5,4},{8,9},{9,8},{12,13},{13,12},{14,15},{15,14... | collective-permute-start | bytes 2064392 | tf_op jit(solution)/shard_map/ppermute | solution.py:411
  65.9 2.3 %collective-permute-start.24 = (bf16[384,896]{1,0:T(8,128)(2,1)S(1)}, bf16[384,896]{1,0:T(8,128)(2,1)S(1)}, u32[]{:S(2)}, u32[]{:S(2)}) collective-permute-start(bf16[384,896]{1,0:T(8,128)(2,1)S(1)} %collective-permute-done.10.refs_0_), channel_id=1, source_target_pairs={{0,1},{1,0},{4,5},{5,4},{8,9},{9,8},{12,13},{13,12},{14,15},{15,14... | collective-permute-start | bytes 2064392 | tf_op jit(solution)/shard_map/ppermute | solution.py:411
  65.9 18.5 %collective-permute-start.1 = (bf16[384,896]{1,0:T(8,128)(2,1)}, bf16[384,896]{1,0:T(8,128)(2,1)S(1)}, u32[]{:S(2)}, u32[]{:S(2)}) collective-permute-start(bf16[384,896]{1,0:T(8,128)(2,1)} %collective-permute-done.refs_0_), channel_id=1, source_target_pairs={{0,4},{1,3},{4,8},{5,1},{8,12},{9,5},{12,14},{13,9},{14,10},{15,13... | collective-permute-start | bytes 2064392 | tf_op jit(solution)/shard_map/ppermute | solution.py:408
  66.0 18.5 %collective-permute-start.6 = (bf16[384,896]{1,0:T(8,128)(2,1)S(1)}, bf16[384,896]{1,0:T(8,128)(2,1)S(1)}, u32[]{:S(2)}, u32[]{:S(2)}) collective-permute-start(bf16[384,896]{1,0:T(8,128)(2,1)S(1)} %collective-permute-done.5.refs_2_), channel_id=1, source_target_pairs={{4,0},{3,1},{8,4},{1,5},{12,8},{5,9},{14,12},{9,13},{10,14},{13,15... | collective-permute-start | bytes 2064392 | tf_op jit(solution)/shard_map/ppermute | solution.py:408
  68.0 17.0 %collective-permute-start.25 = (bf16[384,896]{1,0:T(8,128)(2,1)S(1)}, bf16[384,896]{1,0:T(8,128)(2,1)S(1)}, u32[]{:S(2)}, u32[]{:S(2)}) collective-permute-start(bf16[384,896]{1,0:T(8,128)(2,1)S(1)} %collective-permute-done.14.refs_2_), channel_id=1, source_target_pairs={{0,1},{1,0},{4,5},{5,4},{8,9},{9,8},{12,13},{13,12},{14,15},{15,14... | collective-permute-start | bytes 2064392 | tf_op jit(solution)/shard_map/ppermute | solution.py:411
  68.0 30.6 %collective-permute-start.11 = (bf16[384,896]{1,0:T(8,128)(2,1)S(1)}, bf16[384,896]{1,0:T(8,128)(2,1)S(1)}, u32[]{:S(2)}, u32[]{:S(2)}) collective-permute-start(bf16[384,896]{1,0:T(8,128)(2,1)S(1)} %collective-permute-done.10.refs_0_), channel_id=1, source_target_pairs={{0,4},{1,3},{4,8},{5,1},{8,12},{9,5},{12,14},{13,9},{14,10},{15,13... | collective-permute-start | bytes 2064392 | tf_op jit(solution)/shard_map/ppermute | solution.py:408
  68.3 30.8 %collective-permute-start.15 = (bf16[384,896]{1,0:T(8,128)(2,1)S(1)}, bf16[384,896]{1,0:T(8,128)(2,1)S(1)}, u32[]{:S(2)}, u32[]{:S(2)}) collective-permute-start(bf16[384,896]{1,0:T(8,128)(2,1)S(1)} %collective-permute-done.14.refs_2_), channel_id=1, source_target_pairs={{4,0},{3,1},{8,4},{1,5},{12,8},{5,9},{14,12},{9,13},{10,14},{13,15... | collective-permute-start | bytes 2064392 | tf_op jit(solution)/shard_map/ppermute | solution.py:408
  84.5 16.6 %collective-permute-start.22 = (bf16[384,896]{1,0:T(8,128)(2,1)S(1)}, bf16[384,896]{1,0:T(8,128)(2,1)S(1)}, u32[]{:S(2)}, u32[]{:S(2)}) collective-permute-start(bf16[384,896]{1,0:T(8,128)(2,1)S(1)} %collective-permute-done.1.refs_0_), channel_id=1, source_target_pairs={{0,1},{1,0},{4,5},{5,4},{8,9},{9,8},{12,13},{13,12},{14,15},{15,14... | collective-permute-start | bytes 2064392 | tf_op jit(solution)/shard_map/ppermute | solution.py:411
  84.5 16.6 %collective-permute-start.23 = (bf16[384,896]{1,0:T(8,128)(2,1)S(1)}, bf16[384,896]{1,0:T(8,128)(2,1)S(1)}, u32[]{:S(2)}, u32[]{:S(2)}) collective-permute-start(bf16[384,896]{1,0:T(8,128)(2,1)S(1)} %collective-permute-done.6.refs_2_), channel_id=1, source_target_pairs={{0,1},{1,0},{4,5},{5,4},{8,9},{9,8},{12,13},{13,12},{14,15},{15,14... | collective-permute-start | bytes 2064392 | tf_op jit(solution)/shard_map/ppermute | solution.py:411
  85.0 25.3 %collective-permute-start.2 = (bf16[384,896]{1,0:T(8,128)(2,1)S(1)}, bf16[384,896]{1,0:T(8,128)(2,1)S(1)}, u32[]{:S(2)}, u32[]{:S(2)}) collective-permute-start(bf16[384,896]{1,0:T(8,128)(2,1)S(1)} %collective-permute-done.1.refs_0_), channel_id=1, source_target_pairs={{0,4},{1,3},{4,8},{5,1},{8,12},{9,5},{12,14},{13,9},{14,10},{15,13... | collective-permute-start | bytes 2064392 | tf_op jit(solution)/shard_map/ppermute | solution.py:408
  98.6 11.7 %collective-permute-start.20 = (bf16[384,896]{1,0:T(8,128)(2,1)S(1)}, bf16[384,896]{1,0:T(8,128)(2,1)S(1)}, u32[]{:S(2)}, u32[]{:S(2)}) collective-permute-start(bf16[384,896]{1,0:T(8,128)(2,1)S(1)} %collective-permute-done.11.refs_0_), channel_id=1, source_target_pairs={{0,1},{1,0},{4,5},{5,4},{8,9},{9,8},{12,13},{13,12},{14,15},{15,14... | collective-permute-start | bytes 2064392 | tf_op jit(solution)/shard_map/ppermute | solution.py:411
  99.1 18.3 %collective-permute-start.7 = (bf16[384,896]{1,0:T(8,128)(2,1)S(1)}, bf16[384,896]{1,0:T(8,128)(2,1)S(1)}, u32[]{:S(2)}, u32[]{:S(2)}) collective-permute-start(bf16[384,896]{1,0:T(8,128)(2,1)S(1)} %collective-permute-done.6.refs_2_), channel_id=1, source_target_pairs={{4,0},{3,1},{8,4},{1,5},{12,8},{5,9},{14,12},{9,13},{10,14},{13,15... | collective-permute-start | bytes 2064392 | tf_op jit(solution)/shard_map/ppermute | solution.py:408
  101.0 16.5 %collective-permute-start.21 = (bf16[384,896]{1,0:T(8,128)(2,1)S(1)}, bf16[384,896]{1,0:T(8,128)(2,1)S(1)}, u32[]{:S(2)}, u32[]{:S(2)}) collective-permute-start(bf16[384,896]{1,0:T(8,128)(2,1)S(1)} %collective-permute-done.15.refs_2_), channel_id=1, source_target_pairs={{0,1},{1,0},{4,5},{5,4},{8,9},{9,8},{12,13},{13,12},{14,15},{15,14... | collective-permute-start | bytes 2064392 | tf_op jit(solution)/shard_map/ppermute | solution.py:411
  101.0 23.9 %collective-permute-start.12 = (bf16[384,896]{1,0:T(8,128)(2,1)S(1)}, bf16[384,896]{1,0:T(8,128)(2,1)S(1)}, u32[]{:S(2)}, u32[]{:S(2)}) collective-permute-start(bf16[384,896]{1,0:T(8,128)(2,1)S(1)} %collective-permute-done.11.refs_0_), channel_id=1, source_target_pairs={{0,4},{1,3},{4,8},{5,1},{8,12},{9,5},{12,14},{13,9},{14,10},{15,13... | collective-permute-start | bytes 2064392 | tf_op jit(solution)/shard_map/ppermute | solution.py:408
  110.2 21.9 %collective-permute-start.16 = (bf16[384,896]{1,0:T(8,128)(2,1)S(1)}, bf16[384,896]{1,0:T(8,128)(2,1)S(1)}, u32[]{:S(2)}, u32[]{:S(2)}) collective-permute-start(bf16[384,896]{1,0:T(8,128)(2,1)S(1)} %collective-permute-done.15.refs_2_), channel_id=1, source_target_pairs={{4,0},{3,1},{8,4},{1,5},{12,8},{5,9},{14,12},{9,13},{10,14},{13,15... | collective-permute-start | bytes 2064392 | tf_op jit(solution)/shard_map/ppermute | solution.py:408
  110.3 21.9 %collective-permute-start.3 = (bf16[160,896]{1,0:T(8,128)(2,1)S(1)}, bf16[160,896]{1,0:T(8,128)(2,1)S(1)}, u32[]{:S(2)}, u32[]{:S(2)}) collective-permute-start(bf16[160,896]{1,0:T(8,128)(2,1)S(1)} %slice.37), channel_id=1, source_target_pairs={{0,4},{1,3},{4,8},{5,1},{8,12},{9,5},{12,14},{13,9},{14,10},{15,13... | collective-permute-start | bytes 860168 | tf_op jit(solution)/shard_map/ppermute | solution.py:408
  117.4 23.6 %collective-permute-start.33 = (bf16[224,896]{1,0:T(8,128)(2,1)S(1)}, bf16[224,896]{1,0:T(8,128)(2,1)S(1)}, u32[]{:S(2)}, u32[]{:S(2)}) collective-permute-start(bf16[224,896]{1,0:T(8,128)(2,1)S(1)} %slice.41), channel_id=1, source_target_pairs={{0,4},{1,3},{4,8},{5,1},{8,12},{9,5},{12,14},{13,9},{14,10},{15,13... | collective-permute-start | bytes 1204232 | tf_op jit(solution)/shard_map/ppermute | solution.py:408
  117.6 20.7 %collective-permute-start.8 = (bf16[160,896]{1,0:T(8,128)(2,1)S(1)}, bf16[160,896]{1,0:T(8,128)(2,1)S(1)}, u32[]{:S(2)}, u32[]{:S(2)}) collective-permute-start(bf16[160,896]{1,0:T(8,128)(2,1)S(1)} %slice.38), channel_id=1, source_target_pairs={{4,0},{3,1},{8,4},{1,5},{12,8},{5,9},{14,12},{9,13},{10,14},{13,15... | collective-permute-start | bytes 860168 | tf_op jit(solution)/shard_map/ppermute | solution.py:408
  125.0 29.1 %collective-permute-start.18 = (bf16[384,896]{1,0:T(8,128)(2,1)S(1)}, bf16[384,896]{1,0:T(8,128)(2,1)S(1)}, u32[]{:S(2)}, u32[]{:S(2)}) collective-permute-start(bf16[384,896]{1,0:T(8,128)(2,1)S(1)} %collective-permute-done.2.refs_0_), channel_id=1, source_target_pairs={{0,1},{1,0},{4,5},{5,4},{8,9},{9,8},{12,13},{13,12},{14,15},{15,14... | collective-permute-start | bytes 2064392 | tf_op jit(solution)/shard_map/ppermute | solution.py:411
  132.1 26.4 %collective-permute-start.19 = (bf16[384,896]{1,0:T(8,128)(2,1)S(1)}, bf16[384,896]{1,0:T(8,128)(2,1)S(1)}, u32[]{:S(2)}, u32[]{:S(2)}) collective-permute-start(bf16[384,896]{1,0:T(8,128)(2,1)S(1)} %collective-permute-done.7.refs_2_), channel_id=1, source_target_pairs={{0,1},{1,0},{4,5},{5,4},{8,9},{9,8},{12,13},{13,12},{14,15},{15,14... | collective-permute-start | bytes 2064392 | tf_op jit(solution)/shard_map/ppermute | solution.py:411
  132.1 26.9 %collective-permute-start.13 = (bf16[384,896]{1,0:T(8,128)(2,1)S(1)}, bf16[384,896]{1,0:T(8,128)(2,1)S(1)}, u32[]{:S(2)}, u32[]{:S(2)}) collective-permute-start(bf16[384,896]{1,0:T(8,128)(2,1)S(1)} %collective-permute-done.12.refs_0_), channel_id=1, source_target_pairs={{0,1},{1,0},{4,5},{5,4},{8,9},{9,8},{12,13},{13,12},{14,15},{15,14... | collective-permute-start | bytes 2064392 | tf_op jit(solution)/shard_map/ppermute | solution.py:411
  138.3 15.2 %collective-permute-start.35 = (bf16[224,896]{1,0:T(8,128)(2,1)S(1)}, bf16[224,896]{1,0:T(8,128)(2,1)S(1)}, u32[]{:S(2)}, u32[]{:S(2)}) collective-permute-start(bf16[224,896]{1,0:T(8,128)(2,1)S(1)} %slice.42), channel_id=1, source_target_pairs={{4,0},{3,1},{8,4},{1,5},{12,8},{5,9},{14,12},{9,13},{10,14},{13,15... | collective-permute-start | bytes 1204232 | tf_op jit(solution)/shard_map/ppermute | solution.py:408
  140.9 26.5 %collective-permute-start.17 = (bf16[384,896]{1,0:T(8,128)(2,1)S(1)}, bf16[384,896]{1,0:T(8,128)(2,1)S(1)}, u32[]{:S(2)}, u32[]{:S(2)}) collective-permute-start(bf16[384,896]{1,0:T(8,128)(2,1)S(1)} %collective-permute-done.16.refs_2_), channel_id=1, source_target_pairs={{0,1},{1,0},{4,5},{5,4},{8,9},{9,8},{12,13},{13,12},{14,15},{15,14... | collective-permute-start | bytes 2064392 | tf_op jit(solution)/shard_map/ppermute | solution.py:411
  153.5 18.7 %collective-permute-start.34 = (bf16[224,896]{1,0:T(8,128)(2,1)S(1)}, bf16[224,896]{1,0:T(8,128)(2,1)S(1)}, u32[]{:S(2)}, u32[]{:S(2)}) collective-permute-start(bf16[224,896]{1,0:T(8,128)(2,1)S(1)} %collective-permute-done.33.refs_0_), channel_id=1, source_target_pairs={{0,1},{1,0},{4,5},{5,4},{8,9},{9,8},{12,13},{13,12},{14,15},{15,14... | collective-permute-start | bytes 1204232 | tf_op jit(solution)/shard_map/ppermute | solution.py:411
  154.1 18.2 %collective-permute-start.36 = (bf16[224,896]{1,0:T(8,128)(2,1)S(1)}, bf16[224,896]{1,0:T(8,128)(2,1)S(1)}, u32[]{:S(2)}, u32[]{:S(2)}) collective-permute-start(bf16[224,896]{1,0:T(8,128)(2,1)S(1)} %collective-permute-done.35.refs_2_), channel_id=1, source_target_pairs={{0,1},{1,0},{4,5},{5,4},{8,9},{9,8},{12,13},{13,12},{14,15},{15,14... | collective-permute-start | bytes 1204232 | tf_op jit(solution)/shard_map/ppermute | solution.py:411
  158.5 15.8 %collective-permute-start.4 = (bf16[160,896]{1,0:T(8,128)(2,1)S(1)}, bf16[160,896]{1,0:T(8,128)(2,1)S(1)}, u32[]{:S(2)}, u32[]{:S(2)}) collective-permute-start(bf16[160,896]{1,0:T(8,128)(2,1)S(1)} %collective-permute-done.3.refs_0_), channel_id=1, source_target_pairs={{0,1},{1,0},{4,5},{5,4},{8,9},{9,8},{12,13},{13,12},{14,15},{15,14... | collective-permute-start | bytes 860168 | tf_op jit(solution)/shard_map/ppermute | solution.py:411
  159.0 15.3 %collective-permute-start.9 = (bf16[160,896]{1,0:T(8,128)(2,1)S(1)}, bf16[160,896]{1,0:T(8,128)(2,1)S(1)}, u32[]{:S(2)}, u32[]{:S(2)}) collective-permute-start(bf16[160,896]{1,0:T(8,128)(2,1)S(1)} %collective-permute-done.8.refs_1_), channel_id=1, source_target_pairs={{0,1},{1,0},{4,5},{5,4},{8,9},{9,8},{12,13},{13,12},{14,15},{15,14... | collective-permute-start | bytes 860168 | tf_op jit(solution)/shard_map/ppermute | solution.py:411

commit v8 on v7

--- a/solution.py
+++ b/solution.py
@@ -167,13 +167,20 @@
     return jnp.concatenate([jnp.where(at == 0, part, got), jnp.where(at == 0, got, part)], axis=0)
 
 
+def rounded_pair(summed):
+    rank = summed.shape[1] // 2
+    resident = summed[:, rank:]
+    left = resident - lax.reduce_precision(resident, exponent_bits=8, mantissa_bits=7)
+    return jnp.concatenate([summed[:, :rank], left], axis=1).astype(jnp.bfloat16)
+
+
 def sum_by_stages(mine, other, side, partner, across, lines):
     got = lax.ppermute(other, "row", partner)
     rows = swap(mine + got, side, across)
     size = len(lines[0])
     piece = rows.shape[0] // size
     parts = lax.all_to_all(rows, "row", 0, 0, axis_index_groups=lines, tiled=True)
-    total = jnp.sum(parts.reshape(size, piece, rows.shape[1]), axis=0)
+    total = rounded_pair(jnp.sum(parts.reshape(size, piece, rows.shape[1]), axis=0))
     spread = jnp.broadcast_to(total[None], (size,) + total.shape).reshape(rows.shape)
     whole = lax.all_to_all(spread, "row", 0, 0, axis_index_groups=lines, tiled=True)
     half = join(whole, side, across)
@@ -309,27 +316,18 @@
 
     def body(core_ref, mine_ref, other_ref, l_ref, w_ref, o_ref, s_ref):
         at = core_ref[0]
-        s_ref[pl.ds(pl.multiple_of(at * part, 8), part), :] = mine_ref[...]
-        s_ref[pl.ds(pl.multiple_of((1 - at) * part, 8), part), :] = other_ref[...]
-        summed = s_ref[...]
+        s_ref[pl.ds(pl.multiple_of(at * part, 16), part), :] = mine_ref[...]
+        s_ref[pl.ds(pl.multiple_of((1 - at) * part, 16), part), :] = other_ref[...]
+        pair = s_ref[...]
         label = l_ref[...]
-        shrunk = jnp.where(label != 0, summed, 0.0).astype(jnp.bfloat16).astype(jnp.float32)
-        own = shrunk[:, :rank]
+        own = pair[:, :rank].astype(jnp.float32)
         spread = jnp.concatenate([jnp.where(label == k, own, 0.0) for k in range(count)], axis=1)
         update = jnp.dot(
             spread.astype(jnp.bfloat16), w_ref[...], preferred_element_type=jnp.float32
         )
-        resident = summed[:, rank:]
-        high = resident.astype(jnp.bfloat16)
-        left = resident - high.astype(jnp.float32)
-        middle = left.astype(jnp.bfloat16)
-        low = (left - middle.astype(jnp.float32)).astype(jnp.bfloat16)
-        first = w_ref[:rank, :]
-        taken = shrunk[:, rank:].astype(jnp.bfloat16)
-        base = jnp.dot(low, first, preferred_element_type=jnp.float32)
-        base = base + jnp.dot(middle, first, preferred_element_type=jnp.float32)
-        base = base + jnp.dot(high, first, preferred_element_type=jnp.float32)
-        o_ref[...] = base + (update - jnp.dot(taken, first, preferred_element_type=jnp.float32))
+        o_ref[...] = update + jnp.dot(
+            pair[:, rank:], w_ref[:rank, :], preferred_element_type=jnp.float32
+        )
 
     vmem = pl.BlockSpec(memory_space=pltpu.VMEM)
     return pl.pallas_call(
@@ -337,11 +335,11 @@
         out_shape=jax.ShapeDtypeStruct((total, width), jnp.float32),
         in_specs=[pl.BlockSpec(memory_space=pltpu.SMEM)] + [vmem] * 4,
         out_specs=vmem,
-        scratch_shapes=[pltpu.VMEM((total, cols), jnp.float32)],
+        scratch_shapes=[pltpu.VMEM((total, cols), jnp.bfloat16)],
         cost_estimate=pl.CostEstimate(
-            flops=2 * total * (count + 4) * rank * width,
+            flops=2 * total * (count + 1) * rank * width,
             transcendentals=0,
-            bytes_accessed=2 * count * rank * width + 4 * total * (cols + width),
+            bytes_accessed=2 * count * rank * width + 2 * total * cols + 4 * total * width,
         ),
         compiler_params=pltpu.CompilerParams(vmem_limit_bytes=12 << 20),
     )(core.reshape(1), mine, other, labels[:, None], outputs.reshape(count * rank, width))

time: 176 us -> 168 us (0.955)
  waiting for transfers between devices: 94 us -> 85.8 us
  starting transfers between devices: 26.2 us -> 29.6 us
  blocking collectives: 10.9 us -> 7.98 us
    ppermute x1, waiting for transfers between devices: 11.8 us -> 1.09 us  [join(): got = lax.ppermute(part, 'row', pairs)]
    all_to_all x1, blocking collectives: 10.9 us -> 7.98 us  [sum_by_stages(): lax.all_to_all(spread, 'row', 0, 0, axis_index_groups=lines, tiled=True)]
    ppermute x16, waiting for transfers between devices: 74.7 us -> 77.3 us  [ringed(): data = lax.ppermute(send, 'row', pairs)]
    all_to_all x1, starting transfers between devices: 3.27 us -> 5.37 us  [sum_by_stages(): lax.all_to_all(rows, 'row', 0, 0, axis_index_groups=lines, tiled=True)]
  transfers between devices with their start and end apart: 38 -> 38, of which waited for: 14 -> 17; matrix products, arithmetic and copies ran while one was open for 1% -> 1% of each run, Pallas kernels for 19% -> 20%
where the time goes in v8:
time: 168 us
  waiting for transfers between devices  85.8 us (51%)
  Pallas kernels  39.6 us (24%)
  starting transfers between devices  29.6 us (18%)
  blocking collectives  7.98 us (5%)
  local copies, waits for them, and re-layouts  2.98 us (2%)
    ppermute x16, waiting for transfers between devices, ringed(): data = lax.ppermute(send, 'row', pairs)  77.3 us
    pallas_call x7, Pallas kernels, chunk_matmul(): pl.pallas_call(body, out_shape=[jax.ShapeDtypeStruct((rows, features), ou...  29.2 us
    ppermute x16, starting transfers between devices, ringed(): data = lax.ppermute(send, 'row', pairs)  17.9 us
    all_to_all x1, blocking collectives, sum_by_stages(): lax.all_to_all(spread, 'row', 0, 0, axis_index_groups=lines, tiled=True)  7.98 us
    all_to_all x1, starting transfers between devices, sum_by_stages(): lax.all_to_all(rows, 'row', 0, 0, axis_index_groups=lines, tiled=True)  5.37 us
    pallas_call x3, Pallas kernels, rows_matmul(): pl.pallas_call(body, out_shape=shape, in_specs=[vmem] * (2 * count + 1) +...  4.21 us
    all_to_all x1, waiting for transfers between devices, sum_by_stages(): lax.all_to_all(rows, 'row', 0, 0, axis_index_groups=lines, tiled=True)  3.81 us
    pallas_call x1, Pallas kernels, project_selected(): pl.pallas_call(body, out_shape=(shape, shape), in_specs=[pl.BlockSpec(mem...  3.39 us
  transfers between devices with their start and end apart: 38, of which 17 were waited for; matrix products, arithmetic and copies ran while one was open for 1% of the time, Pallas kernels for 20%

profile of v8, /device:TPU:0, one launch (start us, length us, event | category | flops | bytes accessed | tf_op | source)
XLA Modules:
  0.0 167.8 jit_solution(1676839966622751134)
XLA Ops:
  1.3 1.3 shard_map.73
  2.6 0.9 broadcast_in_dim_reshape.5.l_ref
  3.5 3.4 %shard_map.80 = (f32[192,128]{1,0:T(8,128)S(1)}, f32[192,128]{1,0:T(8,128)S(1)}) custom-call(s32[1]{0:T(128)} %bitcast.2.f_ref.core_ref, bf16[384,896]{1,0:T(8,128)(2,1)S(1)} %get-tuple-element.29.refs_0_.low_ref, bf16[384,896]{1,0:T(8,128)(2,1)S(1)} %get-tuple-element.30.refs_1_.high_ref, s32[384,1]{1,0:T(8,128)S(1)} %broadcast_in_dim_reshape.5.l_ref, ...), custom_call_target="tpu_custom_call" | custom-call | flops 704643072 | bytes 3407872 | tf_op jit(solution)/shard_map/pallas_call | solution.py:94
  8.4 2.9 %collective-permute-start.30 = (f32[96,128]{1,0:T(8,128)S(1)}, f32[96,128]{1,0:T(8,128)S(1)}, u32[]{:S(2)}, u32[]{:S(2)}) collective-permute-start(f32[96,128]{1,0:T(8,128)S(1)} %slice_select_fusion), channel_id=1, source_target_pairs={{0,2},{1,3},{4,6},{5,7},{8,10},{9,11},{12,14},{13,15},{14,12},{15,... | collective-permute-start | bytes 147464 | tf_op jit(solution)/shard_map/ppermute | solution.py:161
  11.4 2.1 %collective-permute-done.30 = f32[96,128]{1,0:T(8,128)S(1)} collective-permute-done((f32[96,128]{1,0:T(8,128)S(1)}, f32[96,128]{1,0:T(8,128)S(1)}, u32[]{:S(2)}, u32[]{:S(2)}) %collective-permute-start.30) | collective-permute-done | bytes 49184 | tf_op jit(solution)/shard_map/ppermute | solution.py:161
  14.1 5.4 %all-to-all-start = ((f32[4,24,128]{2,1,0:T(8,128)}), f32[4,24,128]{2,1,0:T(8,128)S(1)}, u32[]{:S(2)}, u32[]{:S(2)}) async-start(f32[4,24,128]{2,1,0:T(8,128)} %bitcast.5), calls=%async_computation | async-start | bytes 98304 | tf_op jit(solution)/shard_map/all_to_all | solution.py:182
  19.4 2.0 %collective-permute-start = (bf16[384,896]{1,0:T(8,128)(2,1)S(1)}, bf16[384,896]{1,0:T(8,128)(2,1)}, u32[]{:S(2)}, u32[]{:S(2)}) collective-permute-start(bf16[384,896]{1,0:T(8,128)(2,1)S(1)} %get-tuple-element.29.refs_0_.low_ref), channel_id=1, source_target_pairs={{0,4},{1,3},{4,8},{5,1},{8,12},{9,5},{12,14},{13,9},{14,10},{15,13... | collective-permute-start | bytes 2064392 | tf_op jit(solution)/shard_map/ppermute | solution.py:406
  21.5 3.8 %all-to-all-done = f32[4,24,128]{2,1,0:T(8,128)S(1)} async-done(((f32[4,24,128]{2,1,0:T(8,128)}), f32[4,24,128]{2,1,0:T(8,128)S(1)}, u32[]{:S(2)}, u32[]{:S(2)}) %all-to-all-start) | async-done | bytes 49184 | tf_op jit(solution)/shard_map/all_to_all | solution.py:182
  25.5 8.0 %all_to_all.18 = bf16[4,24,128]{2,1,0:T(8,128)(2,1)S(1)} all-to-all(bf16[4,24,128]{2,1,0:T(8,128)(2,1)S(1)} %broadcast_in_dim.2), channel_id=1, replica_groups={{0,4,8,12},{1,5,9,13},{14,10,6,2},{15,11,7,3},{16,20,24,28},{17,21,25,2..., dimensions={0} | all-to-all | bytes 49152 | tf_op jit(solution)/shard_map/all_to_all | solution.py:185
  33.4 1.0 collective-permute-start.31
  34.4 1.1 collective-permute-start.5
  35.5 1.0 collective-permute-start.10
  36.4 1.1 collective-permute-done.31
  37.6 1.2 collective-permute-done.32.other_ref
  38.8 1.0 collective-permute-start.14
  39.8 11.7 %collective-permute-done.5.refs_2_ = bf16[384,896]{1,0:T(8,128)(2,1)S(1)} collective-permute-done((bf16[384,896]{1,0:T(8,128)(2,1)S(1)}, bf16[384,896]{1,0:T(8,128)(2,1)S(1)}, u32[]{:S(2)}, u32[]{:S(2)}) %collective-permute-start.5) | collective-permute-done | bytes 688160 | tf_op jit(solution)/shard_map/ppermute | solution.py:406
  51.5 2.3 %collective-permute-done.10.refs_0_ = bf16[384,896]{1,0:T(8,128)(2,1)S(1)} collective-permute-done((bf16[384,896]{1,0:T(8,128)(2,1)S(1)}, bf16[384,896]{1,0:T(8,128)(2,1)S(1)}, u32[]{:S(2)}, u32[]{:S(2)}) %collective-permute-start.10) | collective-permute-done | bytes 688160 | tf_op jit(solution)/shard_map/ppermute | solution.py:406
  53.8 5.1 %collective-permute-done.14.refs_2_ = bf16[384,896]{1,0:T(8,128)(2,1)S(1)} collective-permute-done((bf16[384,896]{1,0:T(8,128)(2,1)S(1)}, bf16[384,896]{1,0:T(8,128)(2,1)S(1)}, u32[]{:S(2)}, u32[]{:S(2)}) %collective-permute-start.14) | collective-permute-done | bytes 688160 | tf_op jit(solution)/shard_map/ppermute | solution.py:406
  58.9 1.1 collective-permute-start.1
  60.0 0.9 collective-permute-start.6
  60.9 1.2 collective-permute-start.11
  62.1 0.9 collective-permute-start.15
  63.0 14.4 %collective-permute-done.1.refs_0_ = bf16[384,896]{1,0:T(8,128)(2,1)S(1)} collective-permute-done((bf16[384,896]{1,0:T(8,128)(2,1)}, bf16[384,896]{1,0:T(8,128)(2,1)S(1)}, u32[]{:S(2)}, u32[]{:S(2)}) %collective-permute-start.1) | collective-permute-done | bytes 688160 | tf_op jit(solution)/shard_map/ppermute | solution.py:406
  77.4 0.9 collective-permute-done.6.refs_2_
  78.3 1.3 collective-permute-start.2
  79.7 11.3 %collective-permute-done.11.refs_0_ = bf16[384,896]{1,0:T(8,128)(2,1)S(1)} collective-permute-done((bf16[384,896]{1,0:T(8,128)(2,1)S(1)}, bf16[384,896]{1,0:T(8,128)(2,1)S(1)}, u32[]{:S(2)}, u32[]{:S(2)}) %collective-permute-start.11) | collective-permute-done | bytes 688160 | tf_op jit(solution)/shard_map/ppermute | solution.py:406
  90.9 2.1 %collective-permute-done.15.refs_2_ = bf16[384,896]{1,0:T(8,128)(2,1)S(1)} collective-permute-done((bf16[384,896]{1,0:T(8,128)(2,1)S(1)}, bf16[384,896]{1,0:T(8,128)(2,1)S(1)}, u32[]{:S(2)}, u32[]{:S(2)}) %collective-permute-start.15) | collective-permute-done | bytes 688160 | tf_op jit(solution)/shard_map/ppermute | solution.py:406
  93.1 0.9 collective-permute-start.7
  94.0 1.2 collective-permute-start.12
  95.2 7.4 %collective-permute-done.2.refs_0_ = bf16[384,896]{1,0:T(8,128)(2,1)S(1)} collective-permute-done((bf16[384,896]{1,0:T(8,128)(2,1)S(1)}, bf16[384,896]{1,0:T(8,128)(2,1)S(1)}, u32[]{:S(2)}, u32[]{:S(2)}) %collective-permute-start.2) | collective-permute-done | bytes 688160 | tf_op jit(solution)/shard_map/ppermute | solution.py:406
  103.3 1.4 collective-permute-start.3
  104.7 6.6 %collective-permute-done.7.refs_2_ = bf16[384,896]{1,0:T(8,128)(2,1)S(1)} collective-permute-done((bf16[384,896]{1,0:T(8,128)(2,1)S(1)}, bf16[384,896]{1,0:T(8,128)(2,1)S(1)}, u32[]{:S(2)}, u32[]{:S(2)}) %collective-permute-start.7) | collective-permute-done | bytes 688160 | tf_op jit(solution)/shard_map/ppermute | solution.py:406
  111.4 1.3 collective-permute-start.33
  113.5 3.8 %collective-permute-done.12.refs_0_ = bf16[384,896]{1,0:T(8,128)(2,1)S(1)} collective-permute-done((bf16[384,896]{1,0:T(8,128)(2,1)S(1)}, bf16[384,896]{1,0:T(8,128)(2,1)S(1)}, u32[]{:S(2)}, u32[]{:S(2)}) %collective-permute-start.12) | collective-permute-done | bytes 688160 | tf_op jit(solution)/shard_map/ppermute | solution.py:406
  117.3 8.8 %collective-permute-done.16.refs_2_ = bf16[384,896]{1,0:T(8,128)(2,1)S(1)} collective-permute-done((bf16[384,896]{1,0:T(8,128)(2,1)S(1)}, bf16[384,896]{1,0:T(8,128)(2,1)S(1)}, u32[]{:S(2)}, u32[]{:S(2)}) %collective-permute-start.16) | collective-permute-done | bytes 688160 | tf_op jit(solution)/shard_map/ppermute | solution.py:406
  127.4 2.8 %collective-permute-done.8.refs_1_ = bf16[160,896]{1,0:T(8,128)(2,1)S(1)} collective-permute-done((bf16[160,896]{1,0:T(8,128)(2,1)S(1)}, bf16[160,896]{1,0:T(8,128)(2,1)S(1)}, u32[]{:S(2)}, u32[]{:S(2)}) %collective-permute-start.8) | collective-permute-done | bytes 286752 | tf_op jit(solution)/shard_map/ppermute | solution.py:406
  130.1 1.2 collective-permute-start.35
  131.4 1.5 shard_map.81.refs_10_
  132.9 3.8 %shard_map.74.refs_5_ = f32[384,512]{1,0:T(8,128)S(1)} custom-call(s32[35]{0:T(128)S(1)} %dynamic-slice_bitcast_fusion.starts_ref, bf16[384,896]{1,0:T(8,128)(2,1)S(1)} %get-tuple-element.29.refs_0_.low_ref, bf16[384,896]{1,0:T(8,128)(2,1)S(1)} %get-tuple-element.30.refs_1_.high_ref, bf16[384,1792]{1,0:T(8,128)(2,1)S(1)} %collective-permute-done.28.refs_2_, ...), custom_call_target="tpu_custom_call" | custom-call | flops 1409286144 | bytes 7995392 | tf_op jit(solution)/shard_map/pallas_call | solution.py:249
  136.8 4.6 %shard_map.75.refs_5_ = f32[384,512]{1,0:T(8,128)S(1)} custom-call(s32[35]{0:T(128)S(1)} %dynamic-slice_bitcast_fusion.starts_ref, bf16[384,896]{1,0:T(8,128)(2,1)} %collective-permute-done.refs_0_, bf16[384,896]{1,0:T(8,128)(2,1)S(1)} %collective-permute-done.26.refs_1_, bf16[384,896]{1,0:T(8,128)(2,1)S(1)} %collective-permute-done.5.refs_2_, ...), custom_call_target="tpu_custom_call" | custom-call | flops 1409286144 | bytes 7995392 | tf_op jit(solution)/shard_map/pallas_call | solution.py:249
  141.4 4.0 %shard_map.76.refs_5_ = f32[384,512]{1,0:T(8,128)S(1)} custom-call(s32[35]{0:T(128)S(1)} %dynamic-slice_bitcast_fusion.starts_ref, bf16[384,896]{1,0:T(8,128)(2,1)S(1)} %collective-permute-done.10.refs_0_, bf16[384,896]{1,0:T(8,128)(2,1)S(1)} %collective-permute-done.24.refs_1_, bf16[384,896]{1,0:T(8,128)(2,1)S(1)} %collective-permute-done.14.refs_2_, ...), custom_call_target="tpu_custom_call" | custom-call | flops 1409286144 | bytes 7995392 | tf_op jit(solution)/shard_map/pallas_call | solution.py:249
  146.1 4.4 %shard_map.77 = (f32[384,512]{1,0:T(8,128)S(1)}, bf16[512,896]{1,0:T(8,128)(2,1)S(1)}, bf16[512,896]{1,0:T(8,128)(2,1)S(1)}, bf16[512,896]{1,0:T(8,128)(2,1)S(1)}, bf16[512,896]{1,0:T(8,128)(2,1)S(1)}) custom-call(s32[35]{0:T(128)S(1)} %dynamic-slice_bitcast_fusion.starts_ref, bf16[384,896]{1,0:T(8,128)(2,1)S(1)} %collective-permute-done.1.refs_0_, ...), custom_call_target="tpu_custom_call" | custom-call | flops 1409286144 | bytes 11665408 | tf_op jit(solution)/shard_map/pallas_call | solution.py:249
  151.0 4.1 %shard_map.78 = (f32[384,512]{1,0:T(8,128)S(1)}, bf16[512,896]{1,0:T(8,128)(2,1)S(1)}, bf16[512,896]{1,0:T(8,128)(2,1)S(1)}, bf16[512,896]{1,0:T(8,128)(2,1)S(1)}, bf16[512,896]{1,0:T(8,128)(2,1)S(1)}) custom-call(s32[35]{0:T(128)S(1)} %dynamic-slice_bitcast_fusion.starts_ref, bf16[384,896]{1,0:T(8,128)(2,1)S(1)} %collective-permute-done.11.refs_0_, ...), custom_call_target="tpu_custom_call" | custom-call | flops 1409286144 | bytes 11665408 | tf_op jit(solution)/shard_map/pallas_call | solution.py:249
  155.2 4.1 %shard_map.79 = (f32[384,512]{1,0:T(8,128)S(1)}, bf16[512,896]{1,0:T(8,128)(2,1)S(1)}, bf16[512,896]{1,0:T(8,128)(2,1)S(1)}, bf16[512,896]{1,0:T(8,128)(2,1)S(1)}, bf16[512,896]{1,0:T(8,128)(2,1)S(1)}) custom-call(s32[35]{0:T(128)S(1)} %dynamic-slice_bitcast_fusion.starts_ref, bf16[384,896]{1,0:T(8,128)(2,1)S(1)} %collective-permute-done.2.refs_0_, ...), custom_call_target="tpu_custom_call" | custom-call | flops 1409286144 | bytes 11665408 | tf_op jit(solution)/shard_map/pallas_call | solution.py:249
  159.3 4.1 %shard_map.82 = (f32[384,512]{1,0:T(8,128)S(1)}, bf16[512,896]{1,0:T(8,128)(2,1)S(1)}, bf16[512,896]{1,0:T(8,128)(2,1)S(1)}, bf16[512,896]{1,0:T(8,128)(2,1)S(1)}, bf16[512,896]{1,0:T(8,128)(2,1)S(1)}) custom-call(s32[35]{0:T(128)S(1)} %dynamic-slice_bitcast_fusion.starts_ref, bf16[384,896]{1,0:T(8,128)(2,1)S(1)} %collective-permute-done.12.refs_0_, ...), custom_call_target="tpu_custom_call" | custom-call | flops 1409286144 | bytes 11665408 | tf_op jit(solution)/shard_map/pallas_call | solution.py:249
  163.4 0.8 shard_map.83.refs_4_
  164.2 2.0 %shard_map.84.refs_5_ = bf16[384,512]{1,0:T(8,128)(2,1)} custom-call(bf16[224,896]{1,0:T(8,128)(2,1)S(1)} %collective-permute-done.33.refs_0_, bf16[224,896]{1,0:T(8,128)(2,1)S(1)} %collective-permute-done.34.refs_1_, bf16[224,896]{1,0:T(8,128)(2,1)S(1)} %collective-permute-done.35.refs_2_, bf16[224,896]{1,0:T(8,128)(2,1)S(1)} %collective-permute-done.36.refs_3_, ...), custom_call_target="tpu_custom_call" | custom-call | tf_op jit(solution)/shard_map/pallas_call | solution.py:301
  166.3 1.4 shard_map.85
  (62 shorter events, 7.2 us)
Async XLA Ops:
  6.9 1.5 collective-permute-start.29
  8.4 123.0 %copy-start = (bf16[8,64,512]{2,1,0:T(8,128)(2,1)S(1)}, bf16[8,64,512]{2,1,0:T(8,128)(2,1)}, u32[]{:S(2)}) copy-start(bf16[8,64,512]{2,1,0:T(8,128)(2,1)} %param.10) | copy-start | bytes 1572868
  8.4 5.0 %collective-permute-start.30 = (f32[96,128]{1,0:T(8,128)S(1)}, f32[96,128]{1,0:T(8,128)S(1)}, u32[]{:S(2)}, u32[]{:S(2)}) collective-permute-start(f32[96,128]{1,0:T(8,128)S(1)} %slice_select_fusion), channel_id=1, source_target_pairs={{0,2},{1,3},{4,6},{5,7},{8,10},{9,11},{12,14},{13,15},{14,12},{15,... | collective-permute-start | bytes 147464 | tf_op jit(solution)/shard_map/ppermute | solution.py:161
  14.1 11.2 %all-to-all-start = ((f32[4,24,128]{2,1,0:T(8,128)}), f32[4,24,128]{2,1,0:T(8,128)S(1)}, u32[]{:S(2)}, u32[]{:S(2)}) async-start(f32[4,24,128]{2,1,0:T(8,128)} %bitcast.5), calls=%async_computation | async-start | bytes 98304 | tf_op jit(solution)/shard_map/all_to_all | solution.py:182
  19.4 40.6 %collective-permute-start.28 = (bf16[384,1792]{1,0:T(8,128)(2,1)}, bf16[384,1792]{1,0:T(8,128)(2,1)S(1)}, u32[]{:S(2)}, u32[]{:S(2)}) collective-permute-start(bf16[384,1792]{1,0:T(8,128)(2,1)} %bitcast.15), channel_id=1, source_target_pairs={{0,1},{1,0},{4,5},{5,4},{8,9},{9,8},{12,13},{13,12},{14,15},{15,14... | collective-permute-start | bytes 4128776 | tf_op jit(solution)/shard_map/ppermute | solution.py:397
  19.4 20.4 %collective-permute-start = (bf16[384,896]{1,0:T(8,128)(2,1)S(1)}, bf16[384,896]{1,0:T(8,128)(2,1)}, u32[]{:S(2)}, u32[]{:S(2)}) collective-permute-start(bf16[384,896]{1,0:T(8,128)(2,1)S(1)} %get-tuple-element.29.refs_0_.low_ref), channel_id=1, source_target_pairs={{0,4},{1,3},{4,8},{5,1},{8,12},{9,5},{12,14},{13,9},{14,10},{15,13... | collective-permute-start | bytes 2064392 | tf_op jit(solution)/shard_map/ppermute | solution.py:406
  33.4 4.1 %collective-permute-start.31 = (bf16[96,128]{1,0:T(8,128)(2,1)S(1)}, bf16[96,128]{1,0:T(8,128)(2,1)S(1)}, u32[]{:S(2)}, u32[]{:S(2)}) collective-permute-start(bf16[96,128]{1,0:T(8,128)(2,1)S(1)} %bitcast.16), channel_id=1, source_target_pairs={{0,2},{1,3},{4,6},{5,7},{8,10},{9,11},{12,14},{13,15},{14,12},{15,... | collective-permute-start | bytes 73736 | tf_op jit(solution)/shard_map/ppermute | solution.py:166
  34.4 17.1 %collective-permute-start.5 = (bf16[384,896]{1,0:T(8,128)(2,1)S(1)}, bf16[384,896]{1,0:T(8,128)(2,1)S(1)}, u32[]{:S(2)}, u32[]{:S(2)}) collective-permute-start(bf16[384,896]{1,0:T(8,128)(2,1)S(1)} %get-tuple-element.30.refs_1_.high_ref), channel_id=1, source_target_pairs={{4,0},{3,1},{8,4},{1,5},{12,8},{5,9},{14,12},{9,13},{10,14},{13,15... | collective-permute-start | bytes 2064392 | tf_op jit(solution)/shard_map/ppermute | solution.py:406
  35.5 18.3 %collective-permute-start.10 = (bf16[384,896]{1,0:T(8,128)(2,1)S(1)}, bf16[384,896]{1,0:T(8,128)(2,1)S(1)}, u32[]{:S(2)}, u32[]{:S(2)}) collective-permute-start(bf16[384,896]{1,0:T(8,128)(2,1)S(1)} %get-tuple-element.30.refs_1_.high_ref), channel_id=1, source_target_pairs={{0,4},{1,3},{4,8},{5,1},{8,12},{9,5},{12,14},{13,9},{14,10},{15,13... | collective-permute-start | bytes 2064392 | tf_op jit(solution)/shard_map/ppermute | solution.py:406
  37.5 1.3 collective-permute-start.32
  38.8 20.0 %collective-permute-start.14 = (bf16[384,896]{1,0:T(8,128)(2,1)S(1)}, bf16[384,896]{1,0:T(8,128)(2,1)S(1)}, u32[]{:S(2)}, u32[]{:S(2)}) collective-permute-start(bf16[384,896]{1,0:T(8,128)(2,1)S(1)} %get-tuple-element.29.refs_0_.low_ref), channel_id=1, source_target_pairs={{4,0},{3,1},{8,4},{1,5},{12,8},{5,9},{14,12},{9,13},{10,14},{13,15... | collective-permute-start | bytes 2064392 | tf_op jit(solution)/shard_map/ppermute | solution.py:406
  39.8 21.1 %collective-permute-start.26 = (bf16[384,896]{1,0:T(8,128)(2,1)}, bf16[384,896]{1,0:T(8,128)(2,1)S(1)}, u32[]{:S(2)}, u32[]{:S(2)}) collective-permute-start(bf16[384,896]{1,0:T(8,128)(2,1)} %collective-permute-done.refs_0_), channel_id=1, source_target_pairs={{0,1},{1,0},{4,5},{5,4},{8,9},{9,8},{12,13},{13,12},{14,15},{15,14... | collective-permute-start | bytes 2064392 | tf_op jit(solution)/shard_map/ppermute | solution.py:409
  51.5 9.4 %collective-permute-start.27 = (bf16[384,896]{1,0:T(8,128)(2,1)S(1)}, bf16[384,896]{1,0:T(8,128)(2,1)S(1)}, u32[]{:S(2)}, u32[]{:S(2)}) collective-permute-start(bf16[384,896]{1,0:T(8,128)(2,1)S(1)} %collective-permute-done.5.refs_2_), channel_id=1, source_target_pairs={{0,1},{1,0},{4,5},{5,4},{8,9},{9,8},{12,13},{13,12},{14,15},{15,14... | collective-permute-start | bytes 2064392 | tf_op jit(solution)/shard_map/ppermute | solution.py:409
  53.8 8.3 %collective-permute-start.24 = (bf16[384,896]{1,0:T(8,128)(2,1)S(1)}, bf16[384,896]{1,0:T(8,128)(2,1)S(1)}, u32[]{:S(2)}, u32[]{:S(2)}) collective-permute-start(bf16[384,896]{1,0:T(8,128)(2,1)S(1)} %collective-permute-done.10.refs_0_), channel_id=1, source_target_pairs={{0,1},{1,0},{4,5},{5,4},{8,9},{9,8},{12,13},{13,12},{14,15},{15,14... | collective-permute-start | bytes 2064392 | tf_op jit(solution)/shard_map/ppermute | solution.py:409
  58.9 18.5 %collective-permute-start.1 = (bf16[384,896]{1,0:T(8,128)(2,1)}, bf16[384,896]{1,0:T(8,128)(2,1)S(1)}, u32[]{:S(2)}, u32[]{:S(2)}) collective-permute-start(bf16[384,896]{1,0:T(8,128)(2,1)} %collective-permute-done.refs_0_), channel_id=1, source_target_pairs={{0,4},{1,3},{4,8},{5,1},{8,12},{9,5},{12,14},{13,9},{14,10},{15,13... | collective-permute-start | bytes 2064392 | tf_op jit(solution)/shard_map/ppermute | solution.py:406
  60.0 18.3 %collective-permute-start.6 = (bf16[384,896]{1,0:T(8,128)(2,1)S(1)}, bf16[384,896]{1,0:T(8,128)(2,1)S(1)}, u32[]{:S(2)}, u32[]{:S(2)}) collective-permute-start(bf16[384,896]{1,0:T(8,128)(2,1)S(1)} %collective-permute-done.5.refs_2_), channel_id=1, source_target_pairs={{4,0},{3,1},{8,4},{1,5},{12,8},{5,9},{14,12},{9,13},{10,14},{13,15... | collective-permute-start | bytes 2064392 | tf_op jit(solution)/shard_map/ppermute | solution.py:406
  60.9 17.4 %collective-permute-start.25 = (bf16[384,896]{1,0:T(8,128)(2,1)S(1)}, bf16[384,896]{1,0:T(8,128)(2,1)S(1)}, u32[]{:S(2)}, u32[]{:S(2)}) collective-permute-start(bf16[384,896]{1,0:T(8,128)(2,1)S(1)} %collective-permute-done.14.refs_2_), channel_id=1, source_target_pairs={{0,1},{1,0},{4,5},{5,4},{8,9},{9,8},{12,13},{13,12},{14,15},{15,14... | collective-permute-start | bytes 2064392 | tf_op jit(solution)/shard_map/ppermute | solution.py:409
  60.9 30.0 %collective-permute-start.11 = (bf16[384,896]{1,0:T(8,128)(2,1)S(1)}, bf16[384,896]{1,0:T(8,128)(2,1)S(1)}, u32[]{:S(2)}, u32[]{:S(2)}) collective-permute-start(bf16[384,896]{1,0:T(8,128)(2,1)S(1)} %collective-permute-done.10.refs_0_), channel_id=1, source_target_pairs={{0,4},{1,3},{4,8},{5,1},{8,12},{9,5},{12,14},{13,9},{14,10},{15,13... | collective-permute-start | bytes 2064392 | tf_op jit(solution)/shard_map/ppermute | solution.py:406
  62.1 31.0 %collective-permute-start.15 = (bf16[384,896]{1,0:T(8,128)(2,1)S(1)}, bf16[384,896]{1,0:T(8,128)(2,1)S(1)}, u32[]{:S(2)}, u32[]{:S(2)}) collective-permute-start(bf16[384,896]{1,0:T(8,128)(2,1)S(1)} %collective-permute-done.14.refs_2_), channel_id=1, source_target_pairs={{4,0},{3,1},{8,4},{1,5},{12,8},{5,9},{14,12},{9,13},{10,14},{13,15... | collective-permute-start | bytes 2064392 | tf_op jit(solution)/shard_map/ppermute | solution.py:406
  77.4 16.6 %collective-permute-start.22 = (bf16[384,896]{1,0:T(8,128)(2,1)S(1)}, bf16[384,896]{1,0:T(8,128)(2,1)S(1)}, u32[]{:S(2)}, u32[]{:S(2)}) collective-permute-start(bf16[384,896]{1,0:T(8,128)(2,1)S(1)} %collective-permute-done.1.refs_0_), channel_id=1, source_target_pairs={{0,1},{1,0},{4,5},{5,4},{8,9},{9,8},{12,13},{13,12},{14,15},{15,14... | collective-permute-start | bytes 2064392 | tf_op jit(solution)/shard_map/ppermute | solution.py:409
  78.3 15.7 %collective-permute-start.23 = (bf16[384,896]{1,0:T(8,128)(2,1)S(1)}, bf16[384,896]{1,0:T(8,128)(2,1)S(1)}, u32[]{:S(2)}, u32[]{:S(2)}) collective-permute-start(bf16[384,896]{1,0:T(8,128)(2,1)S(1)} %collective-permute-done.6.refs_2_), channel_id=1, source_target_pairs={{0,1},{1,0},{4,5},{5,4},{8,9},{9,8},{12,13},{13,12},{14,15},{15,14... | collective-permute-start | bytes 2064392 | tf_op jit(solution)/shard_map/ppermute | solution.py:409
  78.3 24.3 %collective-permute-start.2 = (bf16[384,896]{1,0:T(8,128)(2,1)S(1)}, bf16[384,896]{1,0:T(8,128)(2,1)S(1)}, u32[]{:S(2)}, u32[]{:S(2)}) collective-permute-start(bf16[384,896]{1,0:T(8,128)(2,1)S(1)} %collective-permute-done.1.refs_0_), channel_id=1, source_target_pairs={{0,4},{1,3},{4,8},{5,1},{8,12},{9,5},{12,14},{13,9},{14,10},{15,13... | collective-permute-start | bytes 2064392 | tf_op jit(solution)/shard_map/ppermute | solution.py:406
  90.9 12.4 %collective-permute-start.20 = (bf16[384,896]{1,0:T(8,128)(2,1)S(1)}, bf16[384,896]{1,0:T(8,128)(2,1)S(1)}, u32[]{:S(2)}, u32[]{:S(2)}) collective-permute-start(bf16[384,896]{1,0:T(8,128)(2,1)S(1)} %collective-permute-done.11.refs_0_), channel_id=1, source_target_pairs={{0,1},{1,0},{4,5},{5,4},{8,9},{9,8},{12,13},{13,12},{14,15},{15,14... | collective-permute-start | bytes 2064392 | tf_op jit(solution)/shard_map/ppermute | solution.py:409
  93.1 18.3 %collective-permute-start.7 = (bf16[384,896]{1,0:T(8,128)(2,1)S(1)}, bf16[384,896]{1,0:T(8,128)(2,1)S(1)}, u32[]{:S(2)}, u32[]{:S(2)}) collective-permute-start(bf16[384,896]{1,0:T(8,128)(2,1)S(1)} %collective-permute-done.6.refs_2_), channel_id=1, source_target_pairs={{4,0},{3,1},{8,4},{1,5},{12,8},{5,9},{14,12},{9,13},{10,14},{13,15... | collective-permute-start | bytes 2064392 | tf_op jit(solution)/shard_map/ppermute | solution.py:406
  94.0 18.8 %collective-permute-start.21 = (bf16[384,896]{1,0:T(8,128)(2,1)S(1)}, bf16[384,896]{1,0:T(8,128)(2,1)S(1)}, u32[]{:S(2)}, u32[]{:S(2)}) collective-permute-start(bf16[384,896]{1,0:T(8,128)(2,1)S(1)} %collective-permute-done.15.refs_2_), channel_id=1, source_target_pairs={{0,1},{1,0},{4,5},{5,4},{8,9},{9,8},{12,13},{13,12},{14,15},{15,14... | collective-permute-start | bytes 2064392 | tf_op jit(solution)/shard_map/ppermute | solution.py:409
  94.0 23.4 %collective-permute-start.12 = (bf16[384,896]{1,0:T(8,128)(2,1)S(1)}, bf16[384,896]{1,0:T(8,128)(2,1)S(1)}, u32[]{:S(2)}, u32[]{:S(2)}) collective-permute-start(bf16[384,896]{1,0:T(8,128)(2,1)S(1)} %collective-permute-done.11.refs_0_), channel_id=1, source_target_pairs={{0,4},{1,3},{4,8},{5,1},{8,12},{9,5},{12,14},{13,9},{14,10},{15,13... | collective-permute-start | bytes 2064392 | tf_op jit(solution)/shard_map/ppermute | solution.py:406
  102.6 23.5 %collective-permute-start.16 = (bf16[384,896]{1,0:T(8,128)(2,1)S(1)}, bf16[384,896]{1,0:T(8,128)(2,1)S(1)}, u32[]{:S(2)}, u32[]{:S(2)}) collective-permute-start(bf16[384,896]{1,0:T(8,128)(2,1)S(1)} %collective-permute-done.15.refs_2_), channel_id=1, source_target_pairs={{4,0},{3,1},{8,4},{1,5},{12,8},{5,9},{14,12},{9,13},{10,14},{13,15... | collective-permute-start | bytes 2064392 | tf_op jit(solution)/shard_map/ppermute | solution.py:406
  103.3 22.8 %collective-permute-start.3 = (bf16[160,896]{1,0:T(8,128)(2,1)S(1)}, bf16[160,896]{1,0:T(8,128)(2,1)S(1)}, u32[]{:S(2)}, u32[]{:S(2)}) collective-permute-start(bf16[160,896]{1,0:T(8,128)(2,1)S(1)} %slice.46), channel_id=1, source_target_pairs={{0,4},{1,3},{4,8},{5,1},{8,12},{9,5},{12,14},{13,9},{14,10},{15,13... | collective-permute-start | bytes 860168 | tf_op jit(solution)/shard_map/ppermute | solution.py:406
  111.4 21.5 %collective-permute-start.33 = (bf16[224,896]{1,0:T(8,128)(2,1)S(1)}, bf16[224,896]{1,0:T(8,128)(2,1)S(1)}, u32[]{:S(2)}, u32[]{:S(2)}) collective-permute-start(bf16[224,896]{1,0:T(8,128)(2,1)S(1)} %slice.52), channel_id=1, source_target_pairs={{0,4},{1,3},{4,8},{5,1},{8,12},{9,5},{12,14},{13,9},{14,10},{15,13... | collective-permute-start | bytes 1204232 | tf_op jit(solution)/shard_map/ppermute | solution.py:406
  112.7 17.4 %collective-permute-start.8 = (bf16[160,896]{1,0:T(8,128)(2,1)S(1)}, bf16[160,896]{1,0:T(8,128)(2,1)S(1)}, u32[]{:S(2)}, u32[]{:S(2)}) collective-permute-start(bf16[160,896]{1,0:T(8,128)(2,1)S(1)} %slice.47), channel_id=1, source_target_pairs={{4,0},{3,1},{8,4},{1,5},{12,8},{5,9},{14,12},{9,13},{10,14},{13,15... | collective-permute-start | bytes 860168 | tf_op jit(solution)/shard_map/ppermute | solution.py:406
  117.3 28.7 %collective-permute-start.18 = (bf16[384,896]{1,0:T(8,128)(2,1)S(1)}, bf16[384,896]{1,0:T(8,128)(2,1)S(1)}, u32[]{:S(2)}, u32[]{:S(2)}) collective-permute-start(bf16[384,896]{1,0:T(8,128)(2,1)S(1)} %collective-permute-done.2.refs_0_), channel_id=1, source_target_pairs={{0,1},{1,0},{4,5},{5,4},{8,9},{9,8},{12,13},{13,12},{14,15},{15,14... | collective-permute-start | bytes 2064392 | tf_op jit(solution)/shard_map/ppermute | solution.py:409
  126.1 24.3 %collective-permute-start.19 = (bf16[384,896]{1,0:T(8,128)(2,1)S(1)}, bf16[384,896]{1,0:T(8,128)(2,1)S(1)}, u32[]{:S(2)}, u32[]{:S(2)}) collective-permute-start(bf16[384,896]{1,0:T(8,128)(2,1)S(1)} %collective-permute-done.7.refs_2_), channel_id=1, source_target_pairs={{0,1},{1,0},{4,5},{5,4},{8,9},{9,8},{12,13},{13,12},{14,15},{15,14... | collective-permute-start | bytes 2064392 | tf_op jit(solution)/shard_map/ppermute | solution.py:409
  126.1 24.8 %collective-permute-start.13 = (bf16[384,896]{1,0:T(8,128)(2,1)S(1)}, bf16[384,896]{1,0:T(8,128)(2,1)S(1)}, u32[]{:S(2)}, u32[]{:S(2)}) collective-permute-start(bf16[384,896]{1,0:T(8,128)(2,1)S(1)} %collective-permute-done.12.refs_0_), channel_id=1, source_target_pairs={{0,1},{1,0},{4,5},{5,4},{8,9},{9,8},{12,13},{13,12},{14,15},{15,14... | collective-permute-start | bytes 2064392 | tf_op jit(solution)/shard_map/ppermute | solution.py:409
  130.1 15.3 %collective-permute-start.35 = (bf16[224,896]{1,0:T(8,128)(2,1)S(1)}, bf16[224,896]{1,0:T(8,128)(2,1)S(1)}, u32[]{:S(2)}, u32[]{:S(2)}) collective-permute-start(bf16[224,896]{1,0:T(8,128)(2,1)S(1)} %slice.53), channel_id=1, source_target_pairs={{4,0},{3,1},{8,4},{1,5},{12,8},{5,9},{14,12},{9,13},{10,14},{13,15... | collective-permute-start | bytes 1204232 | tf_op jit(solution)/shard_map/ppermute | solution.py:406
  132.9 26.5 %collective-permute-start.17 = (bf16[384,896]{1,0:T(8,128)(2,1)S(1)}, bf16[384,896]{1,0:T(8,128)(2,1)S(1)}, u32[]{:S(2)}, u32[]{:S(2)}) collective-permute-start(bf16[384,896]{1,0:T(8,128)(2,1)S(1)} %collective-permute-done.16.refs_2_), channel_id=1, source_target_pairs={{0,1},{1,0},{4,5},{5,4},{8,9},{9,8},{12,13},{13,12},{14,15},{15,14... | collective-permute-start | bytes 2064392 | tf_op jit(solution)/shard_map/ppermute | solution.py:409
  145.4 18.7 %collective-permute-start.34 = (bf16[224,896]{1,0:T(8,128)(2,1)S(1)}, bf16[224,896]{1,0:T(8,128)(2,1)S(1)}, u32[]{:S(2)}, u32[]{:S(2)}) collective-permute-start(bf16[224,896]{1,0:T(8,128)(2,1)S(1)} %collective-permute-done.33.refs_0_), channel_id=1, source_target_pairs={{0,1},{1,0},{4,5},{5,4},{8,9},{9,8},{12,13},{13,12},{14,15},{15,14... | collective-permute-start | bytes 1204232 | tf_op jit(solution)/shard_map/ppermute | solution.py:409
  146.0 18.2 %collective-permute-start.36 = (bf16[224,896]{1,0:T(8,128)(2,1)S(1)}, bf16[224,896]{1,0:T(8,128)(2,1)S(1)}, u32[]{:S(2)}, u32[]{:S(2)}) collective-permute-start(bf16[224,896]{1,0:T(8,128)(2,1)S(1)} %collective-permute-done.35.refs_2_), channel_id=1, source_target_pairs={{0,1},{1,0},{4,5},{5,4},{8,9},{9,8},{12,13},{13,12},{14,15},{15,14... | collective-permute-start | bytes 1204232 | tf_op jit(solution)/shard_map/ppermute | solution.py:409
  150.5 15.8 %collective-permute-start.4 = (bf16[160,896]{1,0:T(8,128)(2,1)S(1)}, bf16[160,896]{1,0:T(8,128)(2,1)S(1)}, u32[]{:S(2)}, u32[]{:S(2)}) collective-permute-start(bf16[160,896]{1,0:T(8,128)(2,1)S(1)} %collective-permute-done.3.refs_0_), channel_id=1, source_target_pairs={{0,1},{1,0},{4,5},{5,4},{8,9},{9,8},{12,13},{13,12},{14,15},{15,14... | collective-permute-start | bytes 860168 | tf_op jit(solution)/shard_map/ppermute | solution.py:409
  151.0 15.3 %collective-permute-start.9 = (bf16[160,896]{1,0:T(8,128)(2,1)S(1)}, bf16[160,896]{1,0:T(8,128)(2,1)S(1)}, u32[]{:S(2)}, u32[]{:S(2)}) collective-permute-start(bf16[160,896]{1,0:T(8,128)(2,1)S(1)} %collective-permute-done.8.refs_1_), channel_id=1, source_target_pairs={{0,1},{1,0},{4,5},{5,4},{8,9},{9,8},{12,13},{13,12},{14,15},{15,14... | collective-permute-start | bytes 860168 | tf_op jit(solution)/shard_map/ppermute | solution.py:409

commit v9 on v8

--- a/solution.py
+++ b/solution.py
@@ -37,7 +37,7 @@
     return pltpu.with_memory_space_constraint(array, pltpu.HBM)
 
 
-def cut_block(block, half):
+def cut_block(block, half, near=False):
     def body(x_ref, a_ref, b_ref, sem):
         copies = [
             pltpu.make_async_copy(x_ref.at[:, pl.ds(k * half, half)], out, sem.at[k])
@@ -53,11 +53,11 @@
     return pl.pallas_call(
         body,
         out_shape=(shape, shape),
-        in_specs=[pl.BlockSpec(memory_space=pltpu.HBM)],
+        in_specs=[vmem if near else pl.BlockSpec(memory_space=pltpu.HBM)],
         out_specs=(vmem, vmem),
         scratch_shapes=[pltpu.SemaphoreType.DMA((2,))],
         compiler_params=pltpu.CompilerParams(vmem_limit_bytes=4 << 20),
-    )(in_hbm(block))
+    )(block if near else in_hbm(block))
 
 
 def project_selected(rows, labels, factors, first):
@@ -268,7 +268,7 @@
 
 def row_cuts(total):
     unit = total // 24
-    return [(0, 14 * unit), (14 * unit, 10 * unit)]
+    return [(0, 12 * unit), (12 * unit, 12 * unit)]
 
 
 def rows_matmul(chunks, blocks, acc, row, out, final):
@@ -392,25 +392,29 @@
         halves = sum_by_stages(mine, other, side, partner, across, lines)
         extra = adapter_kernel(*halves, core, labels, outputs)
 
-        plan = [(s // 2 + 1, s % 2, 0, total) for s in range(2 * long - 2)]
-        plan += [(long, 0, row, rows) for row, rows in cuts]
         beside = lax.ppermute(flat, "row", partner)
         batches = [[(own[part], 0, False, part) for part in range(2)] + [(beside, 0, True, 0)]]
-        held = {"up": list(own), "down": list(own)}
-        for distance, turn, row, rows in plan:
-            found = []
-            for way, pairs, part in (("up", forward, turn), ("down", backward, 1 - turn)):
-                send = held[way][part]
-                if rows < total:
-                    send = send[row : row + rows]
-                data = lax.ppermute(send, "row", pairs)
-                if rows == total:
-                    held[way][part] = data
-                beside = lax.ppermute(data, "row", partner)
-                offset = -distance if way == "up" else distance
-                found.append((data, offset, False, part))
-                found.append((beside, offset, True, part))
+
+        def hop(data, pairs, offset, part):
+            data = lax.ppermute(data, "row", pairs)
+            beside = lax.ppermute(data, "row", partner)
+            return data, [(data, offset, False, part), (beside, offset, True, part)]
+
+        block, whole = hop(flat, forward, -1, 0)
+        ups = list(cut_block(block, half, True))
+        downs = list(own)
+        for s in range(2 * long - 2):
+            distance, turn = s // 2 + 1, s % 2
+            downs[1 - turn], found = hop(downs[1 - turn], backward, distance, 1 - turn)
+            if s == 1:
+                found = whole + found
+            elif s > 1:
+                ups[turn], more = hop(ups[turn], forward, -distance, turn)
+                found = more + found
             batches.append(found)
+        for row, rows in cuts:
+            _, found = hop(ups[0][row : row + rows], forward, -long, 0)
+            batches.append(found + hop(downs[1][row : row + rows], backward, long, 1)[1])
         order = [entry[1:] for found in batches for entry in found]
         table = np.zeros((axis_size, len(order)), np.int32)
         for p, members in enumerate(ring):
@@ -422,11 +426,11 @@
         starts = jnp.asarray(table)[me]
         acc, ready, done = [], [], 0
         ends = len(batches) - len(cuts)
-        settled = min(3, ends - 1)
+        settled = min(4, ends - 1)
         for k, found in enumerate(batches[:ends]):
             coming = batches[k + 1] if k >= settled else []
             at = done + len(found)
-            ahead = [(at + j, half) for j, _ in enumerate(coming)]
+            ahead = [(at + j, min(entry[0].shape[1], device_units)) for j, entry in enumerate(coming)]
             out, ready_next = chunk_matmul(
                 [entry[0] for entry in found],
                 starts,
@@ -476,4 +480,5 @@
         P(None, "groups"),
     )
 
+
     return jax.shard_map(local, mesh=mesh, in_specs=placed, out_specs=P(None, "groups", "row"), check_vma=False)

time: 168 us -> 161 us (0.958)
  waiting for transfers between devices: 85.8 us -> 78.2 us
    ppermute x32 -> x30, waiting for transfers between devices: 77.3 us -> 71.1 us  [the longest x15 71.1 us: hop(): data = lax.ppermute(data, 'row', pairs)]
    ppermute x32 -> x30, starting transfers between devices: 19.7 us -> 20.5 us  [the longest x15 16.7 us: hop(): data = lax.ppermute(data, 'row', pairs)]
  transfers between devices with their start and end apart: 38 -> 36, of which waited for: 17 -> 14; matrix products, arithmetic and copies ran while one was open for 1% -> 1% of each run, Pallas kernels for 20% -> 21%
where the time goes in v9:
time: 161 us; the launch traced here: 160 us
  waiting for transfers between devices  78.2 us (49%)
  Pallas kernels  39.9 us (25%)
  starting transfers between devices  30 us (19%)
  blocking collectives  7.98 us (5%)
  local copies, waits for them, and re-layouts  2.32 us (1%)
    ppermute x15, waiting for transfers between devices, hop(): data = lax.ppermute(data, 'row', pairs)  71.1 us
    pallas_call x7, Pallas kernels, chunk_matmul(): pl.pallas_call(body, out_shape=[jax.ShapeDtypeStruct((rows, features), ou...  29.3 us
    ppermute x15, starting transfers between devices, hop(): data = lax.ppermute(data, 'row', pairs)  16.7 us
    all_to_all x1, blocking collectives, sum_by_stages(): lax.all_to_all(spread, 'row', 0, 0, axis_index_groups=lines, tiled=True)  7.98 us
    all_to_all x1, starting transfers between devices, sum_by_stages(): lax.all_to_all(rows, 'row', 0, 0, axis_index_groups=lines, tiled=True)  5.37 us
    pallas_call x3, Pallas kernels, rows_matmul(): pl.pallas_call(body, out_shape=shape, in_specs=[vmem] * (2 * count + 1) +...  4.31 us
    ppermute x15, starting transfers between devices, hop(): beside = lax.ppermute(data, 'row', partner)  3.82 us
    pallas_call x1, Pallas kernels, project_selected(): pl.pallas_call(body, out_shape=(shape, shape), in_specs=[pl.BlockSpec(mem...  3.39 us
  transfers between devices with their start and end apart: 36, of which 14 were waited for; matrix products, arithmetic and copies ran while one was open for 1% of the time, Pallas kernels for 21%

profile of v9, /device:TPU:0, one launch (start us, length us, event | category | flops | bytes accessed | tf_op | source)
XLA Modules:
  0.0 160.3 jit_solution(16000041649013339384)
XLA Ops:
  0.0 0.7 constant_dynamic-slice_fusion
  0.7 0.6 fusion.3
  1.3 1.3 shard_map.74
  2.8 3.4 %shard_map.81 = (f32[192,128]{1,0:T(8,128)S(1)}, f32[192,128]{1,0:T(8,128)S(1)}) custom-call(s32[1]{0:T(128)} %bitcast.2.f_ref.core_ref, bf16[384,896]{1,0:T(8,128)(2,1)S(1)} %get-tuple-element.29.refs_0_.low_ref, bf16[384,896]{1,0:T(8,128)(2,1)S(1)} %get-tuple-element.27.refs_1_.high_ref, s32[384,1]{1,0:T(8,128)S(1)} %broadcast_in_dim_reshape.5.l_ref, ...), custom_call_target="tpu_custom_call" | custom-call | flops 704643072 | bytes 3407872 | tf_op jit(solution)/shard_map/pallas_call | solution.py:94
  6.2 0.6 collective-permute-start.27
  7.8 2.9 %collective-permute-start.28 = (f32[96,128]{1,0:T(8,128)S(1)}, f32[96,128]{1,0:T(8,128)S(1)}, u32[]{:S(2)}, u32[]{:S(2)}) collective-permute-start(f32[96,128]{1,0:T(8,128)S(1)} %slice_select_fusion), channel_id=1, source_target_pairs={{0,2},{1,3},{4,6},{5,7},{8,10},{9,11},{12,14},{13,15},{14,12},{15,... | collective-permute-start | bytes 147464 | tf_op jit(solution)/shard_map/ppermute | solution.py:161
  10.7 2.1 %collective-permute-done.28 = f32[96,128]{1,0:T(8,128)S(1)} collective-permute-done((f32[96,128]{1,0:T(8,128)S(1)}, f32[96,128]{1,0:T(8,128)S(1)}, u32[]{:S(2)}, u32[]{:S(2)}) %collective-permute-start.28) | collective-permute-done | bytes 49184 | tf_op jit(solution)/shard_map/ppermute | solution.py:161
  12.8 0.6 select_add_fusion
  13.4 5.4 %all-to-all-start = ((f32[4,24,128]{2,1,0:T(8,128)}), f32[4,24,128]{2,1,0:T(8,128)S(1)}, u32[]{:S(2)}, u32[]{:S(2)}) async-start(f32[4,24,128]{2,1,0:T(8,128)} %bitcast.5), calls=%async_computation | async-start | bytes 98304 | tf_op jit(solution)/shard_map/all_to_all | solution.py:182
  18.8 3.5 %collective-permute-start.5 = (bf16[384,896]{1,0:T(8,128)(2,1)S(1)}, bf16[384,896]{1,0:T(8,128)(2,1)}, u32[]{:S(2)}, u32[]{:S(2)}) collective-permute-start(bf16[384,896]{1,0:T(8,128)(2,1)S(1)} %get-tuple-element.27.refs_1_.high_ref), channel_id=1, source_target_pairs={{4,0},{3,1},{8,4},{1,5},{12,8},{5,9},{14,12},{9,13},{10,14},{13,15... | collective-permute-start | bytes 2064392 | tf_op jit(solution)/shard_map/ppermute | solution.py:399
  22.3 2.3 %all-to-all-done = f32[4,24,128]{2,1,0:T(8,128)S(1)} async-done(((f32[4,24,128]{2,1,0:T(8,128)}), f32[4,24,128]{2,1,0:T(8,128)S(1)}, u32[]{:S(2)}, u32[]{:S(2)}) %all-to-all-start) | async-done | bytes 49184 | tf_op jit(solution)/shard_map/all_to_all | solution.py:182
  24.8 8.0 %all_to_all.18 = bf16[4,24,128]{2,1,0:T(8,128)(2,1)S(1)} all-to-all(bf16[4,24,128]{2,1,0:T(8,128)(2,1)S(1)} %broadcast_in_dim.2), channel_id=1, replica_groups={{0,4,8,12},{1,5,9,13},{14,10,6,2},{15,11,7,3},{16,20,24,28},{17,21,25,2..., dimensions={0} | all-to-all | bytes 49152 | tf_op jit(solution)/shard_map/all_to_all | solution.py:185
  32.7 0.5 collective-permute-start.29
  33.3 1.5 collective-permute-start.13
  34.8 0.5 collective-permute-start
  35.3 1.5 collective-permute-done.29
  37.3 0.9 collective-permute-done.30.other_ref
  38.3 13.3 %collective-permute-done.13.refs_2_ = bf16[384,896]{1,0:T(8,128)(2,1)S(1)} collective-permute-done((bf16[384,896]{1,0:T(8,128)(2,1)S(1)}, bf16[384,896]{1,0:T(8,128)(2,1)S(1)}, u32[]{:S(2)}, u32[]{:S(2)}) %collective-permute-start.13) | collective-permute-done | bytes 688160 | tf_op jit(solution)/shard_map/ppermute | solution.py:399
  51.6 1.5 collective-permute-start.14
  53.1 12.4 %collective-permute-done.6.refs_2_ = bf16[384,896]{1,0:T(8,128)(2,1)S(1)} collective-permute-done((bf16[384,896]{1,0:T(8,128)(2,1)}, bf16[384,896]{1,0:T(8,128)(2,1)S(1)}, u32[]{:S(2)}, u32[]{:S(2)}) %collective-permute-start.6) | collective-permute-done | bytes 688160 | tf_op jit(solution)/shard_map/ppermute | solution.py:399
  65.5 1.5 collective-permute-start.7
  67.0 1.0 collective-permute-done.x_ref.refs_0_
  68.2 0.6 collective-permute-start.1
  68.8 5.6 %collective-permute-done.14.refs_2_ = bf16[384,896]{1,0:T(8,128)(2,1)S(1)} collective-permute-done((bf16[384,896]{1,0:T(8,128)(2,1)S(1)}, bf16[384,896]{1,0:T(8,128)(2,1)S(1)}, u32[]{:S(2)}, u32[]{:S(2)}) %collective-permute-start.14) | collective-permute-done | bytes 688160 | tf_op jit(solution)/shard_map/ppermute | solution.py:399
  74.4 0.7 collective-permute-start.10
  75.1 14.1 %collective-permute-done.7.refs_2_ = bf16[384,896]{1,0:T(8,128)(2,1)S(1)} collective-permute-done((bf16[384,896]{1,0:T(8,128)(2,1)S(1)}, bf16[384,896]{1,0:T(8,128)(2,1)S(1)}, u32[]{:S(2)}, u32[]{:S(2)}) %collective-permute-start.7) | collective-permute-done | bytes 688160 | tf_op jit(solution)/shard_map/ppermute | solution.py:399
  89.2 2.3 %collective-permute-start.15 = (bf16[384,896]{1,0:T(8,128)(2,1)S(1)}, bf16[384,896]{1,0:T(8,128)(2,1)S(1)}, u32[]{:S(2)}, u32[]{:S(2)}) collective-permute-start(bf16[384,896]{1,0:T(8,128)(2,1)S(1)} %collective-permute-done.14.refs_2_), channel_id=1, source_target_pairs={{4,0},{3,1},{8,4},{1,5},{12,8},{5,9},{14,12},{9,13},{10,14},{13,15... | collective-permute-start | bytes 2064392 | tf_op jit(solution)/shard_map/ppermute | solution.py:399
  91.7 6.9 %collective-permute-done.10.refs_0_ = bf16[384,896]{1,0:T(8,128)(2,1)S(1)} collective-permute-done((bf16[384,896]{1,0:T(8,128)(2,1)S(1)}, bf16[384,896]{1,0:T(8,128)(2,1)S(1)}, u32[]{:S(2)}, u32[]{:S(2)}) %collective-permute-start.10) | collective-permute-done | bytes 688160 | tf_op jit(solution)/shard_map/ppermute | solution.py:399
  98.8 5.9 %collective-permute-done.15.refs_2_ = bf16[384,896]{1,0:T(8,128)(2,1)S(1)} collective-permute-done((bf16[384,896]{1,0:T(8,128)(2,1)S(1)}, bf16[384,896]{1,0:T(8,128)(2,1)S(1)}, u32[]{:S(2)}, u32[]{:S(2)}) %collective-permute-start.15) | collective-permute-done | bytes 688160 | tf_op jit(solution)/shard_map/ppermute | solution.py:399
  104.8 2.3 %collective-permute-start.8 = (bf16[192,896]{1,0:T(8,128)(2,1)S(1)}, bf16[192,896]{1,0:T(8,128)(2,1)S(1)}, u32[]{:S(2)}, u32[]{:S(2)}) collective-permute-start(bf16[192,896]{1,0:T(8,128)(2,1)S(1)} %get-tuple-element.48), channel_id=1, source_target_pairs={{4,0},{3,1},{8,4},{1,5},{12,8},{5,9},{14,12},{9,13},{10,14},{13,15... | collective-permute-start | bytes 1032200 | tf_op jit(solution)/shard_map/ppermute | solution.py:399
  107.1 5.1 %collective-permute-done.33.refs_2_ = bf16[192,896]{1,0:T(8,128)(2,1)S(1)} collective-permute-done((bf16[192,896]{1,0:T(8,128)(2,1)S(1)}, bf16[192,896]{1,0:T(8,128)(2,1)S(1)}, u32[]{:S(2)}, u32[]{:S(2)}) %collective-permute-start.33) | collective-permute-done | bytes 344096 | tf_op jit(solution)/shard_map/ppermute | solution.py:399
  112.1 0.6 collective-permute-start.11
  112.8 6.7 %collective-permute-done.8.refs_1_ = bf16[192,896]{1,0:T(8,128)(2,1)S(1)} collective-permute-done((bf16[192,896]{1,0:T(8,128)(2,1)S(1)}, bf16[192,896]{1,0:T(8,128)(2,1)S(1)}, u32[]{:S(2)}, u32[]{:S(2)}) %collective-permute-start.8) | collective-permute-done | bytes 344096 | tf_op jit(solution)/shard_map/ppermute | solution.py:399
  119.5 0.5 collective-permute-start.18
  120.0 0.7 dynamic-slice_bitcast_fusion.starts_ref
  120.7 1.5 shard_map.82.refs_10_
  122.8 3.8 %shard_map.75.refs_3_ = f32[384,512]{1,0:T(8,128)S(1)} custom-call(s32[33]{0:T(128)S(1)} %dynamic-slice_bitcast_fusion.starts_ref, bf16[384,896]{1,0:T(8,128)(2,1)S(1)} %get-tuple-element.29.refs_0_.low_ref, bf16[384,896]{1,0:T(8,128)(2,1)S(1)} %get-tuple-element.27.refs_1_.high_ref, bf16[384,1792]{1,0:T(8,128)(2,1)S(1)} %collective-permute-done.26.refs_2_, ...), custom_call_target="tpu_custom_call" | custom-call | flops 1409286144 | bytes 7995392 | tf_op jit(solution)/shard_map/pallas_call | solution.py:249
  126.9 0.7 collective-permute-start.31
  127.9 3.6 %shard_map.76.refs_5_ = f32[384,512]{1,0:T(8,128)S(1)} custom-call(s32[33]{0:T(128)S(1)} %dynamic-slice_bitcast_fusion.starts_ref, bf16[384,896]{1,0:T(8,128)(2,1)} %collective-permute-done.5.refs_0_, bf16[384,896]{1,0:T(8,128)(2,1)S(1)} %collective-permute-done.25.refs_1_, bf16[512,28672]{1,0:T(8,128)(2,1)} %refs_4_.9, f32[384,512]{1,0:T(8,128)S(1)} %shard_map.75.refs_3_), custom_call_target="tpu_custom_call" | custom-call | flops 704643072 | bytes 4784128 | tf_op jit(solution)/shard_map/pallas_call | solution.py:249
  131.5 5.2 %shard_map.77.refs_5_ = f32[384,512]{1,0:T(8,128)S(1)} custom-call(s32[33]{0:T(128)S(1)} %dynamic-slice_bitcast_fusion.starts_ref, bf16[384,1792]{1,0:T(8,128)(2,1)S(1)} %collective-permute-done.x_ref.refs_0_, bf16[384,1792]{1,0:T(8,128)(2,1)S(1)} %collective-permute-done.23.refs_1_, bf16[384,896]{1,0:T(8,128)(2,1)S(1)} %collective-permute-done.13.refs_2_, ...), custom_call_target="tpu_custom_call" | custom-call | flops 2113929216 | bytes 11206656 | tf_op jit(solution)/shard_map/pallas_call | solution.py:249
  136.8 4.0 %shard_map.78.refs_5_ = f32[384,512]{1,0:T(8,128)S(1)} custom-call(s32[33]{0:T(128)S(1)} %dynamic-slice_bitcast_fusion.starts_ref, bf16[384,896]{1,0:T(8,128)(2,1)S(1)} %collective-permute-done.1.refs_0_, bf16[384,896]{1,0:T(8,128)(2,1)S(1)} %collective-permute-done.21.refs_1_, bf16[384,896]{1,0:T(8,128)(2,1)S(1)} %collective-permute-done.6.refs_2_, ...), custom_call_target="tpu_custom_call" | custom-call | flops 1409286144 | bytes 7995392 | tf_op jit(solution)/shard_map/pallas_call | solution.py:249
  140.8 1.8 %collective-permute-start.34 = (bf16[192,896]{1,0:T(8,128)(2,1)S(1)}, bf16[192,896]{1,0:T(8,128)(2,1)S(1)}, u32[]{:S(2)}, u32[]{:S(2)}) collective-permute-start(bf16[192,896]{1,0:T(8,128)(2,1)S(1)} %collective-permute-done.33.refs_2_), channel_id=1, source_target_pairs={{0,1},{1,0},{4,5},{5,4},{8,9},{9,8},{12,13},{13,12},{14,15},{15,14... | collective-permute-start | bytes 1032200 | tf_op jit(solution)/shard_map/ppermute | solution.py:400
  143.2 4.4 %shard_map.79 = (f32[384,512]{1,0:T(8,128)S(1)}, bf16[512,896]{1,0:T(8,128)(2,1)S(1)}, bf16[512,896]{1,0:T(8,128)(2,1)S(1)}, bf16[512,896]{1,0:T(8,128)(2,1)S(1)}, bf16[512,896]{1,0:T(8,128)(2,1)S(1)}) custom-call(s32[33]{0:T(128)S(1)} %dynamic-slice_bitcast_fusion.starts_ref, bf16[384,896]{1,0:T(8,128)(2,1)S(1)} %collective-permute-done.10.refs_0_, ...), custom_call_target="tpu_custom_call" | custom-call | flops 1409286144 | bytes 11665408 | tf_op jit(solution)/shard_map/pallas_call | solution.py:249
  147.5 4.1 %shard_map.80 = (f32[384,512]{1,0:T(8,128)S(1)}, bf16[512,896]{1,0:T(8,128)(2,1)S(1)}, bf16[512,896]{1,0:T(8,128)(2,1)S(1)}, bf16[512,896]{1,0:T(8,128)(2,1)S(1)}, bf16[512,896]{1,0:T(8,128)(2,1)S(1)}) custom-call(s32[33]{0:T(128)S(1)} %dynamic-slice_bitcast_fusion.starts_ref, bf16[384,896]{1,0:T(8,128)(2,1)S(1)} %collective-permute-done.2.refs_0_, ...), custom_call_target="tpu_custom_call" | custom-call | flops 1409286144 | bytes 11665408 | tf_op jit(solution)/shard_map/pallas_call | solution.py:249
  151.7 4.1 %shard_map.83 = (f32[384,512]{1,0:T(8,128)S(1)}, bf16[512,896]{1,0:T(8,128)(2,1)S(1)}, bf16[512,896]{1,0:T(8,128)(2,1)S(1)}, bf16[512,896]{1,0:T(8,128)(2,1)S(1)}, bf16[512,896]{1,0:T(8,128)(2,1)S(1)}) custom-call(s32[33]{0:T(128)S(1)} %dynamic-slice_bitcast_fusion.starts_ref, bf16[384,896]{1,0:T(8,128)(2,1)S(1)} %collective-permute-done.11.refs_0_, ...), custom_call_target="tpu_custom_call" | custom-call | flops 1409286144 | bytes 11665408 | tf_op jit(solution)/shard_map/pallas_call | solution.py:249
  155.8 0.8 shard_map.84.refs_4_
  156.6 2.1 %shard_map.85.refs_5_ = bf16[384,512]{1,0:T(8,128)(2,1)} custom-call(bf16[192,896]{1,0:T(8,128)(2,1)S(1)} %collective-permute-done.31.refs_0_, bf16[192,896]{1,0:T(8,128)(2,1)S(1)} %collective-permute-done.32.refs_1_, bf16[192,896]{1,0:T(8,128)(2,1)S(1)} %collective-permute-done.33.refs_2_, bf16[192,896]{1,0:T(8,128)(2,1)S(1)} %collective-permute-done.34.refs_3_, ...), custom_call_target="tpu_custom_call" | custom-call | tf_op jit(solution)/shard_map/pallas_call | solution.py:301
  158.7 1.5 shard_map.86
  (59 shorter events, 3.6 us)
Async XLA Ops:
  0.0 2.6 %copy-start.1 = (s32[2,192]{1,0:T(2,128)S(1)}, s32[2,192]{1,0:T(2,128)}, u32[]{:S(2)}) copy-start(s32[2,192]{1,0:T(2,128)} %param.11) | copy-start | bytes 4612
  6.2 1.5 collective-permute-start.27
  7.8 5.0 %collective-permute-start.28 = (f32[96,128]{1,0:T(8,128)S(1)}, f32[96,128]{1,0:T(8,128)S(1)}, u32[]{:S(2)}, u32[]{:S(2)}) collective-permute-start(f32[96,128]{1,0:T(8,128)S(1)} %slice_select_fusion), channel_id=1, source_target_pairs={{0,2},{1,3},{4,6},{5,7},{8,10},{9,11},{12,14},{13,15},{14,12},{15,... | collective-permute-start | bytes 147464 | tf_op jit(solution)/shard_map/ppermute | solution.py:161
  13.4 11.2 %all-to-all-start = ((f32[4,24,128]{2,1,0:T(8,128)}), f32[4,24,128]{2,1,0:T(8,128)S(1)}, u32[]{:S(2)}, u32[]{:S(2)}) async-start(f32[4,24,128]{2,1,0:T(8,128)} %bitcast.5), calls=%async_computation | async-start | bytes 98304 | tf_op jit(solution)/shard_map/all_to_all | solution.py:182
  18.8 32.8 %collective-permute-start.26 = (bf16[384,1792]{1,0:T(8,128)(2,1)}, bf16[384,1792]{1,0:T(8,128)(2,1)S(1)}, u32[]{:S(2)}, u32[]{:S(2)}) collective-permute-start(bf16[384,1792]{1,0:T(8,128)(2,1)} %bitcast.15), channel_id=1, source_target_pairs={{0,1},{1,0},{4,5},{5,4},{8,9},{9,8},{12,13},{13,12},{14,15},{15,14... | collective-permute-start | bytes 4128776 | tf_op jit(solution)/shard_map/ppermute | solution.py:395
  18.8 18.2 %collective-permute-start.5 = (bf16[384,896]{1,0:T(8,128)(2,1)S(1)}, bf16[384,896]{1,0:T(8,128)(2,1)}, u32[]{:S(2)}, u32[]{:S(2)}) collective-permute-start(bf16[384,896]{1,0:T(8,128)(2,1)S(1)} %get-tuple-element.27.refs_1_.high_ref), channel_id=1, source_target_pairs={{4,0},{3,1},{8,4},{1,5},{12,8},{5,9},{14,12},{9,13},{10,14},{13,15... | collective-permute-start | bytes 2064392 | tf_op jit(solution)/shard_map/ppermute | solution.py:399
  32.7 4.1 %collective-permute-start.29 = (bf16[96,128]{1,0:T(8,128)(2,1)S(1)}, bf16[96,128]{1,0:T(8,128)(2,1)S(1)}, u32[]{:S(2)}, u32[]{:S(2)}) collective-permute-start(bf16[96,128]{1,0:T(8,128)(2,1)S(1)} %bitcast.17), channel_id=1, source_target_pairs={{0,2},{1,3},{4,6},{5,7},{8,10},{9,11},{12,14},{13,15},{14,12},{15,... | collective-permute-start | bytes 73736 | tf_op jit(solution)/shard_map/ppermute | solution.py:166
  33.3 18.3 %collective-permute-start.13 = (bf16[384,896]{1,0:T(8,128)(2,1)S(1)}, bf16[384,896]{1,0:T(8,128)(2,1)S(1)}, u32[]{:S(2)}, u32[]{:S(2)}) collective-permute-start(bf16[384,896]{1,0:T(8,128)(2,1)S(1)} %get-tuple-element.29.refs_0_.low_ref), channel_id=1, source_target_pairs={{4,0},{3,1},{8,4},{1,5},{12,8},{5,9},{14,12},{9,13},{10,14},{13,15... | collective-permute-start | bytes 2064392 | tf_op jit(solution)/shard_map/ppermute | solution.py:399
  34.8 33.3 %collective-permute-start = (bf16[384,1792]{1,0:T(8,128)(2,1)}, bf16[384,1792]{1,0:T(8,128)(2,1)S(1)}, u32[]{:S(2)}, u32[]{:S(2)}) collective-permute-start(bf16[384,1792]{1,0:T(8,128)(2,1)} %bitcast.16), channel_id=1, source_target_pairs={{0,4},{1,3},{4,8},{5,1},{8,12},{9,5},{12,14},{13,9},{14,10},{15,13... | collective-permute-start | bytes 4128776 | tf_op jit(solution)/shard_map/ppermute | solution.py:399
  36.8 83.9 %copy-start = (bf16[8,64,512]{2,1,0:T(8,128)(2,1)S(1)}, bf16[8,64,512]{2,1,0:T(8,128)(2,1)}, u32[]{:S(2)}) copy-start(bf16[8,64,512]{2,1,0:T(8,128)(2,1)} %param.10) | copy-start | bytes 1572868
  36.9 1.3 collective-permute-start.30
  36.9 28.5 %collective-permute-start.6 = (bf16[384,896]{1,0:T(8,128)(2,1)}, bf16[384,896]{1,0:T(8,128)(2,1)S(1)}, u32[]{:S(2)}, u32[]{:S(2)}) collective-permute-start(bf16[384,896]{1,0:T(8,128)(2,1)} %collective-permute-done.5.refs_0_), channel_id=1, source_target_pairs={{4,0},{3,1},{8,4},{1,5},{12,8},{5,9},{14,12},{9,13},{10,14},{13,15... | collective-permute-start | bytes 2064392 | tf_op jit(solution)/shard_map/ppermute | solution.py:399
  38.2 27.3 %collective-permute-start.25 = (bf16[384,896]{1,0:T(8,128)(2,1)}, bf16[384,896]{1,0:T(8,128)(2,1)S(1)}, u32[]{:S(2)}, u32[]{:S(2)}) collective-permute-start(bf16[384,896]{1,0:T(8,128)(2,1)} %collective-permute-done.5.refs_0_), channel_id=1, source_target_pairs={{0,1},{1,0},{4,5},{5,4},{8,9},{9,8},{12,13},{13,12},{14,15},{15,14... | collective-permute-start | bytes 2064392 | tf_op jit(solution)/shard_map/ppermute | solution.py:400
  51.6 16.6 %collective-permute-start.24 = (bf16[384,896]{1,0:T(8,128)(2,1)S(1)}, bf16[384,896]{1,0:T(8,128)(2,1)S(1)}, u32[]{:S(2)}, u32[]{:S(2)}) collective-permute-start(bf16[384,896]{1,0:T(8,128)(2,1)S(1)} %collective-permute-done.13.refs_2_), channel_id=1, source_target_pairs={{0,1},{1,0},{4,5},{5,4},{8,9},{9,8},{12,13},{13,12},{14,15},{15,14... | collective-permute-start | bytes 2064392 | tf_op jit(solution)/shard_map/ppermute | solution.py:400
  51.6 22.8 %collective-permute-start.14 = (bf16[384,896]{1,0:T(8,128)(2,1)S(1)}, bf16[384,896]{1,0:T(8,128)(2,1)S(1)}, u32[]{:S(2)}, u32[]{:S(2)}) collective-permute-start(bf16[384,896]{1,0:T(8,128)(2,1)S(1)} %collective-permute-done.13.refs_2_), channel_id=1, source_target_pairs={{4,0},{3,1},{8,4},{1,5},{12,8},{5,9},{14,12},{9,13},{10,14},{13,15... | collective-permute-start | bytes 2064392 | tf_op jit(solution)/shard_map/ppermute | solution.py:399
  65.5 8.9 %collective-permute-start.22 = (bf16[384,896]{1,0:T(8,128)(2,1)S(1)}, bf16[384,896]{1,0:T(8,128)(2,1)S(1)}, u32[]{:S(2)}, u32[]{:S(2)}) collective-permute-start(bf16[384,896]{1,0:T(8,128)(2,1)S(1)} %collective-permute-done.6.refs_2_), channel_id=1, source_target_pairs={{0,1},{1,0},{4,5},{5,4},{8,9},{9,8},{12,13},{13,12},{14,15},{15,14... | collective-permute-start | bytes 2064392 | tf_op jit(solution)/shard_map/ppermute | solution.py:400
  65.5 23.6 %collective-permute-start.7 = (bf16[384,896]{1,0:T(8,128)(2,1)S(1)}, bf16[384,896]{1,0:T(8,128)(2,1)S(1)}, u32[]{:S(2)}, u32[]{:S(2)}) collective-permute-start(bf16[384,896]{1,0:T(8,128)(2,1)S(1)} %collective-permute-done.6.refs_2_), channel_id=1, source_target_pairs={{4,0},{3,1},{8,4},{1,5},{12,8},{5,9},{14,12},{9,13},{10,14},{13,15... | collective-permute-start | bytes 2064392 | tf_op jit(solution)/shard_map/ppermute | solution.py:399
  68.0 51.5 %collective-permute-start.23 = (bf16[384,1792]{1,0:T(8,128)(2,1)S(1)}, bf16[384,1792]{1,0:T(8,128)(2,1)S(1)}, u32[]{:S(2)}, u32[]{:S(2)}) collective-permute-start(bf16[384,1792]{1,0:T(8,128)(2,1)S(1)} %collective-permute-done.x_ref.refs_0_), channel_id=1, source_target_pairs={{0,1},{1,0},{4,5},{5,4},{8,9},{9,8},{12,13},{13,12},{14,15},{15,14... | collective-permute-start | bytes 4128776 | tf_op jit(solution)/shard_map/ppermute | solution.py:400
  68.2 23.3 %collective-permute-start.1 = (bf16[384,896]{1,0:T(8,128)(2,1)S(1)}, bf16[384,896]{1,0:T(8,128)(2,1)S(1)}, u32[]{:S(2)}, u32[]{:S(2)}) collective-permute-start(bf16[384,896]{1,0:T(8,128)(2,1)S(1)} %get-tuple-element.26), channel_id=1, source_target_pairs={{0,4},{1,3},{4,8},{5,1},{8,12},{9,5},{12,14},{13,9},{14,10},{15,13... | collective-permute-start | bytes 2064392 | tf_op jit(solution)/shard_map/ppermute | solution.py:399
  74.4 17.2 %collective-permute-start.20 = (bf16[384,896]{1,0:T(8,128)(2,1)S(1)}, bf16[384,896]{1,0:T(8,128)(2,1)S(1)}, u32[]{:S(2)}, u32[]{:S(2)}) collective-permute-start(bf16[384,896]{1,0:T(8,128)(2,1)S(1)} %collective-permute-done.14.refs_2_), channel_id=1, source_target_pairs={{0,1},{1,0},{4,5},{5,4},{8,9},{9,8},{12,13},{13,12},{14,15},{15,14... | collective-permute-start | bytes 2064392 | tf_op jit(solution)/shard_map/ppermute | solution.py:400
  74.4 24.2 %collective-permute-start.10 = (bf16[384,896]{1,0:T(8,128)(2,1)S(1)}, bf16[384,896]{1,0:T(8,128)(2,1)S(1)}, u32[]{:S(2)}, u32[]{:S(2)}) collective-permute-start(bf16[384,896]{1,0:T(8,128)(2,1)S(1)} %get-tuple-element.28), channel_id=1, source_target_pairs={{0,4},{1,3},{4,8},{5,1},{8,12},{9,5},{12,14},{13,9},{14,10},{15,13... | collective-permute-start | bytes 2064392 | tf_op jit(solution)/shard_map/ppermute | solution.py:399
  89.2 15.6 %collective-permute-start.15 = (bf16[384,896]{1,0:T(8,128)(2,1)S(1)}, bf16[384,896]{1,0:T(8,128)(2,1)S(1)}, u32[]{:S(2)}, u32[]{:S(2)}) collective-permute-start(bf16[384,896]{1,0:T(8,128)(2,1)S(1)} %collective-permute-done.14.refs_2_), channel_id=1, source_target_pairs={{4,0},{3,1},{8,4},{1,5},{12,8},{5,9},{14,12},{9,13},{10,14},{13,15... | collective-permute-start | bytes 2064392 | tf_op jit(solution)/shard_map/ppermute | solution.py:399
  91.5 20.6 %collective-permute-start.33 = (bf16[192,896]{1,0:T(8,128)(2,1)S(1)}, bf16[192,896]{1,0:T(8,128)(2,1)S(1)}, u32[]{:S(2)}, u32[]{:S(2)}) collective-permute-start(bf16[192,896]{1,0:T(8,128)(2,1)S(1)} %get-tuple-element.47), channel_id=1, source_target_pairs={{4,0},{3,1},{8,4},{1,5},{12,8},{5,9},{14,12},{9,13},{10,14},{13,15... | collective-permute-start | bytes 1032200 | tf_op jit(solution)/shard_map/ppermute | solution.py:399
  91.6 30.6 %collective-permute-start.21 = (bf16[384,896]{1,0:T(8,128)(2,1)S(1)}, bf16[384,896]{1,0:T(8,128)(2,1)S(1)}, u32[]{:S(2)}, u32[]{:S(2)}) collective-permute-start(bf16[384,896]{1,0:T(8,128)(2,1)S(1)} %collective-permute-done.1.refs_0_), channel_id=1, source_target_pairs={{0,1},{1,0},{4,5},{5,4},{8,9},{9,8},{12,13},{13,12},{14,15},{15,14... | collective-permute-start | bytes 2064392 | tf_op jit(solution)/shard_map/ppermute | solution.py:400
  98.6 23.7 %collective-permute-start.2 = (bf16[384,896]{1,0:T(8,128)(2,1)S(1)}, bf16[384,896]{1,0:T(8,128)(2,1)S(1)}, u32[]{:S(2)}, u32[]{:S(2)}) collective-permute-start(bf16[384,896]{1,0:T(8,128)(2,1)S(1)} %collective-permute-done.1.refs_0_), channel_id=1, source_target_pairs={{0,4},{1,3},{4,8},{5,1},{8,12},{9,5},{12,14},{13,9},{14,10},{15,13... | collective-permute-start | bytes 2064392 | tf_op jit(solution)/shard_map/ppermute | solution.py:399
  104.8 14.7 %collective-permute-start.8 = (bf16[192,896]{1,0:T(8,128)(2,1)S(1)}, bf16[192,896]{1,0:T(8,128)(2,1)S(1)}, u32[]{:S(2)}, u32[]{:S(2)}) collective-permute-start(bf16[192,896]{1,0:T(8,128)(2,1)S(1)} %get-tuple-element.48), channel_id=1, source_target_pairs={{4,0},{3,1},{8,4},{1,5},{12,8},{5,9},{14,12},{9,13},{10,14},{13,15... | collective-permute-start | bytes 1032200 | tf_op jit(solution)/shard_map/ppermute | solution.py:399
  112.1 14.5 %collective-permute-start.11 = (bf16[384,896]{1,0:T(8,128)(2,1)S(1)}, bf16[384,896]{1,0:T(8,128)(2,1)S(1)}, u32[]{:S(2)}, u32[]{:S(2)}) collective-permute-start(bf16[384,896]{1,0:T(8,128)(2,1)S(1)} %collective-permute-done.10.refs_0_), channel_id=1, source_target_pairs={{0,4},{1,3},{4,8},{5,1},{8,12},{9,5},{12,14},{13,9},{14,10},{15,13... | collective-permute-start | bytes 2064392 | tf_op jit(solution)/shard_map/ppermute | solution.py:399
  119.5 7.3 %collective-permute-start.19 = (bf16[384,896]{1,0:T(8,128)(2,1)S(1)}, bf16[384,896]{1,0:T(8,128)(2,1)S(1)}, u32[]{:S(2)}, u32[]{:S(2)}) collective-permute-start(bf16[384,896]{1,0:T(8,128)(2,1)S(1)} %collective-permute-done.10.refs_0_), channel_id=1, source_target_pairs={{0,1},{1,0},{4,5},{5,4},{8,9},{9,8},{12,13},{13,12},{14,15},{15,14... | collective-permute-start | bytes 2064392 | tf_op jit(solution)/shard_map/ppermute | solution.py:400
  119.5 8.1 %collective-permute-start.18 = (bf16[384,896]{1,0:T(8,128)(2,1)S(1)}, bf16[384,896]{1,0:T(8,128)(2,1)S(1)}, u32[]{:S(2)}, u32[]{:S(2)}) collective-permute-start(bf16[384,896]{1,0:T(8,128)(2,1)S(1)} %collective-permute-done.7.refs_2_), channel_id=1, source_target_pairs={{0,1},{1,0},{4,5},{5,4},{8,9},{9,8},{12,13},{13,12},{14,15},{15,14... | collective-permute-start | bytes 2064392 | tf_op jit(solution)/shard_map/ppermute | solution.py:400
  122.2 18.6 %collective-permute-start.16 = (bf16[384,896]{1,0:T(8,128)(2,1)S(1)}, bf16[384,896]{1,0:T(8,128)(2,1)S(1)}, u32[]{:S(2)}, u32[]{:S(2)}) collective-permute-start(bf16[384,896]{1,0:T(8,128)(2,1)S(1)} %collective-permute-done.15.refs_2_), channel_id=1, source_target_pairs={{0,1},{1,0},{4,5},{5,4},{8,9},{9,8},{12,13},{13,12},{14,15},{15,14... | collective-permute-start | bytes 2064392 | tf_op jit(solution)/shard_map/ppermute | solution.py:400
  122.3 20.8 %collective-permute-start.17 = (bf16[384,896]{1,0:T(8,128)(2,1)S(1)}, bf16[384,896]{1,0:T(8,128)(2,1)S(1)}, u32[]{:S(2)}, u32[]{:S(2)}) collective-permute-start(bf16[384,896]{1,0:T(8,128)(2,1)S(1)} %collective-permute-done.2.refs_0_), channel_id=1, source_target_pairs={{0,1},{1,0},{4,5},{5,4},{8,9},{9,8},{12,13},{13,12},{14,15},{15,14... | collective-permute-start | bytes 2064392 | tf_op jit(solution)/shard_map/ppermute | solution.py:400
  126.6 25.1 %collective-permute-start.12 = (bf16[384,896]{1,0:T(8,128)(2,1)S(1)}, bf16[384,896]{1,0:T(8,128)(2,1)S(1)}, u32[]{:S(2)}, u32[]{:S(2)}) collective-permute-start(bf16[384,896]{1,0:T(8,128)(2,1)S(1)} %collective-permute-done.11.refs_0_), channel_id=1, source_target_pairs={{0,1},{1,0},{4,5},{5,4},{8,9},{9,8},{12,13},{13,12},{14,15},{15,14... | collective-permute-start | bytes 2064392 | tf_op jit(solution)/shard_map/ppermute | solution.py:400
  126.9 15.7 %collective-permute-start.31 = (bf16[192,896]{1,0:T(8,128)(2,1)S(1)}, bf16[192,896]{1,0:T(8,128)(2,1)S(1)}, u32[]{:S(2)}, u32[]{:S(2)}) collective-permute-start(bf16[192,896]{1,0:T(8,128)(2,1)S(1)} %get-tuple-element.49), channel_id=1, source_target_pairs={{0,4},{1,3},{4,8},{5,1},{8,12},{9,5},{12,14},{13,9},{14,10},{15,13... | collective-permute-start | bytes 1032200 | tf_op jit(solution)/shard_map/ppermute | solution.py:399
  127.6 15.1 %collective-permute-start.3 = (bf16[192,896]{1,0:T(8,128)(2,1)S(1)}, bf16[192,896]{1,0:T(8,128)(2,1)S(1)}, u32[]{:S(2)}, u32[]{:S(2)}) collective-permute-start(bf16[192,896]{1,0:T(8,128)(2,1)S(1)} %get-tuple-element.50), channel_id=1, source_target_pairs={{0,4},{1,3},{4,8},{5,1},{8,12},{9,5},{12,14},{13,9},{14,10},{15,13... | collective-permute-start | bytes 1032200 | tf_op jit(solution)/shard_map/ppermute | solution.py:399
  140.8 15.8 %collective-permute-start.34 = (bf16[192,896]{1,0:T(8,128)(2,1)S(1)}, bf16[192,896]{1,0:T(8,128)(2,1)S(1)}, u32[]{:S(2)}, u32[]{:S(2)}) collective-permute-start(bf16[192,896]{1,0:T(8,128)(2,1)S(1)} %collective-permute-done.33.refs_2_), channel_id=1, source_target_pairs={{0,1},{1,0},{4,5},{5,4},{8,9},{9,8},{12,13},{13,12},{14,15},{15,14... | collective-permute-start | bytes 1032200 | tf_op jit(solution)/shard_map/ppermute | solution.py:400
  142.6 16.1 %collective-permute-start.9 = (bf16[192,896]{1,0:T(8,128)(2,1)S(1)}, bf16[192,896]{1,0:T(8,128)(2,1)S(1)}, u32[]{:S(2)}, u32[]{:S(2)}) collective-permute-start(bf16[192,896]{1,0:T(8,128)(2,1)S(1)} %collective-permute-done.8.refs_1_), channel_id=1, source_target_pairs={{0,1},{1,0},{4,5},{5,4},{8,9},{9,8},{12,13},{13,12},{14,15},{15,14... | collective-permute-start | bytes 1032200 | tf_op jit(solution)/shard_map/ppermute | solution.py:400
  142.7 13.9 %collective-permute-start.32 = (bf16[192,896]{1,0:T(8,128)(2,1)S(1)}, bf16[192,896]{1,0:T(8,128)(2,1)S(1)}, u32[]{:S(2)}, u32[]{:S(2)}) collective-permute-start(bf16[192,896]{1,0:T(8,128)(2,1)S(1)} %collective-permute-done.31.refs_0_), channel_id=1, source_target_pairs={{0,1},{1,0},{4,5},{5,4},{8,9},{9,8},{12,13},{13,12},{14,15},{15,14... | collective-permute-start | bytes 1032200 | tf_op jit(solution)/shard_map/ppermute | solution.py:400
  143.1 15.6 %collective-permute-start.4 = (bf16[192,896]{1,0:T(8,128)(2,1)S(1)}, bf16[192,896]{1,0:T(8,128)(2,1)S(1)}, u32[]{:S(2)}, u32[]{:S(2)}) collective-permute-start(bf16[192,896]{1,0:T(8,128)(2,1)S(1)} %collective-permute-done.3.refs_0_), channel_id=1, source_target_pairs={{0,1},{1,0},{4,5},{5,4},{8,9},{9,8},{12,13},{13,12},{14,15},{15,14... | collective-permute-start | bytes 1032200 | tf_op jit(solution)/shard_map/ppermute | solution.py:400

commit v10 on v9

--- a/solution.py
+++ b/solution.py
@@ -8,6 +8,7 @@
 
 
 LANES = 128
+FAR = (0, 1, 2, 3, 4)
 
 
 def chip_ring(mesh):
@@ -187,7 +188,7 @@
     return half, lax.ppermute(half, "row", partner)
 
 
-def chunk_matmul(chunks, starts, first, weight, added, out_dtype, ready, ahead):
+def chunk_matmul(chunks, starts, first, weight, added, out_dtype, ready, ahead, far=False):
     count = len(chunks)
     rows = chunks[0].shape[0]
     widths = [c.shape[1] for c in chunks]
@@ -206,6 +207,12 @@
             return w_any.at[:, pl.ds(start, units)]
 
         copies = []
+        if far:
+            near, x_sem, refs = refs[:count], refs[count], refs[count + 1 :]
+            arrivals = [pltpu.make_async_copy(x_refs[k], near[k], x_sem.at[k]) for k in range(count)]
+            for copy in arrivals:
+                copy.start()
+            x_refs = near
         if not ready:
             w_refs, w_sem = refs[:count], refs[count]
             for k in range(count):
@@ -220,6 +227,8 @@
             fetch.start()
         total = None
         for k in range(count):
+            if far:
+                arrivals[k].wait()
             if copies:
                 copies[k].wait()
             part = lax.dot_general(
@@ -238,6 +247,10 @@
     anywhere = pl.BlockSpec(memory_space=pltpu.HBM)
     vmem = pl.BlockSpec(memory_space=pltpu.VMEM)
     scratch = []
+    if far:
+        chunks = [in_hbm(chunk) for chunk in chunks]
+        scratch += [pltpu.VMEM((rows, w), jnp.bfloat16) for w in widths]
+        scratch += [pltpu.SemaphoreType.DMA((count,))]
     if not ready:
         scratch += [pltpu.VMEM((features, w), jnp.bfloat16) for w in widths]
         scratch += [pltpu.SemaphoreType.DMA((count,))]
@@ -251,7 +264,7 @@
         out_shape=[jax.ShapeDtypeStruct((rows, features), out_dtype)]
         + [jax.ShapeDtypeStruct((features, units), jnp.bfloat16) for _, units in ahead],
         in_specs=[pl.BlockSpec(memory_space=pltpu.SMEM)]
-        + [vmem] * count
+        + [anywhere if far else vmem] * count
         + [anywhere]
         + [vmem] * (len(ready) + len(added)),
         out_specs=[vmem] * (1 + later),
@@ -279,19 +292,33 @@
 
     def body(*refs):
         x_refs, w_refs, a_ref, refs = refs[:count], refs[count : 2 * count], refs[2 * count], refs[2 * count + 1 :]
-        value = a_ref[...] if a_ref.shape[0] == rows else a_ref[row : row + rows, :]
-        for x_ref, w_ref in zip(x_refs, w_refs):
-            value = value + lax.dot_general(
-                x_ref[...], w_ref[...], (((1,), (1,)), ((), ())), preferred_element_type=jnp.float32
-            )
-        if final:
-            o_ref, s_ref, sem = refs[-3:]
-            s_ref[...] = value.astype(jnp.bfloat16)
-            copy = pltpu.make_async_copy(s_ref, o_ref.at[pl.ds(row, rows)], sem)
-            copy.start()
+        first = 0 if a_ref.shape[0] == rows else row
+        pieces = 2 if final else 1
+        wide = features // pieces
+        copies = []
+        for j in range(pieces):
+            columns = pl.ds(j * wide, wide)
+            value = a_ref[first : first + rows, j * wide : (j + 1) * wide]
+            for x_ref, w_ref in zip(x_refs, w_refs):
+                value = value + lax.dot_general(
+                    x_ref[...],
+                    w_ref[columns, :],
+                    (((1,), (1,)), ((), ())),
+                    preferred_element_type=jnp.float32,
+                )
+            if final:
+                o_ref, s_ref, sem = refs[-3:]
+                s_ref[:, columns] = value.astype(jnp.bfloat16)
+                copies.append(
+                    pltpu.make_async_copy(
+                        s_ref.at[:, columns], o_ref.at[pl.ds(row, rows), columns], sem.at[j]
+                    )
+                )
+                copies[-1].start()
+            else:
+                refs[0][...] = value
+        for copy in copies:
             copy.wait()
-        else:
-            refs[0][...] = value
 
     anywhere = pl.BlockSpec(memory_space=pltpu.HBM)
     vmem = pl.BlockSpec(memory_space=pltpu.VMEM)
@@ -303,7 +330,7 @@
         out_shape=shape,
         in_specs=[vmem] * (2 * count + 1) + ([] if out is None else [anywhere]),
         out_specs=anywhere if final else vmem,
-        scratch_shapes=[pltpu.VMEM((rows, features), jnp.bfloat16), pltpu.SemaphoreType.DMA] if final else [],
+        scratch_shapes=[pltpu.VMEM((rows, features), jnp.bfloat16), pltpu.SemaphoreType.DMA((2,))] if final else [],
         input_output_aliases={} if out is None else {2 * count + 1: 0},
         compiler_params=pltpu.CompilerParams(vmem_limit_bytes=16 << 20),
     )(*chunks, *blocks, acc, *([] if out is None else [out]))
@@ -426,7 +453,7 @@
         starts = jnp.asarray(table)[me]
         acc, ready, done = [], [], 0
         ends = len(batches) - len(cuts)
-        settled = min(4, ends - 1)
+        settled = min(5, ends - 1)
         for k, found in enumerate(batches[:ends]):
             coming = batches[k + 1] if k >= settled else []
             at = done + len(found)
@@ -440,6 +467,7 @@
                 jnp.float32,
                 ready,
                 ahead,
+                k in FAR,
             )
             acc, ready, done = [out], list(ready_next), at
         out = None

time: 161 us -> 163 us (1.012)
  Pallas kernels: 39.9 us -> 42 us
    pallas_call x7, Pallas kernels: 29.3 us -> 31.3 us  [chunk_matmul(): pl.pallas_call(body, out_shape=[jax.ShapeDtypeStruct((rows, features), ou...]
  transfers between devices with their start and end apart: 36 -> 36, of which waited for: 14 -> 14; matrix products, arithmetic and copies ran while one was open for 1% -> 1% of each run, Pallas kernels for 21% -> 22%
where the time goes in v10:
time: 163 us
  waiting for transfers between devices  77.9 us (48%)
  Pallas kernels  42 us (26%)
  starting transfers between devices  30.4 us (19%)
  blocking collectives  7.98 us (5%)
  local copies, waits for them, and re-layouts  2.38 us (1%)
    ppermute x15, waiting for transfers between devices, hop(): data = lax.ppermute(data, 'row', pairs)  70.8 us
    pallas_call x7, Pallas kernels, chunk_matmul(): pl.pallas_call(body, out_shape=[jax.ShapeDtypeStruct((rows, features), ou...  31.3 us
    ppermute x15, starting transfers between devices, hop(): data = lax.ppermute(data, 'row', pairs)  16.9 us
    all_to_all x1, blocking collectives, sum_by_stages(): lax.all_to_all(spread, 'row', 0, 0, axis_index_groups=lines, tiled=True)  7.98 us
    all_to_all x1, starting transfers between devices, sum_by_stages(): lax.all_to_all(rows, 'row', 0, 0, axis_index_groups=lines, tiled=True)  5.37 us
    pallas_call x3, Pallas kernels, rows_matmul(): pl.pallas_call(body, out_shape=shape, in_specs=[vmem] * (2 * count + 1) +...  4.32 us
    ppermute x15, starting transfers between devices, hop(): beside = lax.ppermute(data, 'row', partner)  4.09 us
    pallas_call x1, Pallas kernels, project_selected(): pl.pallas_call(body, out_shape=(shape, shape), in_specs=[pl.BlockSpec(mem...  3.38 us
  transfers between devices with their start and end apart: 36, of which 14 were waited for; matrix products, arithmetic and copies ran while one was open for 1% of the time, Pallas kernels for 22%

profile of v10, /device:TPU:0, one launch (start us, length us, event | category | flops | bytes accessed | tf_op | source)
XLA Modules:
  0.0 162.8 jit_solution(1696628539787219819)
XLA Ops:
  0.0 0.7 constant_dynamic-slice_fusion
  0.7 0.6 fusion.3
  1.3 1.3 shard_map.74
  2.9 3.4 %shard_map.81 = (f32[192,128]{1,0:T(8,128)S(1)}, f32[192,128]{1,0:T(8,128)S(1)}) custom-call(s32[1]{0:T(128)} %bitcast.2.f_ref.core_ref, bf16[384,896]{1,0:T(8,128)(2,1)S(1)} %get-tuple-element.24.refs_0_.low_ref, bf16[384,896]{1,0:T(8,128)(2,1)S(1)} %get-tuple-element.22.refs_1_.high_ref, s32[384,1]{1,0:T(8,128)S(1)} %broadcast_in_dim_reshape.5.l_ref, ...), custom_call_target="tpu_custom_call" | custom-call | flops 704643072 | bytes 3407872 | tf_op jit(solution)/shard_map/pallas_call | solution.py:95
  6.3 0.6 collective-permute-start.27
  7.8 2.9 %collective-permute-start.28 = (f32[96,128]{1,0:T(8,128)S(1)}, f32[96,128]{1,0:T(8,128)S(1)}, u32[]{:S(2)}, u32[]{:S(2)}) collective-permute-start(f32[96,128]{1,0:T(8,128)S(1)} %slice_select_fusion), channel_id=1, source_target_pairs={{0,2},{1,3},{4,6},{5,7},{8,10},{9,11},{12,14},{13,15},{14,12},{15,... | collective-permute-start | bytes 147464 | tf_op jit(solution)/shard_map/ppermute | solution.py:162
  10.7 2.1 %collective-permute-done.28 = f32[96,128]{1,0:T(8,128)S(1)} collective-permute-done((f32[96,128]{1,0:T(8,128)S(1)}, f32[96,128]{1,0:T(8,128)S(1)}, u32[]{:S(2)}, u32[]{:S(2)}) %collective-permute-start.28) | collective-permute-done | bytes 49184 | tf_op jit(solution)/shard_map/ppermute | solution.py:162
  12.8 0.6 select_add_fusion
  13.4 5.4 %all-to-all-start = ((f32[4,24,128]{2,1,0:T(8,128)}), f32[4,24,128]{2,1,0:T(8,128)S(1)}, u32[]{:S(2)}, u32[]{:S(2)}) async-start(f32[4,24,128]{2,1,0:T(8,128)} %bitcast.5), calls=%async_computation | async-start | bytes 98304 | tf_op jit(solution)/shard_map/all_to_all | solution.py:183
  18.8 3.5 %collective-permute-start.5 = (bf16[384,896]{1,0:T(8,128)(2,1)S(1)}, bf16[384,896]{1,0:T(8,128)(2,1)}, u32[]{:S(2)}, u32[]{:S(2)}) collective-permute-start(bf16[384,896]{1,0:T(8,128)(2,1)S(1)} %get-tuple-element.22.refs_1_.high_ref), channel_id=1, source_target_pairs={{4,0},{3,1},{8,4},{1,5},{12,8},{5,9},{14,12},{9,13},{10,14},{13,15... | collective-permute-start | bytes 2064392 | tf_op jit(solution)/shard_map/ppermute | solution.py:426
  22.3 2.3 %all-to-all-done = f32[4,24,128]{2,1,0:T(8,128)S(1)} async-done(((f32[4,24,128]{2,1,0:T(8,128)}), f32[4,24,128]{2,1,0:T(8,128)S(1)}, u32[]{:S(2)}, u32[]{:S(2)}) %all-to-all-start) | async-done | bytes 49184 | tf_op jit(solution)/shard_map/all_to_all | solution.py:183
  24.8 8.0 %all_to_all.18 = bf16[4,24,128]{2,1,0:T(8,128)(2,1)S(1)} all-to-all(bf16[4,24,128]{2,1,0:T(8,128)(2,1)S(1)} %broadcast_in_dim.2), channel_id=1, replica_groups={{0,4,8,12},{1,5,9,13},{14,10,6,2},{15,11,7,3},{16,20,24,28},{17,21,25,2..., dimensions={0} | all-to-all | bytes 49152 | tf_op jit(solution)/shard_map/all_to_all | solution.py:186
  32.8 0.5 collective-permute-start.29
  33.3 1.5 collective-permute-start.13
  34.8 0.5 collective-permute-start
  35.3 1.5 collective-permute-done.29
  37.3 0.9 collective-permute-done.30.other_ref
  38.3 13.3 %collective-permute-done.13.refs_2_ = bf16[384,896]{1,0:T(8,128)(2,1)S(1)} collective-permute-done((bf16[384,896]{1,0:T(8,128)(2,1)S(1)}, bf16[384,896]{1,0:T(8,128)(2,1)S(1)}, u32[]{:S(2)}, u32[]{:S(2)}) %collective-permute-start.13) | collective-permute-done | bytes 688160 | tf_op jit(solution)/shard_map/ppermute | solution.py:426
  51.6 1.5 collective-permute-start.14
  53.2 12.4 %collective-permute-done.6.refs_2_ = bf16[384,896]{1,0:T(8,128)(2,1)S(1)} collective-permute-done((bf16[384,896]{1,0:T(8,128)(2,1)}, bf16[384,896]{1,0:T(8,128)(2,1)S(1)}, u32[]{:S(2)}, u32[]{:S(2)}) %collective-permute-start.6) | collective-permute-done | bytes 688160 | tf_op jit(solution)/shard_map/ppermute | solution.py:426
  65.5 1.7 %collective-permute-start.7 = (bf16[384,896]{1,0:T(8,128)(2,1)S(1)}, bf16[384,896]{1,0:T(8,128)(2,1)S(1)}, u32[]{:S(2)}, u32[]{:S(2)}) collective-permute-start(bf16[384,896]{1,0:T(8,128)(2,1)S(1)} %collective-permute-done.6.refs_2_), channel_id=1, source_target_pairs={{4,0},{3,1},{8,4},{1,5},{12,8},{5,9},{14,12},{9,13},{10,14},{13,15... | collective-permute-start | bytes 2064392 | tf_op jit(solution)/shard_map/ppermute | solution.py:426
  67.2 0.8 collective-permute-done.x_ref.refs_0_
  68.2 0.6 collective-permute-start.1
  68.8 5.7 %collective-permute-done.14.refs_2_ = bf16[384,896]{1,0:T(8,128)(2,1)S(1)} collective-permute-done((bf16[384,896]{1,0:T(8,128)(2,1)S(1)}, bf16[384,896]{1,0:T(8,128)(2,1)S(1)}, u32[]{:S(2)}, u32[]{:S(2)}) %collective-permute-start.14) | collective-permute-done | bytes 688160 | tf_op jit(solution)/shard_map/ppermute | solution.py:426
  74.5 0.6 collective-permute-start.10
  75.1 14.1 %collective-permute-done.7.refs_2_ = bf16[384,896]{1,0:T(8,128)(2,1)S(1)} collective-permute-done((bf16[384,896]{1,0:T(8,128)(2,1)S(1)}, bf16[384,896]{1,0:T(8,128)(2,1)S(1)}, u32[]{:S(2)}, u32[]{:S(2)}) %collective-permute-start.7) | collective-permute-done | bytes 688160 | tf_op jit(solution)/shard_map/ppermute | solution.py:426
  89.2 2.5 %collective-permute-start.15 = (bf16[384,896]{1,0:T(8,128)(2,1)S(1)}, bf16[384,896]{1,0:T(8,128)(2,1)S(1)}, u32[]{:S(2)}, u32[]{:S(2)}) collective-permute-start(bf16[384,896]{1,0:T(8,128)(2,1)S(1)} %collective-permute-done.14.refs_2_), channel_id=1, source_target_pairs={{4,0},{3,1},{8,4},{1,5},{12,8},{5,9},{14,12},{9,13},{10,14},{13,15... | collective-permute-start | bytes 2064392 | tf_op jit(solution)/shard_map/ppermute | solution.py:426
  92.0 6.6 %collective-permute-done.10.refs_0_ = bf16[384,896]{1,0:T(8,128)(2,1)S(1)} collective-permute-done((bf16[384,896]{1,0:T(8,128)(2,1)S(1)}, bf16[384,896]{1,0:T(8,128)(2,1)S(1)}, u32[]{:S(2)}, u32[]{:S(2)}) %collective-permute-start.10) | collective-permute-done | bytes 688160 | tf_op jit(solution)/shard_map/ppermute | solution.py:426
  98.6 6.2 %collective-permute-done.15.refs_2_ = bf16[384,896]{1,0:T(8,128)(2,1)S(1)} collective-permute-done((bf16[384,896]{1,0:T(8,128)(2,1)S(1)}, bf16[384,896]{1,0:T(8,128)(2,1)S(1)}, u32[]{:S(2)}, u32[]{:S(2)}) %collective-permute-start.15) | collective-permute-done | bytes 688160 | tf_op jit(solution)/shard_map/ppermute | solution.py:426
  104.8 2.5 %collective-permute-start.8 = (bf16[192,896]{1,0:T(8,128)(2,1)S(1)}, bf16[192,896]{1,0:T(8,128)(2,1)S(1)}, u32[]{:S(2)}, u32[]{:S(2)}) collective-permute-start(bf16[192,896]{1,0:T(8,128)(2,1)S(1)} %get-tuple-element.38), channel_id=1, source_target_pairs={{4,0},{3,1},{8,4},{1,5},{12,8},{5,9},{14,12},{9,13},{10,14},{13,15... | collective-permute-start | bytes 1032200 | tf_op jit(solution)/shard_map/ppermute | solution.py:426
  107.3 4.9 %collective-permute-done.33.refs_2_ = bf16[192,896]{1,0:T(8,128)(2,1)S(1)} collective-permute-done((bf16[192,896]{1,0:T(8,128)(2,1)S(1)}, bf16[192,896]{1,0:T(8,128)(2,1)S(1)}, u32[]{:S(2)}, u32[]{:S(2)}) %collective-permute-start.33) | collective-permute-done | bytes 344096 | tf_op jit(solution)/shard_map/ppermute | solution.py:426
  112.2 0.6 collective-permute-start.11
  112.8 6.8 %collective-permute-done.8.refs_1_ = bf16[192,896]{1,0:T(8,128)(2,1)S(1)} collective-permute-done((bf16[192,896]{1,0:T(8,128)(2,1)S(1)}, bf16[192,896]{1,0:T(8,128)(2,1)S(1)}, u32[]{:S(2)}, u32[]{:S(2)}) %collective-permute-start.8) | collective-permute-done | bytes 344096 | tf_op jit(solution)/shard_map/ppermute | solution.py:426
  119.6 0.5 collective-permute-start.18
  120.1 0.7 dynamic-slice_bitcast_fusion.starts_ref
  120.8 1.5 shard_map.82.refs_10_
  122.9 4.4 %shard_map.75.refs_3_ = f32[384,512]{1,0:T(8,128)S(1)} custom-call(s32[33]{0:T(128)S(1)} %dynamic-slice_bitcast_fusion.starts_ref, bf16[384,896]{1,0:T(8,128)(2,1)} %copy-done.1, bf16[384,896]{1,0:T(8,128)(2,1)} %copy-done.2, bf16[384,1792]{1,0:T(8,128)(2,1)} %copy-done.4, bf16[512,28672]{1,0:T(8,128)(2,1)} %refs_4_.9), custom_call_target="tpu_custom_call" | custom-call | flops 1409286144 | bytes 7995392 | tf_op jit(solution)/shard_map/pallas_call | solution.py:262
  127.6 0.6 collective-permute-start.31
  128.6 3.5 %shard_map.76.refs_5_ = f32[384,512]{1,0:T(8,128)S(1)} custom-call(s32[33]{0:T(128)S(1)} %dynamic-slice_bitcast_fusion.starts_ref, bf16[384,896]{1,0:T(8,128)(2,1)} %collective-permute-done.5.refs_0_, bf16[384,896]{1,0:T(8,128)(2,1)} %copy-done.16, bf16[512,28672]{1,0:T(8,128)(2,1)} %refs_4_.9, f32[384,512]{1,0:T(8,128)S(1)} %shard_map.75.refs_3_), custom_call_target="tpu_custom_call" | custom-call | flops 704643072 | bytes 4784128 | tf_op jit(solution)/shard_map/pallas_call | solution.py:262
  132.1 6.1 %shard_map.77.refs_5_ = f32[384,512]{1,0:T(8,128)S(1)} custom-call(s32[33]{0:T(128)S(1)} %dynamic-slice_bitcast_fusion.starts_ref, bf16[384,1792]{1,0:T(8,128)(2,1)} %copy-done, bf16[384,1792]{1,0:T(8,128)(2,1)} %copy-done.5, bf16[384,896]{1,0:T(8,128)(2,1)} %copy-done.6, bf16[384,896]{1,0:T(8,128)(2,1)} %copy-done.9, bf16[512,28672]{1,0:T(8,128)(2,1)} %refs_4_.9, ...), custom_call_target="tpu_custom_call" | custom-call | flops 2113929216 | bytes 11206656 | tf_op jit(solution)/shard_map/pallas_call | solution.py:262
  138.2 4.5 %shard_map.78.refs_5_ = f32[384,512]{1,0:T(8,128)S(1)} custom-call(s32[33]{0:T(128)S(1)} %dynamic-slice_bitcast_fusion.starts_ref, bf16[384,896]{1,0:T(8,128)(2,1)} %copy-done.13, bf16[384,896]{1,0:T(8,128)(2,1)} %copy-done.15, bf16[384,896]{1,0:T(8,128)(2,1)} %copy-done.8, bf16[384,896]{1,0:T(8,128)(2,1)} %copy-done.11, bf16[512,28672]{1,0:T(8,128)(2,1)} %refs_4_.9, ...), custom_call_target="tpu_custom_call" | custom-call | flops 1409286144 | bytes 7995392 | tf_op jit(solution)/shard_map/pallas_call | solution.py:262
  142.7 2.0 %collective-permute-start.34 = (bf16[192,896]{1,0:T(8,128)(2,1)S(1)}, bf16[192,896]{1,0:T(8,128)(2,1)S(1)}, u32[]{:S(2)}, u32[]{:S(2)}) collective-permute-start(bf16[192,896]{1,0:T(8,128)(2,1)S(1)} %collective-permute-done.33.refs_2_), channel_id=1, source_target_pairs={{0,1},{1,0},{4,5},{5,4},{8,9},{9,8},{12,13},{13,12},{14,15},{15,14... | collective-permute-start | bytes 1032200 | tf_op jit(solution)/shard_map/ppermute | solution.py:427
  145.3 4.5 %shard_map.79.refs_5_ = f32[384,512]{1,0:T(8,128)S(1)} custom-call(s32[33]{0:T(128)S(1)} %dynamic-slice_bitcast_fusion.starts_ref, bf16[384,896]{1,0:T(8,128)(2,1)} %copy-done.12, bf16[384,896]{1,0:T(8,128)(2,1)} %copy-done.14, bf16[384,896]{1,0:T(8,128)(2,1)} %copy-done.7, bf16[384,896]{1,0:T(8,128)(2,1)} %copy-done.10, bf16[512,28672]{1,0:T(8,128)(2,1)} %refs_4_.9, ...), custom_call_target="tpu_custom_call" | custom-call | flops 1409286144 | bytes 7995392 | tf_op jit(solution)/shard_map/pallas_call | solution.py:262
  149.8 4.4 %shard_map.80 = (f32[384,512]{1,0:T(8,128)S(1)}, bf16[512,896]{1,0:T(8,128)(2,1)S(1)}, bf16[512,896]{1,0:T(8,128)(2,1)S(1)}, bf16[512,896]{1,0:T(8,128)(2,1)S(1)}, bf16[512,896]{1,0:T(8,128)(2,1)S(1)}) custom-call(s32[33]{0:T(128)S(1)} %dynamic-slice_bitcast_fusion.starts_ref, bf16[384,896]{1,0:T(8,128)(2,1)S(1)} %collective-permute-done.2.refs_0_, ...), custom_call_target="tpu_custom_call" | custom-call | flops 1409286144 | bytes 11665408 | tf_op jit(solution)/shard_map/pallas_call | solution.py:262
  154.2 4.1 %shard_map.83 = (f32[384,512]{1,0:T(8,128)S(1)}, bf16[512,896]{1,0:T(8,128)(2,1)S(1)}, bf16[512,896]{1,0:T(8,128)(2,1)S(1)}, bf16[512,896]{1,0:T(8,128)(2,1)S(1)}, bf16[512,896]{1,0:T(8,128)(2,1)S(1)}) custom-call(s32[33]{0:T(128)S(1)} %dynamic-slice_bitcast_fusion.starts_ref, bf16[384,896]{1,0:T(8,128)(2,1)S(1)} %collective-permute-done.11.refs_0_, ...), custom_call_target="tpu_custom_call" | custom-call | flops 1409286144 | bytes 11665408 | tf_op jit(solution)/shard_map/pallas_call | solution.py:262
  158.3 0.8 shard_map.84.refs_4_
  159.1 2.1 %shard_map.85.refs_5_ = bf16[384,512]{1,0:T(8,128)(2,1)} custom-call(bf16[192,896]{1,0:T(8,128)(2,1)S(1)} %collective-permute-done.31.refs_0_, bf16[192,896]{1,0:T(8,128)(2,1)S(1)} %collective-permute-done.32.refs_1_, bf16[192,896]{1,0:T(8,128)(2,1)S(1)} %collective-permute-done.33.refs_2_, bf16[192,896]{1,0:T(8,128)(2,1)S(1)} %collective-permute-done.34.refs_3_, ...), custom_call_target="tpu_custom_call" | custom-call | tf_op jit(solution)/shard_map/pallas_call | solution.py:328
  161.2 1.5 shard_map.86
  (91 shorter events, 3.5 us)
Async XLA Ops:
  2.6 30.6 %copy-start.1 = (bf16[384,896]{1,0:T(8,128)(2,1)}, bf16[384,896]{1,0:T(8,128)(2,1)S(1)}, u32[]{:S(2)}) copy-start(bf16[384,896]{1,0:T(8,128)(2,1)S(1)} %get-tuple-element.24.refs_0_.low_ref) | copy-start | bytes 2064388
  6.3 1.5 collective-permute-start.27
  7.8 5.0 %collective-permute-start.28 = (f32[96,128]{1,0:T(8,128)S(1)}, f32[96,128]{1,0:T(8,128)S(1)}, u32[]{:S(2)}, u32[]{:S(2)}) collective-permute-start(f32[96,128]{1,0:T(8,128)S(1)} %slice_select_fusion), channel_id=1, source_target_pairs={{0,2},{1,3},{4,6},{5,7},{8,10},{9,11},{12,14},{13,15},{14,12},{15,... | collective-permute-start | bytes 147464 | tf_op jit(solution)/shard_map/ppermute | solution.py:162
  13.4 11.2 %all-to-all-start = ((f32[4,24,128]{2,1,0:T(8,128)}), f32[4,24,128]{2,1,0:T(8,128)S(1)}, u32[]{:S(2)}, u32[]{:S(2)}) async-start(f32[4,24,128]{2,1,0:T(8,128)} %bitcast.5), calls=%async_computation | async-start | bytes 98304 | tf_op jit(solution)/shard_map/all_to_all | solution.py:183
  18.8 32.8 %collective-permute-start.26 = (bf16[384,1792]{1,0:T(8,128)(2,1)}, bf16[384,1792]{1,0:T(8,128)(2,1)S(1)}, u32[]{:S(2)}, u32[]{:S(2)}) collective-permute-start(bf16[384,1792]{1,0:T(8,128)(2,1)} %bitcast.15), channel_id=1, source_target_pairs={{0,1},{1,0},{4,5},{5,4},{8,9},{9,8},{12,13},{13,12},{14,15},{15,14... | collective-permute-start | bytes 4128776 | tf_op jit(solution)/shard_map/ppermute | solution.py:422
  18.8 18.2 %collective-permute-start.5 = (bf16[384,896]{1,0:T(8,128)(2,1)S(1)}, bf16[384,896]{1,0:T(8,128)(2,1)}, u32[]{:S(2)}, u32[]{:S(2)}) collective-permute-start(bf16[384,896]{1,0:T(8,128)(2,1)S(1)} %get-tuple-element.22.refs_1_.high_ref), channel_id=1, source_target_pairs={{4,0},{3,1},{8,4},{1,5},{12,8},{5,9},{14,12},{9,13},{10,14},{13,15... | collective-permute-start | bytes 2064392 | tf_op jit(solution)/shard_map/ppermute | solution.py:426
  32.8 4.1 %collective-permute-start.29 = (bf16[96,128]{1,0:T(8,128)(2,1)S(1)}, bf16[96,128]{1,0:T(8,128)(2,1)S(1)}, u32[]{:S(2)}, u32[]{:S(2)}) collective-permute-start(bf16[96,128]{1,0:T(8,128)(2,1)S(1)} %bitcast.17), channel_id=1, source_target_pairs={{0,2},{1,3},{4,6},{5,7},{8,10},{9,11},{12,14},{13,15},{14,12},{15,... | collective-permute-start | bytes 73736 | tf_op jit(solution)/shard_map/ppermute | solution.py:167
  33.3 18.3 %collective-permute-start.13 = (bf16[384,896]{1,0:T(8,128)(2,1)S(1)}, bf16[384,896]{1,0:T(8,128)(2,1)S(1)}, u32[]{:S(2)}, u32[]{:S(2)}) collective-permute-start(bf16[384,896]{1,0:T(8,128)(2,1)S(1)} %get-tuple-element.24.refs_0_.low_ref), channel_id=1, source_target_pairs={{4,0},{3,1},{8,4},{1,5},{12,8},{5,9},{14,12},{9,13},{10,14},{13,15... | collective-permute-start | bytes 2064392 | tf_op jit(solution)/shard_map/ppermute | solution.py:426
  34.8 33.3 %collective-permute-start = (bf16[384,1792]{1,0:T(8,128)(2,1)}, bf16[384,1792]{1,0:T(8,128)(2,1)S(1)}, u32[]{:S(2)}, u32[]{:S(2)}) collective-permute-start(bf16[384,1792]{1,0:T(8,128)(2,1)} %bitcast.16), channel_id=1, source_target_pairs={{0,4},{1,3},{4,8},{5,1},{8,12},{9,5},{12,14},{13,9},{14,10},{15,13... | collective-permute-start | bytes 4128776 | tf_op jit(solution)/shard_map/ppermute | solution.py:426
  36.9 83.9 %copy-start.3 = (bf16[8,64,512]{2,1,0:T(8,128)(2,1)S(1)}, bf16[8,64,512]{2,1,0:T(8,128)(2,1)}, u32[]{:S(2)}) copy-start(bf16[8,64,512]{2,1,0:T(8,128)(2,1)} %param.10) | copy-start | bytes 1572868
  36.9 1.3 collective-permute-start.30
  37.0 28.6 %collective-permute-start.6 = (bf16[384,896]{1,0:T(8,128)(2,1)}, bf16[384,896]{1,0:T(8,128)(2,1)S(1)}, u32[]{:S(2)}, u32[]{:S(2)}) collective-permute-start(bf16[384,896]{1,0:T(8,128)(2,1)} %collective-permute-done.5.refs_0_), channel_id=1, source_target_pairs={{4,0},{3,1},{8,4},{1,5},{12,8},{5,9},{14,12},{9,13},{10,14},{13,15... | collective-permute-start | bytes 2064392 | tf_op jit(solution)/shard_map/ppermute | solution.py:426
  38.2 27.4 %collective-permute-start.25 = (bf16[384,896]{1,0:T(8,128)(2,1)}, bf16[384,896]{1,0:T(8,128)(2,1)S(1)}, u32[]{:S(2)}, u32[]{:S(2)}) collective-permute-start(bf16[384,896]{1,0:T(8,128)(2,1)} %collective-permute-done.5.refs_0_), channel_id=1, source_target_pairs={{0,1},{1,0},{4,5},{5,4},{8,9},{9,8},{12,13},{13,12},{14,15},{15,14... | collective-permute-start | bytes 2064392 | tf_op jit(solution)/shard_map/ppermute | solution.py:427
  51.6 75.7 %copy-start.6 = (bf16[384,896]{1,0:T(8,128)(2,1)}, bf16[384,896]{1,0:T(8,128)(2,1)S(1)}, u32[]{:S(2)}) copy-start(bf16[384,896]{1,0:T(8,128)(2,1)S(1)} %collective-permute-done.13.refs_2_) | copy-start | bytes 2064388
  51.6 16.6 %collective-permute-start.24 = (bf16[384,896]{1,0:T(8,128)(2,1)S(1)}, bf16[384,896]{1,0:T(8,128)(2,1)S(1)}, u32[]{:S(2)}, u32[]{:S(2)}) collective-permute-start(bf16[384,896]{1,0:T(8,128)(2,1)S(1)} %collective-permute-done.13.refs_2_), channel_id=1, source_target_pairs={{0,1},{1,0},{4,5},{5,4},{8,9},{9,8},{12,13},{13,12},{14,15},{15,14... | collective-permute-start | bytes 2064392 | tf_op jit(solution)/shard_map/ppermute | solution.py:427
  51.6 40.2 %copy-start.4 = (bf16[384,1792]{1,0:T(8,128)(2,1)}, bf16[384,1792]{1,0:T(8,128)(2,1)S(1)}, u32[]{:S(2)}) copy-start(bf16[384,1792]{1,0:T(8,128)(2,1)S(1)} %collective-permute-done.26.refs_2_) | copy-start | bytes 4128772
  51.6 22.9 %collective-permute-start.14 = (bf16[384,896]{1,0:T(8,128)(2,1)S(1)}, bf16[384,896]{1,0:T(8,128)(2,1)S(1)}, u32[]{:S(2)}, u32[]{:S(2)}) collective-permute-start(bf16[384,896]{1,0:T(8,128)(2,1)S(1)} %collective-permute-done.13.refs_2_), channel_id=1, source_target_pairs={{4,0},{3,1},{8,4},{1,5},{12,8},{5,9},{14,12},{9,13},{10,14},{13,15... | collective-permute-start | bytes 2064392 | tf_op jit(solution)/shard_map/ppermute | solution.py:426
  65.5 61.8 %copy-start.8 = (bf16[384,896]{1,0:T(8,128)(2,1)}, bf16[384,896]{1,0:T(8,128)(2,1)S(1)}, u32[]{:S(2)}) copy-start(bf16[384,896]{1,0:T(8,128)(2,1)S(1)} %collective-permute-done.6.refs_2_) | copy-start | bytes 2064388
  65.5 9.0 %collective-permute-start.22 = (bf16[384,896]{1,0:T(8,128)(2,1)S(1)}, bf16[384,896]{1,0:T(8,128)(2,1)S(1)}, u32[]{:S(2)}, u32[]{:S(2)}) collective-permute-start(bf16[384,896]{1,0:T(8,128)(2,1)S(1)} %collective-permute-done.6.refs_2_), channel_id=1, source_target_pairs={{0,1},{1,0},{4,5},{5,4},{8,9},{9,8},{12,13},{13,12},{14,15},{15,14... | collective-permute-start | bytes 2064392 | tf_op jit(solution)/shard_map/ppermute | solution.py:427
  65.5 61.8 %copy-start.16 = (bf16[384,896]{1,0:T(8,128)(2,1)}, bf16[384,896]{1,0:T(8,128)(2,1)S(1)}, u32[]{:S(2)}) copy-start(bf16[384,896]{1,0:T(8,128)(2,1)S(1)} %collective-permute-done.25.refs_1_) | copy-start | bytes 2064388
  65.5 23.7 %collective-permute-start.7 = (bf16[384,896]{1,0:T(8,128)(2,1)S(1)}, bf16[384,896]{1,0:T(8,128)(2,1)S(1)}, u32[]{:S(2)}, u32[]{:S(2)}) collective-permute-start(bf16[384,896]{1,0:T(8,128)(2,1)S(1)} %collective-permute-done.6.refs_2_), channel_id=1, source_target_pairs={{4,0},{3,1},{8,4},{1,5},{12,8},{5,9},{14,12},{9,13},{10,14},{13,15... | collective-permute-start | bytes 2064392 | tf_op jit(solution)/shard_map/ppermute | solution.py:426
  68.0 51.5 %collective-permute-start.23 = (bf16[384,1792]{1,0:T(8,128)(2,1)S(1)}, bf16[384,1792]{1,0:T(8,128)(2,1)S(1)}, u32[]{:S(2)}, u32[]{:S(2)}) collective-permute-start(bf16[384,1792]{1,0:T(8,128)(2,1)S(1)} %collective-permute-done.x_ref.refs_0_), channel_id=1, source_target_pairs={{0,1},{1,0},{4,5},{5,4},{8,9},{9,8},{12,13},{13,12},{14,15},{15,14... | collective-permute-start | bytes 4128776 | tf_op jit(solution)/shard_map/ppermute | solution.py:427
  68.2 54.1 %copy-start.9 = (bf16[384,896]{1,0:T(8,128)(2,1)}, bf16[384,896]{1,0:T(8,128)(2,1)S(1)}, u32[]{:S(2)}) copy-start(bf16[384,896]{1,0:T(8,128)(2,1)S(1)} %collective-permute-done.24.refs_3_) | copy-start | bytes 2064388
  68.2 23.6 %collective-permute-start.1 = (bf16[384,896]{1,0:T(8,128)(2,1)S(1)}, bf16[384,896]{1,0:T(8,128)(2,1)S(1)}, u32[]{:S(2)}, u32[]{:S(2)}) collective-permute-start(bf16[384,896]{1,0:T(8,128)(2,1)S(1)} %get-tuple-element.21), channel_id=1, source_target_pairs={{0,4},{1,3},{4,8},{5,1},{8,12},{9,5},{12,14},{13,9},{14,10},{15,13... | collective-permute-start | bytes 2064392 | tf_op jit(solution)/shard_map/ppermute | solution.py:426
  74.5 47.8 %copy-start.7 = (bf16[384,896]{1,0:T(8,128)(2,1)}, bf16[384,896]{1,0:T(8,128)(2,1)S(1)}, u32[]{:S(2)}) copy-start(bf16[384,896]{1,0:T(8,128)(2,1)S(1)} %collective-permute-done.14.refs_2_) | copy-start | bytes 2064388
  74.5 17.4 %collective-permute-start.20 = (bf16[384,896]{1,0:T(8,128)(2,1)S(1)}, bf16[384,896]{1,0:T(8,128)(2,1)S(1)}, u32[]{:S(2)}, u32[]{:S(2)}) collective-permute-start(bf16[384,896]{1,0:T(8,128)(2,1)S(1)} %collective-permute-done.14.refs_2_), channel_id=1, source_target_pairs={{0,1},{1,0},{4,5},{5,4},{8,9},{9,8},{12,13},{13,12},{14,15},{15,14... | collective-permute-start | bytes 2064392 | tf_op jit(solution)/shard_map/ppermute | solution.py:427
  74.5 52.8 %copy-start.11 = (bf16[384,896]{1,0:T(8,128)(2,1)}, bf16[384,896]{1,0:T(8,128)(2,1)S(1)}, u32[]{:S(2)}) copy-start(bf16[384,896]{1,0:T(8,128)(2,1)S(1)} %collective-permute-done.22.refs_3_) | copy-start | bytes 2064388
  74.5 24.1 %collective-permute-start.10 = (bf16[384,896]{1,0:T(8,128)(2,1)S(1)}, bf16[384,896]{1,0:T(8,128)(2,1)S(1)}, u32[]{:S(2)}, u32[]{:S(2)}) collective-permute-start(bf16[384,896]{1,0:T(8,128)(2,1)S(1)} %get-tuple-element.23), channel_id=1, source_target_pairs={{0,4},{1,3},{4,8},{5,1},{8,12},{9,5},{12,14},{13,9},{14,10},{15,13... | collective-permute-start | bytes 2064392 | tf_op jit(solution)/shard_map/ppermute | solution.py:426
  89.2 15.6 %collective-permute-start.15 = (bf16[384,896]{1,0:T(8,128)(2,1)S(1)}, bf16[384,896]{1,0:T(8,128)(2,1)S(1)}, u32[]{:S(2)}, u32[]{:S(2)}) collective-permute-start(bf16[384,896]{1,0:T(8,128)(2,1)S(1)} %collective-permute-done.14.refs_2_), channel_id=1, source_target_pairs={{4,0},{3,1},{8,4},{1,5},{12,8},{5,9},{14,12},{9,13},{10,14},{13,15... | collective-permute-start | bytes 2064392 | tf_op jit(solution)/shard_map/ppermute | solution.py:426
  91.8 35.5 %copy-start.13 = (bf16[384,896]{1,0:T(8,128)(2,1)}, bf16[384,896]{1,0:T(8,128)(2,1)S(1)}, u32[]{:S(2)}) copy-start(bf16[384,896]{1,0:T(8,128)(2,1)S(1)} %collective-permute-done.1.refs_0_) | copy-start | bytes 2064388
  91.8 20.4 %collective-permute-start.33 = (bf16[192,896]{1,0:T(8,128)(2,1)S(1)}, bf16[192,896]{1,0:T(8,128)(2,1)S(1)}, u32[]{:S(2)}, u32[]{:S(2)}) collective-permute-start(bf16[192,896]{1,0:T(8,128)(2,1)S(1)} %get-tuple-element.37), channel_id=1, source_target_pairs={{4,0},{3,1},{8,4},{1,5},{12,8},{5,9},{14,12},{9,13},{10,14},{13,15... | collective-permute-start | bytes 1032200 | tf_op jit(solution)/shard_map/ppermute | solution.py:426
  91.9 35.5 %copy-start.10 = (bf16[384,896]{1,0:T(8,128)(2,1)}, bf16[384,896]{1,0:T(8,128)(2,1)S(1)}, u32[]{:S(2)}) copy-start(bf16[384,896]{1,0:T(8,128)(2,1)S(1)} %collective-permute-done.20.refs_3_) | copy-start | bytes 2064388
  91.9 30.4 %collective-permute-start.21 = (bf16[384,896]{1,0:T(8,128)(2,1)S(1)}, bf16[384,896]{1,0:T(8,128)(2,1)S(1)}, u32[]{:S(2)}, u32[]{:S(2)}) collective-permute-start(bf16[384,896]{1,0:T(8,128)(2,1)S(1)} %collective-permute-done.1.refs_0_), channel_id=1, source_target_pairs={{0,1},{1,0},{4,5},{5,4},{8,9},{9,8},{12,13},{13,12},{14,15},{15,14... | collective-permute-start | bytes 2064392 | tf_op jit(solution)/shard_map/ppermute | solution.py:427
  98.6 28.7 %copy-start.12 = (bf16[384,896]{1,0:T(8,128)(2,1)}, bf16[384,896]{1,0:T(8,128)(2,1)S(1)}, u32[]{:S(2)}) copy-start(bf16[384,896]{1,0:T(8,128)(2,1)S(1)} %collective-permute-done.10.refs_0_) | copy-start | bytes 2064388
  98.6 23.9 %collective-permute-start.2 = (bf16[384,896]{1,0:T(8,128)(2,1)S(1)}, bf16[384,896]{1,0:T(8,128)(2,1)S(1)}, u32[]{:S(2)}, u32[]{:S(2)}) collective-permute-start(bf16[384,896]{1,0:T(8,128)(2,1)S(1)} %collective-permute-done.1.refs_0_), channel_id=1, source_target_pairs={{0,4},{1,3},{4,8},{5,1},{8,12},{9,5},{12,14},{13,9},{14,10},{15,13... | collective-permute-start | bytes 2064392 | tf_op jit(solution)/shard_map/ppermute | solution.py:426
  104.8 14.7 %collective-permute-start.8 = (bf16[192,896]{1,0:T(8,128)(2,1)S(1)}, bf16[192,896]{1,0:T(8,128)(2,1)S(1)}, u32[]{:S(2)}, u32[]{:S(2)}) collective-permute-start(bf16[192,896]{1,0:T(8,128)(2,1)S(1)} %get-tuple-element.38), channel_id=1, source_target_pairs={{4,0},{3,1},{8,4},{1,5},{12,8},{5,9},{14,12},{9,13},{10,14},{13,15... | collective-permute-start | bytes 1032200 | tf_op jit(solution)/shard_map/ppermute | solution.py:426
  112.2 15.2 %collective-permute-start.11 = (bf16[384,896]{1,0:T(8,128)(2,1)S(1)}, bf16[384,896]{1,0:T(8,128)(2,1)S(1)}, u32[]{:S(2)}, u32[]{:S(2)}) collective-permute-start(bf16[384,896]{1,0:T(8,128)(2,1)S(1)} %collective-permute-done.10.refs_0_), channel_id=1, source_target_pairs={{0,4},{1,3},{4,8},{5,1},{8,12},{9,5},{12,14},{13,9},{14,10},{15,13... | collective-permute-start | bytes 2064392 | tf_op jit(solution)/shard_map/ppermute | solution.py:426
  119.6 8.1 %collective-permute-start.19 = (bf16[384,896]{1,0:T(8,128)(2,1)S(1)}, bf16[384,896]{1,0:T(8,128)(2,1)S(1)}, u32[]{:S(2)}, u32[]{:S(2)}) collective-permute-start(bf16[384,896]{1,0:T(8,128)(2,1)S(1)} %collective-permute-done.10.refs_0_), channel_id=1, source_target_pairs={{0,1},{1,0},{4,5},{5,4},{8,9},{9,8},{12,13},{13,12},{14,15},{15,14... | collective-permute-start | bytes 2064392 | tf_op jit(solution)/shard_map/ppermute | solution.py:427
  119.6 8.7 %collective-permute-start.18 = (bf16[384,896]{1,0:T(8,128)(2,1)S(1)}, bf16[384,896]{1,0:T(8,128)(2,1)S(1)}, u32[]{:S(2)}, u32[]{:S(2)}) collective-permute-start(bf16[384,896]{1,0:T(8,128)(2,1)S(1)} %collective-permute-done.7.refs_2_), channel_id=1, source_target_pairs={{0,1},{1,0},{4,5},{5,4},{8,9},{9,8},{12,13},{13,12},{14,15},{15,14... | collective-permute-start | bytes 2064392 | tf_op jit(solution)/shard_map/ppermute | solution.py:427
  122.3 20.4 %collective-permute-start.16 = (bf16[384,896]{1,0:T(8,128)(2,1)S(1)}, bf16[384,896]{1,0:T(8,128)(2,1)S(1)}, u32[]{:S(2)}, u32[]{:S(2)}) collective-permute-start(bf16[384,896]{1,0:T(8,128)(2,1)S(1)} %collective-permute-done.15.refs_2_), channel_id=1, source_target_pairs={{0,1},{1,0},{4,5},{5,4},{8,9},{9,8},{12,13},{13,12},{14,15},{15,14... | collective-permute-start | bytes 2064392 | tf_op jit(solution)/shard_map/ppermute | solution.py:427
  122.5 22.7 %collective-permute-start.17 = (bf16[384,896]{1,0:T(8,128)(2,1)S(1)}, bf16[384,896]{1,0:T(8,128)(2,1)S(1)}, u32[]{:S(2)}, u32[]{:S(2)}) collective-permute-start(bf16[384,896]{1,0:T(8,128)(2,1)S(1)} %collective-permute-done.2.refs_0_), channel_id=1, source_target_pairs={{0,1},{1,0},{4,5},{5,4},{8,9},{9,8},{12,13},{13,12},{14,15},{15,14... | collective-permute-start | bytes 2064392 | tf_op jit(solution)/shard_map/ppermute | solution.py:427
  127.4 26.8 %collective-permute-start.12 = (bf16[384,896]{1,0:T(8,128)(2,1)S(1)}, bf16[384,896]{1,0:T(8,128)(2,1)S(1)}, u32[]{:S(2)}, u32[]{:S(2)}) collective-permute-start(bf16[384,896]{1,0:T(8,128)(2,1)S(1)} %collective-permute-done.11.refs_0_), channel_id=1, source_target_pairs={{0,1},{1,0},{4,5},{5,4},{8,9},{9,8},{12,13},{13,12},{14,15},{15,14... | collective-permute-start | bytes 2064392 | tf_op jit(solution)/shard_map/ppermute | solution.py:427
  127.6 17.1 %collective-permute-start.31 = (bf16[192,896]{1,0:T(8,128)(2,1)S(1)}, bf16[192,896]{1,0:T(8,128)(2,1)S(1)}, u32[]{:S(2)}, u32[]{:S(2)}) collective-permute-start(bf16[192,896]{1,0:T(8,128)(2,1)S(1)} %get-tuple-element.39), channel_id=1, source_target_pairs={{0,4},{1,3},{4,8},{5,1},{8,12},{9,5},{12,14},{13,9},{14,10},{15,13... | collective-permute-start | bytes 1032200 | tf_op jit(solution)/shard_map/ppermute | solution.py:426
  128.3 16.5 %collective-permute-start.3 = (bf16[192,896]{1,0:T(8,128)(2,1)S(1)}, bf16[192,896]{1,0:T(8,128)(2,1)S(1)}, u32[]{:S(2)}, u32[]{:S(2)}) collective-permute-start(bf16[192,896]{1,0:T(8,128)(2,1)S(1)} %get-tuple-element.40), channel_id=1, source_target_pairs={{0,4},{1,3},{4,8},{5,1},{8,12},{9,5},{12,14},{13,9},{14,10},{15,13... | collective-permute-start | bytes 1032200 | tf_op jit(solution)/shard_map/ppermute | solution.py:426
  142.7 16.3 %collective-permute-start.34 = (bf16[192,896]{1,0:T(8,128)(2,1)S(1)}, bf16[192,896]{1,0:T(8,128)(2,1)S(1)}, u32[]{:S(2)}, u32[]{:S(2)}) collective-permute-start(bf16[192,896]{1,0:T(8,128)(2,1)S(1)} %collective-permute-done.33.refs_2_), channel_id=1, source_target_pairs={{0,1},{1,0},{4,5},{5,4},{8,9},{9,8},{12,13},{13,12},{14,15},{15,14... | collective-permute-start | bytes 1032200 | tf_op jit(solution)/shard_map/ppermute | solution.py:427
  144.7 16.4 %collective-permute-start.9 = (bf16[192,896]{1,0:T(8,128)(2,1)S(1)}, bf16[192,896]{1,0:T(8,128)(2,1)S(1)}, u32[]{:S(2)}, u32[]{:S(2)}) collective-permute-start(bf16[192,896]{1,0:T(8,128)(2,1)S(1)} %collective-permute-done.8.refs_1_), channel_id=1, source_target_pairs={{0,1},{1,0},{4,5},{5,4},{8,9},{9,8},{12,13},{13,12},{14,15},{15,14... | collective-permute-start | bytes 1032200 | tf_op jit(solution)/shard_map/ppermute | solution.py:427
  144.8 14.3 %collective-permute-start.32 = (bf16[192,896]{1,0:T(8,128)(2,1)S(1)}, bf16[192,896]{1,0:T(8,128)(2,1)S(1)}, u32[]{:S(2)}, u32[]{:S(2)}) collective-permute-start(bf16[192,896]{1,0:T(8,128)(2,1)S(1)} %collective-permute-done.31.refs_0_), channel_id=1, source_target_pairs={{0,1},{1,0},{4,5},{5,4},{8,9},{9,8},{12,13},{13,12},{14,15},{15,14... | collective-permute-start | bytes 1032200 | tf_op jit(solution)/shard_map/ppermute | solution.py:427
  145.2 15.9 %collective-permute-start.4 = (bf16[192,896]{1,0:T(8,128)(2,1)S(1)}, bf16[192,896]{1,0:T(8,128)(2,1)S(1)}, u32[]{:S(2)}, u32[]{:S(2)}) collective-permute-start(bf16[192,896]{1,0:T(8,128)(2,1)S(1)} %collective-permute-done.3.refs_0_), channel_id=1, source_target_pairs={{0,1},{1,0},{4,5},{5,4},{8,9},{9,8},{12,13},{13,12},{14,15},{15,14... | collective-permute-start | bytes 1032200 | tf_op jit(solution)/shard_map/ppermute | solution.py:427
  (6 other events, 59.9 us)

commit v11 on v9

--- a/solution.py
+++ b/solution.py
@@ -8,6 +8,7 @@
 
 
 LANES = 128
+FAR = (1, 2, 3, 4)
 
 
 def chip_ring(mesh):
@@ -187,7 +188,7 @@
     return half, lax.ppermute(half, "row", partner)
 
 
-def chunk_matmul(chunks, starts, first, weight, added, out_dtype, ready, ahead):
+def chunk_matmul(chunks, starts, first, weight, added, out_dtype, ready, ahead, far=False):
     count = len(chunks)
     rows = chunks[0].shape[0]
     widths = [c.shape[1] for c in chunks]
@@ -206,6 +207,12 @@
             return w_any.at[:, pl.ds(start, units)]
 
         copies = []
+        if far:
+            near, x_sem, refs = refs[:count], refs[count], refs[count + 1 :]
+            arrivals = [pltpu.make_async_copy(x_refs[k], near[k], x_sem.at[k]) for k in range(count)]
+            for copy in arrivals:
+                copy.start()
+            x_refs = near
         if not ready:
             w_refs, w_sem = refs[:count], refs[count]
             for k in range(count):
@@ -220,6 +227,8 @@
             fetch.start()
         total = None
         for k in range(count):
+            if far:
+                arrivals[k].wait()
             if copies:
                 copies[k].wait()
             part = lax.dot_general(
@@ -238,6 +247,10 @@
     anywhere = pl.BlockSpec(memory_space=pltpu.HBM)
     vmem = pl.BlockSpec(memory_space=pltpu.VMEM)
     scratch = []
+    if far:
+        chunks = [in_hbm(chunk) for chunk in chunks]
+        scratch += [pltpu.VMEM((rows, w), jnp.bfloat16) for w in widths]
+        scratch += [pltpu.SemaphoreType.DMA((count,))]
     if not ready:
         scratch += [pltpu.VMEM((features, w), jnp.bfloat16) for w in widths]
         scratch += [pltpu.SemaphoreType.DMA((count,))]
@@ -251,7 +264,7 @@
         out_shape=[jax.ShapeDtypeStruct((rows, features), out_dtype)]
         + [jax.ShapeDtypeStruct((features, units), jnp.bfloat16) for _, units in ahead],
         in_specs=[pl.BlockSpec(memory_space=pltpu.SMEM)]
-        + [vmem] * count
+        + [anywhere if far else vmem] * count
         + [anywhere]
         + [vmem] * (len(ready) + len(added)),
         out_specs=[vmem] * (1 + later),
@@ -268,7 +281,7 @@
 
 def row_cuts(total):
     unit = total // 24
-    return [(0, 12 * unit), (12 * unit, 12 * unit)]
+    return [(0, 13 * unit), (13 * unit, 11 * unit)]
 
 
 def rows_matmul(chunks, blocks, acc, row, out, final):
@@ -426,7 +439,7 @@
         starts = jnp.asarray(table)[me]
         acc, ready, done = [], [], 0
         ends = len(batches) - len(cuts)
-        settled = min(4, ends - 1)
+        settled = min(5, ends - 1)
         for k, found in enumerate(batches[:ends]):
             coming = batches[k + 1] if k >= settled else []
             at = done + len(found)
@@ -440,6 +453,7 @@
                 jnp.float32,
                 ready,
                 ahead,
+                k in FAR,
             )
             acc, ready, done = [out], list(ready_next), at
         out = None

time: 161 us -> 163 us (1.012)
  waiting for transfers between devices: 78.2 us -> 81.5 us
  starting transfers between devices: 30 us -> 27.2 us
    ppermute x15, waiting for transfers between devices: 71.1 us -> 74.4 us  [hop(): data = lax.ppermute(data, 'row', pairs)]
  transfers between devices with their start and end apart: 36 -> 36, of which waited for: 14 -> 16; matrix products, arithmetic and copies ran while one was open for 1% -> 1% of each run, Pallas kernels for 21% -> 22%
where the time goes in v11:
time: 163 us
  waiting for transfers between devices  81.5 us (50%)
  Pallas kernels  41.3 us (25%)
  starting transfers between devices  27.2 us (17%)
  blocking collectives  7.98 us (5%)
  local copies, waits for them, and re-layouts  2.38 us (1%)
    ppermute x15, waiting for transfers between devices, hop(): data = lax.ppermute(data, 'row', pairs)  74.4 us
    pallas_call x7, Pallas kernels, chunk_matmul(): pl.pallas_call(body, out_shape=[jax.ShapeDtypeStruct((rows, features), ou...  30.8 us
    ppermute x15, starting transfers between devices, hop(): data = lax.ppermute(data, 'row', pairs)  15.5 us
    all_to_all x1, blocking collectives, sum_by_stages(): lax.all_to_all(spread, 'row', 0, 0, axis_index_groups=lines, tiled=True)  7.98 us
    all_to_all x1, starting transfers between devices, sum_by_stages(): lax.all_to_all(rows, 'row', 0, 0, axis_index_groups=lines, tiled=True)  5.37 us
    pallas_call x3, Pallas kernels, rows_matmul(): pl.pallas_call(body, out_shape=shape, in_specs=[vmem] * (2 * count + 1) +...  4.25 us
    pallas_call x1, Pallas kernels, project_selected(): pl.pallas_call(body, out_shape=(shape, shape), in_specs=[pl.BlockSpec(mem...  3.36 us
  transfers between devices with their start and end apart: 36, of which 16 were waited for; matrix products, arithmetic and copies ran while one was open for 1% of the time, Pallas kernels for 22%

profile of v11, /device:TPU:0, one launch (start us, length us, event | category | flops | bytes accessed | tf_op | source)
XLA Modules:
  0.0 162.5 jit_solution(5933771705603110518)
XLA Ops:
  0.0 0.7 constant_dynamic-slice_fusion
  0.7 0.6 fusion.1
  1.3 1.3 shard_map.74
  2.8 3.4 %shard_map.81 = (f32[192,128]{1,0:T(8,128)S(1)}, f32[192,128]{1,0:T(8,128)S(1)}) custom-call(s32[1]{0:T(128)} %bitcast.2.f_ref.core_ref, bf16[384,896]{1,0:T(8,128)(2,1)S(1)} %get-tuple-element.24.refs_0_.low_ref, bf16[384,896]{1,0:T(8,128)(2,1)S(1)} %get-tuple-element.22.refs_1_.high_ref, s32[384,1]{1,0:T(8,128)S(1)} %broadcast_in_dim_reshape.5.l_ref, ...), custom_call_target="tpu_custom_call" | custom-call | flops 704643072 | bytes 3407872 | tf_op jit(solution)/shard_map/pallas_call | solution.py:95
  6.2 0.6 collective-permute-start.27
  7.7 2.9 %collective-permute-start.28 = (f32[96,128]{1,0:T(8,128)S(1)}, f32[96,128]{1,0:T(8,128)S(1)}, u32[]{:S(2)}, u32[]{:S(2)}) collective-permute-start(f32[96,128]{1,0:T(8,128)S(1)} %slice_select_fusion), channel_id=1, source_target_pairs={{0,2},{1,3},{4,6},{5,7},{8,10},{9,11},{12,14},{13,15},{14,12},{15,... | collective-permute-start | bytes 147464 | tf_op jit(solution)/shard_map/ppermute | solution.py:162
  10.7 2.1 %collective-permute-done.28 = f32[96,128]{1,0:T(8,128)S(1)} collective-permute-done((f32[96,128]{1,0:T(8,128)S(1)}, f32[96,128]{1,0:T(8,128)S(1)}, u32[]{:S(2)}, u32[]{:S(2)}) %collective-permute-start.28) | collective-permute-done | bytes 49184 | tf_op jit(solution)/shard_map/ppermute | solution.py:162
  12.7 0.6 select_add_fusion
  13.4 5.4 %all-to-all-start = ((f32[4,24,128]{2,1,0:T(8,128)}), f32[4,24,128]{2,1,0:T(8,128)S(1)}, u32[]{:S(2)}, u32[]{:S(2)}) async-start(f32[4,24,128]{2,1,0:T(8,128)} %bitcast.5), calls=%async_computation | async-start | bytes 98304 | tf_op jit(solution)/shard_map/all_to_all | solution.py:183
  18.8 3.5 %collective-permute-start.5 = (bf16[384,896]{1,0:T(8,128)(2,1)S(1)}, bf16[384,896]{1,0:T(8,128)(2,1)}, u32[]{:S(2)}, u32[]{:S(2)}) collective-permute-start(bf16[384,896]{1,0:T(8,128)(2,1)S(1)} %get-tuple-element.22.refs_1_.high_ref), channel_id=1, source_target_pairs={{4,0},{3,1},{8,4},{1,5},{12,8},{5,9},{14,12},{9,13},{10,14},{13,15... | collective-permute-start | bytes 2064392 | tf_op jit(solution)/shard_map/ppermute | solution.py:412
  22.2 2.3 %all-to-all-done = f32[4,24,128]{2,1,0:T(8,128)S(1)} async-done(((f32[4,24,128]{2,1,0:T(8,128)}), f32[4,24,128]{2,1,0:T(8,128)S(1)}, u32[]{:S(2)}, u32[]{:S(2)}) %all-to-all-start) | async-done | bytes 49184 | tf_op jit(solution)/shard_map/all_to_all | solution.py:183
  24.7 8.0 %all_to_all.18 = bf16[4,24,128]{2,1,0:T(8,128)(2,1)S(1)} all-to-all(bf16[4,24,128]{2,1,0:T(8,128)(2,1)S(1)} %broadcast_in_dim.2), channel_id=1, replica_groups={{0,4,8,12},{1,5,9,13},{14,10,6,2},{15,11,7,3},{16,20,24,28},{17,21,25,2..., dimensions={0} | all-to-all | bytes 49152 | tf_op jit(solution)/shard_map/all_to_all | solution.py:186
  32.7 0.5 collective-permute-start.29
  33.2 1.5 collective-permute-start.13
  35.3 1.5 collective-permute-done.29
  37.3 0.9 collective-permute-done.30.other_ref
  38.3 13.3 %collective-permute-done.13.refs_2_ = bf16[384,896]{1,0:T(8,128)(2,1)S(1)} collective-permute-done((bf16[384,896]{1,0:T(8,128)(2,1)S(1)}, bf16[384,896]{1,0:T(8,128)(2,1)S(1)}, u32[]{:S(2)}, u32[]{:S(2)}) %collective-permute-start.13) | collective-permute-done | bytes 688160 | tf_op jit(solution)/shard_map/ppermute | solution.py:412
  51.6 1.5 collective-permute-start.14
  53.1 12.4 %collective-permute-done.6.refs_2_ = bf16[384,896]{1,0:T(8,128)(2,1)S(1)} collective-permute-done((bf16[384,896]{1,0:T(8,128)(2,1)}, bf16[384,896]{1,0:T(8,128)(2,1)S(1)}, u32[]{:S(2)}, u32[]{:S(2)}) %collective-permute-start.6) | collective-permute-done | bytes 688160 | tf_op jit(solution)/shard_map/ppermute | solution.py:412
  65.5 1.6 collective-permute-start.7
  67.0 1.0 collective-permute-done.x_ref.refs_0_
  68.2 0.6 collective-permute-start.1
  68.8 5.6 %collective-permute-done.14.refs_2_ = bf16[384,896]{1,0:T(8,128)(2,1)S(1)} collective-permute-done((bf16[384,896]{1,0:T(8,128)(2,1)S(1)}, bf16[384,896]{1,0:T(8,128)(2,1)S(1)}, u32[]{:S(2)}, u32[]{:S(2)}) %collective-permute-start.14) | collective-permute-done | bytes 688160 | tf_op jit(solution)/shard_map/ppermute | solution.py:412
  74.4 0.7 collective-permute-start.10
  75.1 14.0 %collective-permute-done.7.refs_2_ = bf16[384,896]{1,0:T(8,128)(2,1)S(1)} collective-permute-done((bf16[384,896]{1,0:T(8,128)(2,1)S(1)}, bf16[384,896]{1,0:T(8,128)(2,1)S(1)}, u32[]{:S(2)}, u32[]{:S(2)}) %collective-permute-start.7) | collective-permute-done | bytes 688160 | tf_op jit(solution)/shard_map/ppermute | solution.py:412
  89.1 2.3 %collective-permute-start.15 = (bf16[384,896]{1,0:T(8,128)(2,1)S(1)}, bf16[384,896]{1,0:T(8,128)(2,1)S(1)}, u32[]{:S(2)}, u32[]{:S(2)}) collective-permute-start(bf16[384,896]{1,0:T(8,128)(2,1)S(1)} %collective-permute-done.14.refs_2_), channel_id=1, source_target_pairs={{4,0},{3,1},{8,4},{1,5},{12,8},{5,9},{14,12},{9,13},{10,14},{13,15... | collective-permute-start | bytes 2064392 | tf_op jit(solution)/shard_map/ppermute | solution.py:412
  91.7 6.9 %collective-permute-done.10.refs_0_ = bf16[384,896]{1,0:T(8,128)(2,1)S(1)} collective-permute-done((bf16[384,896]{1,0:T(8,128)(2,1)S(1)}, bf16[384,896]{1,0:T(8,128)(2,1)S(1)}, u32[]{:S(2)}, u32[]{:S(2)}) %collective-permute-start.10) | collective-permute-done | bytes 688160 | tf_op jit(solution)/shard_map/ppermute | solution.py:412
  98.6 3.8 %collective-permute-done.15.refs_2_ = bf16[384,896]{1,0:T(8,128)(2,1)S(1)} collective-permute-done((bf16[384,896]{1,0:T(8,128)(2,1)S(1)}, bf16[384,896]{1,0:T(8,128)(2,1)S(1)}, u32[]{:S(2)}, u32[]{:S(2)}) %collective-permute-start.15) | collective-permute-done | bytes 688160 | tf_op jit(solution)/shard_map/ppermute | solution.py:412
  102.3 0.6 collective-permute-start.2
  102.9 3.9 %collective-permute-done.8.refs_1_ = bf16[176,896]{1,0:T(8,128)(2,1)S(1)} collective-permute-done((bf16[176,896]{1,0:T(8,128)(2,1)S(1)}, bf16[176,896]{1,0:T(8,128)(2,1)S(1)}, u32[]{:S(2)}, u32[]{:S(2)}) %collective-permute-start.8) | collective-permute-done | bytes 315424 | tf_op jit(solution)/shard_map/ppermute | solution.py:412
  106.8 0.7 collective-permute-start.11
  107.5 7.3 %collective-permute-done.33.refs_2_ = bf16[208,896]{1,0:T(8,128)(2,1)S(1)} collective-permute-done((bf16[208,896]{1,0:T(8,128)(2,1)S(1)}, bf16[208,896]{1,0:T(8,128)(2,1)S(1)}, u32[]{:S(2)}, u32[]{:S(2)}) %collective-permute-start.33) | collective-permute-done | bytes 372768 | tf_op jit(solution)/shard_map/ppermute | solution.py:412
  115.4 1.5 collective-permute-done.2.refs_0_
  117.2 0.7 dynamic-slice_bitcast_fusion.starts_ref
  117.9 1.5 shard_map.82.refs_10_
  119.4 4.9 %collective-permute-done.11.refs_0_ = bf16[384,896]{1,0:T(8,128)(2,1)S(1)} collective-permute-done((bf16[384,896]{1,0:T(8,128)(2,1)S(1)}, bf16[384,896]{1,0:T(8,128)(2,1)S(1)}, u32[]{:S(2)}, u32[]{:S(2)}) %collective-permute-start.11) | collective-permute-done | bytes 688160 | tf_op jit(solution)/shard_map/ppermute | solution.py:412
  124.4 3.8 %shard_map.75.refs_3_ = f32[384,512]{1,0:T(8,128)S(1)} custom-call(s32[33]{0:T(128)S(1)} %dynamic-slice_bitcast_fusion.starts_ref, bf16[384,896]{1,0:T(8,128)(2,1)S(1)} %get-tuple-element.24.refs_0_.low_ref, bf16[384,896]{1,0:T(8,128)(2,1)S(1)} %get-tuple-element.22.refs_1_.high_ref, bf16[384,1792]{1,0:T(8,128)(2,1)S(1)} %collective-permute-done.26.refs_2_, ...), custom_call_target="tpu_custom_call" | custom-call | flops 1409286144 | bytes 7995392 | tf_op jit(solution)/shard_map/pallas_call | solution.py:262
  128.3 0.6 collective-permute-start.31
  128.9 3.5 %shard_map.76.refs_5_ = f32[384,512]{1,0:T(8,128)S(1)} custom-call(s32[33]{0:T(128)S(1)} %dynamic-slice_bitcast_fusion.starts_ref, bf16[384,896]{1,0:T(8,128)(2,1)} %collective-permute-done.5.refs_0_, bf16[384,896]{1,0:T(8,128)(2,1)} %copy-done.13, bf16[512,28672]{1,0:T(8,128)(2,1)} %refs_4_.9, f32[384,512]{1,0:T(8,128)S(1)} %shard_map.75.refs_3_), custom_call_target="tpu_custom_call" | custom-call | flops 704643072 | bytes 4784128 | tf_op jit(solution)/shard_map/pallas_call | solution.py:262
  132.4 1.0 collective-permute-start.3
  133.4 6.1 %shard_map.77.refs_5_ = f32[384,512]{1,0:T(8,128)S(1)} custom-call(s32[33]{0:T(128)S(1)} %dynamic-slice_bitcast_fusion.starts_ref, bf16[384,1792]{1,0:T(8,128)(2,1)} %copy-done, bf16[384,1792]{1,0:T(8,128)(2,1)} %copy-done.2, bf16[384,896]{1,0:T(8,128)(2,1)} %copy-done.3, bf16[384,896]{1,0:T(8,128)(2,1)} %copy-done.6, bf16[512,28672]{1,0:T(8,128)(2,1)} %refs_4_.9, ...), custom_call_target="tpu_custom_call" | custom-call | flops 2113929216 | bytes 11206656 | tf_op jit(solution)/shard_map/pallas_call | solution.py:262
  139.5 4.5 %shard_map.78.refs_5_ = f32[384,512]{1,0:T(8,128)S(1)} custom-call(s32[33]{0:T(128)S(1)} %dynamic-slice_bitcast_fusion.starts_ref, bf16[384,896]{1,0:T(8,128)(2,1)} %copy-done.10, bf16[384,896]{1,0:T(8,128)(2,1)} %copy-done.12, bf16[384,896]{1,0:T(8,128)(2,1)} %copy-done.5, bf16[384,896]{1,0:T(8,128)(2,1)} %copy-done.8, bf16[512,28672]{1,0:T(8,128)(2,1)} %refs_4_.9, ...), custom_call_target="tpu_custom_call" | custom-call | flops 1409286144 | bytes 7995392 | tf_op jit(solution)/shard_map/pallas_call | solution.py:262
  145.1 4.5 %shard_map.79.refs_5_ = f32[384,512]{1,0:T(8,128)S(1)} custom-call(s32[33]{0:T(128)S(1)} %dynamic-slice_bitcast_fusion.starts_ref, bf16[384,896]{1,0:T(8,128)(2,1)} %copy-done.9, bf16[384,896]{1,0:T(8,128)(2,1)} %copy-done.11, bf16[384,896]{1,0:T(8,128)(2,1)} %copy-done.4, bf16[384,896]{1,0:T(8,128)(2,1)} %copy-done.7, bf16[512,28672]{1,0:T(8,128)(2,1)} %refs_4_.9, ...), custom_call_target="tpu_custom_call" | custom-call | flops 1409286144 | bytes 7995392 | tf_op jit(solution)/shard_map/pallas_call | solution.py:262
  149.6 4.4 %shard_map.80 = (f32[384,512]{1,0:T(8,128)S(1)}, bf16[512,896]{1,0:T(8,128)(2,1)S(1)}, bf16[512,896]{1,0:T(8,128)(2,1)S(1)}, bf16[512,896]{1,0:T(8,128)(2,1)S(1)}, bf16[512,896]{1,0:T(8,128)(2,1)S(1)}) custom-call(s32[33]{0:T(128)S(1)} %dynamic-slice_bitcast_fusion.starts_ref, bf16[384,896]{1,0:T(8,128)(2,1)S(1)} %collective-permute-done.2.refs_0_, ...), custom_call_target="tpu_custom_call" | custom-call | flops 1409286144 | bytes 11665408 | tf_op jit(solution)/shard_map/pallas_call | solution.py:262
  154.0 4.1 %shard_map.83 = (f32[384,512]{1,0:T(8,128)S(1)}, bf16[512,896]{1,0:T(8,128)(2,1)S(1)}, bf16[512,896]{1,0:T(8,128)(2,1)S(1)}, bf16[512,896]{1,0:T(8,128)(2,1)S(1)}, bf16[512,896]{1,0:T(8,128)(2,1)S(1)}) custom-call(s32[33]{0:T(128)S(1)} %dynamic-slice_bitcast_fusion.starts_ref, bf16[384,896]{1,0:T(8,128)(2,1)S(1)} %collective-permute-done.11.refs_0_, ...), custom_call_target="tpu_custom_call" | custom-call | flops 1409286144 | bytes 11665408 | tf_op jit(solution)/shard_map/pallas_call | solution.py:262
  158.1 0.8 shard_map.84.refs_4_
  158.8 2.0 %shard_map.85.refs_5_ = bf16[384,512]{1,0:T(8,128)(2,1)} custom-call(bf16[208,896]{1,0:T(8,128)(2,1)S(1)} %collective-permute-done.31.refs_0_, bf16[208,896]{1,0:T(8,128)(2,1)S(1)} %collective-permute-done.32.refs_1_, bf16[208,896]{1,0:T(8,128)(2,1)S(1)} %collective-permute-done.33.refs_2_, bf16[208,896]{1,0:T(8,128)(2,1)S(1)} %collective-permute-done.34.refs_3_, ...), custom_call_target="tpu_custom_call" | custom-call | tf_op jit(solution)/shard_map/pallas_call | solution.py:314
  160.9 1.5 shard_map.86
  (87 shorter events, 4.4 us)
Async XLA Ops:
  6.2 1.5 collective-permute-start.27
  7.7 5.0 %collective-permute-start.28 = (f32[96,128]{1,0:T(8,128)S(1)}, f32[96,128]{1,0:T(8,128)S(1)}, u32[]{:S(2)}, u32[]{:S(2)}) collective-permute-start(f32[96,128]{1,0:T(8,128)S(1)} %slice_select_fusion), channel_id=1, source_target_pairs={{0,2},{1,3},{4,6},{5,7},{8,10},{9,11},{12,14},{13,15},{14,12},{15,... | collective-permute-start | bytes 147464 | tf_op jit(solution)/shard_map/ppermute | solution.py:162
  13.4 11.2 %all-to-all-start = ((f32[4,24,128]{2,1,0:T(8,128)}), f32[4,24,128]{2,1,0:T(8,128)S(1)}, u32[]{:S(2)}, u32[]{:S(2)}) async-start(f32[4,24,128]{2,1,0:T(8,128)} %bitcast.5), calls=%async_computation | async-start | bytes 98304 | tf_op jit(solution)/shard_map/all_to_all | solution.py:183
  18.7 32.8 %collective-permute-start.26 = (bf16[384,1792]{1,0:T(8,128)(2,1)}, bf16[384,1792]{1,0:T(8,128)(2,1)S(1)}, u32[]{:S(2)}, u32[]{:S(2)}) collective-permute-start(bf16[384,1792]{1,0:T(8,128)(2,1)} %bitcast.15), channel_id=1, source_target_pairs={{0,1},{1,0},{4,5},{5,4},{8,9},{9,8},{12,13},{13,12},{14,15},{15,14... | collective-permute-start | bytes 4128776 | tf_op jit(solution)/shard_map/ppermute | solution.py:408
  18.8 18.2 %collective-permute-start.5 = (bf16[384,896]{1,0:T(8,128)(2,1)S(1)}, bf16[384,896]{1,0:T(8,128)(2,1)}, u32[]{:S(2)}, u32[]{:S(2)}) collective-permute-start(bf16[384,896]{1,0:T(8,128)(2,1)S(1)} %get-tuple-element.22.refs_1_.high_ref), channel_id=1, source_target_pairs={{4,0},{3,1},{8,4},{1,5},{12,8},{5,9},{14,12},{9,13},{10,14},{13,15... | collective-permute-start | bytes 2064392 | tf_op jit(solution)/shard_map/ppermute | solution.py:412
  32.7 4.1 %collective-permute-start.29 = (bf16[96,128]{1,0:T(8,128)(2,1)S(1)}, bf16[96,128]{1,0:T(8,128)(2,1)S(1)}, u32[]{:S(2)}, u32[]{:S(2)}) collective-permute-start(bf16[96,128]{1,0:T(8,128)(2,1)S(1)} %bitcast.17), channel_id=1, source_target_pairs={{0,2},{1,3},{4,6},{5,7},{8,10},{9,11},{12,14},{13,15},{14,12},{15,... | collective-permute-start | bytes 73736 | tf_op jit(solution)/shard_map/ppermute | solution.py:167
  33.2 18.3 %collective-permute-start.13 = (bf16[384,896]{1,0:T(8,128)(2,1)S(1)}, bf16[384,896]{1,0:T(8,128)(2,1)S(1)}, u32[]{:S(2)}, u32[]{:S(2)}) collective-permute-start(bf16[384,896]{1,0:T(8,128)(2,1)S(1)} %get-tuple-element.24.refs_0_.low_ref), channel_id=1, source_target_pairs={{4,0},{3,1},{8,4},{1,5},{12,8},{5,9},{14,12},{9,13},{10,14},{13,15... | collective-permute-start | bytes 2064392 | tf_op jit(solution)/shard_map/ppermute | solution.py:412
  34.7 33.3 %collective-permute-start = (bf16[384,1792]{1,0:T(8,128)(2,1)}, bf16[384,1792]{1,0:T(8,128)(2,1)S(1)}, u32[]{:S(2)}, u32[]{:S(2)}) collective-permute-start(bf16[384,1792]{1,0:T(8,128)(2,1)} %bitcast.16), channel_id=1, source_target_pairs={{0,4},{1,3},{4,8},{5,1},{8,12},{9,5},{12,14},{13,9},{14,10},{15,13... | collective-permute-start | bytes 4128776 | tf_op jit(solution)/shard_map/ppermute | solution.py:412
  36.8 81.1 %copy-start.1 = (bf16[8,64,512]{2,1,0:T(8,128)(2,1)S(1)}, bf16[8,64,512]{2,1,0:T(8,128)(2,1)}, u32[]{:S(2)}) copy-start(bf16[8,64,512]{2,1,0:T(8,128)(2,1)} %param.10) | copy-start | bytes 1572868
  36.8 1.3 collective-permute-start.30
  36.9 28.5 %collective-permute-start.6 = (bf16[384,896]{1,0:T(8,128)(2,1)}, bf16[384,896]{1,0:T(8,128)(2,1)S(1)}, u32[]{:S(2)}, u32[]{:S(2)}) collective-permute-start(bf16[384,896]{1,0:T(8,128)(2,1)} %collective-permute-done.5.refs_0_), channel_id=1, source_target_pairs={{4,0},{3,1},{8,4},{1,5},{12,8},{5,9},{14,12},{9,13},{10,14},{13,15... | collective-permute-start | bytes 2064392 | tf_op jit(solution)/shard_map/ppermute | solution.py:412
  38.1 27.4 %collective-permute-start.25 = (bf16[384,896]{1,0:T(8,128)(2,1)}, bf16[384,896]{1,0:T(8,128)(2,1)S(1)}, u32[]{:S(2)}, u32[]{:S(2)}) collective-permute-start(bf16[384,896]{1,0:T(8,128)(2,1)} %collective-permute-done.5.refs_0_), channel_id=1, source_target_pairs={{0,1},{1,0},{4,5},{5,4},{8,9},{9,8},{12,13},{13,12},{14,15},{15,14... | collective-permute-start | bytes 2064392 | tf_op jit(solution)/shard_map/ppermute | solution.py:413
  51.6 40.0 %copy-start.3 = (bf16[384,896]{1,0:T(8,128)(2,1)}, bf16[384,896]{1,0:T(8,128)(2,1)S(1)}, u32[]{:S(2)}) copy-start(bf16[384,896]{1,0:T(8,128)(2,1)S(1)} %collective-permute-done.13.refs_2_) | copy-start | bytes 2064388
  51.6 16.6 %collective-permute-start.24 = (bf16[384,896]{1,0:T(8,128)(2,1)S(1)}, bf16[384,896]{1,0:T(8,128)(2,1)S(1)}, u32[]{:S(2)}, u32[]{:S(2)}) collective-permute-start(bf16[384,896]{1,0:T(8,128)(2,1)S(1)} %collective-permute-done.13.refs_2_), channel_id=1, source_target_pairs={{0,1},{1,0},{4,5},{5,4},{8,9},{9,8},{12,13},{13,12},{14,15},{15,14... | collective-permute-start | bytes 2064392 | tf_op jit(solution)/shard_map/ppermute | solution.py:413
  51.6 22.8 %collective-permute-start.14 = (bf16[384,896]{1,0:T(8,128)(2,1)S(1)}, bf16[384,896]{1,0:T(8,128)(2,1)S(1)}, u32[]{:S(2)}, u32[]{:S(2)}) collective-permute-start(bf16[384,896]{1,0:T(8,128)(2,1)S(1)} %collective-permute-done.13.refs_2_), channel_id=1, source_target_pairs={{4,0},{3,1},{8,4},{1,5},{12,8},{5,9},{14,12},{9,13},{10,14},{13,15... | collective-permute-start | bytes 2064392 | tf_op jit(solution)/shard_map/ppermute | solution.py:412
  65.5 26.1 %copy-start.5 = (bf16[384,896]{1,0:T(8,128)(2,1)}, bf16[384,896]{1,0:T(8,128)(2,1)S(1)}, u32[]{:S(2)}) copy-start(bf16[384,896]{1,0:T(8,128)(2,1)S(1)} %collective-permute-done.6.refs_2_) | copy-start | bytes 2064388
  65.5 8.9 %collective-permute-start.22 = (bf16[384,896]{1,0:T(8,128)(2,1)S(1)}, bf16[384,896]{1,0:T(8,128)(2,1)S(1)}, u32[]{:S(2)}, u32[]{:S(2)}) collective-permute-start(bf16[384,896]{1,0:T(8,128)(2,1)S(1)} %collective-permute-done.6.refs_2_), channel_id=1, source_target_pairs={{0,1},{1,0},{4,5},{5,4},{8,9},{9,8},{12,13},{13,12},{14,15},{15,14... | collective-permute-start | bytes 2064392 | tf_op jit(solution)/shard_map/ppermute | solution.py:413
  65.5 62.7 %copy-start.13 = (bf16[384,896]{1,0:T(8,128)(2,1)}, bf16[384,896]{1,0:T(8,128)(2,1)S(1)}, u32[]{:S(2)}) copy-start(bf16[384,896]{1,0:T(8,128)(2,1)S(1)} %collective-permute-done.25.refs_1_) | copy-start | bytes 2064388
  65.5 23.6 %collective-permute-start.7 = (bf16[384,896]{1,0:T(8,128)(2,1)S(1)}, bf16[384,896]{1,0:T(8,128)(2,1)S(1)}, u32[]{:S(2)}, u32[]{:S(2)}) collective-permute-start(bf16[384,896]{1,0:T(8,128)(2,1)S(1)} %collective-permute-done.6.refs_2_), channel_id=1, source_target_pairs={{4,0},{3,1},{8,4},{1,5},{12,8},{5,9},{14,12},{9,13},{10,14},{13,15... | collective-permute-start | bytes 2064392 | tf_op jit(solution)/shard_map/ppermute | solution.py:412
  68.0 23.6 %copy-start = (bf16[384,1792]{1,0:T(8,128)(2,1)}, bf16[384,1792]{1,0:T(8,128)(2,1)S(1)}, u32[]{:S(2)}) copy-start(bf16[384,1792]{1,0:T(8,128)(2,1)S(1)} %collective-permute-done.x_ref.refs_0_) | copy-start | bytes 4128772
  68.0 46.8 %collective-permute-start.23 = (bf16[384,1792]{1,0:T(8,128)(2,1)S(1)}, bf16[384,1792]{1,0:T(8,128)(2,1)S(1)}, u32[]{:S(2)}, u32[]{:S(2)}) collective-permute-start(bf16[384,1792]{1,0:T(8,128)(2,1)S(1)} %collective-permute-done.x_ref.refs_0_), channel_id=1, source_target_pairs={{0,1},{1,0},{4,5},{5,4},{8,9},{9,8},{12,13},{13,12},{14,15},{15,14... | collective-permute-start | bytes 4128776 | tf_op jit(solution)/shard_map/ppermute | solution.py:413
  68.2 51.2 %copy-start.6 = (bf16[384,896]{1,0:T(8,128)(2,1)}, bf16[384,896]{1,0:T(8,128)(2,1)S(1)}, u32[]{:S(2)}) copy-start(bf16[384,896]{1,0:T(8,128)(2,1)S(1)} %collective-permute-done.24.refs_3_) | copy-start | bytes 2064388
  68.2 23.3 %collective-permute-start.1 = (bf16[384,896]{1,0:T(8,128)(2,1)S(1)}, bf16[384,896]{1,0:T(8,128)(2,1)S(1)}, u32[]{:S(2)}, u32[]{:S(2)}) collective-permute-start(bf16[384,896]{1,0:T(8,128)(2,1)S(1)} %get-tuple-element.21), channel_id=1, source_target_pairs={{0,4},{1,3},{4,8},{5,1},{8,12},{9,5},{12,14},{13,9},{14,10},{15,13... | collective-permute-start | bytes 2064392 | tf_op jit(solution)/shard_map/ppermute | solution.py:412
  74.4 45.0 %copy-start.4 = (bf16[384,896]{1,0:T(8,128)(2,1)}, bf16[384,896]{1,0:T(8,128)(2,1)S(1)}, u32[]{:S(2)}) copy-start(bf16[384,896]{1,0:T(8,128)(2,1)S(1)} %collective-permute-done.14.refs_2_) | copy-start | bytes 2064388
  74.4 17.2 %collective-permute-start.20 = (bf16[384,896]{1,0:T(8,128)(2,1)S(1)}, bf16[384,896]{1,0:T(8,128)(2,1)S(1)}, u32[]{:S(2)}, u32[]{:S(2)}) collective-permute-start(bf16[384,896]{1,0:T(8,128)(2,1)S(1)} %collective-permute-done.14.refs_2_), channel_id=1, source_target_pairs={{0,1},{1,0},{4,5},{5,4},{8,9},{9,8},{12,13},{13,12},{14,15},{15,14... | collective-permute-start | bytes 2064392 | tf_op jit(solution)/shard_map/ppermute | solution.py:413
  74.4 53.8 %copy-start.8 = (bf16[384,896]{1,0:T(8,128)(2,1)}, bf16[384,896]{1,0:T(8,128)(2,1)S(1)}, u32[]{:S(2)}) copy-start(bf16[384,896]{1,0:T(8,128)(2,1)S(1)} %collective-permute-done.22.refs_3_) | copy-start | bytes 2064388
  74.4 24.2 %collective-permute-start.10 = (bf16[384,896]{1,0:T(8,128)(2,1)S(1)}, bf16[384,896]{1,0:T(8,128)(2,1)S(1)}, u32[]{:S(2)}, u32[]{:S(2)}) collective-permute-start(bf16[384,896]{1,0:T(8,128)(2,1)S(1)} %get-tuple-element.23), channel_id=1, source_target_pairs={{0,4},{1,3},{4,8},{5,1},{8,12},{9,5},{12,14},{13,9},{14,10},{15,13... | collective-permute-start | bytes 2064392 | tf_op jit(solution)/shard_map/ppermute | solution.py:412
  89.1 13.2 %collective-permute-start.15 = (bf16[384,896]{1,0:T(8,128)(2,1)S(1)}, bf16[384,896]{1,0:T(8,128)(2,1)S(1)}, u32[]{:S(2)}, u32[]{:S(2)}) collective-permute-start(bf16[384,896]{1,0:T(8,128)(2,1)S(1)} %collective-permute-done.14.refs_2_), channel_id=1, source_target_pairs={{4,0},{3,1},{8,4},{1,5},{12,8},{5,9},{14,12},{9,13},{10,14},{13,15... | collective-permute-start | bytes 2064392 | tf_op jit(solution)/shard_map/ppermute | solution.py:412
  91.5 36.8 %copy-start.10 = (bf16[384,896]{1,0:T(8,128)(2,1)}, bf16[384,896]{1,0:T(8,128)(2,1)S(1)}, u32[]{:S(2)}) copy-start(bf16[384,896]{1,0:T(8,128)(2,1)S(1)} %collective-permute-done.1.refs_0_) | copy-start | bytes 2064388
  91.5 15.3 %collective-permute-start.8 = (bf16[176,896]{1,0:T(8,128)(2,1)S(1)}, bf16[176,896]{1,0:T(8,128)(2,1)S(1)}, u32[]{:S(2)}, u32[]{:S(2)}) collective-permute-start(bf16[176,896]{1,0:T(8,128)(2,1)S(1)} %slice.47), channel_id=1, source_target_pairs={{4,0},{3,1},{8,4},{1,5},{12,8},{5,9},{14,12},{9,13},{10,14},{13,15... | collective-permute-start | bytes 946184 | tf_op jit(solution)/shard_map/ppermute | solution.py:412
  91.6 36.6 %copy-start.7 = (bf16[384,896]{1,0:T(8,128)(2,1)}, bf16[384,896]{1,0:T(8,128)(2,1)S(1)}, u32[]{:S(2)}) copy-start(bf16[384,896]{1,0:T(8,128)(2,1)S(1)} %collective-permute-done.20.refs_3_) | copy-start | bytes 2064388
  91.6 23.2 %collective-permute-start.33 = (bf16[208,896]{1,0:T(8,128)(2,1)S(1)}, bf16[208,896]{1,0:T(8,128)(2,1)S(1)}, u32[]{:S(2)}, u32[]{:S(2)}) collective-permute-start(bf16[208,896]{1,0:T(8,128)(2,1)S(1)} %slice.53), channel_id=1, source_target_pairs={{4,0},{3,1},{8,4},{1,5},{12,8},{5,9},{14,12},{9,13},{10,14},{13,15... | collective-permute-start | bytes 1118216 | tf_op jit(solution)/shard_map/ppermute | solution.py:412
  98.6 29.7 %copy-start.9 = (bf16[384,896]{1,0:T(8,128)(2,1)}, bf16[384,896]{1,0:T(8,128)(2,1)S(1)}, u32[]{:S(2)}) copy-start(bf16[384,896]{1,0:T(8,128)(2,1)S(1)} %collective-permute-done.10.refs_0_) | copy-start | bytes 2064388
  98.6 16.8 %collective-permute-start.21 = (bf16[384,896]{1,0:T(8,128)(2,1)S(1)}, bf16[384,896]{1,0:T(8,128)(2,1)S(1)}, u32[]{:S(2)}, u32[]{:S(2)}) collective-permute-start(bf16[384,896]{1,0:T(8,128)(2,1)S(1)} %collective-permute-done.1.refs_0_), channel_id=1, source_target_pairs={{0,1},{1,0},{4,5},{5,4},{8,9},{9,8},{12,13},{13,12},{14,15},{15,14... | collective-permute-start | bytes 2064392 | tf_op jit(solution)/shard_map/ppermute | solution.py:413
  102.3 14.6 %collective-permute-start.2 = (bf16[384,896]{1,0:T(8,128)(2,1)S(1)}, bf16[384,896]{1,0:T(8,128)(2,1)S(1)}, u32[]{:S(2)}, u32[]{:S(2)}) collective-permute-start(bf16[384,896]{1,0:T(8,128)(2,1)S(1)} %collective-permute-done.1.refs_0_), channel_id=1, source_target_pairs={{0,4},{1,3},{4,8},{5,1},{8,12},{9,5},{12,14},{13,9},{14,10},{15,13... | collective-permute-start | bytes 2064392 | tf_op jit(solution)/shard_map/ppermute | solution.py:412
  106.8 17.4 %collective-permute-start.11 = (bf16[384,896]{1,0:T(8,128)(2,1)S(1)}, bf16[384,896]{1,0:T(8,128)(2,1)S(1)}, u32[]{:S(2)}, u32[]{:S(2)}) collective-permute-start(bf16[384,896]{1,0:T(8,128)(2,1)S(1)} %collective-permute-done.10.refs_0_), channel_id=1, source_target_pairs={{0,4},{1,3},{4,8},{5,1},{8,12},{9,5},{12,14},{13,9},{14,10},{15,13... | collective-permute-start | bytes 2064392 | tf_op jit(solution)/shard_map/ppermute | solution.py:412
  114.8 13.5 %collective-permute-start.19 = (bf16[384,896]{1,0:T(8,128)(2,1)S(1)}, bf16[384,896]{1,0:T(8,128)(2,1)S(1)}, u32[]{:S(2)}, u32[]{:S(2)}) collective-permute-start(bf16[384,896]{1,0:T(8,128)(2,1)S(1)} %collective-permute-done.10.refs_0_), channel_id=1, source_target_pairs={{0,1},{1,0},{4,5},{5,4},{8,9},{9,8},{12,13},{13,12},{14,15},{15,14... | collective-permute-start | bytes 2064392 | tf_op jit(solution)/shard_map/ppermute | solution.py:413
  114.8 13.5 %copy-start.2 = (bf16[384,1792]{1,0:T(8,128)(2,1)}, bf16[384,1792]{1,0:T(8,128)(2,1)S(1)}, u32[]{:S(2)}) copy-start(bf16[384,1792]{1,0:T(8,128)(2,1)S(1)} %collective-permute-done.23.refs_1_) | copy-start | bytes 4128772
  114.8 17.6 %collective-permute-start.18 = (bf16[384,896]{1,0:T(8,128)(2,1)S(1)}, bf16[384,896]{1,0:T(8,128)(2,1)S(1)}, u32[]{:S(2)}, u32[]{:S(2)}) collective-permute-start(bf16[384,896]{1,0:T(8,128)(2,1)S(1)} %collective-permute-done.7.refs_2_), channel_id=1, source_target_pairs={{0,1},{1,0},{4,5},{5,4},{8,9},{9,8},{12,13},{13,12},{14,15},{15,14... | collective-permute-start | bytes 2064392 | tf_op jit(solution)/shard_map/ppermute | solution.py:413
  115.3 28.7 %collective-permute-start.16 = (bf16[384,896]{1,0:T(8,128)(2,1)S(1)}, bf16[384,896]{1,0:T(8,128)(2,1)S(1)}, u32[]{:S(2)}, u32[]{:S(2)}) collective-permute-start(bf16[384,896]{1,0:T(8,128)(2,1)S(1)} %collective-permute-done.15.refs_2_), channel_id=1, source_target_pairs={{0,1},{1,0},{4,5},{5,4},{8,9},{9,8},{12,13},{13,12},{14,15},{15,14... | collective-permute-start | bytes 2064392 | tf_op jit(solution)/shard_map/ppermute | solution.py:413
  116.9 27.8 %collective-permute-start.17 = (bf16[384,896]{1,0:T(8,128)(2,1)S(1)}, bf16[384,896]{1,0:T(8,128)(2,1)S(1)}, u32[]{:S(2)}, u32[]{:S(2)}) collective-permute-start(bf16[384,896]{1,0:T(8,128)(2,1)S(1)} %collective-permute-done.2.refs_0_), channel_id=1, source_target_pairs={{0,1},{1,0},{4,5},{5,4},{8,9},{9,8},{12,13},{13,12},{14,15},{15,14... | collective-permute-start | bytes 2064392 | tf_op jit(solution)/shard_map/ppermute | solution.py:413
  124.3 29.7 %collective-permute-start.12 = (bf16[384,896]{1,0:T(8,128)(2,1)S(1)}, bf16[384,896]{1,0:T(8,128)(2,1)S(1)}, u32[]{:S(2)}, u32[]{:S(2)}) collective-permute-start(bf16[384,896]{1,0:T(8,128)(2,1)S(1)} %collective-permute-done.11.refs_0_), channel_id=1, source_target_pairs={{0,1},{1,0},{4,5},{5,4},{8,9},{9,8},{12,13},{13,12},{14,15},{15,14... | collective-permute-start | bytes 2064392 | tf_op jit(solution)/shard_map/ppermute | solution.py:413
  128.3 16.2 %collective-permute-start.31 = (bf16[208,896]{1,0:T(8,128)(2,1)S(1)}, bf16[208,896]{1,0:T(8,128)(2,1)S(1)}, u32[]{:S(2)}, u32[]{:S(2)}) collective-permute-start(bf16[208,896]{1,0:T(8,128)(2,1)S(1)} %slice.52), channel_id=1, source_target_pairs={{0,4},{1,3},{4,8},{5,1},{8,12},{9,5},{12,14},{13,9},{14,10},{15,13... | collective-permute-start | bytes 1118216 | tf_op jit(solution)/shard_map/ppermute | solution.py:412
  132.4 11.7 %collective-permute-start.3 = (bf16[176,896]{1,0:T(8,128)(2,1)S(1)}, bf16[176,896]{1,0:T(8,128)(2,1)S(1)}, u32[]{:S(2)}, u32[]{:S(2)}) collective-permute-start(bf16[176,896]{1,0:T(8,128)(2,1)S(1)} %slice.46), channel_id=1, source_target_pairs={{0,4},{1,3},{4,8},{5,1},{8,12},{9,5},{12,14},{13,9},{14,10},{15,13... | collective-permute-start | bytes 946184 | tf_op jit(solution)/shard_map/ppermute | solution.py:412
  144.0 16.9 %collective-permute-start.9 = (bf16[176,896]{1,0:T(8,128)(2,1)S(1)}, bf16[176,896]{1,0:T(8,128)(2,1)S(1)}, u32[]{:S(2)}, u32[]{:S(2)}) collective-permute-start(bf16[176,896]{1,0:T(8,128)(2,1)S(1)} %collective-permute-done.8.refs_1_), channel_id=1, source_target_pairs={{0,1},{1,0},{4,5},{5,4},{8,9},{9,8},{12,13},{13,12},{14,15},{15,14... | collective-permute-start | bytes 946184 | tf_op jit(solution)/shard_map/ppermute | solution.py:413
  144.1 14.7 %collective-permute-start.34 = (bf16[208,896]{1,0:T(8,128)(2,1)S(1)}, bf16[208,896]{1,0:T(8,128)(2,1)S(1)}, u32[]{:S(2)}, u32[]{:S(2)}) collective-permute-start(bf16[208,896]{1,0:T(8,128)(2,1)S(1)} %collective-permute-done.33.refs_2_), channel_id=1, source_target_pairs={{0,1},{1,0},{4,5},{5,4},{8,9},{9,8},{12,13},{13,12},{14,15},{15,14... | collective-permute-start | bytes 1118216 | tf_op jit(solution)/shard_map/ppermute | solution.py:413
  144.6 16.3 %collective-permute-start.4 = (bf16[176,896]{1,0:T(8,128)(2,1)S(1)}, bf16[176,896]{1,0:T(8,128)(2,1)S(1)}, u32[]{:S(2)}, u32[]{:S(2)}) collective-permute-start(bf16[176,896]{1,0:T(8,128)(2,1)S(1)} %collective-permute-done.3.refs_0_), channel_id=1, source_target_pairs={{0,1},{1,0},{4,5},{5,4},{8,9},{9,8},{12,13},{13,12},{14,15},{15,14... | collective-permute-start | bytes 946184 | tf_op jit(solution)/shard_map/ppermute | solution.py:413
  144.7 14.2 %collective-permute-start.32 = (bf16[208,896]{1,0:T(8,128)(2,1)S(1)}, bf16[208,896]{1,0:T(8,128)(2,1)S(1)}, u32[]{:S(2)}, u32[]{:S(2)}) collective-permute-start(bf16[208,896]{1,0:T(8,128)(2,1)S(1)} %collective-permute-done.31.refs_0_), channel_id=1, source_target_pairs={{0,1},{1,0},{4,5},{5,4},{8,9},{9,8},{12,13},{13,12},{14,15},{15,14... | collective-permute-start | bytes 1118216 | tf_op jit(solution)/shard_map/ppermute | solution.py:413
  (3 other events, 19.6 us)
